TPU v7x, 512 devices: a whole 4x8x8 slice. The times are simulated.
512 devices in a mesh: range: 64 (over x, z, core), grp: 8 (over y).
Axes of the slice: x: 4, y: 8, z: 8, core: 2. Of those that a mesh axis runs over, the one named last changes fastest.
Arguments:
- amplitudes: float32 [512, 128, 16, 128], P(('range', 'grp')), may hold values from -6 to 6
- integrals: float32 [65536, 1024], P(('range', 'grp')), may hold values from -0.046875 to 0.046875
- occupancy: int32 [512, 128], P(('range', 'grp')), may hold values from 0 to 511, as said below
- tile_place: int32 [512], replicated, may hold values from 0 to 511, as said below
Outputs:
- ladder: float32 [8192, 1024], P(('range', 'grp'))
Inputs may be any that keep to these rules, and one draw needn't show every extreme that they name: `occupancy`: each block row lists 128 distinct contracted tiles. At most 4 tiles of one block row have tile_place // 8 equal to the same value, and in every draw one such value is reached by exactly 4 tiles in every block row. `tile_place`: a permutation of 0 to 511; the range index tile_place[k] // 8 owns tile k.
All inputs are finite; a program needn't handle non-finite values.
Results may differ from a plain program's by a relative error of at most 0.0003.
Values sent between devices are 32-bit elements; how exact they have to be, the bound alone decides.
No kernel may reach another device: no remote copies, remote signals or barrier semaphores. Data moves between devices by JAX's collectives and lax.ppermute only.
A program may use at most 64 MiB of HBM per device.

v0:
```python
import jax
import jax.numpy as jnp
from jax import lax
from jax.sharding import PartitionSpec as P


def on_device(amplitudes, integrals, occupancy, tile_place):
    n_range = lax.axis_size("range")
    kt_dev = tile_place.shape[0] // n_range
    tile_rows = amplitudes.shape[2]
    tile_width = amplitudes.shape[3]
    panel_rows = lax.all_gather(integrals, "grp", axis=0, tiled=True)
    out_cols = panel_rows.shape[1]
    panel_blocks = panel_rows.reshape(kt_dev, tile_width, out_cols)
    amp_tiles = amplitudes[0]
    occ_list = occupancy[0]
    places = tile_place[occ_list]
    outgoing = (
        jnp.zeros((n_range * kt_dev, tile_rows, tile_width), jnp.float32).at[places].set(amp_tiles)
    )
    outgoing = outgoing.reshape(n_range, kt_dev, tile_rows, tile_width)
    by_slot = lax.all_to_all(outgoing, "range", split_axis=0, concat_axis=0, tiled=True)
    partial_value = jnp.einsum(
        "nsrt,stc->nrc", by_slot, panel_blocks, precision=lax.Precision.HIGHEST
    )
    partial_value = partial_value.reshape(n_range * tile_rows, out_cols)
    return lax.psum_scatter(partial_value, "range", scatter_dimension=0, tiled=True)


def solution(mesh):
    return jax.shard_map(
        on_device,
        mesh=mesh,
        in_specs=(
            P(("range", "grp"), None, None, None),
            P(("range", "grp"), None),
            P(("range", "grp"), None),
            P(),
        ),
        out_specs=P(("range", "grp"), None),
        check_vma=False,
    )
```

profile of v0, /device:TPU:8, one launch (start us, length us, event | category | flops | bytes accessed | tf_op | source)
XLA Modules:
  0.0 312.9 jit_solution(7821422313293247114)
XLA Ops:
  6.5 0.0 copy-start
  6.5 0.0 copy-start.1
  6.5 0.7 fusion
  7.3 0.0 copy-done
  7.3 1.3 gather_fusion
  8.6 2.2 broadcast_in_dim.2
  10.8 0.0 copy-done.1
  10.8 13.7 %scatter_fusion = f32[512,16,128]{2,1,0:T(8,128)} fusion(f32[512,16,128]{2,1,0:T(8,128)} %broadcast_in_dim.2, s32[128]{0:T(128)S(1)} %fusion.1, f32[128,16,128]{2,1,0:T(8,128)S(1)} %bitcast.19), kind=kCustom, calls=%fused_computation.1 | custom fusion | bytes 3146240 | tf_op jit(solution)/shard_map/scatter | solution.py:19
  24.5 14.0 %all-to-all-start = ((f32[64,8,16,128]{3,2,1,0:T(8,128)}), f32[64,8,16,128]{3,2,1,0:T(8,128)}, u32[]{:S(2)}, u32[]{:S(2)}) async-start(f32[64,8,16,128]{3,2,1,0:T(8,128)} %bitcast.17), calls=%async_computation | async-start | bytes 8388608 | tf_op jit(solution)/shard_map/all_to_all | solution.py:22
  38.6 0.0 all-gather.2.cloned.1.call-start
  38.6 0.7 all-gather.2.cloned.1.call-update
  39.3 0.0 reduce-scatter.2.cloned.1.call-start
  39.3 94.9 %all-to-all-done = f32[64,8,16,128]{3,2,1,0:T(8,128)} async-done(((f32[64,8,16,128]{3,2,1,0:T(8,128)}), f32[64,8,16,128]{3,2,1,0:T(8,128)}, u32[]{:S(2)}, u32[]{:S(2)}) %all-to-all-start) | async-done | bytes 4194336 | tf_op jit(solution)/shard_map/all_to_all | solution.py:22
  134.3 4.5 %copy.5 = f32[64,16,8,128]{3,1,0,2:T(8,128)} copy(f32[64,16,8,128]{3,1,2,0:T(8,128)} %bitcast.6) | data formatting | bytes 8388608 | tf_op jit(solution)/shard_map/nsrt,stc->nrc/dot_general | solution.py:23
  138.8 0.0 all-gather.2.cloned.1.call-done
  138.8 17.6 %convolution_bitcast_fusion = f32[1024,1024]{1,0:T(8,128)} fusion(f32[1024,8,128]{2,0,1:T(8,128)} %bitcast.18, f32[8,128,1024]{2,1,0:T(8,128)} %bitcast.20), kind=kOutput, calls=%fused_computation.2 | convolution fusion | flops 12884901888 | bytes 12582912 | tf_op jit(solution)/shard_map/nsrt,stc->nrc/dot_general | solution.py:23
  156.4 0.0 reduce-scatter.2.cloned.1.call-update
  156.4 149.6 %reduce-scatter.2.cloned.1.call-done = f32[16,1024]{1,0:T(8,128)} async-done(((f32[1024,1024]{1,0:T(8,128)}), f32[16,1024]{1,0:T(8,128)}) %reduce-scatter.2.cloned.1.call-update) | async-done | bytes 65552 | tf_op jit(solution)/shard_map/reduce_scatter | solution.py:27
  (2 shorter events, 0.0 us)
Async XLA Ops:
  6.5 0.8 copy-start
  6.5 4.3 %copy-start.1 = (f32[1,128,16,128]{3,2,1,0:T(8,128)S(1)}, f32[1,128,16,128]{3,2,1,0:T(8,128)}, u32[]{:S(2)}) copy-start(f32[1,128,16,128]{3,2,1,0:T(8,128)} %param.4) | copy-start | bytes 3145732
  24.5 109.7 %all-to-all-start = ((f32[64,8,16,128]{3,2,1,0:T(8,128)}), f32[64,8,16,128]{3,2,1,0:T(8,128)}, u32[]{:S(2)}, u32[]{:S(2)}) async-start(f32[64,8,16,128]{3,2,1,0:T(8,128)} %bitcast.17), calls=%async_computation | async-start | bytes 8388608 | tf_op jit(solution)/shard_map/all_to_all | solution.py:22
  38.6 100.2 %all-gather.2.cloned.1.call-start = ((), (), s32[]{:S(2)}) async-start(), calls=%async_computation.2 | async-start | bytes 4718592 | tf_op jit(solution)/shard_map/all_gather | solution.py:12
  39.3 266.7 %reduce-scatter.2.cloned.1.call-start = ((), (), s32[]{:S(2)}) async-start(), calls=%async_computation.3 | async-start | bytes 4259840 | tf_op jit(solution)/shard_map/reduce_scatter | solution.py:27
Sparse Core Ops, SparseCore 0:
  41.5 56.7 all-gather.1
  156.5 149.4 reduce-scatter.1
where the time goes:
time: 314 us; the launch traced here: 313 us
  waiting for transfers between devices  245 us (78%)
  local copies, waits for them, and re-layouts  21.7 us (7%)
  matrix products  17.6 us (6%)
  starting transfers between devices  14.1 us (4%)
  between operations  13.4 us (4%)
    reduce_scatter x1, waiting for transfers between devices, on_device(): lax.psum_scatter(partial_value, 'range', scatter_dimension=0, tiled=True)  150 us
    all_to_all x1, waiting for transfers between devices, on_device(): lax.all_to_all(outgoing, 'range', split_axis=0, concat_axis=0, tiled=True)  94.9 us
    dot_general x1, matrix products, on_device(): jnp.einsum('nsrt,stc->nrc', by_slot, panel_blocks, precision=lax.Precisio...  17.6 us
    all_to_all x1, starting transfers between devices, on_device(): lax.all_to_all(outgoing, 'range', split_axis=0, concat_axis=0, tiled=True)  14 us
    scatter x1, local copies, waits for them, and re-layouts, on_device(): jnp.zeros((n_range * kt_dev, tile_rows, tile_width), jnp.float32).at[places]  13.7 us
  transfers between devices with their start and end apart: 3, of which 2 were waited for; matrix products, arithmetic and copies ran while one was open for 1% of the time, Pallas kernels for 0%

commit v1 on v0

v1 whole, which is shorter than its diff:
```python
import jax
import jax.numpy as jnp
import numpy as np
from jax import lax
from jax.experimental import pallas as pl
from jax.experimental.pallas import tpu as pltpu
from jax.sharding import Mesh, PartitionSpec as P

NX, NZ, NC = 4, 8, 2
CAP = 4
RANGE = ("x", "z", "core")
VMEM = pl.BlockSpec(memory_space=pltpu.VMEM)
SMEM = pl.BlockSpec(memory_space=pltpu.SMEM)


def pack_kernel(n_tiles, occ_ref, place_ref, amp_ref, out_ref, slot_ref, count_ref):
    slot_ref[...] = jnp.full(slot_ref.shape, -1, jnp.int32)

    def clear(i, carry):
        count_ref[i] = 0
        return carry

    lax.fori_loop(0, count_ref.shape[0], clear, 0)

    def step(j, carry):
        place = place_ref[occ_ref[j]]
        owner = place // n_tiles
        tile = place % n_tiles
        slot = count_ref[owner]
        count_ref[owner] = slot + 1
        out_ref[owner * CAP + slot] = amp_ref[j]
        slot_ref[owner, pl.ds(slot, 1), :] = jnp.full((1, 128), tile, jnp.int32)
        return carry

    lax.fori_loop(0, occ_ref.shape[0], step, 0, unroll=4)


def pack(occ, place, amp, n_range, n_tiles):
    occ_n, rows, width = amp.shape
    return pl.pallas_call(
        lambda *refs: pack_kernel(n_tiles, *refs),
        out_shape=(
            jax.ShapeDtypeStruct((n_range * CAP, rows, width), jnp.float32),
            jax.ShapeDtypeStruct((n_range, 8, 128), jnp.int32),
        ),
        in_specs=[SMEM, SMEM, VMEM],
        out_specs=(VMEM, VMEM),
        scratch_shapes=[pltpu.SMEM((n_range,), jnp.int32)],
        cost_estimate=pl.CostEstimate(flops=0, bytes_accessed=8 << 20, transcendentals=0),
        name="pack",
    )(occ, place, amp)


def spread_kernel(n_tiles, slot_ref, pos_ref, in_ref, out_ref):
    rows = in_ref.shape[1]
    n_src = slot_ref.shape[0]
    core, grp = pos_ref[0], pos_ref[1]
    out_ref[...] = jnp.zeros_like(out_ref)

    def step(n, carry):
        half = 1 - ((n % NC) ^ core)
        row = pl.multiple_of((half * (n_src // NC) + n // NC) * rows, rows)
        for s in range(CAP):
            tile = slot_ref[n, s]

            @pl.when(tile >= 0)
            def _():
                col = pl.multiple_of(((grp - tile + n_tiles) % n_tiles) * 128, 128)
                out_ref[pl.ds(row, rows), pl.ds(col, 128)] = in_ref[n * CAP + s]

        return carry

    lax.fori_loop(0, n_src, step, 0)


def spread(slots, pos, tiles, n_tiles):
    n_src = slots.shape[0]
    rows, width = tiles.shape[1:]
    return pl.pallas_call(
        lambda *refs: spread_kernel(n_tiles, *refs),
        out_shape=jax.ShapeDtypeStruct((n_src * rows, n_tiles * width), jnp.float32),
        in_specs=[SMEM, SMEM, VMEM],
        out_specs=VMEM,
        cost_estimate=pl.CostEstimate(flops=0, bytes_accessed=8 << 20, transcendentals=0),
        name="spread",
    )(slots, pos, tiles)


def ring(n, step):
    return [(i, (i + step) % n) for i in range(n)]


def gather_panel(block):
    n = lax.axis_size("grp")
    right, left = [block], [block]
    half = block.shape[0] // 2
    for _ in range(n // 2 - 1):
        right.append(lax.ppermute(right[-1], "grp", ring(n, 1)))
        left.append(lax.ppermute(left[-1], "grp", ring(n, -1)))
    far_top = lax.ppermute(right[-1][:half], "grp", ring(n, 1))
    far_bottom = lax.ppermute(left[-1][half:], "grp", ring(n, -1))
    return jnp.concatenate(right + [far_top, far_bottom] + left[:0:-1], axis=0)


def on_device(amplitudes, integrals, occupancy, tile_place):
    n_range = NX * NZ * NC
    n_tiles = tile_place.shape[0] // n_range
    rows, width = amplitudes.shape[2:]
    out_cols = integrals.shape[1]
    panel = gather_panel(integrals)
    sent, slots = pack(occupancy[0], tile_place, amplitudes[0], n_range, n_tiles)
    sent = sent.reshape(n_range, CAP, rows, width)
    tiles = lax.all_to_all(sent, RANGE, 0, 0, tiled=True)
    slots = lax.all_to_all(slots, RANGE, 0, 0, tiled=True)[:, :CAP, 0]
    pos = jnp.stack([lax.axis_index("core"), lax.axis_index("grp")]).astype(jnp.int32)
    left = spread(slots, pos, tiles.reshape(n_range * CAP, rows, width), n_tiles)
    half = left.shape[0] // NC
    other = jnp.dot(left[:half], panel, precision=lax.Precision.HIGH)
    other = lax.ppermute(other, "core", ring(NC, 1))
    mine = jnp.dot(left[half:], panel, precision=lax.Precision.HIGH) + other
    mine = mine.reshape(NX, half // NX, out_cols)
    mine = lax.all_to_all(mine, "x", 0, 0, tiled=True).sum(axis=0)
    mine = mine.reshape(NZ, rows, out_cols)
    return lax.all_to_all(mine, "z", 0, 0, tiled=True).sum(axis=0)


def solution(mesh):
    split = Mesh(mesh.devices.reshape(NX, NZ, NC, -1), RANGE + ("grp",))
    every = RANGE + ("grp",)
    return jax.shard_map(
        on_device,
        mesh=split,
        in_specs=(
            P(every, None, None, None),
            P(every, None),
            P(every, None),
            P(),
        ),
        out_specs=P(every, None),
        check_vma=False,
    )
```

time: 314 us -> 186 us (0.59)
  the two profiles are of different devices: /device:TPU:8 before, /device:TPU:24 now
where the time goes in v1:
time: 186 us; the launch traced here: 185 us
  blocking collectives  79.8 us (43%)
  starting transfers between devices  37.1 us (20%)
  waiting for transfers between devices  30.6 us (16%)
  local copies, waits for them, and re-layouts  14.1 us (8%)
  Pallas kernels  11.9 us (6%)
  matrix products  9.99 us (5%)
    all_to_all x1, blocking collectives, on_device(): mine = lax.all_to_all(mine, 'x', 0, 0, tiled=True).sum(axis=0)  31.8 us
    all_to_all x1, blocking collectives, on_device(): slots = lax.all_to_all(slots, RANGE, 0, 0, tiled=True)[:, :CAP, 0]  25.8 us
    ppermute x3, waiting for transfers between devices, gather_panel(): right.append(lax.ppermute(right[-1], 'grp', ring(n, 1)))  22.4 us
    all_to_all x1, blocking collectives, on_device(): return lax.all_to_all(mine, 'z', 0, 0, tiled=True).sum(axis=0)  22.2 us
    ppermute x3, starting transfers between devices, gather_panel(): right.append(lax.ppermute(right[-1], 'grp', ring(n, 1)))  16 us
    unnamed x23, local copies, waits for them, and re-layouts  13.2 us
    pallas_call x1, Pallas kernels, spread(): pl.pallas_call(lambda *refs: spread_kernel(n_tiles, *refs), out_shape=jax...  7.44 us
    dot_general x1, matrix products, on_device(): other = jnp.dot(left[:half], panel, precision=lax.Precision.HIGH)  6.43 us
  transfers between devices with their start and end apart: 10, of which 5 were waited for; matrix products, arithmetic and copies ran while one was open for 7% of the time, Pallas kernels for 0%

profile of v1, /device:TPU:24, one launch (start us, length us, event | category | flops | bytes accessed | tf_op | source)
XLA Modules:
  0.0 185.1 jit_solution(9146138324052030623)
XLA Ops:
  0.0 4.5 %pack.1 = (f32[256,16,128]{2,1,0:T(8,128)}, s32[64,8,128]{2,1,0:T(8,128)}) custom-call(s32[128]{0:T(128)} %bitcast.17, s32[512]{0:T(512)} %refs_1_.1, f32[128,16,128]{2,1,0:T(8,128)} %bitcast.15), custom_call_target="tpu_custom_call" | custom-call | bytes 8388608 | tf_op jit(solution)/shard_map/pack/pallas_call | solution.py:40
  4.5 25.8 %all_to_all.20 = s32[64,8,128]{2,1,0:T(8,128)S(1)} all-to-all(s32[64,8,128]{2,1,0:T(8,128)} %get-tuple-element.7), channel_id=1, replica_groups=mesh['x'=4,'z'=8,'core'=2,'grp'=8] {'x','z','core'}, dimensions={0} | all-to-all | bytes 524288 | tf_op jit(solution)/shard_map/all_to_all | solution.py:114
  30.3 6.0 %all-to-all-start.1 = ((f32[64,4,16,128]{3,2,1,0:T(8,128)}), f32[64,4,16,128]{3,2,1,0:T(8,128)S(1)}, u32[]{:S(2)}, u32[]{:S(2)}) async-start(f32[64,4,16,128]{3,2,1,0:T(8,128)} %bitcast.13), calls=%async_computation.1 | async-start | bytes 4194304 | tf_op jit(solution)/shard_map/all_to_all | solution.py:113
  36.3 4.7 %collective-permute-start = (f32[128,1024]{1,0:T(8,128)S(1)}, f32[128,1024]{1,0:T(8,128)S(1)}, u32[]{:S(2)}, u32[]{:S(2)}) collective-permute-start(f32[128,1024]{1,0:T(8,128)S(1)} %copy-done.3), channel_id=1, source_target_pairs={{0,1},{1,2},{2,3},{3,4},{4,5},{5,6},{6,7},{7,0},{8,9},{9,10},{10,1... | collective-permute-start | bytes 1572872 | tf_op jit(solution)/shard_map/ppermute | solution.py:98
  41.0 1.9 %collective-permute-start.4 = (f32[128,1024]{1,0:T(8,128)S(1)}, f32[128,1024]{1,0:T(8,128)S(1)}, u32[]{:S(2)}, u32[]{:S(2)}) collective-permute-start(f32[128,1024]{1,0:T(8,128)S(1)} %copy-done.3), channel_id=1, source_target_pairs={{0,7},{1,0},{2,1},{3,2},{4,3},{5,4},{6,5},{7,6},{8,15},{9,8},{10,9... | collective-permute-start | bytes 1572872 | tf_op jit(solution)/shard_map/ppermute | solution.py:99
  42.9 9.5 %collective-permute-done = f32[128,1024]{1,0:T(8,128)S(1)} collective-permute-done((f32[128,1024]{1,0:T(8,128)S(1)}, f32[128,1024]{1,0:T(8,128)S(1)}, u32[]{:S(2)}, u32[]{:S(2)}) %collective-permute-start) | collective-permute-done | bytes 524320 | tf_op jit(solution)/shard_map/ppermute | solution.py:98
  52.4 5.6 %collective-permute-start.1 = (f32[128,1024]{1,0:T(8,128)S(1)}, f32[128,1024]{1,0:T(8,128)}, u32[]{:S(2)}, u32[]{:S(2)}) collective-permute-start(f32[128,1024]{1,0:T(8,128)S(1)} %collective-permute-done), channel_id=1, source_target_pairs={{0,1},{1,2},{2,3},{3,4},{4,5},{5,6},{6,7},{7,0},{8,9},{9,10},{10,1... | collective-permute-start | bytes 1572872 | tf_op jit(solution)/shard_map/ppermute | solution.py:98
  58.0 1.9 %collective-permute-start.5 = (f32[128,1024]{1,0:T(8,128)S(1)}, f32[128,1024]{1,0:T(8,128)}, u32[]{:S(2)}, u32[]{:S(2)}) collective-permute-start(f32[128,1024]{1,0:T(8,128)S(1)} %collective-permute-done.4), channel_id=1, source_target_pairs={{0,7},{1,0},{2,1},{3,2},{4,3},{5,4},{6,5},{7,6},{8,15},{9,8},{10,9... | collective-permute-start | bytes 1572872 | tf_op jit(solution)/shard_map/ppermute | solution.py:99
  59.9 8.6 %collective-permute-done.1 = f32[128,1024]{1,0:T(8,128)} collective-permute-done((f32[128,1024]{1,0:T(8,128)S(1)}, f32[128,1024]{1,0:T(8,128)}, u32[]{:S(2)}, u32[]{:S(2)}) %collective-permute-start.1) | collective-permute-done | bytes 524320 | tf_op jit(solution)/shard_map/ppermute | solution.py:98
  68.5 5.7 %collective-permute-start.2 = (f32[128,1024]{1,0:T(8,128)}, f32[128,1024]{1,0:T(8,128)S(1)}, u32[]{:S(2)}, u32[]{:S(2)}) collective-permute-start(f32[128,1024]{1,0:T(8,128)} %collective-permute-done.1), channel_id=1, source_target_pairs={{0,1},{1,2},{2,3},{3,4},{4,5},{5,6},{6,7},{7,0},{8,9},{9,10},{10,1... | collective-permute-start | bytes 1572872 | tf_op jit(solution)/shard_map/ppermute | solution.py:98
  74.3 1.9 %collective-permute-start.6 = (f32[128,1024]{1,0:T(8,128)}, f32[128,1024]{1,0:T(8,128)S(1)}, u32[]{:S(2)}, u32[]{:S(2)}) collective-permute-start(f32[128,1024]{1,0:T(8,128)} %collective-permute-done.5), channel_id=1, source_target_pairs={{0,7},{1,0},{2,1},{3,2},{4,3},{5,4},{6,5},{7,6},{8,15},{9,8},{10,9... | collective-permute-start | bytes 1572872 | tf_op jit(solution)/shard_map/ppermute | solution.py:99
  79.8 4.4 %collective-permute-done.2 = f32[128,1024]{1,0:T(8,128)S(1)} collective-permute-done((f32[128,1024]{1,0:T(8,128)}, f32[128,1024]{1,0:T(8,128)S(1)}, u32[]{:S(2)}, u32[]{:S(2)}) %collective-permute-start.2) | collective-permute-done | bytes 524320 | tf_op jit(solution)/shard_map/ppermute | solution.py:98
  84.2 5.5 %collective-permute-start.3 = (f32[64,1024]{1,0:T(8,128)S(1)}, f32[64,1024]{1,0:T(8,128)S(1)}, u32[]{:S(2)}, u32[]{:S(2)}) collective-permute-start(f32[64,1024]{1,0:T(8,128)S(1)} %slice.22), channel_id=1, source_target_pairs={{0,1},{1,2},{2,3},{3,4},{4,5},{5,6},{6,7},{7,0},{8,9},{9,10},{10,1... | collective-permute-start | bytes 786440 | tf_op jit(solution)/shard_map/ppermute | solution.py:100
  89.7 1.9 %constant_dynamic-update-slice_fusion.7 = f32[1024,1024]{1,0:T(8,128)} fusion(f32[1024,1024]{1,0:T(8,128)} %constant_dynamic-update-slice_fusion.8, f32[128,1024]{1,0:T(8,128)} %copy-done.6), kind=kLoop, calls=%fused_computation.12 | loop fusion | bytes 1048576
  91.6 1.9 %collective-permute-start.7 = (f32[64,1024]{1,0:T(8,128)S(1)}, f32[64,1024]{1,0:T(8,128)S(1)}, u32[]{:S(2)}, u32[]{:S(2)}) collective-permute-start(f32[64,1024]{1,0:T(8,128)S(1)} %slice.23), channel_id=1, source_target_pairs={{0,7},{1,0},{2,1},{3,2},{4,3},{5,4},{6,5},{7,6},{8,15},{9,8},{10,9... | collective-permute-start | bytes 786440 | tf_op jit(solution)/shard_map/ppermute | solution.py:101
  93.5 1.9 %constant_dynamic-update-slice_fusion.6 = f32[1024,1024]{1,0:T(8,128)} fusion(f32[1024,1024]{1,0:T(8,128)} %constant_dynamic-update-slice_fusion.7, f32[128,1024]{1,0:T(8,128)} %collective-permute-done.1), kind=kLoop, calls=%fused_computation.11 | loop fusion | bytes 1048576
  97.0 4.1 %collective-permute-done.7 = f32[64,1024]{1,0:T(8,128)S(1)} collective-permute-done((f32[64,1024]{1,0:T(8,128)S(1)}, f32[64,1024]{1,0:T(8,128)S(1)}, u32[]{:S(2)}, u32[]{:S(2)}) %collective-permute-start.7) | collective-permute-done | bytes 262176 | tf_op jit(solution)/shard_map/ppermute | solution.py:101
  106.7 7.4 %spread.1 = f32[1024,1024]{1,0:T(8,128)} custom-call(s32[64,4]{1,0:T(8,128)} %bitcast.16, s32[2]{0:T(128)} %pad_add_fusion.refs_1_, f32[256,16,128]{2,1,0:T(8,128)} %bitcast.11), custom_call_target="tpu_custom_call" | custom-call | bytes 8388608 | tf_op jit(solution)/shard_map/spread/pallas_call | solution.py:79
  114.2 6.4 %fusion = f32[512,1024]{1,0:T(8,128)S(1)} fusion(f32[1024,1024]{1,0:T(8,128)} %constant_dynamic-update-slice_fusion, f32[1024,1024]{1,0:T(8,128)} %spread.1), kind=kOutput, calls=%fused_computation | convolution fusion | flops 3221225472 | bytes 8388608 | tf_op jit(solution)/shard_map/dot_general | solution.py:118
  120.6 1.9 %collective-permute-start.8 = (f32[512,1024]{1,0:T(8,128)S(1)}, f32[512,1024]{1,0:T(8,128)S(1)}, u32[]{:S(2)}, u32[]{:S(2)}) collective-permute-start(f32[512,1024]{1,0:T(8,128)S(1)} %fusion), channel_id=1, source_target_pairs={{0,8},{8,0},{1,9},{9,1},{2,10},{10,2},{3,11},{11,3},{4,12},{12,4},... | collective-permute-start | bytes 6291464 | tf_op jit(solution)/shard_map/ppermute | solution.py:119
  122.6 4.1 %collective-permute-done.8 = f32[512,1024]{1,0:T(8,128)S(1)} collective-permute-done((f32[512,1024]{1,0:T(8,128)S(1)}, f32[512,1024]{1,0:T(8,128)S(1)}, u32[]{:S(2)}, u32[]{:S(2)}) %collective-permute-start.8) | collective-permute-done | bytes 2097184 | tf_op jit(solution)/shard_map/ppermute | solution.py:119
  126.7 3.6 %fusion.4 = f32[512,1024]{1,0:T(8,128)S(1)} fusion(f32[512,1024]{1,0:T(8,128)S(1)} %collective-permute-done.8, f32[1024,1024]{1,0:T(8,128)S(1)} %copy-done, f32[1024,1024]{1,0:T(8,128)S(1)} %copy-done.1), kind=kOutput, calls=%fused_computation.4 | convolution fusion | flops 3221749760 | bytes 10485760 | tf_op jit(solution)/shard_map/dot_general | solution.py:120
  130.3 31.8 %all_to_all.21 = f32[4,128,1024]{2,1,0:T(8,128)S(1)} all-to-all(f32[4,128,1024]{2,1,0:T(8,128)S(1)} %bitcast.12), channel_id=1, replica_groups=mesh['x'=4,'z'=8,'core'=2,'grp'=8] {'x'}, dimensions={0} | all-to-all | bytes 4194304 | tf_op jit(solution)/shard_map/all_to_all | solution.py:122
  162.2 22.2 %all_to_all.22 = f32[8,16,1024]{2,1,0:T(8,128)S(1)} all-to-all(f32[8,16,1024]{2,1,0:T(8,128)S(1)} %bitcast.14), channel_id=1, replica_groups=mesh['x'=4,'z'=8,'core'=2,'grp'=8] {'z'}, dimensions={0} | all-to-all | bytes 1048576 | tf_op jit(solution)/shard_map/all_to_all | solution.py:124
  (33 shorter events, 11.7 us)
Async XLA Ops:
  0.0 36.3 %copy-start.3 = (f32[128,1024]{1,0:T(8,128)S(1)}, f32[128,1024]{1,0:T(8,128)}, u32[]{:S(2)}) copy-start(f32[128,1024]{1,0:T(8,128)} %param.5) | copy-start | bytes 1572868
  30.3 75.1 %all-to-all-start.1 = ((f32[64,4,16,128]{3,2,1,0:T(8,128)}), f32[64,4,16,128]{3,2,1,0:T(8,128)S(1)}, u32[]{:S(2)}, u32[]{:S(2)}) async-start(f32[64,4,16,128]{3,2,1,0:T(8,128)} %bitcast.13), calls=%async_computation.1 | async-start | bytes 4194304 | tf_op jit(solution)/shard_map/all_to_all | solution.py:113
  36.3 16.1 %collective-permute-start = (f32[128,1024]{1,0:T(8,128)S(1)}, f32[128,1024]{1,0:T(8,128)S(1)}, u32[]{:S(2)}, u32[]{:S(2)}) collective-permute-start(f32[128,1024]{1,0:T(8,128)S(1)} %copy-done.3), channel_id=1, source_target_pairs={{0,1},{1,2},{2,3},{3,4},{4,5},{5,6},{6,7},{7,0},{8,9},{9,10},{10,1... | collective-permute-start | bytes 1572872 | tf_op jit(solution)/shard_map/ppermute | solution.py:98
  41.0 17.0 %collective-permute-start.4 = (f32[128,1024]{1,0:T(8,128)S(1)}, f32[128,1024]{1,0:T(8,128)S(1)}, u32[]{:S(2)}, u32[]{:S(2)}) collective-permute-start(f32[128,1024]{1,0:T(8,128)S(1)} %copy-done.3), channel_id=1, source_target_pairs={{0,7},{1,0},{2,1},{3,2},{4,3},{5,4},{6,5},{7,6},{8,15},{9,8},{10,9... | collective-permute-start | bytes 1572872 | tf_op jit(solution)/shard_map/ppermute | solution.py:99
  52.4 21.9 %copy-start.6 = (f32[128,1024]{1,0:T(8,128)}, f32[128,1024]{1,0:T(8,128)S(1)}, u32[]{:S(2)}) copy-start(f32[128,1024]{1,0:T(8,128)S(1)} %collective-permute-done) | copy-start | bytes 1572868
  52.4 16.1 %collective-permute-start.1 = (f32[128,1024]{1,0:T(8,128)S(1)}, f32[128,1024]{1,0:T(8,128)}, u32[]{:S(2)}, u32[]{:S(2)}) collective-permute-start(f32[128,1024]{1,0:T(8,128)S(1)} %collective-permute-done), channel_id=1, source_target_pairs={{0,1},{1,2},{2,3},{3,4},{4,5},{5,6},{6,7},{7,0},{8,9},{9,10},{10,1... | collective-permute-start | bytes 1572872 | tf_op jit(solution)/shard_map/ppermute | solution.py:98
  58.0 16.2 %copy-start.4 = (f32[128,1024]{1,0:T(8,128)}, f32[128,1024]{1,0:T(8,128)S(1)}, u32[]{:S(2)}) copy-start(f32[128,1024]{1,0:T(8,128)S(1)} %collective-permute-done.4) | copy-start | bytes 1572868
  58.0 16.2 %collective-permute-start.5 = (f32[128,1024]{1,0:T(8,128)S(1)}, f32[128,1024]{1,0:T(8,128)}, u32[]{:S(2)}, u32[]{:S(2)}) collective-permute-start(f32[128,1024]{1,0:T(8,128)S(1)} %collective-permute-done.4), channel_id=1, source_target_pairs={{0,7},{1,0},{2,1},{3,2},{4,3},{5,4},{6,5},{7,6},{8,15},{9,8},{10,9... | collective-permute-start | bytes 1572872 | tf_op jit(solution)/shard_map/ppermute | solution.py:99
  68.5 15.6 %collective-permute-start.2 = (f32[128,1024]{1,0:T(8,128)}, f32[128,1024]{1,0:T(8,128)S(1)}, u32[]{:S(2)}, u32[]{:S(2)}) collective-permute-start(f32[128,1024]{1,0:T(8,128)} %collective-permute-done.1), channel_id=1, source_target_pairs={{0,1},{1,2},{2,3},{3,4},{4,5},{5,6},{6,7},{7,0},{8,9},{9,10},{10,1... | collective-permute-start | bytes 1572872 | tf_op jit(solution)/shard_map/ppermute | solution.py:98
  74.3 17.3 %collective-permute-start.6 = (f32[128,1024]{1,0:T(8,128)}, f32[128,1024]{1,0:T(8,128)S(1)}, u32[]{:S(2)}, u32[]{:S(2)}) collective-permute-start(f32[128,1024]{1,0:T(8,128)} %collective-permute-done.5), channel_id=1, source_target_pairs={{0,7},{1,0},{2,1},{3,2},{4,3},{5,4},{6,5},{7,6},{8,15},{9,8},{10,9... | collective-permute-start | bytes 1572872 | tf_op jit(solution)/shard_map/ppermute | solution.py:99
  79.8 24.7 %copy-start.5 = (f32[128,1024]{1,0:T(8,128)S(1)}, f32[128,1024]{1,0:T(8,128)}, u32[]{:S(2)}) copy-start(f32[128,1024]{1,0:T(8,128)} %copy-done.4) | copy-start | bytes 1572868
  84.2 12.1 %collective-permute-start.3 = (f32[64,1024]{1,0:T(8,128)S(1)}, f32[64,1024]{1,0:T(8,128)S(1)}, u32[]{:S(2)}, u32[]{:S(2)}) collective-permute-start(f32[64,1024]{1,0:T(8,128)S(1)} %slice.22), channel_id=1, source_target_pairs={{0,1},{1,2},{2,3},{3,4},{4,5},{5,6},{6,7},{7,0},{8,9},{9,10},{10,1... | collective-permute-start | bytes 786440 | tf_op jit(solution)/shard_map/ppermute | solution.py:100
  91.6 9.5 %collective-permute-start.7 = (f32[64,1024]{1,0:T(8,128)S(1)}, f32[64,1024]{1,0:T(8,128)S(1)}, u32[]{:S(2)}, u32[]{:S(2)}) collective-permute-start(f32[64,1024]{1,0:T(8,128)S(1)} %slice.23), channel_id=1, source_target_pairs={{0,7},{1,0},{2,1},{3,2},{4,3},{5,4},{6,5},{7,6},{8,15},{9,8},{10,9... | collective-permute-start | bytes 786440 | tf_op jit(solution)/shard_map/ppermute | solution.py:101
  105.4 1.4 copy-start.2
  114.2 12.5 %copy-start = (f32[1024,1024]{1,0:T(8,128)S(1)}, f32[1024,1024]{1,0:T(8,128)}, u32[]{:S(2)}) copy-start(f32[1024,1024]{1,0:T(8,128)} %constant_dynamic-update-slice_fusion) | copy-start | bytes 12582916
  114.2 12.5 %copy-start.1 = (f32[1024,1024]{1,0:T(8,128)S(1)}, f32[1024,1024]{1,0:T(8,128)}, u32[]{:S(2)}) copy-start(f32[1024,1024]{1,0:T(8,128)} %spread.1) | copy-start | bytes 12582916
  120.6 6.1 %collective-permute-start.8 = (f32[512,1024]{1,0:T(8,128)S(1)}, f32[512,1024]{1,0:T(8,128)S(1)}, u32[]{:S(2)}, u32[]{:S(2)}) collective-permute-start(f32[512,1024]{1,0:T(8,128)S(1)} %fusion), channel_id=1, source_target_pairs={{0,8},{8,0},{1,9},{9,1},{2,10},{10,2},{3,11},{11,3},{4,12},{12,4},... | collective-permute-start | bytes 6291464 | tf_op jit(solution)/shard_map/ppermute | solution.py:119

commit v2 on v0

v2 whole, which is shorter than its diff:
```python
import jax
import jax.numpy as jnp
from jax import lax
from jax.experimental import pallas as pl
from jax.experimental.pallas import tpu as pltpu
from jax.sharding import Mesh, PartitionSpec as P

NX, NZ, NC = 4, 8, 2
CAP = 4
CHIPS = ("x", "z")
EVERY = ("x", "z", "core", "grp")
LANES = 128
HEAD = 8
VMEM = pl.BlockSpec(memory_space=pltpu.VMEM)
SMEM = pl.BlockSpec(memory_space=pltpu.SMEM)
ANY = pl.BlockSpec(memory_space=pl.ANY)


def pack_kernel(per_chip, occ_ref, place_ref, amp_ref, out_ref, count_ref):
    rows = amp_ref.shape[1]
    heading = jnp.full((HEAD, LANES), -1.0, jnp.float32)
    lane = lax.broadcasted_iota(jnp.int32, (HEAD, LANES), 1)

    def clear(i, carry):
        count_ref[i] = 0
        out_ref[i, pl.ds(0, HEAD), :] = heading
        return carry

    lax.fori_loop(0, count_ref.shape[0], clear, 0)

    def step(j, carry):
        place = place_ref[occ_ref[j]]
        chip = place // per_chip
        tile = place % per_chip
        slot = count_ref[chip]
        count_ref[chip] = slot + 1
        out_ref[chip, pl.ds(pl.multiple_of(HEAD + slot * rows, 8), rows), :] = amp_ref[j]
        out_ref[chip, pl.ds(0, HEAD), :] = jnp.where(
            lane == slot, tile.astype(jnp.float32), out_ref[chip, pl.ds(0, HEAD), :]
        )
        return carry

    lax.fori_loop(0, occ_ref.shape[0], step, 0, unroll=4)


def pack(occ, place, amp, chips, per_chip):
    rows, width = amp.shape[1:]
    return pl.pallas_call(
        lambda *refs: pack_kernel(per_chip, *refs),
        out_shape=jax.ShapeDtypeStruct((chips, HEAD + NC * CAP * rows, width), jnp.float32),
        in_specs=[SMEM, SMEM, VMEM],
        out_specs=VMEM,
        scratch_shapes=[pltpu.SMEM((chips,), jnp.int32)],
        cost_estimate=pl.CostEstimate(flops=0, bytes_accessed=8 << 20, transcendentals=0),
        name="pack",
    )(occ, place, amp)


def split(value):
    high = value.astype(jnp.bfloat16)
    return high, (value - high.astype(jnp.float32)).astype(jnp.bfloat16)


def split_kernel(*refs):
    blocks, (high_ref, low_ref) = refs[:-2], refs[-2:]
    at = 0
    for ref in blocks:
        for i in range(0, ref.shape[0], 64):
            high, low = split(ref[i : i + 64, :])
            high_ref[at : at + 64, :] = high
            low_ref[at : at + 64, :] = low
            at += 64


def split_panel(blocks):
    depth = sum(block.shape[0] for block in blocks)
    out = jax.ShapeDtypeStruct((depth, blocks[0].shape[1]), jnp.bfloat16)
    return pl.pallas_call(
        split_kernel,
        out_shape=(out, out),
        in_specs=[VMEM] * len(blocks),
        out_specs=(VMEM, VMEM),
        cost_estimate=pl.CostEstimate(flops=0, bytes_accessed=8 * depth * 1024, transcendentals=0),
        name="split_panel",
    )(*blocks)


def ladder_kernel(pos_ref, got_hbm, high_hbm, low_hbm, out_ref, *scratch):
    got, head, where, v_high, v_low, a_high, a_low, sems = scratch
    chips = got.shape[0]
    per_chip = where.shape[0]
    per_core = per_chip // NC
    rows = out_ref.shape[0] // chips
    core, grp = pos_ref[0], pos_ref[1]
    copies = [
        pltpu.make_async_copy(got_hbm.at[:, pl.ds(0, HEAD), :], head, sems.at[0]),
        pltpu.make_async_copy(got_hbm, got, sems.at[1]),
        pltpu.make_async_copy(high_hbm, v_high, sems.at[2]),
        pltpu.make_async_copy(low_hbm, v_low, sems.at[3]),
    ]
    for copy in copies:
        copy.start()
    a_high[...] = jnp.zeros_like(a_high)
    a_low[...] = jnp.zeros_like(a_low)
    for of_core in range(NC):
        for of_grp in range(per_core):
            where[of_core * per_core + of_grp] = panel_position(core, grp, of_core, of_grp, per_core)
    copies[0].wait()
    copies[1].wait()

    def step(n, carry):
        row = pl.multiple_of(n * rows, rows)
        for s in range(NC * CAP):
            tile = head[n, 0, s].astype(jnp.int32)

            @pl.when(tile >= 0)
            def _():
                col = pl.multiple_of(where[tile] * LANES, LANES)
                high, low = split(got[n, HEAD + s * rows : HEAD + (s + 1) * rows, :])
                a_high[pl.ds(row, rows), pl.ds(col, LANES)] = high
                a_low[pl.ds(row, rows), pl.ds(col, LANES)] = low

        return carry

    lax.fori_loop(0, chips, step, 0)
    copies[2].wait()
    copies[3].wait()
    dot = lambda a, b: jnp.dot(a, b, preferred_element_type=jnp.float32)
    wide = 256

    def columns(i, carry):
        cols = pl.ds(pl.multiple_of(i * wide, wide), wide)
        b_high, b_low = v_high[:, cols], v_low[:, cols]
        out_ref[:, cols] = (
            dot(a_high[...], b_high) + dot(a_high[...], b_low) + dot(a_low[...], b_high)
        )
        return carry

    lax.fori_loop(0, out_ref.shape[1] // wide, columns, 0)


def panel_position(core, grp, of_core, of_grp, n):
    ahead = jnp.where(core == 0, grp - of_grp + n, of_grp - grp + n) % n
    other = jnp.where(core == of_core, 0, 1)
    near = 2 * ahead + other
    swapped = n + 2 * (n - ahead - 1) + 1 - other
    return jnp.where(ahead < n // 2, near, jnp.where(ahead == n // 2, 2 * n - 2 + other, swapped))


def ladder(pos, got, high, low, rows):
    chips = got.shape[0]
    depth, cols = high.shape
    return pl.pallas_call(
        ladder_kernel,
        out_shape=jax.ShapeDtypeStruct((chips * rows, cols), jnp.float32),
        in_specs=[SMEM, ANY, ANY, ANY],
        out_specs=VMEM,
        scratch_shapes=[
            pltpu.VMEM(got.shape, jnp.float32),
            pltpu.SMEM((chips, HEAD, LANES), jnp.float32),
            pltpu.SMEM((depth // LANES,), jnp.int32),
            pltpu.VMEM(high.shape, jnp.bfloat16),
            pltpu.VMEM(low.shape, jnp.bfloat16),
            pltpu.VMEM((chips * rows, depth), jnp.bfloat16),
            pltpu.VMEM((chips * rows, depth), jnp.bfloat16),
            pltpu.SemaphoreType.DMA((4,)),
        ],
        cost_estimate=pl.CostEstimate(
            flops=6 * chips * rows * depth * cols, bytes_accessed=16 << 20, transcendentals=0
        ),
        name="ladder",
    )(pos, got, high, low)


def swap_core(block):
    return lax.ppermute(block, "core", [(0, 1), (1, 0)])


def along_ring(block):
    n = lax.axis_size("grp")
    pairs = [(i, (i + 1) % n) for i in range(n)]
    pairs += [(n + i, n + (i - 1) % n) for i in range(n)]
    return lax.ppermute(block, ("core", "grp"), pairs)


def gather_panel(block):
    n = lax.axis_size("grp")
    near = [jnp.concatenate([block, swap_core(block)], axis=0)]
    swapped = []
    for _ in range(n // 2 - 1):
        near.append(along_ring(near[-1]))
        swapped.append(swap_core(near[-1]))
    far = along_ring(near[-1][: block.shape[0]])
    return near + swapped + [far, swap_core(far)]


def on_device(amplitudes, integrals, occupancy, tile_place):
    chips = NX * NZ
    per_chip = tile_place.shape[0] // chips
    rows, width = amplitudes.shape[2:]
    cols = integrals.shape[1]
    panel = gather_panel(integrals)
    sent = pack(occupancy[0], tile_place, amplitudes[0], chips, per_chip)
    got = lax.all_to_all(sent, CHIPS, 0, 0, tiled=True)
    high, low = split_panel(panel)
    pos = jnp.stack([lax.axis_index("core"), lax.axis_index("grp")]).astype(jnp.int32)
    part = ladder(pos, got, high, low, rows)
    part = part.reshape(NX, NZ * rows, cols)
    part = lax.all_to_all(part, "x", 0, 0, tiled=True).sum(axis=0)
    part = part.reshape(NZ, rows, cols)
    return lax.all_to_all(part, "z", 0, 0, tiled=True).sum(axis=0)


def solution(mesh):
    split_mesh = Mesh(mesh.devices.reshape(NX, NZ, NC, -1), EVERY)
    return jax.shard_map(
        on_device,
        mesh=split_mesh,
        in_specs=(
            P(EVERY, None, None, None),
            P(EVERY, None),
            P(EVERY, None),
            P(),
        ),
        out_specs=P(EVERY, None),
        check_vma=False,
    )
```

time: 314 us -> 170 us (0.54)
  the two profiles are of different devices: /device:TPU:8 before, /device:TPU:32 now
where the time goes in v2:
time: 170 us; the launch traced here: 169 us
  blocking collectives  54.4 us (32%)
  waiting for transfers between devices  53.4 us (31%)
  starting transfers between devices  31.8 us (19%)
  Pallas kernels  27.7 us (16%)
    ppermute x4, waiting for transfers between devices, along_ring(): return lax.ppermute(block, ('core', 'grp'), pairs)  51.8 us
    all_to_all x1, blocking collectives, on_device(): part = lax.all_to_all(part, 'x', 0, 0, tiled=True).sum(axis=0)  31.2 us
    all_to_all x1, blocking collectives, on_device(): return lax.all_to_all(part, 'z', 0, 0, tiled=True).sum(axis=0)  23.2 us
    pallas_call x1, Pallas kernels, ladder(): pl.pallas_call(ladder_kernel, out_shape=jax.ShapeDtypeStruct((chips * row...  15.6 us
    all_to_all x1, starting transfers between devices, on_device(): got = lax.all_to_all(sent, CHIPS, 0, 0, tiled=True)  13.4 us
    ppermute x5, starting transfers between devices, swap_core(): return lax.ppermute(block, 'core', [(0, 1), (1, 0)])  10.1 us
    ppermute x4, starting transfers between devices, along_ring(): return lax.ppermute(block, ('core', 'grp'), pairs)  8.33 us
    pallas_call x1, Pallas kernels, split_panel(): pl.pallas_call(split_kernel, out_shape=(out, out), in_specs=[VMEM] * len(...  7.87 us
  transfers between devices with their start and end apart: 10, of which 5 were waited for; matrix products, arithmetic and copies ran while one was open for 0% of the time, Pallas kernels for 7%

profile of v2, /device:TPU:32, one launch (start us, length us, event | category | flops | bytes accessed | tf_op | source)
XLA Modules:
  0.0 169.0 jit_solution(594709003758693025)
XLA Ops:
  0.0 1.9 %collective-permute-start = (f32[128,1024]{1,0:T(8,128)}, f32[128,1024]{1,0:T(8,128)S(1)}, u32[]{:S(2)}, u32[]{:S(2)}) collective-permute-start(f32[128,1024]{1,0:T(8,128)} %param.5), channel_id=1, source_target_pairs={{0,8},{8,0},{1,9},{9,1},{2,10},{10,2},{3,11},{11,3},{4,12},{12,4},... | collective-permute-start | bytes 1572872 | tf_op jit(solution)/shard_map/ppermute | solution.py:176
  1.9 4.2 %pack.1 = f32[32,136,128]{2,1,0:T(8,128)} custom-call(s32[128]{0:T(128)} %bitcast.9, s32[512]{0:T(512)} %refs_1_.1, f32[128,16,128]{2,1,0:T(8,128)} %bitcast.8), custom_call_target="tpu_custom_call" | custom-call | bytes 8388608 | tf_op jit(solution)/shard_map/pack/pallas_call | solution.py:48
  6.2 13.4 %all-to-all-start = ((f32[32,136,128]{2,1,0:T(8,128)}), f32[32,136,128]{2,1,0:T(8,128)}, u32[]{:S(2)}, u32[]{:S(2)}) async-start(f32[32,136,128]{2,1,0:T(8,128)} %pack.1), calls=%async_computation | async-start | bytes 4456448 | tf_op jit(solution)/shard_map/all_to_all | solution.py:204
  19.7 2.6 %collective-permute-start.1 = (f32[256,1024]{1,0:T(8,128)S(1)}, f32[256,1024]{1,0:T(8,128)S(1)}, u32[]{:S(2)}, u32[]{:S(2)}) collective-permute-start(f32[256,1024]{1,0:T(8,128)S(1)} %constant_dynamic-update-slice_fusion.refs_0_), channel_id=1, source_target_pairs={{0,1},{1,2},{2,3},{3,4},{4,5},{5,6},{6,7},{7,0},{8,15},{9,8},{10,9... | collective-permute-start | bytes 3145736 | tf_op jit(solution)/shard_map/ppermute | solution.py:183
  22.3 15.3 %collective-permute-done.1.refs_1_ = f32[256,1024]{1,0:T(8,128)S(1)} collective-permute-done((f32[256,1024]{1,0:T(8,128)S(1)}, f32[256,1024]{1,0:T(8,128)S(1)}, u32[]{:S(2)}, u32[]{:S(2)}) %collective-permute-start.1) | collective-permute-done | bytes 1048608 | tf_op jit(solution)/shard_map/ppermute | solution.py:183
  37.6 1.9 %collective-permute-start.2 = (f32[256,1024]{1,0:T(8,128)S(1)}, f32[256,1024]{1,0:T(8,128)}, u32[]{:S(2)}, u32[]{:S(2)}) collective-permute-start(f32[256,1024]{1,0:T(8,128)S(1)} %collective-permute-done.1.refs_1_), channel_id=1, source_target_pairs={{0,1},{1,2},{2,3},{3,4},{4,5},{5,6},{6,7},{7,0},{8,15},{9,8},{10,9... | collective-permute-start | bytes 3145736 | tf_op jit(solution)/shard_map/ppermute | solution.py:183
  39.5 16.1 %collective-permute-done.2.refs_2_ = f32[256,1024]{1,0:T(8,128)} collective-permute-done((f32[256,1024]{1,0:T(8,128)S(1)}, f32[256,1024]{1,0:T(8,128)}, u32[]{:S(2)}, u32[]{:S(2)}) %collective-permute-start.2) | collective-permute-done | bytes 1048608 | tf_op jit(solution)/shard_map/ppermute | solution.py:183
  55.6 1.9 %collective-permute-start.3 = (f32[256,1024]{1,0:T(8,128)}, f32[256,1024]{1,0:T(8,128)S(1)}, u32[]{:S(2)}, u32[]{:S(2)}) collective-permute-start(f32[256,1024]{1,0:T(8,128)} %collective-permute-done.2.refs_2_), channel_id=1, source_target_pairs={{0,1},{1,2},{2,3},{3,4},{4,5},{5,6},{6,7},{7,0},{8,15},{9,8},{10,9... | collective-permute-start | bytes 3145736 | tf_op jit(solution)/shard_map/ppermute | solution.py:183
  57.5 1.9 %collective-permute-start.4 = (f32[256,1024]{1,0:T(8,128)S(1)}, f32[256,1024]{1,0:T(8,128)}, u32[]{:S(2)}, u32[]{:S(2)}) collective-permute-start(f32[256,1024]{1,0:T(8,128)S(1)} %collective-permute-done.1.refs_1_), channel_id=1, source_target_pairs={{0,8},{8,0},{1,9},{9,1},{2,10},{10,2},{3,11},{11,3},{4,12},{12,4},... | collective-permute-start | bytes 3145736 | tf_op jit(solution)/shard_map/ppermute | solution.py:176
  59.4 2.4 %collective-permute-start.5 = (f32[256,1024]{1,0:T(8,128)}, f32[256,1024]{1,0:T(8,128)}, u32[]{:S(2)}, u32[]{:S(2)}) collective-permute-start(f32[256,1024]{1,0:T(8,128)} %collective-permute-done.2.refs_2_), channel_id=1, source_target_pairs={{0,8},{8,0},{1,9},{9,1},{2,10},{10,2},{3,11},{11,3},{4,12},{12,4},... | collective-permute-start | bytes 3145736 | tf_op jit(solution)/shard_map/ppermute | solution.py:176
  61.9 11.8 %collective-permute-done.3.refs_3_ = f32[256,1024]{1,0:T(8,128)S(1)} collective-permute-done((f32[256,1024]{1,0:T(8,128)}, f32[256,1024]{1,0:T(8,128)S(1)}, u32[]{:S(2)}, u32[]{:S(2)}) %collective-permute-start.3) | collective-permute-done | bytes 1048608 | tf_op jit(solution)/shard_map/ppermute | solution.py:183
  73.7 1.9 %collective-permute-start.7 = (f32[128,1024]{1,0:T(8,128)S(1)}, f32[128,1024]{1,0:T(8,128)}, u32[]{:S(2)}, u32[]{:S(2)}) collective-permute-start(f32[128,1024]{1,0:T(8,128)S(1)} %slice.4), channel_id=1, source_target_pairs={{0,1},{1,2},{2,3},{3,4},{4,5},{5,6},{6,7},{7,0},{8,15},{9,8},{10,9... | collective-permute-start | bytes 1572872 | tf_op jit(solution)/shard_map/ppermute | solution.py:183
  75.7 1.9 %collective-permute-start.6 = (f32[256,1024]{1,0:T(8,128)S(1)}, f32[256,1024]{1,0:T(8,128)}, u32[]{:S(2)}, u32[]{:S(2)}) collective-permute-start(f32[256,1024]{1,0:T(8,128)S(1)} %collective-permute-done.3.refs_3_), channel_id=1, source_target_pairs={{0,8},{8,0},{1,9},{9,1},{2,10},{10,2},{3,11},{11,3},{4,12},{12,4},... | collective-permute-start | bytes 3145736 | tf_op jit(solution)/shard_map/ppermute | solution.py:176
  77.6 8.5 %collective-permute-done.7.refs_7_ = f32[128,1024]{1,0:T(8,128)} collective-permute-done((f32[128,1024]{1,0:T(8,128)S(1)}, f32[128,1024]{1,0:T(8,128)}, u32[]{:S(2)}, u32[]{:S(2)}) %collective-permute-start.7) | collective-permute-done | bytes 524320 | tf_op jit(solution)/shard_map/ppermute | solution.py:183
  86.1 1.9 %collective-permute-start.8 = (f32[128,1024]{1,0:T(8,128)}, f32[128,1024]{1,0:T(8,128)}, u32[]{:S(2)}, u32[]{:S(2)}) collective-permute-start(f32[128,1024]{1,0:T(8,128)} %collective-permute-done.7.refs_7_), channel_id=1, source_target_pairs={{0,8},{8,0},{1,9},{9,1},{2,10},{10,2},{3,11},{11,3},{4,12},{12,4},... | collective-permute-start | bytes 1572872 | tf_op jit(solution)/shard_map/ppermute | solution.py:176
  88.1 0.6 pad_add_fusion.pos_ref
  88.7 0.0 collective-permute-done.4.refs_4_
  88.7 1.6 collective-permute-done.8.refs_8_
  90.3 7.9 %split_panel.1 = (bf16[2048,1024]{1,0:T(8,128)(2,1)}, bf16[2048,1024]{1,0:T(8,128)(2,1)}) custom-call(f32[256,1024]{1,0:T(8,128)} %copy-done.1, f32[256,1024]{1,0:T(8,128)} %copy-done.2, f32[256,1024]{1,0:T(8,128)} %collective-permute-done.2.refs_2_, f32[256,1024]{1,0:T(8,128)} %copy-done, f32[256,1024]{1,0:T(8,128)} %collective-permute-done.4.refs_4_, ...), custom_call_target="tpu_custom_call" | custom-call | bytes 16777216 | tf_op jit(solution)/shard_map/split_panel/pallas_call | solution.py:78
  98.2 15.6 %ladder.1 = f32[512,1024]{1,0:T(8,128)} custom-call(s32[2]{0:T(128)} %pad_add_fusion.pos_ref, f32[32,136,128]{2,1,0:T(8,128)} %all-to-all-done.got_hbm, bf16[2048,1024]{1,0:T(8,128)(2,1)} %get-tuple-element.7.high_hbm, bf16[2048,1024]{1,0:T(8,128)(2,1)} %get-tuple-element.8.low_hbm), custom_call_target="tpu_custom_call" | custom-call | flops 6442450944 | bytes 16777216 | tf_op jit(solution)/shard_map/ladder/pallas_call | solution.py:153
  113.7 31.2 %all_to_all.15 = f32[4,128,1024]{2,1,0:T(8,128)S(1)} all-to-all(f32[4,128,1024]{2,1,0:T(8,128)} %bitcast.6), channel_id=1, replica_groups=mesh['x'=4,'z'=8,'core'=2,'grp'=8] {'x'}, dimensions={0} | all-to-all | bytes 4194304 | tf_op jit(solution)/shard_map/all_to_all | solution.py:209
  144.9 0.2 reduce_sum.18
  145.1 23.2 %all_to_all.16 = f32[8,16,1024]{2,1,0:T(8,128)S(1)} all-to-all(f32[8,16,1024]{2,1,0:T(8,128)S(1)} %bitcast.7), channel_id=1, replica_groups=mesh['x'=4,'z'=8,'core'=2,'grp'=8] {'z'}, dimensions={0} | all-to-all | bytes 1048576 | tf_op jit(solution)/shard_map/all_to_all | solution.py:211
  168.3 0.7 reduce_sum.19
  (15 shorter events, 0.1 us)
Async XLA Ops:
  0.0 19.6 %collective-permute-start = (f32[128,1024]{1,0:T(8,128)}, f32[128,1024]{1,0:T(8,128)S(1)}, u32[]{:S(2)}, u32[]{:S(2)}) collective-permute-start(f32[128,1024]{1,0:T(8,128)} %param.5), channel_id=1, source_target_pairs={{0,8},{8,0},{1,9},{9,1},{2,10},{10,2},{3,11},{11,3},{4,12},{12,4},... | collective-permute-start | bytes 1572872 | tf_op jit(solution)/shard_map/ppermute | solution.py:176
  6.2 13.4 %copy-start.3 = (f32[128,1024]{1,0:T(8,128)S(1)}, f32[128,1024]{1,0:T(8,128)}, u32[]{:S(2)}) copy-start(f32[128,1024]{1,0:T(8,128)} %param.5) | copy-start | bytes 1572868
  6.2 92.0 %all-to-all-start = ((f32[32,136,128]{2,1,0:T(8,128)}), f32[32,136,128]{2,1,0:T(8,128)}, u32[]{:S(2)}, u32[]{:S(2)}) async-start(f32[32,136,128]{2,1,0:T(8,128)} %pack.1), calls=%async_computation | async-start | bytes 4456448 | tf_op jit(solution)/shard_map/all_to_all | solution.py:204
  19.7 70.6 %copy-start.1 = (f32[256,1024]{1,0:T(8,128)}, f32[256,1024]{1,0:T(8,128)S(1)}, u32[]{:S(2)}) copy-start(f32[256,1024]{1,0:T(8,128)S(1)} %constant_dynamic-update-slice_fusion.refs_0_) | copy-start | bytes 3145732
  19.7 17.9 %collective-permute-start.1 = (f32[256,1024]{1,0:T(8,128)S(1)}, f32[256,1024]{1,0:T(8,128)S(1)}, u32[]{:S(2)}, u32[]{:S(2)}) collective-permute-start(f32[256,1024]{1,0:T(8,128)S(1)} %constant_dynamic-update-slice_fusion.refs_0_), channel_id=1, source_target_pairs={{0,1},{1,2},{2,3},{3,4},{4,5},{5,6},{6,7},{7,0},{8,15},{9,8},{10,9... | collective-permute-start | bytes 3145736 | tf_op jit(solution)/shard_map/ppermute | solution.py:183
  37.6 52.7 %copy-start.2 = (f32[256,1024]{1,0:T(8,128)}, f32[256,1024]{1,0:T(8,128)S(1)}, u32[]{:S(2)}) copy-start(f32[256,1024]{1,0:T(8,128)S(1)} %collective-permute-done.1.refs_1_) | copy-start | bytes 3145732
  37.6 18.0 %collective-permute-start.2 = (f32[256,1024]{1,0:T(8,128)S(1)}, f32[256,1024]{1,0:T(8,128)}, u32[]{:S(2)}, u32[]{:S(2)}) collective-permute-start(f32[256,1024]{1,0:T(8,128)S(1)} %collective-permute-done.1.refs_1_), channel_id=1, source_target_pairs={{0,1},{1,2},{2,3},{3,4},{4,5},{5,6},{6,7},{7,0},{8,15},{9,8},{10,9... | collective-permute-start | bytes 3145736 | tf_op jit(solution)/shard_map/ppermute | solution.py:183
  55.6 18.1 %collective-permute-start.3 = (f32[256,1024]{1,0:T(8,128)}, f32[256,1024]{1,0:T(8,128)S(1)}, u32[]{:S(2)}, u32[]{:S(2)}) collective-permute-start(f32[256,1024]{1,0:T(8,128)} %collective-permute-done.2.refs_2_), channel_id=1, source_target_pairs={{0,1},{1,2},{2,3},{3,4},{4,5},{5,6},{6,7},{7,0},{8,15},{9,8},{10,9... | collective-permute-start | bytes 3145736 | tf_op jit(solution)/shard_map/ppermute | solution.py:183
  57.5 31.2 %collective-permute-start.4 = (f32[256,1024]{1,0:T(8,128)S(1)}, f32[256,1024]{1,0:T(8,128)}, u32[]{:S(2)}, u32[]{:S(2)}) collective-permute-start(f32[256,1024]{1,0:T(8,128)S(1)} %collective-permute-done.1.refs_1_), channel_id=1, source_target_pairs={{0,8},{8,0},{1,9},{9,1},{2,10},{10,2},{3,11},{11,3},{4,12},{12,4},... | collective-permute-start | bytes 3145736 | tf_op jit(solution)/shard_map/ppermute | solution.py:176
  59.4 29.2 %collective-permute-start.5 = (f32[256,1024]{1,0:T(8,128)}, f32[256,1024]{1,0:T(8,128)}, u32[]{:S(2)}, u32[]{:S(2)}) collective-permute-start(f32[256,1024]{1,0:T(8,128)} %collective-permute-done.2.refs_2_), channel_id=1, source_target_pairs={{0,8},{8,0},{1,9},{9,1},{2,10},{10,2},{3,11},{11,3},{4,12},{12,4},... | collective-permute-start | bytes 3145736 | tf_op jit(solution)/shard_map/ppermute | solution.py:176
  73.7 16.6 %copy-start = (f32[256,1024]{1,0:T(8,128)}, f32[256,1024]{1,0:T(8,128)S(1)}, u32[]{:S(2)}) copy-start(f32[256,1024]{1,0:T(8,128)S(1)} %collective-permute-done.3.refs_3_) | copy-start | bytes 3145732
  73.7 12.4 %collective-permute-start.7 = (f32[128,1024]{1,0:T(8,128)S(1)}, f32[128,1024]{1,0:T(8,128)}, u32[]{:S(2)}, u32[]{:S(2)}) collective-permute-start(f32[128,1024]{1,0:T(8,128)S(1)} %slice.4), channel_id=1, source_target_pairs={{0,1},{1,2},{2,3},{3,4},{4,5},{5,6},{6,7},{7,0},{8,15},{9,8},{10,9... | collective-permute-start | bytes 1572872 | tf_op jit(solution)/shard_map/ppermute | solution.py:183
  75.7 14.6 %collective-permute-start.6 = (f32[256,1024]{1,0:T(8,128)S(1)}, f32[256,1024]{1,0:T(8,128)}, u32[]{:S(2)}, u32[]{:S(2)}) collective-permute-start(f32[256,1024]{1,0:T(8,128)S(1)} %collective-permute-done.3.refs_3_), channel_id=1, source_target_pairs={{0,8},{8,0},{1,9},{9,1},{2,10},{10,2},{3,11},{11,3},{4,12},{12,4},... | collective-permute-start | bytes 3145736 | tf_op jit(solution)/shard_map/ppermute | solution.py:176
  86.1 4.1 %collective-permute-start.8 = (f32[128,1024]{1,0:T(8,128)}, f32[128,1024]{1,0:T(8,128)}, u32[]{:S(2)}, u32[]{:S(2)}) collective-permute-start(f32[128,1024]{1,0:T(8,128)} %collective-permute-done.7.refs_7_), channel_id=1, source_target_pairs={{0,8},{8,0},{1,9},{9,1},{2,10},{10,2},{3,11},{11,3},{4,12},{12,4},... | collective-permute-start | bytes 1572872 | tf_op jit(solution)/shard_map/ppermute | solution.py:176

commit v3 on v2

v3 whole, which is shorter than its diff:
```python
import jax
import jax.numpy as jnp
from jax import lax
from jax.experimental import pallas as pl
from jax.experimental.pallas import tpu as pltpu
from jax.sharding import Mesh, PartitionSpec as P

NX, NZ, NC = 4, 8, 2
CAP = 4
CHIPS = ("x", "z")
EVERY = ("x", "z", "core", "grp")
LANES = 128
HEAD = 8
LATE = 4
VMEM = pl.BlockSpec(memory_space=pltpu.VMEM)
SMEM = pl.BlockSpec(memory_space=pltpu.SMEM)
ANY = pl.BlockSpec(memory_space=pl.ANY)


def panel_position(core, grp, of_core, of_grp, n):
    ahead = jnp.where(core == 0, grp - of_grp + n, of_grp - grp + n) % n
    other = jnp.where(core == of_core, 0, 1)
    near = jnp.where(ahead == 0, 0, 4 * ahead - 2) + other
    back = 4 * (n - ahead) + 1 - other
    return jnp.where(ahead <= n // 2, near, back)


def pack_kernel(pos_ref, occ_ref, place_ref, amp_ref, out_ref, count_ref, where_ref):
    rows = amp_ref.shape[1]
    per_chip = where_ref.shape[0]
    per_core = per_chip // NC
    heading = jnp.full((HEAD, LANES), per_chip, jnp.int32).astype(jnp.float32)
    lane = lax.broadcasted_iota(jnp.int32, (HEAD, LANES), 1)

    def clear(i, carry):
        count_ref[i] = 0
        out_ref[i, pl.ds(0, HEAD), :] = heading
        return carry

    lax.fori_loop(0, count_ref.shape[0], clear, 0, unroll=4)
    for core in range(NC):
        for grp in range(per_core):
            where_ref[core * per_core + grp] = panel_position(
                pos_ref[0], pos_ref[1], core, grp, per_core
            )

    def step(j, carry):
        place = place_ref[occ_ref[j]]
        chip = place // per_chip
        at = where_ref[place % per_chip]
        slot = count_ref[chip]
        count_ref[chip] = slot + 1
        out_ref[chip, pl.ds(pl.multiple_of(HEAD + slot * rows, 8), rows), :] = amp_ref[j]
        out_ref[chip, pl.ds(0, HEAD), :] = jnp.where(
            lane == slot, at.astype(jnp.float32), out_ref[chip, pl.ds(0, HEAD), :]
        )
        return carry

    lax.fori_loop(0, occ_ref.shape[0], step, 0, unroll=4)


def pack(pos, occ, place, amp, chips, per_chip):
    rows, width = amp.shape[1:]
    return pl.pallas_call(
        pack_kernel,
        out_shape=jax.ShapeDtypeStruct((chips, HEAD + NC * CAP * rows, width), jnp.float32),
        in_specs=[SMEM, SMEM, SMEM, VMEM],
        out_specs=VMEM,
        scratch_shapes=[pltpu.SMEM((chips,), jnp.int32), pltpu.SMEM((per_chip,), jnp.int32)],
        cost_estimate=pl.CostEstimate(flops=0, bytes_accessed=8 << 20, transcendentals=0),
        compiler_params=pltpu.CompilerParams(vmem_limit_bytes=8 << 20),
        name="pack",
    )(pos, occ, place, amp)


def split(value):
    high = value.astype(jnp.bfloat16)
    return high, (value - high.astype(jnp.float32)).astype(jnp.bfloat16)


def split_kernel(*refs):
    blocks, (high_ref, low_ref) = refs[:-2], refs[-2:]
    at = 0
    for ref in blocks:
        for i in range(0, ref.shape[0], 64):
            high, low = split(ref[i : i + 64, :])
            high_ref[at : at + 64, :] = high
            low_ref[at : at + 64, :] = low
            at += 64


def split_panel(blocks):
    depth = sum(block.shape[0] for block in blocks)
    out = jax.ShapeDtypeStruct((depth, blocks[0].shape[1]), jnp.bfloat16)
    return pl.pallas_call(
        split_kernel,
        out_shape=(out, out),
        in_specs=[VMEM] * len(blocks),
        out_specs=(VMEM, VMEM),
        cost_estimate=pl.CostEstimate(flops=0, bytes_accessed=8 * depth * 1024, transcendentals=0),
        compiler_params=pltpu.CompilerParams(vmem_limit_bytes=18 << 20),
        name="split_panel",
    )(*blocks)


def ladder_kernel(parts, got_hbm, *refs):
    panel_hbm, (out_ref, got, head, v_high, v_low, left, sems) = refs[: 2 * parts], refs[2 * parts :]
    chips = got.shape[0]
    rows = out_ref.shape[0] // chips
    height = out_ref.shape[0]
    depth = v_high.shape[0]
    first = [
        pltpu.make_async_copy(got_hbm.at[:, pl.ds(0, HEAD), :], head, sems.at[0]),
        pltpu.make_async_copy(got_hbm, got, sems.at[1]),
    ]
    panel = []
    at = 0
    for i in range(parts):
        size = panel_hbm[2 * i].shape[0]
        for j, ref in enumerate((v_high, v_low)):
            panel.append(
                pltpu.make_async_copy(
                    panel_hbm[2 * i + j], ref.at[pl.ds(at, size), :], sems.at[2 + 2 * i + j]
                )
            )
        at += size
    for copy in first + panel:
        copy.start()

    def clear(i, carry):
        left[pl.ds(pl.multiple_of(i * 32, 32), 32), :] = jnp.zeros((32, left.shape[1]), left.dtype)
        return carry

    lax.fori_loop(0, left.shape[0] // 32, clear, 0)
    for copy in first:
        copy.wait()

    def step(n, carry):
        row = pl.multiple_of(n * rows, rows)
        for s in range(NC * CAP):
            col = pl.multiple_of(head[n, 0, s].astype(jnp.int32) * LANES, LANES)
            high, low = split(got[n, HEAD + s * rows : HEAD + (s + 1) * rows, :])
            left[pl.ds(row, rows), pl.ds(col, LANES)] = high
            left[pl.ds(height + row, rows), pl.ds(col, LANES)] = low
        return carry

    lax.fori_loop(0, chips, step, 0, unroll=2)
    for copy in panel:
        copy.wait()
    dot = lambda a, b: jnp.dot(a, b, preferred_element_type=jnp.float32)
    wide = 256

    def columns(i, carry):
        cols = pl.ds(pl.multiple_of(i * wide, wide), wide)
        both = dot(left[:, :depth], v_high[:, cols])
        out_ref[:, cols] = both[:height] + (both[height:] + dot(left[:height, :depth], v_low[:, cols]))
        return carry

    lax.fori_loop(0, out_ref.shape[1] // wide, columns, 0)


def ladder(got, panels, rows):
    chips = got.shape[0]
    depth = sum(high.shape[0] for high, _ in panels)
    cols = panels[0][0].shape[1]
    parts = len(panels)
    return pl.pallas_call(
        lambda *refs: ladder_kernel(parts, *refs),
        out_shape=jax.ShapeDtypeStruct((chips * rows, cols), jnp.float32),
        in_specs=[ANY] * (1 + 2 * parts),
        out_specs=VMEM,
        scratch_shapes=[
            pltpu.VMEM(got.shape, jnp.float32),
            pltpu.SMEM((chips, HEAD, LANES), jnp.float32),
            pltpu.VMEM((depth, cols), jnp.bfloat16),
            pltpu.VMEM((depth, cols), jnp.bfloat16),
            pltpu.VMEM((2 * chips * rows, depth + LANES), jnp.bfloat16),
            pltpu.SemaphoreType.DMA((2 + 2 * parts,)),
        ],
        cost_estimate=pl.CostEstimate(
            flops=6 * chips * rows * depth * cols, bytes_accessed=16 << 20, transcendentals=0
        ),
        compiler_params=pltpu.CompilerParams(vmem_limit_bytes=50 << 20),
        name="ladder",
    )(got, *[half for panel in panels for half in panel])


def swap_core(block):
    return lax.ppermute(block, "core", [(0, 1), (1, 0)])


def along_ring(block):
    n = lax.axis_size("grp")
    pairs = [(i, (i + 1) % n) for i in range(n)]
    pairs += [(n + i, n + (i - 1) % n) for i in range(n)]
    return lax.ppermute(block, ("core", "grp"), pairs)


def gather_panel(block):
    n = lax.axis_size("grp")
    own, mate = block, swap_core(block)
    blocks = [own, mate]
    for _ in range(n // 2 - 1):
        own, mate = along_ring(own), along_ring(mate)
        blocks += [own, mate, swap_core(own), swap_core(mate)]
    own = along_ring(own)
    return blocks + [own, swap_core(own)]


def on_device(amplitudes, integrals, occupancy, tile_place):
    chips = NX * NZ
    per_chip = tile_place.shape[0] // chips
    rows, width = amplitudes.shape[2:]
    cols = integrals.shape[1]
    panel = gather_panel(integrals)
    pos = jnp.stack([lax.axis_index("core"), lax.axis_index("grp")]).astype(jnp.int32)
    sent = pack(pos, occupancy[0], tile_place, amplitudes[0], chips, per_chip)
    got = lax.all_to_all(sent, CHIPS, 0, 0, tiled=True)
    panels = [split_panel(panel[:-LATE]), split_panel(panel[-LATE:])]
    part = ladder(got, panels, rows)
    part = part.reshape(NX, NZ * rows, cols)
    part = lax.all_to_all(part, "x", 0, 0, tiled=True).sum(axis=0)
    part = part.reshape(NZ, rows, cols)
    return lax.all_to_all(part, "z", 0, 0, tiled=True).sum(axis=0)


def solution(mesh):
    split_mesh = Mesh(mesh.devices.reshape(NX, NZ, NC, -1), EVERY)
    return jax.shard_map(
        on_device,
        mesh=split_mesh,
        in_specs=(
            P(EVERY, None, None, None),
            P(EVERY, None),
            P(EVERY, None),
            P(),
        ),
        out_specs=P(EVERY, None),
        check_vma=False,
    )
```

time: 170 us -> 152 us (0.89)
  the two profiles are of different devices: /device:TPU:32 before, /device:TPU:24 now
where the time goes in v3:
time: 152 us; the launch traced here: 151 us
  starting transfers between devices  61.5 us (40%)
  blocking collectives  54.9 us (36%)
  Pallas kernels  17.6 us (12%)
  waiting for transfers between devices  9.61 us (6%)
  local copies, waits for them, and re-layouts  5.89 us (4%)
    all_to_all x1, blocking collectives, on_device(): part = lax.all_to_all(part, 'x', 0, 0, tiled=True).sum(axis=0)  31.4 us
    ppermute x7, starting transfers between devices, along_ring(): return lax.ppermute(block, ('core', 'grp'), pairs)  31.3 us
    all_to_all x1, blocking collectives, on_device(): return lax.all_to_all(part, 'z', 0, 0, tiled=True).sum(axis=0)  23.5 us
    ppermute x8, starting transfers between devices, swap_core(): return lax.ppermute(block, 'core', [(0, 1), (1, 0)])  16.9 us
    all_to_all x1, starting transfers between devices, on_device(): got = lax.all_to_all(sent, CHIPS, 0, 0, tiled=True)  13.4 us
    pallas_call x1, Pallas kernels, ladder(): pl.pallas_call(lambda *refs: ladder_kernel(parts, *refs), out_shape=jax.S...  12.8 us
    ppermute x7, waiting for transfers between devices, along_ring(): return lax.ppermute(block, ('core', 'grp'), pairs)  9.59 us
    unnamed x12, local copies, waits for them, and re-layouts  5.89 us
  transfers between devices with their start and end apart: 16, of which 3 were waited for; matrix products, arithmetic and copies ran while one was open for 0% of the time, Pallas kernels for 1%

profile of v3, /device:TPU:24, one launch (start us, length us, event | category | flops | bytes accessed | tf_op | source)
XLA Modules:
  0.0 150.8 jit_solution(808074102192091971)
XLA Ops:
  2.6 3.6 %pack.1 = f32[32,136,128]{2,1,0:T(8,128)} custom-call(s32[2]{0:T(128)S(1)} %pad_add_fusion.pos_ref, s32[128]{0:T(128)S(1)} %bitcast.7, s32[512]{0:T(512)S(1)} %copy-done.2, f32[128,16,128]{2,1,0:T(8,128)S(1)} %bitcast.6), custom_call_target="tpu_custom_call" | custom-call | bytes 8388608 | tf_op jit(solution)/shard_map/pack/pallas_call | solution.py:64
  6.2 13.4 %all-to-all-start = ((f32[32,136,128]{2,1,0:T(8,128)}), f32[32,136,128]{2,1,0:T(8,128)}, u32[]{:S(2)}, u32[]{:S(2)}) async-start(f32[32,136,128]{2,1,0:T(8,128)} %pack.1), calls=%async_computation | async-start | bytes 4456448 | tf_op jit(solution)/shard_map/all_to_all | solution.py:218
  19.6 4.7 %collective-permute-start.1 = (f32[128,1024]{1,0:T(8,128)S(1)}, f32[128,1024]{1,0:T(8,128)S(1)}, u32[]{:S(2)}, u32[]{:S(2)}) collective-permute-start(f32[128,1024]{1,0:T(8,128)S(1)} %copy-done.1), channel_id=1, source_target_pairs={{0,1},{1,2},{2,3},{3,4},{4,5},{5,6},{6,7},{7,0},{8,15},{9,8},{10,9... | collective-permute-start | bytes 1572872 | tf_op jit(solution)/shard_map/ppermute | solution.py:196
  24.3 1.9 %collective-permute-start = (f32[128,1024]{1,0:T(8,128)S(1)}, f32[128,1024]{1,0:T(8,128)S(1)}, u32[]{:S(2)}, u32[]{:S(2)}) collective-permute-start(f32[128,1024]{1,0:T(8,128)S(1)} %copy-done.1), channel_id=1, source_target_pairs={{0,8},{8,0},{1,9},{9,1},{2,10},{10,2},{3,11},{11,3},{4,12},{12,4},... | collective-permute-start | bytes 1572872 | tf_op jit(solution)/shard_map/ppermute | solution.py:189
  26.3 4.7 %collective-permute-done.1.refs_2_ = f32[128,1024]{1,0:T(8,128)S(1)} collective-permute-done((f32[128,1024]{1,0:T(8,128)S(1)}, f32[128,1024]{1,0:T(8,128)S(1)}, u32[]{:S(2)}, u32[]{:S(2)}) %collective-permute-start.1) | collective-permute-done | bytes 524320 | tf_op jit(solution)/shard_map/ppermute | solution.py:196
  31.0 5.6 %collective-permute-start.5 = (f32[128,1024]{1,0:T(8,128)S(1)}, f32[128,1024]{1,0:T(8,128)S(1)}, u32[]{:S(2)}, u32[]{:S(2)}) collective-permute-start(f32[128,1024]{1,0:T(8,128)S(1)} %collective-permute-done.1.refs_2_), channel_id=1, source_target_pairs={{0,1},{1,2},{2,3},{3,4},{4,5},{5,6},{6,7},{7,0},{8,15},{9,8},{10,9... | collective-permute-start | bytes 1572872 | tf_op jit(solution)/shard_map/ppermute | solution.py:196
  36.6 1.9 %collective-permute-start.2 = (f32[128,1024]{1,0:T(8,128)S(1)}, f32[128,1024]{1,0:T(8,128)S(1)}, u32[]{:S(2)}, u32[]{:S(2)}) collective-permute-start(f32[128,1024]{1,0:T(8,128)S(1)} %collective-permute-done.refs_1_), channel_id=1, source_target_pairs={{0,1},{1,2},{2,3},{3,4},{4,5},{5,6},{6,7},{7,0},{8,15},{9,8},{10,9... | collective-permute-start | bytes 1572872 | tf_op jit(solution)/shard_map/ppermute | solution.py:196
  38.6 4.7 %collective-permute-done.5.refs_6_ = f32[128,1024]{1,0:T(8,128)S(1)} collective-permute-done((f32[128,1024]{1,0:T(8,128)S(1)}, f32[128,1024]{1,0:T(8,128)S(1)}, u32[]{:S(2)}, u32[]{:S(2)}) %collective-permute-start.5) | collective-permute-done | bytes 524320 | tf_op jit(solution)/shard_map/ppermute | solution.py:196
  43.3 5.6 %collective-permute-start.9 = (f32[128,1024]{1,0:T(8,128)S(1)}, f32[128,1024]{1,0:T(8,128)S(1)}, u32[]{:S(2)}, u32[]{:S(2)}) collective-permute-start(f32[128,1024]{1,0:T(8,128)S(1)} %collective-permute-done.5.refs_6_), channel_id=1, source_target_pairs={{0,1},{1,2},{2,3},{3,4},{4,5},{5,6},{6,7},{7,0},{8,15},{9,8},{10,9... | collective-permute-start | bytes 1572872 | tf_op jit(solution)/shard_map/ppermute | solution.py:196
  48.9 5.6 %collective-permute-start.6 = (f32[128,1024]{1,0:T(8,128)S(1)}, f32[128,1024]{1,0:T(8,128)S(1)}, u32[]{:S(2)}, u32[]{:S(2)}) collective-permute-start(f32[128,1024]{1,0:T(8,128)S(1)} %collective-permute-done.2.refs_3_), channel_id=1, source_target_pairs={{0,1},{1,2},{2,3},{3,4},{4,5},{5,6},{6,7},{7,0},{8,15},{9,8},{10,9... | collective-permute-start | bytes 1572872 | tf_op jit(solution)/shard_map/ppermute | solution.py:196
  54.5 1.9 %collective-permute-start.3 = (f32[128,1024]{1,0:T(8,128)S(1)}, f32[128,1024]{1,0:T(8,128)S(1)}, u32[]{:S(2)}, u32[]{:S(2)}) collective-permute-start(f32[128,1024]{1,0:T(8,128)S(1)} %collective-permute-done.1.refs_2_), channel_id=1, source_target_pairs={{0,8},{8,0},{1,9},{9,1},{2,10},{10,2},{3,11},{11,3},{4,12},{12,4},... | collective-permute-start | bytes 1572872 | tf_op jit(solution)/shard_map/ppermute | solution.py:189
  56.4 2.4 %collective-permute-start.7 = (f32[128,1024]{1,0:T(8,128)S(1)}, f32[128,1024]{1,0:T(8,128)S(1)}, u32[]{:S(2)}, u32[]{:S(2)}) collective-permute-start(f32[128,1024]{1,0:T(8,128)S(1)} %collective-permute-done.5.refs_6_), channel_id=1, source_target_pairs={{0,8},{8,0},{1,9},{9,1},{2,10},{10,2},{3,11},{11,3},{4,12},{12,4},... | collective-permute-start | bytes 1572872 | tf_op jit(solution)/shard_map/ppermute | solution.py:189
  58.9 2.3 %collective-permute-start.13 = (f32[128,1024]{1,0:T(8,128)S(1)}, f32[128,1024]{1,0:T(8,128)S(1)}, u32[]{:S(2)}, u32[]{:S(2)}) collective-permute-start(f32[128,1024]{1,0:T(8,128)S(1)} %collective-permute-done.9.refs_10_), channel_id=1, source_target_pairs={{0,1},{1,2},{2,3},{3,4},{4,5},{5,6},{6,7},{7,0},{8,15},{9,8},{10,9... | collective-permute-start | bytes 1572872 | tf_op jit(solution)/shard_map/ppermute | solution.py:196
  61.2 5.6 %collective-permute-start.10 = (f32[128,1024]{1,0:T(8,128)S(1)}, f32[128,1024]{1,0:T(8,128)S(1)}, u32[]{:S(2)}, u32[]{:S(2)}) collective-permute-start(f32[128,1024]{1,0:T(8,128)S(1)} %collective-permute-done.6.refs_7_), channel_id=1, source_target_pairs={{0,1},{1,2},{2,3},{3,4},{4,5},{5,6},{6,7},{7,0},{8,15},{9,8},{10,9... | collective-permute-start | bytes 1572872 | tf_op jit(solution)/shard_map/ppermute | solution.py:196
  66.8 1.9 %collective-permute-start.4 = (f32[128,1024]{1,0:T(8,128)S(1)}, f32[128,1024]{1,0:T(8,128)S(1)}, u32[]{:S(2)}, u32[]{:S(2)}) collective-permute-start(f32[128,1024]{1,0:T(8,128)S(1)} %collective-permute-done.2.refs_3_), channel_id=1, source_target_pairs={{0,8},{8,0},{1,9},{9,1},{2,10},{10,2},{3,11},{11,3},{4,12},{12,4},... | collective-permute-start | bytes 1572872 | tf_op jit(solution)/shard_map/ppermute | solution.py:189
  68.7 2.4 %collective-permute-start.8 = (f32[128,1024]{1,0:T(8,128)S(1)}, f32[128,1024]{1,0:T(8,128)S(1)}, u32[]{:S(2)}, u32[]{:S(2)}) collective-permute-start(f32[128,1024]{1,0:T(8,128)S(1)} %collective-permute-done.6.refs_7_), channel_id=1, source_target_pairs={{0,8},{8,0},{1,9},{9,1},{2,10},{10,2},{3,11},{11,3},{4,12},{12,4},... | collective-permute-start | bytes 1572872 | tf_op jit(solution)/shard_map/ppermute | solution.py:189
  71.1 1.9 %collective-permute-start.11 = (f32[128,1024]{1,0:T(8,128)S(1)}, f32[128,1024]{1,0:T(8,128)S(1)}, u32[]{:S(2)}, u32[]{:S(2)}) collective-permute-start(f32[128,1024]{1,0:T(8,128)S(1)} %collective-permute-done.9.refs_10_), channel_id=1, source_target_pairs={{0,8},{8,0},{1,9},{9,1},{2,10},{10,2},{3,11},{11,3},{4,12},{12,4},... | collective-permute-start | bytes 1572872 | tf_op jit(solution)/shard_map/ppermute | solution.py:189
  73.1 2.4 %collective-permute-start.14 = (f32[128,1024]{1,0:T(8,128)S(1)}, f32[128,1024]{1,0:T(8,128)S(1)}, u32[]{:S(2)}, u32[]{:S(2)}) collective-permute-start(f32[128,1024]{1,0:T(8,128)S(1)} %collective-permute-done.13.refs_2_), channel_id=1, source_target_pairs={{0,8},{8,0},{1,9},{9,1},{2,10},{10,2},{3,11},{11,3},{4,12},{12,4},... | collective-permute-start | bytes 1572872 | tf_op jit(solution)/shard_map/ppermute | solution.py:189
  75.6 2.0 %collective-permute-start.12 = (f32[128,1024]{1,0:T(8,128)S(1)}, f32[128,1024]{1,0:T(8,128)S(1)}, u32[]{:S(2)}, u32[]{:S(2)}) collective-permute-start(f32[128,1024]{1,0:T(8,128)S(1)} %collective-permute-done.10.refs_11_), channel_id=1, source_target_pairs={{0,8},{8,0},{1,9},{9,1},{2,10},{10,2},{3,11},{11,3},{4,12},{12,4},... | collective-permute-start | bytes 1572872 | tf_op jit(solution)/shard_map/ppermute | solution.py:189
  78.6 1.6 %copy-done.4 = bf16[1536,1024]{1,0:T(8,128)(2,1)} copy-done((bf16[1536,1024]{1,0:T(8,128)(2,1)}, bf16[1536,1024]{1,0:T(8,128)(2,1)S(1)}, u32[]{:S(2)}) %copy-start.4) | copy-done | bytes 3145752
  80.2 1.7 %copy-done.5 = bf16[1536,1024]{1,0:T(8,128)(2,1)} copy-done((bf16[1536,1024]{1,0:T(8,128)(2,1)}, bf16[1536,1024]{1,0:T(8,128)(2,1)S(1)}, u32[]{:S(2)}) %copy-start.5) | copy-done | bytes 3145752
  82.2 12.8 %ladder.1 = f32[512,1024]{1,0:T(8,128)} custom-call(f32[32,136,128]{2,1,0:T(8,128)} %all-to-all-done.refs_0_, bf16[1536,1024]{1,0:T(8,128)(2,1)} %copy-done.4, bf16[1536,1024]{1,0:T(8,128)(2,1)} %copy-done.5, bf16[512,1024]{1,0:T(8,128)(2,1)S(1)} %get-tuple-element.11.refs_3_, bf16[512,1024]{1,0:T(8,128)(2,1)S(1)} %get-tuple-element.12.refs_4_), custom_call_target="tpu_custom_call" | custom-call | flops 6442450944 | bytes 16777216 | tf_op jit(solution)/shard_map/ladder/pallas_call | solution.py:167
  95.0 31.4 %all_to_all.15 = f32[4,128,1024]{2,1,0:T(8,128)S(1)} all-to-all(f32[4,128,1024]{2,1,0:T(8,128)} %bitcast.8), channel_id=1, replica_groups=mesh['x'=4,'z'=8,'core'=2,'grp'=8] {'x'}, dimensions={0} | all-to-all | bytes 4194304 | tf_op jit(solution)/shard_map/all_to_all | solution.py:222
  126.6 23.5 %all_to_all.16 = f32[8,16,1024]{2,1,0:T(8,128)S(1)} all-to-all(f32[8,16,1024]{2,1,0:T(8,128)S(1)} %bitcast.9), channel_id=1, replica_groups=mesh['x'=4,'z'=8,'core'=2,'grp'=8] {'z'}, dimensions={0} | all-to-all | bytes 1048576 | tf_op jit(solution)/shard_map/all_to_all | solution.py:224
  (29 shorter events, 4.9 us)
Async XLA Ops:
  0.1 1.2 copy-start
  1.3 0.7 copy-start.2
  2.0 0.7 copy-start.3
  6.2 13.4 %copy-start.1 = (f32[128,1024]{1,0:T(8,128)S(1)}, f32[128,1024]{1,0:T(8,128)}, u32[]{:S(2)}) copy-start(f32[128,1024]{1,0:T(8,128)} %refs_0_.1) | copy-start | bytes 1572868
  6.2 76.0 %all-to-all-start = ((f32[32,136,128]{2,1,0:T(8,128)}), f32[32,136,128]{2,1,0:T(8,128)}, u32[]{:S(2)}, u32[]{:S(2)}) async-start(f32[32,136,128]{2,1,0:T(8,128)} %pack.1), calls=%async_computation | async-start | bytes 4456448 | tf_op jit(solution)/shard_map/all_to_all | solution.py:218
  19.6 11.4 %collective-permute-start.1 = (f32[128,1024]{1,0:T(8,128)S(1)}, f32[128,1024]{1,0:T(8,128)S(1)}, u32[]{:S(2)}, u32[]{:S(2)}) collective-permute-start(f32[128,1024]{1,0:T(8,128)S(1)} %copy-done.1), channel_id=1, source_target_pairs={{0,1},{1,2},{2,3},{3,4},{4,5},{5,6},{6,7},{7,0},{8,15},{9,8},{10,9... | collective-permute-start | bytes 1572872 | tf_op jit(solution)/shard_map/ppermute | solution.py:196
  24.3 12.3 %collective-permute-start = (f32[128,1024]{1,0:T(8,128)S(1)}, f32[128,1024]{1,0:T(8,128)S(1)}, u32[]{:S(2)}, u32[]{:S(2)}) collective-permute-start(f32[128,1024]{1,0:T(8,128)S(1)} %copy-done.1), channel_id=1, source_target_pairs={{0,8},{8,0},{1,9},{9,1},{2,10},{10,2},{3,11},{11,3},{4,12},{12,4},... | collective-permute-start | bytes 1572872 | tf_op jit(solution)/shard_map/ppermute | solution.py:189
  31.0 12.3 %collective-permute-start.5 = (f32[128,1024]{1,0:T(8,128)S(1)}, f32[128,1024]{1,0:T(8,128)S(1)}, u32[]{:S(2)}, u32[]{:S(2)}) collective-permute-start(f32[128,1024]{1,0:T(8,128)S(1)} %collective-permute-done.1.refs_2_), channel_id=1, source_target_pairs={{0,1},{1,2},{2,3},{3,4},{4,5},{5,6},{6,7},{7,0},{8,15},{9,8},{10,9... | collective-permute-start | bytes 1572872 | tf_op jit(solution)/shard_map/ppermute | solution.py:196
  36.6 12.3 %collective-permute-start.2 = (f32[128,1024]{1,0:T(8,128)S(1)}, f32[128,1024]{1,0:T(8,128)S(1)}, u32[]{:S(2)}, u32[]{:S(2)}) collective-permute-start(f32[128,1024]{1,0:T(8,128)S(1)} %collective-permute-done.refs_1_), channel_id=1, source_target_pairs={{0,1},{1,2},{2,3},{3,4},{4,5},{5,6},{6,7},{7,0},{8,15},{9,8},{10,9... | collective-permute-start | bytes 1572872 | tf_op jit(solution)/shard_map/ppermute | solution.py:196
  43.3 15.6 %collective-permute-start.9 = (f32[128,1024]{1,0:T(8,128)S(1)}, f32[128,1024]{1,0:T(8,128)S(1)}, u32[]{:S(2)}, u32[]{:S(2)}) collective-permute-start(f32[128,1024]{1,0:T(8,128)S(1)} %collective-permute-done.5.refs_6_), channel_id=1, source_target_pairs={{0,1},{1,2},{2,3},{3,4},{4,5},{5,6},{6,7},{7,0},{8,15},{9,8},{10,9... | collective-permute-start | bytes 1572872 | tf_op jit(solution)/shard_map/ppermute | solution.py:196
  48.9 12.3 %collective-permute-start.6 = (f32[128,1024]{1,0:T(8,128)S(1)}, f32[128,1024]{1,0:T(8,128)S(1)}, u32[]{:S(2)}, u32[]{:S(2)}) collective-permute-start(f32[128,1024]{1,0:T(8,128)S(1)} %collective-permute-done.2.refs_3_), channel_id=1, source_target_pairs={{0,1},{1,2},{2,3},{3,4},{4,5},{5,6},{6,7},{7,0},{8,15},{9,8},{10,9... | collective-permute-start | bytes 1572872 | tf_op jit(solution)/shard_map/ppermute | solution.py:196
  54.5 14.2 %collective-permute-start.3 = (f32[128,1024]{1,0:T(8,128)S(1)}, f32[128,1024]{1,0:T(8,128)S(1)}, u32[]{:S(2)}, u32[]{:S(2)}) collective-permute-start(f32[128,1024]{1,0:T(8,128)S(1)} %collective-permute-done.1.refs_2_), channel_id=1, source_target_pairs={{0,8},{8,0},{1,9},{9,1},{2,10},{10,2},{3,11},{11,3},{4,12},{12,4},... | collective-permute-start | bytes 1572872 | tf_op jit(solution)/shard_map/ppermute | solution.py:189
  56.4 14.7 %collective-permute-start.7 = (f32[128,1024]{1,0:T(8,128)S(1)}, f32[128,1024]{1,0:T(8,128)S(1)}, u32[]{:S(2)}, u32[]{:S(2)}) collective-permute-start(f32[128,1024]{1,0:T(8,128)S(1)} %collective-permute-done.5.refs_6_), channel_id=1, source_target_pairs={{0,8},{8,0},{1,9},{9,1},{2,10},{10,2},{3,11},{11,3},{4,12},{12,4},... | collective-permute-start | bytes 1572872 | tf_op jit(solution)/shard_map/ppermute | solution.py:189
  58.9 14.2 %collective-permute-start.13 = (f32[128,1024]{1,0:T(8,128)S(1)}, f32[128,1024]{1,0:T(8,128)S(1)}, u32[]{:S(2)}, u32[]{:S(2)}) collective-permute-start(f32[128,1024]{1,0:T(8,128)S(1)} %collective-permute-done.9.refs_10_), channel_id=1, source_target_pairs={{0,1},{1,2},{2,3},{3,4},{4,5},{5,6},{6,7},{7,0},{8,15},{9,8},{10,9... | collective-permute-start | bytes 1572872 | tf_op jit(solution)/shard_map/ppermute | solution.py:196
  61.2 14.4 %collective-permute-start.10 = (f32[128,1024]{1,0:T(8,128)S(1)}, f32[128,1024]{1,0:T(8,128)S(1)}, u32[]{:S(2)}, u32[]{:S(2)}) collective-permute-start(f32[128,1024]{1,0:T(8,128)S(1)} %collective-permute-done.6.refs_7_), channel_id=1, source_target_pairs={{0,1},{1,2},{2,3},{3,4},{4,5},{5,6},{6,7},{7,0},{8,15},{9,8},{10,9... | collective-permute-start | bytes 1572872 | tf_op jit(solution)/shard_map/ppermute | solution.py:196
  66.8 10.8 %collective-permute-start.4 = (f32[128,1024]{1,0:T(8,128)S(1)}, f32[128,1024]{1,0:T(8,128)S(1)}, u32[]{:S(2)}, u32[]{:S(2)}) collective-permute-start(f32[128,1024]{1,0:T(8,128)S(1)} %collective-permute-done.2.refs_3_), channel_id=1, source_target_pairs={{0,8},{8,0},{1,9},{9,1},{2,10},{10,2},{3,11},{11,3},{4,12},{12,4},... | collective-permute-start | bytes 1572872 | tf_op jit(solution)/shard_map/ppermute | solution.py:189
  68.7 8.8 %collective-permute-start.8 = (f32[128,1024]{1,0:T(8,128)S(1)}, f32[128,1024]{1,0:T(8,128)S(1)}, u32[]{:S(2)}, u32[]{:S(2)}) collective-permute-start(f32[128,1024]{1,0:T(8,128)S(1)} %collective-permute-done.6.refs_7_), channel_id=1, source_target_pairs={{0,8},{8,0},{1,9},{9,1},{2,10},{10,2},{3,11},{11,3},{4,12},{12,4},... | collective-permute-start | bytes 1572872 | tf_op jit(solution)/shard_map/ppermute | solution.py:189
  71.1 10.7 %collective-permute-start.11 = (f32[128,1024]{1,0:T(8,128)S(1)}, f32[128,1024]{1,0:T(8,128)S(1)}, u32[]{:S(2)}, u32[]{:S(2)}) collective-permute-start(f32[128,1024]{1,0:T(8,128)S(1)} %collective-permute-done.9.refs_10_), channel_id=1, source_target_pairs={{0,8},{8,0},{1,9},{9,1},{2,10},{10,2},{3,11},{11,3},{4,12},{12,4},... | collective-permute-start | bytes 1572872 | tf_op jit(solution)/shard_map/ppermute | solution.py:189
  73.1 8.8 %collective-permute-start.14 = (f32[128,1024]{1,0:T(8,128)S(1)}, f32[128,1024]{1,0:T(8,128)S(1)}, u32[]{:S(2)}, u32[]{:S(2)}) collective-permute-start(f32[128,1024]{1,0:T(8,128)S(1)} %collective-permute-done.13.refs_2_), channel_id=1, source_target_pairs={{0,8},{8,0},{1,9},{9,1},{2,10},{10,2},{3,11},{11,3},{4,12},{12,4},... | collective-permute-start | bytes 1572872 | tf_op jit(solution)/shard_map/ppermute | solution.py:189
  75.6 6.3 %collective-permute-start.12 = (f32[128,1024]{1,0:T(8,128)S(1)}, f32[128,1024]{1,0:T(8,128)S(1)}, u32[]{:S(2)}, u32[]{:S(2)}) collective-permute-start(f32[128,1024]{1,0:T(8,128)S(1)} %collective-permute-done.10.refs_11_), channel_id=1, source_target_pairs={{0,8},{8,0},{1,9},{9,1},{2,10},{10,2},{3,11},{11,3},{4,12},{12,4},... | collective-permute-start | bytes 1572872 | tf_op jit(solution)/shard_map/ppermute | solution.py:189
  78.5 1.6 %copy-start.4 = (bf16[1536,1024]{1,0:T(8,128)(2,1)}, bf16[1536,1024]{1,0:T(8,128)(2,1)S(1)}, u32[]{:S(2)}) copy-start(bf16[1536,1024]{1,0:T(8,128)(2,1)S(1)} %get-tuple-element.9.refs_1_) | copy-start | bytes 9437188
  80.2 1.7 %copy-start.5 = (bf16[1536,1024]{1,0:T(8,128)(2,1)}, bf16[1536,1024]{1,0:T(8,128)(2,1)S(1)}, u32[]{:S(2)}) copy-start(bf16[1536,1024]{1,0:T(8,128)(2,1)S(1)} %get-tuple-element.10.refs_2_) | copy-start | bytes 9437188

commit v4 on v3

--- a/solution.py
+++ b/solution.py
@@ -11,7 +11,7 @@
 EVERY = ("x", "z", "core", "grp")
 LANES = 128
 HEAD = 8
-LATE = 4
+BAND = 4
 VMEM = pl.BlockSpec(memory_space=pltpu.VMEM)
 SMEM = pl.BlockSpec(memory_space=pltpu.SMEM)
 ANY = pl.BlockSpec(memory_space=pl.ANY)
@@ -68,7 +68,6 @@
         out_specs=VMEM,
         scratch_shapes=[pltpu.SMEM((chips,), jnp.int32), pltpu.SMEM((per_chip,), jnp.int32)],
         cost_estimate=pl.CostEstimate(flops=0, bytes_accessed=8 << 20, transcendentals=0),
-        compiler_params=pltpu.CompilerParams(vmem_limit_bytes=8 << 20),
         name="pack",
     )(pos, occ, place, amp)
 
@@ -104,26 +103,30 @@
 
 
 def ladder_kernel(parts, got_hbm, *refs):
-    panel_hbm, (out_ref, got, head, v_high, v_low, left, sems) = refs[: 2 * parts], refs[2 * parts :]
+    panel_hbm, (out_hbm, got, head, v_high, v_low, left, total, sems, out_sems) = (
+        refs[: 2 * parts],
+        refs[2 * parts :],
+    )
     chips = got.shape[0]
-    rows = out_ref.shape[0] // chips
-    height = out_ref.shape[0]
-    depth = v_high.shape[0]
+    height = total.shape[0]
+    rows = height // chips
     first = [
         pltpu.make_async_copy(got_hbm.at[:, pl.ds(0, HEAD), :], head, sems.at[0]),
         pltpu.make_async_copy(got_hbm, got, sems.at[1]),
     ]
     panel = []
-    at = 0
+    starts = [0]
     for i in range(parts):
         size = panel_hbm[2 * i].shape[0]
         for j, ref in enumerate((v_high, v_low)):
             panel.append(
                 pltpu.make_async_copy(
-                    panel_hbm[2 * i + j], ref.at[pl.ds(at, size), :], sems.at[2 + 2 * i + j]
+                    panel_hbm[2 * i + j],
+                    ref.at[pl.ds(starts[-1], size), :],
+                    sems.at[2 + 2 * i + j],
                 )
             )
-        at += size
+        starts.append(starts[-1] + size)
     for copy in first + panel:
         copy.start()
 
@@ -145,18 +148,34 @@
         return carry
 
     lax.fori_loop(0, chips, step, 0, unroll=2)
-    for copy in panel:
-        copy.wait()
     dot = lambda a, b: jnp.dot(a, b, preferred_element_type=jnp.float32)
     wide = 256
-
-    def columns(i, carry):
+    steps = total.shape[1] // wide
+
+    def product(lo, hi, cols):
+        both = dot(left[:, lo:hi], v_high[lo:hi, cols])
+        return both[:height] + (both[height:] + dot(left[:height, lo:hi], v_low[lo:hi, cols]))
+
+    middle = parts // 2
+    for copy in panel[: 2 * middle]:
+        copy.wait()
+
+    def near(i, carry):
         cols = pl.ds(pl.multiple_of(i * wide, wide), wide)
-        both = dot(left[:, :depth], v_high[:, cols])
-        out_ref[:, cols] = both[:height] + (both[height:] + dot(left[:height, :depth], v_low[:, cols]))
-        return carry
-
-    lax.fori_loop(0, out_ref.shape[1] // wide, columns, 0)
+        total[:, cols] = product(0, starts[middle], cols)
+        return carry
+
+    lax.fori_loop(0, steps, near, 0)
+    for copy in panel[2 * middle :]:
+        copy.wait()
+    done = []
+    for i in range(steps):
+        cols = pl.ds(i * wide, wide)
+        total[:, cols] += product(starts[middle], starts[parts], cols)
+        done.append(pltpu.make_async_copy(total.at[:, cols], out_hbm.at[:, cols], out_sems.at[i]))
+        done[-1].start()
+    for copy in done:
+        copy.wait()
 
 
 def ladder(got, panels, rows):
@@ -168,14 +187,16 @@
         lambda *refs: ladder_kernel(parts, *refs),
         out_shape=jax.ShapeDtypeStruct((chips * rows, cols), jnp.float32),
         in_specs=[ANY] * (1 + 2 * parts),
-        out_specs=VMEM,
+        out_specs=ANY,
         scratch_shapes=[
             pltpu.VMEM(got.shape, jnp.float32),
             pltpu.SMEM((chips, HEAD, LANES), jnp.float32),
             pltpu.VMEM((depth, cols), jnp.bfloat16),
             pltpu.VMEM((depth, cols), jnp.bfloat16),
             pltpu.VMEM((2 * chips * rows, depth + LANES), jnp.bfloat16),
+            pltpu.VMEM((chips * rows, cols), jnp.float32),
             pltpu.SemaphoreType.DMA((2 + 2 * parts,)),
+            pltpu.SemaphoreType.DMA((cols // 256,)),
         ],
         cost_estimate=pl.CostEstimate(
             flops=6 * chips * rows * depth * cols, bytes_accessed=16 << 20, transcendentals=0
@@ -196,9 +217,8 @@
     return lax.ppermute(block, ("core", "grp"), pairs)
 
 
-def gather_panel(block):
+def gather_panel(own, mate):
     n = lax.axis_size("grp")
-    own, mate = block, swap_core(block)
     blocks = [own, mate]
     for _ in range(n // 2 - 1):
         own, mate = along_ring(own), along_ring(mate)
@@ -212,11 +232,13 @@
     per_chip = tile_place.shape[0] // chips
     rows, width = amplitudes.shape[2:]
     cols = integrals.shape[1]
-    panel = gather_panel(integrals)
+    mate = swap_core(integrals)
     pos = jnp.stack([lax.axis_index("core"), lax.axis_index("grp")]).astype(jnp.int32)
     sent = pack(pos, occupancy[0], tile_place, amplitudes[0], chips, per_chip)
+    sent, mate = lax.optimization_barrier((sent, mate))
+    panel = gather_panel(integrals, mate)
     got = lax.all_to_all(sent, CHIPS, 0, 0, tiled=True)
-    panels = [split_panel(panel[:-LATE]), split_panel(panel[-LATE:])]
+    panels = [split_panel(panel[i : i + BAND]) for i in range(0, len(panel), BAND)]
     part = ladder(got, panels, rows)
     part = part.reshape(NX, NZ * rows, cols)
     part = lax.all_to_all(part, "x", 0, 0, tiled=True).sum(axis=0)

time: 152 us -> 153 us (level)
  waiting for transfers between devices: 9.61 us -> 11.6 us
  local copies, waits for them, and re-layouts: 5.89 us -> 4.05 us
    ppermute x7, waiting for transfers between devices: 9.59 us -> 11.5 us  [along_ring(): return lax.ppermute(block, ('core', 'grp'), pairs)]
    unnamed x12, local copies, waits for them, and re-layouts: 5.89 us -> 4.05 us
  transfers between devices with their start and end apart: 16 -> 16, of which waited for: 3 -> 3; matrix products, arithmetic and copies ran while one was open for 0% -> 0% of each run, Pallas kernels for 1% -> 4%
where the time goes in v4:
time: 153 us; the launch traced here: 152 us
  starting transfers between devices  61.5 us (40%)
  blocking collectives  54.9 us (36%)
  Pallas kernels  18.1 us (12%)
  waiting for transfers between devices  11.6 us (8%)
  local copies, waits for them, and re-layouts  4.05 us (3%)
    all_to_all x1, blocking collectives, on_device(): part = lax.all_to_all(part, 'x', 0, 0, tiled=True).sum(axis=0)  31.4 us
    ppermute x7, starting transfers between devices, along_ring(): return lax.ppermute(block, ('core', 'grp'), pairs)  31.3 us
    all_to_all x1, blocking collectives, on_device(): return lax.all_to_all(part, 'z', 0, 0, tiled=True).sum(axis=0)  23.5 us
    ppermute x8, starting transfers between devices, swap_core(): return lax.ppermute(block, 'core', [(0, 1), (1, 0)])  16.9 us
    all_to_all x1, starting transfers between devices, on_device(): got = lax.all_to_all(sent, CHIPS, 0, 0, tiled=True)  13.4 us
    pallas_call x1, Pallas kernels, ladder(): pl.pallas_call(lambda *refs: ladder_kernel(parts, *refs), out_shape=jax.S...  12.7 us
    ppermute x7, waiting for transfers between devices, along_ring(): return lax.ppermute(block, ('core', 'grp'), pairs)  11.5 us
    pallas_call x1, Pallas kernels, pack(): pl.pallas_call(pack_kernel, out_shape=jax.ShapeDtypeStruct((chips, HEAD +...  4.17 us
  transfers between devices with their start and end apart: 16, of which 3 were waited for; matrix products, arithmetic and copies ran while one was open for 0% of the time, Pallas kernels for 4%

profile of v4, /device:TPU:24, one launch (start us, length us, event | category | flops | bytes accessed | tf_op | source)
XLA Modules:
  0.0 151.9 jit_solution(1534016534345983403)
XLA Ops:
  0.0 1.9 %collective-permute-start = (f32[128,1024]{1,0:T(8,128)}, f32[128,1024]{1,0:T(8,128)S(1)}, u32[]{:S(2)}, u32[]{:S(2)}) collective-permute-start(f32[128,1024]{1,0:T(8,128)} %refs_0_.1), channel_id=1, source_target_pairs={{0,8},{8,0},{1,9},{9,1},{2,10},{10,2},{3,11},{11,3},{4,12},{12,4},... | collective-permute-start | bytes 1572872 | tf_op jit(solution)/shard_map/ppermute | solution.py:210
  2.5 4.2 %pack.1 = f32[32,136,128]{2,1,0:T(8,128)} custom-call(s32[2]{0:T(128)} %pad_add_fusion.pos_ref, s32[128]{0:T(128)} %bitcast.9, s32[512]{0:T(512)} %place_ref.1, f32[128,16,128]{2,1,0:T(8,128)} %bitcast.8), custom_call_target="tpu_custom_call" | custom-call | bytes 8388608 | tf_op jit(solution)/shard_map/pack/pallas_call | solution.py:64
  6.7 13.4 %all-to-all-start = ((f32[32,136,128]{2,1,0:T(8,128)}), f32[32,136,128]{2,1,0:T(8,128)}, u32[]{:S(2)}, u32[]{:S(2)}) async-start(f32[32,136,128]{2,1,0:T(8,128)} %pack.1), calls=%async_computation | async-start | bytes 4456448 | tf_op jit(solution)/shard_map/all_to_all | solution.py:240
  20.1 4.7 %collective-permute-start.1 = (f32[128,1024]{1,0:T(8,128)S(1)}, f32[128,1024]{1,0:T(8,128)S(1)}, u32[]{:S(2)}, u32[]{:S(2)}) collective-permute-start(f32[128,1024]{1,0:T(8,128)S(1)} %copy-done), channel_id=1, source_target_pairs={{0,1},{1,2},{2,3},{3,4},{4,5},{5,6},{6,7},{7,0},{8,15},{9,8},{10,9... | collective-permute-start | bytes 1572872 | tf_op jit(solution)/shard_map/ppermute | solution.py:217
  24.8 6.7 %collective-permute-done.1.refs_2_ = f32[128,1024]{1,0:T(8,128)S(1)} collective-permute-done((f32[128,1024]{1,0:T(8,128)S(1)}, f32[128,1024]{1,0:T(8,128)S(1)}, u32[]{:S(2)}, u32[]{:S(2)}) %collective-permute-start.1) | collective-permute-done | bytes 524320 | tf_op jit(solution)/shard_map/ppermute | solution.py:217
  31.5 5.6 %collective-permute-start.5 = (f32[128,1024]{1,0:T(8,128)S(1)}, f32[128,1024]{1,0:T(8,128)S(1)}, u32[]{:S(2)}, u32[]{:S(2)}) collective-permute-start(f32[128,1024]{1,0:T(8,128)S(1)} %collective-permute-done.1.refs_2_), channel_id=1, source_target_pairs={{0,1},{1,2},{2,3},{3,4},{4,5},{5,6},{6,7},{7,0},{8,15},{9,8},{10,9... | collective-permute-start | bytes 1572872 | tf_op jit(solution)/shard_map/ppermute | solution.py:217
  37.1 1.9 %collective-permute-start.2 = (f32[128,1024]{1,0:T(8,128)S(1)}, f32[128,1024]{1,0:T(8,128)S(1)}, u32[]{:S(2)}, u32[]{:S(2)}) collective-permute-start(f32[128,1024]{1,0:T(8,128)S(1)} %collective-permute-done.refs_1_), channel_id=1, source_target_pairs={{0,1},{1,2},{2,3},{3,4},{4,5},{5,6},{6,7},{7,0},{8,15},{9,8},{10,9... | collective-permute-start | bytes 1572872 | tf_op jit(solution)/shard_map/ppermute | solution.py:217
  39.0 4.7 %collective-permute-done.5.refs_2_ = f32[128,1024]{1,0:T(8,128)S(1)} collective-permute-done((f32[128,1024]{1,0:T(8,128)S(1)}, f32[128,1024]{1,0:T(8,128)S(1)}, u32[]{:S(2)}, u32[]{:S(2)}) %collective-permute-start.5) | collective-permute-done | bytes 524320 | tf_op jit(solution)/shard_map/ppermute | solution.py:217
  43.8 5.6 %collective-permute-start.9 = (f32[128,1024]{1,0:T(8,128)S(1)}, f32[128,1024]{1,0:T(8,128)S(1)}, u32[]{:S(2)}, u32[]{:S(2)}) collective-permute-start(f32[128,1024]{1,0:T(8,128)S(1)} %collective-permute-done.5.refs_2_), channel_id=1, source_target_pairs={{0,1},{1,2},{2,3},{3,4},{4,5},{5,6},{6,7},{7,0},{8,15},{9,8},{10,9... | collective-permute-start | bytes 1572872 | tf_op jit(solution)/shard_map/ppermute | solution.py:217
  49.4 5.6 %collective-permute-start.6 = (f32[128,1024]{1,0:T(8,128)S(1)}, f32[128,1024]{1,0:T(8,128)S(1)}, u32[]{:S(2)}, u32[]{:S(2)}) collective-permute-start(f32[128,1024]{1,0:T(8,128)S(1)} %collective-permute-done.2.refs_3_), channel_id=1, source_target_pairs={{0,1},{1,2},{2,3},{3,4},{4,5},{5,6},{6,7},{7,0},{8,15},{9,8},{10,9... | collective-permute-start | bytes 1572872 | tf_op jit(solution)/shard_map/ppermute | solution.py:217
  55.0 1.9 %collective-permute-start.3 = (f32[128,1024]{1,0:T(8,128)S(1)}, f32[128,1024]{1,0:T(8,128)S(1)}, u32[]{:S(2)}, u32[]{:S(2)}) collective-permute-start(f32[128,1024]{1,0:T(8,128)S(1)} %collective-permute-done.1.refs_2_), channel_id=1, source_target_pairs={{0,8},{8,0},{1,9},{9,1},{2,10},{10,2},{3,11},{11,3},{4,12},{12,4},... | collective-permute-start | bytes 1572872 | tf_op jit(solution)/shard_map/ppermute | solution.py:210
  56.9 2.4 %collective-permute-start.4 = (f32[128,1024]{1,0:T(8,128)S(1)}, f32[128,1024]{1,0:T(8,128)S(1)}, u32[]{:S(2)}, u32[]{:S(2)}) collective-permute-start(f32[128,1024]{1,0:T(8,128)S(1)} %collective-permute-done.2.refs_3_), channel_id=1, source_target_pairs={{0,8},{8,0},{1,9},{9,1},{2,10},{10,2},{3,11},{11,3},{4,12},{12,4},... | collective-permute-start | bytes 1572872 | tf_op jit(solution)/shard_map/ppermute | solution.py:210
  59.4 2.3 %collective-permute-start.13 = (f32[128,1024]{1,0:T(8,128)S(1)}, f32[128,1024]{1,0:T(8,128)S(1)}, u32[]{:S(2)}, u32[]{:S(2)}) collective-permute-start(f32[128,1024]{1,0:T(8,128)S(1)} %collective-permute-done.9.refs_2_), channel_id=1, source_target_pairs={{0,1},{1,2},{2,3},{3,4},{4,5},{5,6},{6,7},{7,0},{8,15},{9,8},{10,9... | collective-permute-start | bytes 1572872 | tf_op jit(solution)/shard_map/ppermute | solution.py:217
  61.7 5.6 %collective-permute-start.10 = (f32[128,1024]{1,0:T(8,128)S(1)}, f32[128,1024]{1,0:T(8,128)S(1)}, u32[]{:S(2)}, u32[]{:S(2)}) collective-permute-start(f32[128,1024]{1,0:T(8,128)S(1)} %collective-permute-done.6.refs_3_), channel_id=1, source_target_pairs={{0,1},{1,2},{2,3},{3,4},{4,5},{5,6},{6,7},{7,0},{8,15},{9,8},{10,9... | collective-permute-start | bytes 1572872 | tf_op jit(solution)/shard_map/ppermute | solution.py:217
  67.3 1.9 %collective-permute-start.7 = (f32[128,1024]{1,0:T(8,128)S(1)}, f32[128,1024]{1,0:T(8,128)S(1)}, u32[]{:S(2)}, u32[]{:S(2)}) collective-permute-start(f32[128,1024]{1,0:T(8,128)S(1)} %collective-permute-done.5.refs_2_), channel_id=1, source_target_pairs={{0,8},{8,0},{1,9},{9,1},{2,10},{10,2},{3,11},{11,3},{4,12},{12,4},... | collective-permute-start | bytes 1572872 | tf_op jit(solution)/shard_map/ppermute | solution.py:210
  69.2 2.4 %collective-permute-start.11 = (f32[128,1024]{1,0:T(8,128)S(1)}, f32[128,1024]{1,0:T(8,128)S(1)}, u32[]{:S(2)}, u32[]{:S(2)}) collective-permute-start(f32[128,1024]{1,0:T(8,128)S(1)} %collective-permute-done.9.refs_2_), channel_id=1, source_target_pairs={{0,8},{8,0},{1,9},{9,1},{2,10},{10,2},{3,11},{11,3},{4,12},{12,4},... | collective-permute-start | bytes 1572872 | tf_op jit(solution)/shard_map/ppermute | solution.py:210
  71.6 1.9 %collective-permute-start.8 = (f32[128,1024]{1,0:T(8,128)S(1)}, f32[128,1024]{1,0:T(8,128)S(1)}, u32[]{:S(2)}, u32[]{:S(2)}) collective-permute-start(f32[128,1024]{1,0:T(8,128)S(1)} %collective-permute-done.6.refs_3_), channel_id=1, source_target_pairs={{0,8},{8,0},{1,9},{9,1},{2,10},{10,2},{3,11},{11,3},{4,12},{12,4},... | collective-permute-start | bytes 1572872 | tf_op jit(solution)/shard_map/ppermute | solution.py:210
  73.6 2.4 %collective-permute-start.14 = (f32[128,1024]{1,0:T(8,128)S(1)}, f32[128,1024]{1,0:T(8,128)S(1)}, u32[]{:S(2)}, u32[]{:S(2)}) collective-permute-start(f32[128,1024]{1,0:T(8,128)S(1)} %collective-permute-done.13.refs_2_), channel_id=1, source_target_pairs={{0,8},{8,0},{1,9},{9,1},{2,10},{10,2},{3,11},{11,3},{4,12},{12,4},... | collective-permute-start | bytes 1572872 | tf_op jit(solution)/shard_map/ppermute | solution.py:210
  76.0 2.0 %collective-permute-start.12 = (f32[128,1024]{1,0:T(8,128)S(1)}, f32[128,1024]{1,0:T(8,128)S(1)}, u32[]{:S(2)}, u32[]{:S(2)}) collective-permute-start(f32[128,1024]{1,0:T(8,128)S(1)} %collective-permute-done.10.refs_3_), channel_id=1, source_target_pairs={{0,8},{8,0},{1,9},{9,1},{2,10},{10,2},{3,11},{11,3},{4,12},{12,4},... | collective-permute-start | bytes 1572872 | tf_op jit(solution)/shard_map/ppermute | solution.py:210
  81.4 1.1 copy-done.4
  82.5 1.0 copy-done.5
  83.5 12.7 %ladder.1 = f32[512,1024]{1,0:T(8,128)} custom-call(f32[32,136,128]{2,1,0:T(8,128)} %all-to-all-done.refs_0_, bf16[512,1024]{1,0:T(8,128)(2,1)S(1)} %get-tuple-element.17.refs_1_, bf16[512,1024]{1,0:T(8,128)(2,1)S(1)} %get-tuple-element.18.refs_2_, bf16[512,1024]{1,0:T(8,128)(2,1)S(1)} %get-tuple-element.19.refs_3_, bf16[512,1024]{1,0:T(8,128)(2,1)} %copy-done.1, ...), custom_call_target="tpu_custom_call" | custom-call | flops 6442450944 | bytes 16777216 | tf_op jit(solution)/shard_map/ladder/pallas_call | solution.py:186
  96.1 31.4 %all_to_all.15 = f32[4,128,1024]{2,1,0:T(8,128)S(1)} all-to-all(f32[4,128,1024]{2,1,0:T(8,128)} %bitcast.6), channel_id=1, replica_groups=mesh['x'=4,'z'=8,'core'=2,'grp'=8] {'x'}, dimensions={0} | all-to-all | bytes 4194304 | tf_op jit(solution)/shard_map/all_to_all | solution.py:244
  127.8 23.5 %all_to_all.16 = f32[8,16,1024]{2,1,0:T(8,128)S(1)} all-to-all(f32[8,16,1024]{2,1,0:T(8,128)S(1)} %bitcast.7), channel_id=1, replica_groups=mesh['x'=4,'z'=8,'core'=2,'grp'=8] {'z'}, dimensions={0} | all-to-all | bytes 1048576 | tf_op jit(solution)/shard_map/all_to_all | solution.py:246
  (31 shorter events, 4.9 us)
Async XLA Ops:
  0.0 6.7 %collective-permute-start = (f32[128,1024]{1,0:T(8,128)}, f32[128,1024]{1,0:T(8,128)S(1)}, u32[]{:S(2)}, u32[]{:S(2)}) collective-permute-start(f32[128,1024]{1,0:T(8,128)} %refs_0_.1), channel_id=1, source_target_pairs={{0,8},{8,0},{1,9},{9,1},{2,10},{10,2},{3,11},{11,3},{4,12},{12,4},... | collective-permute-start | bytes 1572872 | tf_op jit(solution)/shard_map/ppermute | solution.py:210
  6.7 13.4 %copy-start = (f32[128,1024]{1,0:T(8,128)S(1)}, f32[128,1024]{1,0:T(8,128)}, u32[]{:S(2)}) copy-start(f32[128,1024]{1,0:T(8,128)} %refs_0_.1) | copy-start | bytes 1572868
  6.7 76.8 %all-to-all-start = ((f32[32,136,128]{2,1,0:T(8,128)}), f32[32,136,128]{2,1,0:T(8,128)}, u32[]{:S(2)}, u32[]{:S(2)}) async-start(f32[32,136,128]{2,1,0:T(8,128)} %pack.1), calls=%async_computation | async-start | bytes 4456448 | tf_op jit(solution)/shard_map/all_to_all | solution.py:240
  20.1 11.4 %collective-permute-start.1 = (f32[128,1024]{1,0:T(8,128)S(1)}, f32[128,1024]{1,0:T(8,128)S(1)}, u32[]{:S(2)}, u32[]{:S(2)}) collective-permute-start(f32[128,1024]{1,0:T(8,128)S(1)} %copy-done), channel_id=1, source_target_pairs={{0,1},{1,2},{2,3},{3,4},{4,5},{5,6},{6,7},{7,0},{8,15},{9,8},{10,9... | collective-permute-start | bytes 1572872 | tf_op jit(solution)/shard_map/ppermute | solution.py:217
  31.5 12.3 %collective-permute-start.5 = (f32[128,1024]{1,0:T(8,128)S(1)}, f32[128,1024]{1,0:T(8,128)S(1)}, u32[]{:S(2)}, u32[]{:S(2)}) collective-permute-start(f32[128,1024]{1,0:T(8,128)S(1)} %collective-permute-done.1.refs_2_), channel_id=1, source_target_pairs={{0,1},{1,2},{2,3},{3,4},{4,5},{5,6},{6,7},{7,0},{8,15},{9,8},{10,9... | collective-permute-start | bytes 1572872 | tf_op jit(solution)/shard_map/ppermute | solution.py:217
  37.1 12.3 %collective-permute-start.2 = (f32[128,1024]{1,0:T(8,128)S(1)}, f32[128,1024]{1,0:T(8,128)S(1)}, u32[]{:S(2)}, u32[]{:S(2)}) collective-permute-start(f32[128,1024]{1,0:T(8,128)S(1)} %collective-permute-done.refs_1_), channel_id=1, source_target_pairs={{0,1},{1,2},{2,3},{3,4},{4,5},{5,6},{6,7},{7,0},{8,15},{9,8},{10,9... | collective-permute-start | bytes 1572872 | tf_op jit(solution)/shard_map/ppermute | solution.py:217
  43.8 15.6 %collective-permute-start.9 = (f32[128,1024]{1,0:T(8,128)S(1)}, f32[128,1024]{1,0:T(8,128)S(1)}, u32[]{:S(2)}, u32[]{:S(2)}) collective-permute-start(f32[128,1024]{1,0:T(8,128)S(1)} %collective-permute-done.5.refs_2_), channel_id=1, source_target_pairs={{0,1},{1,2},{2,3},{3,4},{4,5},{5,6},{6,7},{7,0},{8,15},{9,8},{10,9... | collective-permute-start | bytes 1572872 | tf_op jit(solution)/shard_map/ppermute | solution.py:217
  49.4 12.3 %collective-permute-start.6 = (f32[128,1024]{1,0:T(8,128)S(1)}, f32[128,1024]{1,0:T(8,128)S(1)}, u32[]{:S(2)}, u32[]{:S(2)}) collective-permute-start(f32[128,1024]{1,0:T(8,128)S(1)} %collective-permute-done.2.refs_3_), channel_id=1, source_target_pairs={{0,1},{1,2},{2,3},{3,4},{4,5},{5,6},{6,7},{7,0},{8,15},{9,8},{10,9... | collective-permute-start | bytes 1572872 | tf_op jit(solution)/shard_map/ppermute | solution.py:217
  55.0 14.2 %collective-permute-start.3 = (f32[128,1024]{1,0:T(8,128)S(1)}, f32[128,1024]{1,0:T(8,128)S(1)}, u32[]{:S(2)}, u32[]{:S(2)}) collective-permute-start(f32[128,1024]{1,0:T(8,128)S(1)} %collective-permute-done.1.refs_2_), channel_id=1, source_target_pairs={{0,8},{8,0},{1,9},{9,1},{2,10},{10,2},{3,11},{11,3},{4,12},{12,4},... | collective-permute-start | bytes 1572872 | tf_op jit(solution)/shard_map/ppermute | solution.py:210
  56.9 14.7 %collective-permute-start.4 = (f32[128,1024]{1,0:T(8,128)S(1)}, f32[128,1024]{1,0:T(8,128)S(1)}, u32[]{:S(2)}, u32[]{:S(2)}) collective-permute-start(f32[128,1024]{1,0:T(8,128)S(1)} %collective-permute-done.2.refs_3_), channel_id=1, source_target_pairs={{0,8},{8,0},{1,9},{9,1},{2,10},{10,2},{3,11},{11,3},{4,12},{12,4},... | collective-permute-start | bytes 1572872 | tf_op jit(solution)/shard_map/ppermute | solution.py:210
  59.4 14.2 %collective-permute-start.13 = (f32[128,1024]{1,0:T(8,128)S(1)}, f32[128,1024]{1,0:T(8,128)S(1)}, u32[]{:S(2)}, u32[]{:S(2)}) collective-permute-start(f32[128,1024]{1,0:T(8,128)S(1)} %collective-permute-done.9.refs_2_), channel_id=1, source_target_pairs={{0,1},{1,2},{2,3},{3,4},{4,5},{5,6},{6,7},{7,0},{8,15},{9,8},{10,9... | collective-permute-start | bytes 1572872 | tf_op jit(solution)/shard_map/ppermute | solution.py:217
  61.7 14.4 %collective-permute-start.10 = (f32[128,1024]{1,0:T(8,128)S(1)}, f32[128,1024]{1,0:T(8,128)S(1)}, u32[]{:S(2)}, u32[]{:S(2)}) collective-permute-start(f32[128,1024]{1,0:T(8,128)S(1)} %collective-permute-done.6.refs_3_), channel_id=1, source_target_pairs={{0,1},{1,2},{2,3},{3,4},{4,5},{5,6},{6,7},{7,0},{8,15},{9,8},{10,9... | collective-permute-start | bytes 1572872 | tf_op jit(solution)/shard_map/ppermute | solution.py:217
  67.3 11.4 %collective-permute-start.7 = (f32[128,1024]{1,0:T(8,128)S(1)}, f32[128,1024]{1,0:T(8,128)S(1)}, u32[]{:S(2)}, u32[]{:S(2)}) collective-permute-start(f32[128,1024]{1,0:T(8,128)S(1)} %collective-permute-done.5.refs_2_), channel_id=1, source_target_pairs={{0,8},{8,0},{1,9},{9,1},{2,10},{10,2},{3,11},{11,3},{4,12},{12,4},... | collective-permute-start | bytes 1572872 | tf_op jit(solution)/shard_map/ppermute | solution.py:210
  69.2 11.8 %collective-permute-start.11 = (f32[128,1024]{1,0:T(8,128)S(1)}, f32[128,1024]{1,0:T(8,128)S(1)}, u32[]{:S(2)}, u32[]{:S(2)}) collective-permute-start(f32[128,1024]{1,0:T(8,128)S(1)} %collective-permute-done.9.refs_2_), channel_id=1, source_target_pairs={{0,8},{8,0},{1,9},{9,1},{2,10},{10,2},{3,11},{11,3},{4,12},{12,4},... | collective-permute-start | bytes 1572872 | tf_op jit(solution)/shard_map/ppermute | solution.py:210
  71.6 7.1 %collective-permute-start.8 = (f32[128,1024]{1,0:T(8,128)S(1)}, f32[128,1024]{1,0:T(8,128)S(1)}, u32[]{:S(2)}, u32[]{:S(2)}) collective-permute-start(f32[128,1024]{1,0:T(8,128)S(1)} %collective-permute-done.6.refs_3_), channel_id=1, source_target_pairs={{0,8},{8,0},{1,9},{9,1},{2,10},{10,2},{3,11},{11,3},{4,12},{12,4},... | collective-permute-start | bytes 1572872 | tf_op jit(solution)/shard_map/ppermute | solution.py:210
  73.6 7.5 %collective-permute-start.14 = (f32[128,1024]{1,0:T(8,128)S(1)}, f32[128,1024]{1,0:T(8,128)S(1)}, u32[]{:S(2)}, u32[]{:S(2)}) collective-permute-start(f32[128,1024]{1,0:T(8,128)S(1)} %collective-permute-done.13.refs_2_), channel_id=1, source_target_pairs={{0,8},{8,0},{1,9},{9,1},{2,10},{10,2},{3,11},{11,3},{4,12},{12,4},... | collective-permute-start | bytes 1572872 | tf_op jit(solution)/shard_map/ppermute | solution.py:210
  76.0 5.0 %collective-permute-start.12 = (f32[128,1024]{1,0:T(8,128)S(1)}, f32[128,1024]{1,0:T(8,128)S(1)}, u32[]{:S(2)}, u32[]{:S(2)}) collective-permute-start(f32[128,1024]{1,0:T(8,128)S(1)} %collective-permute-done.10.refs_3_), channel_id=1, source_target_pairs={{0,8},{8,0},{1,9},{9,1},{2,10},{10,2},{3,11},{11,3},{4,12},{12,4},... | collective-permute-start | bytes 1572872 | tf_op jit(solution)/shard_map/ppermute | solution.py:210
  78.7 2.3 %copy-start.1 = (bf16[512,1024]{1,0:T(8,128)(2,1)}, bf16[512,1024]{1,0:T(8,128)(2,1)S(1)}, u32[]{:S(2)}) copy-start(bf16[512,1024]{1,0:T(8,128)(2,1)S(1)} %get-tuple-element.20.refs_4_) | copy-start | bytes 3145732
  79.1 1.0 copy-start.2
  80.1 1.0 copy-start.3
  81.4 1.1 copy-start.4
  82.5 1.0 copy-start.5

commit v5 on v4

--- a/solution.py
+++ b/solution.py
@@ -11,7 +11,6 @@
 EVERY = ("x", "z", "core", "grp")
 LANES = 128
 HEAD = 8
-BAND = 4
 VMEM = pl.BlockSpec(memory_space=pltpu.VMEM)
 SMEM = pl.BlockSpec(memory_space=pltpu.SMEM)
 ANY = pl.BlockSpec(memory_space=pl.ANY)
@@ -77,57 +76,31 @@
     return high, (value - high.astype(jnp.float32)).astype(jnp.bfloat16)
 
 
-def split_kernel(*refs):
-    blocks, (high_ref, low_ref) = refs[:-2], refs[-2:]
-    at = 0
-    for ref in blocks:
-        for i in range(0, ref.shape[0], 64):
-            high, low = split(ref[i : i + 64, :])
-            high_ref[at : at + 64, :] = high
-            low_ref[at : at + 64, :] = low
-            at += 64
-
-
-def split_panel(blocks):
-    depth = sum(block.shape[0] for block in blocks)
-    out = jax.ShapeDtypeStruct((depth, blocks[0].shape[1]), jnp.bfloat16)
-    return pl.pallas_call(
-        split_kernel,
-        out_shape=(out, out),
-        in_specs=[VMEM] * len(blocks),
-        out_specs=(VMEM, VMEM),
-        cost_estimate=pl.CostEstimate(flops=0, bytes_accessed=8 * depth * 1024, transcendentals=0),
-        compiler_params=pltpu.CompilerParams(vmem_limit_bytes=18 << 20),
-        name="split_panel",
-    )(*blocks)
-
-
-def ladder_kernel(parts, got_hbm, *refs):
-    panel_hbm, (out_hbm, got, head, v_high, v_low, left, total, sems, out_sems) = (
-        refs[: 2 * parts],
-        refs[2 * parts :],
+def ladder_kernel(pieces, got_hbm, *refs):
+    blocks = len({piece[0] for piece in pieces})
+    panel_hbm, (out_hbm, got, head, panel, v_high, v_low, left, total, sems, out_sems) = (
+        refs[:blocks],
+        refs[blocks:],
     )
     chips = got.shape[0]
     height = total.shape[0]
     rows = height // chips
+    depth = panel.shape[0]
     first = [
         pltpu.make_async_copy(got_hbm.at[:, pl.ds(0, HEAD), :], head, sems.at[0]),
         pltpu.make_async_copy(got_hbm, got, sems.at[1]),
     ]
-    panel = []
-    starts = [0]
-    for i in range(parts):
-        size = panel_hbm[2 * i].shape[0]
-        for j, ref in enumerate((v_high, v_low)):
-            panel.append(
-                pltpu.make_async_copy(
-                    panel_hbm[2 * i + j],
-                    ref.at[pl.ds(starts[-1], size), :],
-                    sems.at[2 + 2 * i + j],
-                )
-            )
-        starts.append(starts[-1] + size)
-    for copy in first + panel:
+    halves = ([], [])
+    at = 0
+    for i, (block, start, size) in enumerate(pieces):
+        copy = pltpu.make_async_copy(
+            panel_hbm[block].at[pl.ds(start, size), :],
+            panel.at[pl.ds(at, size), :],
+            sems.at[2 + i],
+        )
+        halves[at * 2 // depth].append(copy)
+        at += size
+    for copy in first + halves[0] + halves[1]:
         copy.start()
 
     def clear(i, carry):
@@ -151,51 +124,52 @@
     dot = lambda a, b: jnp.dot(a, b, preferred_element_type=jnp.float32)
     wide = 256
     steps = total.shape[1] // wide
-
-    def product(lo, hi, cols):
-        both = dot(left[:, lo:hi], v_high[lo:hi, cols])
-        return both[:height] + (both[height:] + dot(left[:height, lo:hi], v_low[lo:hi, cols]))
-
-    middle = parts // 2
-    for copy in panel[: 2 * middle]:
-        copy.wait()
-
-    def near(i, carry):
-        cols = pl.ds(pl.multiple_of(i * wide, wide), wide)
-        total[:, cols] = product(0, starts[middle], cols)
-        return carry
-
-    lax.fori_loop(0, steps, near, 0)
-    for copy in panel[2 * middle :]:
-        copy.wait()
     done = []
-    for i in range(steps):
-        cols = pl.ds(i * wide, wide)
-        total[:, cols] += product(starts[middle], starts[parts], cols)
-        done.append(pltpu.make_async_copy(total.at[:, cols], out_hbm.at[:, cols], out_sems.at[i]))
-        done[-1].start()
+    for which in range(2):
+        lo, hi = which * depth // 2, (which + 1) * depth // 2
+        for copy in halves[which]:
+            copy.wait()
+
+        def split_rows(i, carry):
+            at = pl.ds(pl.multiple_of(lo + i * 32, 32), 32)
+            v_high[at, :], v_low[at, :] = split(panel[at, :])
+            return carry
+
+        lax.fori_loop(0, (hi - lo) // 32, split_rows, 0)
+        for i in range(steps):
+            cols = pl.ds(i * wide, wide)
+            both = dot(left[:, lo:hi], v_high[lo:hi, cols])
+            part = both[:height] + (both[height:] + dot(left[:height, lo:hi], v_low[lo:hi, cols]))
+            if which == 0:
+                total[:, cols] = part
+            else:
+                total[:, cols] += part
+                done.append(
+                    pltpu.make_async_copy(total.at[:, cols], out_hbm.at[:, cols], out_sems.at[i])
+                )
+                done[-1].start()
     for copy in done:
         copy.wait()
 
 
-def ladder(got, panels, rows):
+def ladder(got, blocks, pieces, rows):
     chips = got.shape[0]
-    depth = sum(high.shape[0] for high, _ in panels)
-    cols = panels[0][0].shape[1]
-    parts = len(panels)
+    depth = sum(size for _, _, size in pieces)
+    cols = blocks[0].shape[1]
     return pl.pallas_call(
-        lambda *refs: ladder_kernel(parts, *refs),
+        lambda *refs: ladder_kernel(pieces, *refs),
         out_shape=jax.ShapeDtypeStruct((chips * rows, cols), jnp.float32),
-        in_specs=[ANY] * (1 + 2 * parts),
+        in_specs=[ANY] * (1 + len(blocks)),
         out_specs=ANY,
         scratch_shapes=[
             pltpu.VMEM(got.shape, jnp.float32),
             pltpu.SMEM((chips, HEAD, LANES), jnp.float32),
+            pltpu.VMEM((depth, cols), jnp.float32),
             pltpu.VMEM((depth, cols), jnp.bfloat16),
             pltpu.VMEM((depth, cols), jnp.bfloat16),
             pltpu.VMEM((2 * chips * rows, depth + LANES), jnp.bfloat16),
             pltpu.VMEM((chips * rows, cols), jnp.float32),
-            pltpu.SemaphoreType.DMA((2 + 2 * parts,)),
+            pltpu.SemaphoreType.DMA((2 + len(pieces),)),
             pltpu.SemaphoreType.DMA((cols // 256,)),
         ],
         cost_estimate=pl.CostEstimate(
@@ -203,7 +177,7 @@
         ),
         compiler_params=pltpu.CompilerParams(vmem_limit_bytes=50 << 20),
         name="ladder",
-    )(got, *[half for panel in panels for half in panel])
+    )(got, *blocks)
 
 
 def swap_core(block):
@@ -219,12 +193,33 @@
 
 def gather_panel(own, mate):
     n = lax.axis_size("grp")
-    blocks = [own, mate]
+    size = own.shape[0]
+    blocks, pieces = [], []
+
+    def place(block, start=0, length=None):
+        for known, other in enumerate(blocks):
+            if other is block:
+                break
+        else:
+            known = len(blocks)
+            blocks.append(block)
+        pieces.append((known, start, length or block.shape[0]))
+
+    place(own)
+    place(mate)
     for _ in range(n // 2 - 1):
         own, mate = along_ring(own), along_ring(mate)
-        blocks += [own, mate, swap_core(own), swap_core(mate)]
-    own = along_ring(own)
-    return blocks + [own, swap_core(own)]
+        place(own)
+        place(mate)
+        place(swap_core(jnp.concatenate([own, mate], axis=0)))
+    half = size // 2
+    top, bottom = along_ring(own[:half]), along_ring(mate[half:])
+    swapped = swap_core(jnp.concatenate([top, bottom], axis=0))
+    place(top)
+    place(swapped, half, half)
+    place(swapped, 0, half)
+    place(bottom)
+    return blocks, pieces
 
 
 def on_device(amplitudes, integrals, occupancy, tile_place):
@@ -236,10 +231,9 @@
     pos = jnp.stack([lax.axis_index("core"), lax.axis_index("grp")]).astype(jnp.int32)
     sent = pack(pos, occupancy[0], tile_place, amplitudes[0], chips, per_chip)
     sent, mate = lax.optimization_barrier((sent, mate))
-    panel = gather_panel(integrals, mate)
+    blocks, pieces = gather_panel(integrals, mate)
     got = lax.all_to_all(sent, CHIPS, 0, 0, tiled=True)
-    panels = [split_panel(panel[i : i + BAND]) for i in range(0, len(panel), BAND)]
-    part = ladder(got, panels, rows)
+    part = ladder(got, blocks, pieces, rows)
     part = part.reshape(NX, NZ * rows, cols)
     part = lax.all_to_all(part, "x", 0, 0, tiled=True).sum(axis=0)
     part = part.reshape(NZ, rows, cols)

time: 153 us -> 152 us (level)
  waiting for transfers between devices: 11.6 us -> 15.5 us
  local copies, waits for them, and re-layouts: 4.05 us -> 1.95 us
    ppermute x8 -> x5, starting transfers between devices: 16.9 us -> 10.1 us  [swap_core(): return lax.ppermute(block, 'core', [(0, 1), (1, 0)])]
    ppermute x7 -> x8, starting transfers between devices: 31.3 us -> 37.2 us  [along_ring(): return lax.ppermute(block, ('core', 'grp'), pairs)]
    unnamed x12 -> x16, local copies, waits for them, and re-layouts: 4.05 us -> 1.91 us
    ppermute x7 -> x8, waiting for transfers between devices: 11.5 us -> 13.6 us  [along_ring(): return lax.ppermute(block, ('core', 'grp'), pairs)]
    ppermute x8 -> x5, waiting for transfers between devices: 0.02 us -> 1.85 us  [swap_core(): return lax.ppermute(block, 'core', [(0, 1), (1, 0)])]
    pallas_call x5 -> x1, Pallas kernels: 14 us -> 13.5 us  [ladder(): pl.pallas_call(lambda *refs: ladder_kernel(pieces, *refs), out_shape=jax....]
  transfers between devices with their start and end apart: 16 -> 14, of which waited for: 3 -> 6; matrix products, arithmetic and copies ran while one was open for 0% -> 1% of each run, Pallas kernels for 4% -> 3%
where the time goes in v5:
time: 152 us
  starting transfers between devices  60.7 us (40%)
  blocking collectives  54 us (36%)
  Pallas kernels  17.7 us (12%)
  waiting for transfers between devices  15.5 us (10%)
  local copies, waits for them, and re-layouts  1.95 us (1%)
  other arithmetic  1.74 us (1%)
    ppermute x8, starting transfers between devices, along_ring(): return lax.ppermute(block, ('core', 'grp'), pairs)  37.2 us
    all_to_all x1, blocking collectives, on_device(): part = lax.all_to_all(part, 'x', 0, 0, tiled=True).sum(axis=0)  31.2 us
    all_to_all x1, blocking collectives, on_device(): return lax.all_to_all(part, 'z', 0, 0, tiled=True).sum(axis=0)  22.8 us
    ppermute x8, waiting for transfers between devices, along_ring(): return lax.ppermute(block, ('core', 'grp'), pairs)  13.6 us
    pallas_call x1, Pallas kernels, ladder(): pl.pallas_call(lambda *refs: ladder_kernel(pieces, *refs), out_shape=jax....  13.5 us
    all_to_all x1, starting transfers between devices, on_device(): got = lax.all_to_all(sent, CHIPS, 0, 0, tiled=True)  13.4 us
    ppermute x5, starting transfers between devices, swap_core(): return lax.ppermute(block, 'core', [(0, 1), (1, 0)])  10.1 us
    pallas_call x1, Pallas kernels, pack(): pl.pallas_call(pack_kernel, out_shape=jax.ShapeDtypeStruct((chips, HEAD +...  4.16 us
  transfers between devices with their start and end apart: 14, of which 6 were waited for; matrix products, arithmetic and copies ran while one was open for 1% of the time, Pallas kernels for 3%

profile of v5, /device:TPU:24, one launch (start us, length us, event | category | flops | bytes accessed | tf_op | source)
XLA Modules:
  0.0 151.7 jit_solution(671978680896996099)
XLA Ops:
  0.0 1.9 %collective-permute-start = (f32[128,1024]{1,0:T(8,128)}, f32[128,1024]{1,0:T(8,128)S(1)}, u32[]{:S(2)}, u32[]{:S(2)}) collective-permute-start(f32[128,1024]{1,0:T(8,128)} %refs_1_.1), channel_id=1, source_target_pairs={{0,8},{8,0},{1,9},{9,1},{2,10},{10,2},{3,11},{11,3},{4,12},{12,4},... | collective-permute-start | bytes 1572872 | tf_op jit(solution)/shard_map/ppermute | solution.py:184
  2.5 4.2 %pack.1 = f32[32,136,128]{2,1,0:T(8,128)} custom-call(s32[2]{0:T(128)} %pad_add_fusion.pos_ref, s32[128]{0:T(128)} %bitcast.9, s32[512]{0:T(512)} %place_ref.1, f32[128,16,128]{2,1,0:T(8,128)} %bitcast.8), custom_call_target="tpu_custom_call" | custom-call | bytes 8388608 | tf_op jit(solution)/shard_map/pack/pallas_call | solution.py:63
  6.6 13.4 %all-to-all-start = ((f32[32,136,128]{2,1,0:T(8,128)}), f32[32,136,128]{2,1,0:T(8,128)}, u32[]{:S(2)}, u32[]{:S(2)}) async-start(f32[32,136,128]{2,1,0:T(8,128)} %pack.1), calls=%async_computation | async-start | bytes 4456448 | tf_op jit(solution)/shard_map/all_to_all | solution.py:235
  20.1 4.7 %collective-permute-start.1 = (f32[128,1024]{1,0:T(8,128)S(1)}, f32[128,1024]{1,0:T(8,128)S(1)}, u32[]{:S(2)}, u32[]{:S(2)}) collective-permute-start(f32[128,1024]{1,0:T(8,128)S(1)} %copy-done), channel_id=1, source_target_pairs={{0,1},{1,2},{2,3},{3,4},{4,5},{5,6},{6,7},{7,0},{8,15},{9,8},{10,9... | collective-permute-start | bytes 1572872 | tf_op jit(solution)/shard_map/ppermute | solution.py:191
  24.8 2.6 %collective-permute-start.2 = (f32[128,1024]{1,0:T(8,128)S(1)}, f32[128,1024]{1,0:T(8,128)S(1)}, u32[]{:S(2)}, u32[]{:S(2)}) collective-permute-start(f32[128,1024]{1,0:T(8,128)S(1)} %collective-permute-done.refs_2_), channel_id=1, source_target_pairs={{0,1},{1,2},{2,3},{3,4},{4,5},{5,6},{6,7},{7,0},{8,15},{9,8},{10,9... | collective-permute-start | bytes 1572872 | tf_op jit(solution)/shard_map/ppermute | solution.py:191
  27.4 4.1 %collective-permute-done.1.refs_3_ = f32[128,1024]{1,0:T(8,128)S(1)} collective-permute-done((f32[128,1024]{1,0:T(8,128)S(1)}, f32[128,1024]{1,0:T(8,128)S(1)}, u32[]{:S(2)}, u32[]{:S(2)}) %collective-permute-start.1) | collective-permute-done | bytes 524320 | tf_op jit(solution)/shard_map/ppermute | solution.py:191
  31.5 5.6 %collective-permute-start.4 = (f32[128,1024]{1,0:T(8,128)S(1)}, f32[128,1024]{1,0:T(8,128)S(1)}, u32[]{:S(2)}, u32[]{:S(2)}) collective-permute-start(f32[128,1024]{1,0:T(8,128)S(1)} %collective-permute-done.1.refs_3_), channel_id=1, source_target_pairs={{0,1},{1,2},{2,3},{3,4},{4,5},{5,6},{6,7},{7,0},{8,15},{9,8},{10,9... | collective-permute-start | bytes 1572872 | tf_op jit(solution)/shard_map/ppermute | solution.py:191
  37.1 5.6 %collective-permute-start.5 = (f32[128,1024]{1,0:T(8,128)S(1)}, f32[128,1024]{1,0:T(8,128)S(1)}, u32[]{:S(2)}, u32[]{:S(2)}) collective-permute-start(f32[128,1024]{1,0:T(8,128)S(1)} %collective-permute-done.2.refs_4_), channel_id=1, source_target_pairs={{0,1},{1,2},{2,3},{3,4},{4,5},{5,6},{6,7},{7,0},{8,15},{9,8},{10,9... | collective-permute-start | bytes 1572872 | tf_op jit(solution)/shard_map/ppermute | solution.py:191
  42.7 1.1 collective-permute-done.4.refs_6_
  43.7 5.6 %collective-permute-start.7 = (f32[128,1024]{1,0:T(8,128)S(1)}, f32[128,1024]{1,0:T(8,128)S(1)}, u32[]{:S(2)}, u32[]{:S(2)}) collective-permute-start(f32[128,1024]{1,0:T(8,128)S(1)} %collective-permute-done.4.refs_6_), channel_id=1, source_target_pairs={{0,1},{1,2},{2,3},{3,4},{4,5},{5,6},{6,7},{7,0},{8,15},{9,8},{10,9... | collective-permute-start | bytes 1572872 | tf_op jit(solution)/shard_map/ppermute | solution.py:191
  49.4 5.6 %collective-permute-start.8 = (f32[128,1024]{1,0:T(8,128)S(1)}, f32[128,1024]{1,0:T(8,128)S(1)}, u32[]{:S(2)}, u32[]{:S(2)}) collective-permute-start(f32[128,1024]{1,0:T(8,128)S(1)} %collective-permute-done.5.refs_7_), channel_id=1, source_target_pairs={{0,1},{1,2},{2,3},{3,4},{4,5},{5,6},{6,7},{7,0},{8,15},{9,8},{10,9... | collective-permute-start | bytes 1572872 | tf_op jit(solution)/shard_map/ppermute | solution.py:191
  55.1 1.9 %collective-permute-start.3 = (f32[256,1024]{1,0:T(8,128)S(1)}, f32[256,1024]{1,0:T(8,128)S(1)}, u32[]{:S(2)}, u32[]{:S(2)}) collective-permute-start(f32[256,1024]{1,0:T(8,128)S(1)} %pad_maximum_fusion), channel_id=1, source_target_pairs={{0,8},{8,0},{1,9},{9,1},{2,10},{10,2},{3,11},{11,3},{4,12},{12,4},... | collective-permute-start | bytes 3145736 | tf_op jit(solution)/shard_map/ppermute | solution.py:184
  57.1 2.4 %collective-permute-start.6 = (f32[256,1024]{1,0:T(8,128)S(1)}, f32[256,1024]{1,0:T(8,128)S(1)}, u32[]{:S(2)}, u32[]{:S(2)}) collective-permute-start(f32[256,1024]{1,0:T(8,128)S(1)} %pad_maximum_fusion.1), channel_id=1, source_target_pairs={{0,8},{8,0},{1,9},{9,1},{2,10},{10,2},{3,11},{11,3},{4,12},{12,4},... | collective-permute-start | bytes 3145736 | tf_op jit(solution)/shard_map/ppermute | solution.py:184
  59.5 2.1 %collective-permute-done.8.refs_10_ = f32[128,1024]{1,0:T(8,128)S(1)} collective-permute-done((f32[128,1024]{1,0:T(8,128)S(1)}, f32[128,1024]{1,0:T(8,128)S(1)}, u32[]{:S(2)}, u32[]{:S(2)}) %collective-permute-start.8) | collective-permute-done | bytes 524320 | tf_op jit(solution)/shard_map/ppermute | solution.py:191
  61.7 1.9 %collective-permute-start.9 = (f32[256,1024]{1,0:T(8,128)S(1)}, f32[256,1024]{1,0:T(8,128)}, u32[]{:S(2)}, u32[]{:S(2)}) collective-permute-start(f32[256,1024]{1,0:T(8,128)S(1)} %pad_maximum_fusion.2), channel_id=1, source_target_pairs={{0,8},{8,0},{1,9},{9,1},{2,10},{10,2},{3,11},{11,3},{4,12},{12,4},... | collective-permute-start | bytes 3145736 | tf_op jit(solution)/shard_map/ppermute | solution.py:184
  63.7 5.6 %collective-permute-start.10 = (f32[64,1024]{1,0:T(8,128)S(1)}, f32[64,1024]{1,0:T(8,128)S(1)}, u32[]{:S(2)}, u32[]{:S(2)}) collective-permute-start(f32[64,1024]{1,0:T(8,128)S(1)} %slice.8), channel_id=1, source_target_pairs={{0,1},{1,2},{2,3},{3,4},{4,5},{5,6},{6,7},{7,0},{8,15},{9,8},{10,9... | collective-permute-start | bytes 786440 | tf_op jit(solution)/shard_map/ppermute | solution.py:191
  69.3 1.9 %collective-permute-start.11 = (f32[64,1024]{1,0:T(8,128)S(1)}, f32[64,1024]{1,0:T(8,128)S(1)}, u32[]{:S(2)}, u32[]{:S(2)}) collective-permute-start(f32[64,1024]{1,0:T(8,128)S(1)} %slice.9), channel_id=1, source_target_pairs={{0,1},{1,2},{2,3},{3,4},{4,5},{5,6},{6,7},{7,0},{8,15},{9,8},{10,9... | collective-permute-start | bytes 786440 | tf_op jit(solution)/shard_map/ppermute | solution.py:191
  71.3 1.9 %collective-permute-done.10.refs_12_ = f32[64,1024]{1,0:T(8,128)S(1)} collective-permute-done((f32[64,1024]{1,0:T(8,128)S(1)}, f32[64,1024]{1,0:T(8,128)S(1)}, u32[]{:S(2)}, u32[]{:S(2)}) %collective-permute-start.10) | collective-permute-done | bytes 262176 | tf_op jit(solution)/shard_map/ppermute | solution.py:191
  73.2 4.4 %collective-permute-done.11.refs_14_ = f32[64,1024]{1,0:T(8,128)S(1)} collective-permute-done((f32[64,1024]{1,0:T(8,128)S(1)}, f32[64,1024]{1,0:T(8,128)S(1)}, u32[]{:S(2)}, u32[]{:S(2)}) %collective-permute-start.11) | collective-permute-done | bytes 262176 | tf_op jit(solution)/shard_map/ppermute | solution.py:191
  77.7 1.9 %collective-permute-start.12 = (f32[128,1024]{1,0:T(8,128)S(1)}, f32[128,1024]{1,0:T(8,128)S(1)}, u32[]{:S(2)}, u32[]{:S(2)}) collective-permute-start(f32[128,1024]{1,0:T(8,128)S(1)} %pad_maximum_fusion.3), channel_id=1, source_target_pairs={{0,8},{8,0},{1,9},{9,1},{2,10},{10,2},{3,11},{11,3},{4,12},{12,4},... | collective-permute-start | bytes 1572872 | tf_op jit(solution)/shard_map/ppermute | solution.py:184
  79.6 1.8 %collective-permute-done.12.refs_13_ = f32[128,1024]{1,0:T(8,128)S(1)} collective-permute-done((f32[128,1024]{1,0:T(8,128)S(1)}, f32[128,1024]{1,0:T(8,128)S(1)}, u32[]{:S(2)}, u32[]{:S(2)}) %collective-permute-start.12) | collective-permute-done | bytes 524320 | tf_op jit(solution)/shard_map/ppermute | solution.py:184
  83.4 13.5 %ladder.1 = f32[512,1024]{1,0:T(8,128)} custom-call(f32[32,136,128]{2,1,0:T(8,128)} %all-to-all-done.refs_0_, f32[128,1024]{1,0:T(8,128)S(1)} %copy-done, f32[128,1024]{1,0:T(8,128)S(1)} %copy-done.2, f32[128,1024]{1,0:T(8,128)S(1)} %collective-permute-done.1.refs_3_, f32[128,1024]{1,0:T(8,128)S(1)} %collective-permute-done.2.refs_4_, ...), custom_call_target="tpu_custom_call" | custom-call | flops 6442450944 | bytes 16777216 | tf_op jit(solution)/shard_map/ladder/pallas_call | solution.py:159
  96.9 31.2 %all_to_all.15 = f32[4,128,1024]{2,1,0:T(8,128)S(1)} all-to-all(f32[4,128,1024]{2,1,0:T(8,128)} %bitcast.6), channel_id=1, replica_groups=mesh['x'=4,'z'=8,'core'=2,'grp'=8] {'x'}, dimensions={0} | all-to-all | bytes 4194304 | tf_op jit(solution)/shard_map/all_to_all | solution.py:238
  128.3 22.8 %all_to_all.16 = f32[8,16,1024]{2,1,0:T(8,128)S(1)} all-to-all(f32[8,16,1024]{2,1,0:T(8,128)S(1)} %bitcast.7), channel_id=1, replica_groups=mesh['x'=4,'z'=8,'core'=2,'grp'=8] {'z'}, dimensions={0} | all-to-all | bytes 1048576 | tf_op jit(solution)/shard_map/all_to_all | solution.py:240
  (33 shorter events, 3.7 us)
Async XLA Ops:
  0.0 6.6 %collective-permute-start = (f32[128,1024]{1,0:T(8,128)}, f32[128,1024]{1,0:T(8,128)S(1)}, u32[]{:S(2)}, u32[]{:S(2)}) collective-permute-start(f32[128,1024]{1,0:T(8,128)} %refs_1_.1), channel_id=1, source_target_pairs={{0,8},{8,0},{1,9},{9,1},{2,10},{10,2},{3,11},{11,3},{4,12},{12,4},... | collective-permute-start | bytes 1572872 | tf_op jit(solution)/shard_map/ppermute | solution.py:184
  6.6 13.4 %copy-start = (f32[128,1024]{1,0:T(8,128)S(1)}, f32[128,1024]{1,0:T(8,128)}, u32[]{:S(2)}) copy-start(f32[128,1024]{1,0:T(8,128)} %refs_1_.1) | copy-start | bytes 1572868
  6.6 30.4 %copy-start.1 = (f32[128,1024]{1,0:T(8,128)}, f32[128,1024]{1,0:T(8,128)S(1)}, u32[]{:S(2)}) copy-start(f32[128,1024]{1,0:T(8,128)S(1)} %collective-permute-done.refs_2_) | copy-start | bytes 1572868
  6.6 75.7 %all-to-all-start = ((f32[32,136,128]{2,1,0:T(8,128)}), f32[32,136,128]{2,1,0:T(8,128)}, u32[]{:S(2)}, u32[]{:S(2)}) async-start(f32[32,136,128]{2,1,0:T(8,128)} %pack.1), calls=%async_computation | async-start | bytes 4456448 | tf_op jit(solution)/shard_map/all_to_all | solution.py:235
  20.1 11.4 %collective-permute-start.1 = (f32[128,1024]{1,0:T(8,128)S(1)}, f32[128,1024]{1,0:T(8,128)S(1)}, u32[]{:S(2)}, u32[]{:S(2)}) collective-permute-start(f32[128,1024]{1,0:T(8,128)S(1)} %copy-done), channel_id=1, source_target_pairs={{0,1},{1,2},{2,3},{3,4},{4,5},{5,6},{6,7},{7,0},{8,15},{9,8},{10,9... | collective-permute-start | bytes 1572872 | tf_op jit(solution)/shard_map/ppermute | solution.py:191
  24.8 12.3 %collective-permute-start.2 = (f32[128,1024]{1,0:T(8,128)S(1)}, f32[128,1024]{1,0:T(8,128)S(1)}, u32[]{:S(2)}, u32[]{:S(2)}) collective-permute-start(f32[128,1024]{1,0:T(8,128)S(1)} %collective-permute-done.refs_2_), channel_id=1, source_target_pairs={{0,1},{1,2},{2,3},{3,4},{4,5},{5,6},{6,7},{7,0},{8,15},{9,8},{10,9... | collective-permute-start | bytes 1572872 | tf_op jit(solution)/shard_map/ppermute | solution.py:191
  31.5 12.3 %collective-permute-start.4 = (f32[128,1024]{1,0:T(8,128)S(1)}, f32[128,1024]{1,0:T(8,128)S(1)}, u32[]{:S(2)}, u32[]{:S(2)}) collective-permute-start(f32[128,1024]{1,0:T(8,128)S(1)} %collective-permute-done.1.refs_3_), channel_id=1, source_target_pairs={{0,1},{1,2},{2,3},{3,4},{4,5},{5,6},{6,7},{7,0},{8,15},{9,8},{10,9... | collective-permute-start | bytes 1572872 | tf_op jit(solution)/shard_map/ppermute | solution.py:191
  37.1 12.3 %collective-permute-start.5 = (f32[128,1024]{1,0:T(8,128)S(1)}, f32[128,1024]{1,0:T(8,128)S(1)}, u32[]{:S(2)}, u32[]{:S(2)}) collective-permute-start(f32[128,1024]{1,0:T(8,128)S(1)} %collective-permute-done.2.refs_4_), channel_id=1, source_target_pairs={{0,1},{1,2},{2,3},{3,4},{4,5},{5,6},{6,7},{7,0},{8,15},{9,8},{10,9... | collective-permute-start | bytes 1572872 | tf_op jit(solution)/shard_map/ppermute | solution.py:191
  43.7 15.8 %collective-permute-start.7 = (f32[128,1024]{1,0:T(8,128)S(1)}, f32[128,1024]{1,0:T(8,128)S(1)}, u32[]{:S(2)}, u32[]{:S(2)}) collective-permute-start(f32[128,1024]{1,0:T(8,128)S(1)} %collective-permute-done.4.refs_6_), channel_id=1, source_target_pairs={{0,1},{1,2},{2,3},{3,4},{4,5},{5,6},{6,7},{7,0},{8,15},{9,8},{10,9... | collective-permute-start | bytes 1572872 | tf_op jit(solution)/shard_map/ppermute | solution.py:191
  49.4 12.3 %collective-permute-start.8 = (f32[128,1024]{1,0:T(8,128)S(1)}, f32[128,1024]{1,0:T(8,128)S(1)}, u32[]{:S(2)}, u32[]{:S(2)}) collective-permute-start(f32[128,1024]{1,0:T(8,128)S(1)} %collective-permute-done.5.refs_7_), channel_id=1, source_target_pairs={{0,1},{1,2},{2,3},{3,4},{4,5},{5,6},{6,7},{7,0},{8,15},{9,8},{10,9... | collective-permute-start | bytes 1572872 | tf_op jit(solution)/shard_map/ppermute | solution.py:191
  55.1 24.5 %collective-permute-start.3 = (f32[256,1024]{1,0:T(8,128)S(1)}, f32[256,1024]{1,0:T(8,128)S(1)}, u32[]{:S(2)}, u32[]{:S(2)}) collective-permute-start(f32[256,1024]{1,0:T(8,128)S(1)} %pad_maximum_fusion), channel_id=1, source_target_pairs={{0,8},{8,0},{1,9},{9,1},{2,10},{10,2},{3,11},{11,3},{4,12},{12,4},... | collective-permute-start | bytes 3145736 | tf_op jit(solution)/shard_map/ppermute | solution.py:184
  57.1 22.5 %collective-permute-start.6 = (f32[256,1024]{1,0:T(8,128)S(1)}, f32[256,1024]{1,0:T(8,128)S(1)}, u32[]{:S(2)}, u32[]{:S(2)}) collective-permute-start(f32[256,1024]{1,0:T(8,128)S(1)} %pad_maximum_fusion.1), channel_id=1, source_target_pairs={{0,8},{8,0},{1,9},{9,1},{2,10},{10,2},{3,11},{11,3},{4,12},{12,4},... | collective-permute-start | bytes 3145736 | tf_op jit(solution)/shard_map/ppermute | solution.py:184
  59.5 18.1 %copy-start.3 = (f32[128,1024]{1,0:T(8,128)}, f32[128,1024]{1,0:T(8,128)S(1)}, u32[]{:S(2)}) copy-start(f32[128,1024]{1,0:T(8,128)S(1)} %collective-permute-done.7.refs_9_) | copy-start | bytes 1572868
  61.6 16.0 %copy-start.4 = (f32[128,1024]{1,0:T(8,128)}, f32[128,1024]{1,0:T(8,128)S(1)}, u32[]{:S(2)}) copy-start(f32[128,1024]{1,0:T(8,128)S(1)} %collective-permute-done.8.refs_10_) | copy-start | bytes 1572868
  61.7 20.6 %collective-permute-start.9 = (f32[256,1024]{1,0:T(8,128)S(1)}, f32[256,1024]{1,0:T(8,128)}, u32[]{:S(2)}, u32[]{:S(2)}) collective-permute-start(f32[256,1024]{1,0:T(8,128)S(1)} %pad_maximum_fusion.2), channel_id=1, source_target_pairs={{0,8},{8,0},{1,9},{9,1},{2,10},{10,2},{3,11},{11,3},{4,12},{12,4},... | collective-permute-start | bytes 3145736 | tf_op jit(solution)/shard_map/ppermute | solution.py:184
  63.7 9.5 %collective-permute-start.10 = (f32[64,1024]{1,0:T(8,128)S(1)}, f32[64,1024]{1,0:T(8,128)S(1)}, u32[]{:S(2)}, u32[]{:S(2)}) collective-permute-start(f32[64,1024]{1,0:T(8,128)S(1)} %slice.8), channel_id=1, source_target_pairs={{0,1},{1,2},{2,3},{3,4},{4,5},{5,6},{6,7},{7,0},{8,15},{9,8},{10,9... | collective-permute-start | bytes 786440 | tf_op jit(solution)/shard_map/ppermute | solution.py:191
  69.3 8.3 %collective-permute-start.11 = (f32[64,1024]{1,0:T(8,128)S(1)}, f32[64,1024]{1,0:T(8,128)S(1)}, u32[]{:S(2)}, u32[]{:S(2)}) collective-permute-start(f32[64,1024]{1,0:T(8,128)S(1)} %slice.9), channel_id=1, source_target_pairs={{0,1},{1,2},{2,3},{3,4},{4,5},{5,6},{6,7},{7,0},{8,15},{9,8},{10,9... | collective-permute-start | bytes 786440 | tf_op jit(solution)/shard_map/ppermute | solution.py:191
  77.7 3.8 %collective-permute-start.12 = (f32[128,1024]{1,0:T(8,128)S(1)}, f32[128,1024]{1,0:T(8,128)S(1)}, u32[]{:S(2)}, u32[]{:S(2)}) collective-permute-start(f32[128,1024]{1,0:T(8,128)S(1)} %pad_maximum_fusion.3), channel_id=1, source_target_pairs={{0,8},{8,0},{1,9},{9,1},{2,10},{10,2},{3,11},{11,3},{4,12},{12,4},... | collective-permute-start | bytes 1572872 | tf_op jit(solution)/shard_map/ppermute | solution.py:184
  79.6 1.9 %copy-start.5 = (f32[256,1024]{1,0:T(8,128)}, f32[256,1024]{1,0:T(8,128)S(1)}, u32[]{:S(2)}) copy-start(f32[256,1024]{1,0:T(8,128)S(1)} %collective-permute-done.3.refs_5_) | copy-start | bytes 3145732
  79.6 1.9 %copy-start.6 = (f32[256,1024]{1,0:T(8,128)}, f32[256,1024]{1,0:T(8,128)S(1)}, u32[]{:S(2)}) copy-start(f32[256,1024]{1,0:T(8,128)S(1)} %collective-permute-done.6.refs_8_) | copy-start | bytes 3145732
  81.5 0.8 copy-start.7
  82.3 1.0 copy-start.2

commit v6 on v5

v6 whole, which is shorter than its diff:
```python
import jax
import jax.numpy as jnp
from jax import lax
from jax.experimental import pallas as pl
from jax.experimental.pallas import tpu as pltpu
from jax.sharding import Mesh, PartitionSpec as P

NX, NZ, NC = 4, 8, 2
CAP = 4
CHIPS = ("x", "z")
EVERY = ("x", "z", "core", "grp")
LANES = 128
HEAD = 8
EARLY = 10
VMEM_LIMIT = 20 << 20
VMEM = pl.BlockSpec(memory_space=pltpu.VMEM)
SMEM = pl.BlockSpec(memory_space=pltpu.SMEM)
ANY = pl.BlockSpec(memory_space=pl.ANY)


def panel_position(core, grp, of_core, of_grp, n):
    ahead = jnp.where(core == 0, grp - of_grp + n, of_grp - grp + n) % n
    other = jnp.where(core == of_core, 0, 1)
    near = jnp.where(ahead == 0, 0, 4 * ahead - 2) + other
    back = 4 * (n - ahead) + 1 - other
    return jnp.where(ahead <= n // 2, near, back)


def pack_kernel(occ_ref, place_ref, amp_ref, out_ref, count_ref, where_ref):
    rows = amp_ref.shape[1]
    per_chip = where_ref.shape[0]
    per_core = per_chip // NC
    here = lax.axis_index("core"), lax.axis_index("grp")
    heading = jnp.full((HEAD, LANES), per_chip, jnp.int32).astype(jnp.float32)
    lane = lax.broadcasted_iota(jnp.int32, (HEAD, LANES), 1)

    def clear(i, carry):
        count_ref[i] = 0
        out_ref[i, pl.ds(0, HEAD), :] = heading
        return carry

    lax.fori_loop(0, count_ref.shape[0], clear, 0, unroll=4)
    for core in range(NC):
        for grp in range(per_core):
            where_ref[core * per_core + grp] = panel_position(*here, core, grp, per_core)

    def step(j, carry):
        place = place_ref[occ_ref[j]]
        chip = place // per_chip
        at = where_ref[place % per_chip]
        slot = count_ref[chip]
        count_ref[chip] = slot + 1
        out_ref[chip, pl.ds(pl.multiple_of(HEAD + slot * rows, 8), rows), :] = amp_ref[j]
        out_ref[chip, pl.ds(0, HEAD), :] = jnp.where(
            lane == slot, at.astype(jnp.float32), out_ref[chip, pl.ds(0, HEAD), :]
        )
        return carry

    lax.fori_loop(0, occ_ref.shape[0], step, 0, unroll=4)


def pack(occ, place, amp, chips, per_chip):
    rows, width = amp.shape[1:]
    return pl.pallas_call(
        pack_kernel,
        out_shape=jax.ShapeDtypeStruct((chips, HEAD + NC * CAP * rows, width), jnp.float32),
        in_specs=[SMEM, SMEM, VMEM],
        out_specs=VMEM,
        scratch_shapes=[pltpu.SMEM((chips,), jnp.int32), pltpu.SMEM((per_chip,), jnp.int32)],
        cost_estimate=pl.CostEstimate(flops=0, bytes_accessed=8 << 20, transcendentals=0),
        name="pack",
    )(occ, place, amp)


def split(value):
    high = value.astype(jnp.bfloat16)
    return high, (value - high.astype(jnp.float32)).astype(jnp.bfloat16)


def spread_kernel(got_ref, left_ref, head, sem):
    chips = got_ref.shape[0]
    height = left_ref.shape[0] // 2
    rows = height // chips
    copy = pltpu.make_async_copy(got_ref.at[:, pl.ds(0, HEAD), :], head, sem)
    copy.start()

    def clear(i, carry):
        at = pl.ds(pl.multiple_of(i * 32, 32), 32)
        left_ref[at, :] = jnp.zeros((32, left_ref.shape[1]), left_ref.dtype)
        return carry

    lax.fori_loop(0, left_ref.shape[0] // 32, clear, 0)
    copy.wait()

    def step(n, carry):
        row = pl.multiple_of(n * rows, rows)
        for s in range(NC * CAP):
            col = pl.multiple_of(head[n, 0, s].astype(jnp.int32) * LANES, LANES)
            high, low = split(got_ref[n, HEAD + s * rows : HEAD + (s + 1) * rows, :])
            left_ref[pl.ds(row, rows), pl.ds(col, LANES)] = high
            left_ref[pl.ds(height + row, rows), pl.ds(col, LANES)] = low
        return carry

    lax.fori_loop(0, chips, step, 0, unroll=2)


def spread(got, rows, depth):
    chips = got.shape[0]
    return pl.pallas_call(
        spread_kernel,
        out_shape=jax.ShapeDtypeStruct((2 * chips * rows, depth + LANES), jnp.bfloat16),
        in_specs=[VMEM],
        out_specs=VMEM,
        scratch_shapes=[
            pltpu.SMEM((chips, HEAD, LANES), jnp.float32),
            pltpu.SemaphoreType.DMA,
        ],
        cost_estimate=pl.CostEstimate(flops=0, bytes_accessed=8 << 20, transcendentals=0),
        compiler_params=pltpu.CompilerParams(vmem_limit_bytes=VMEM_LIMIT),
        name="spread",
    )(got)


def product_kernel(pieces, start, has_total, *refs):
    left_ref, refs = refs[0], refs[1:]
    if has_total:
        total_ref, refs = refs[0], refs[1:]
    panel, (out_ref, v_high, v_low) = refs[:-3], refs[-3:]
    height = out_ref.shape[0]
    depth = v_high.shape[0]
    at = 0
    for block, first, size in pieces:
        for i in range(0, size, 64):
            value = panel[block][first + i : first + i + 64, :]
            v_high[at : at + 64, :], v_low[at : at + 64, :] = split(value)
            at += 64
    dot = lambda a, b: jnp.dot(a, b, preferred_element_type=jnp.float32)
    wide = 256
    for i in range(0, out_ref.shape[1], wide):
        cols = pl.ds(i, wide)
        both = dot(left_ref[:, start : start + depth], v_high[:, cols])
        part = both[height:] + dot(left_ref[:height, start : start + depth], v_low[:, cols])
        part = both[:height] + part
        out_ref[:, cols] = part + total_ref[:, cols] if has_total else part


def product(left, start, blocks, pieces, total=None):
    height = left.shape[0] // 2
    depth = sum(size for _, _, size in pieces)
    cols = blocks[0].shape[1]
    used = sorted({piece[0] for piece in pieces})
    pieces = [(used.index(block), first, size) for block, first, size in pieces]
    extra = [] if total is None else [total]
    operands = [left] + extra + [blocks[i] for i in used]
    return pl.pallas_call(
        lambda *refs: product_kernel(pieces, start, bool(extra), *refs),
        out_shape=jax.ShapeDtypeStruct((height, cols), jnp.float32),
        in_specs=[VMEM] * len(operands),
        out_specs=VMEM,
        scratch_shapes=[
            pltpu.VMEM((depth, cols), jnp.bfloat16),
            pltpu.VMEM((depth, cols), jnp.bfloat16),
        ],
        cost_estimate=pl.CostEstimate(
            flops=6 * height * depth * cols, bytes_accessed=4 << 20, transcendentals=0
        ),
        compiler_params=pltpu.CompilerParams(vmem_limit_bytes=VMEM_LIMIT),
        name="product",
    )(*operands)


def swap_core(block):
    return lax.ppermute(block, "core", [(0, 1), (1, 0)])


def along_ring(block, cross=False):
    n = lax.axis_size("grp")
    up, down = (n, 0) if cross else (0, n)
    pairs = [(up + i, (i + 1) % n) for i in range(n)]
    pairs += [(down + i, n + (i - 1) % n) for i in range(n)]
    return lax.ppermute(block, ("core", "grp"), pairs)


def gather_panel(block):
    n = lax.axis_size("grp")
    size = block.shape[0]
    blocks, pieces = [], []

    def place(block, start=0, length=None):
        for known, other in enumerate(blocks):
            if other is block:
                break
        else:
            known = len(blocks)
            blocks.append(block)
        pieces.append((known, start, length or block.shape[0]))

    place(block)
    place(swap_core(block))
    for step in range(n // 2 - 1):
        own = along_ring(own if step else block)
        mate = along_ring(mate) if step else along_ring(block, cross=True)
        place(own)
        place(mate)
        place(swap_core(jnp.concatenate([own, mate], axis=0)))
    half = size // 2
    top, bottom = along_ring(own[:half]), along_ring(mate[half:])
    swapped = swap_core(jnp.concatenate([top, bottom], axis=0))
    place(top)
    place(swapped, half, half)
    place(swapped, 0, half)
    place(bottom)
    return blocks, pieces


def on_device(amplitudes, integrals, occupancy, tile_place):
    chips = NX * NZ
    per_chip = tile_place.shape[0] // chips
    rows, width = amplitudes.shape[2:]
    cols = integrals.shape[1]
    sent = pack(occupancy[0], tile_place, amplitudes[0], chips, per_chip)
    got = lax.all_to_all(sent, CHIPS, 0, 0, tiled=True)
    blocks, pieces = gather_panel(integrals)
    left = spread(got, rows, per_chip * width)
    early, depth = 0, 0
    while depth < EARLY * width:
        depth += pieces[early][2]
        early += 1
    part = product(left, 0, blocks, pieces[:early])
    part = product(left, depth, blocks, pieces[early:], part)
    part = part.reshape(NX, NZ * rows, cols)
    part = lax.all_to_all(part, "x", 0, 0, tiled=True).sum(axis=0)
    part = part.reshape(NZ, rows, cols)
    return lax.all_to_all(part, "z", 0, 0, tiled=True).sum(axis=0)


def solution(mesh):
    split_mesh = Mesh(mesh.devices.reshape(NX, NZ, NC, -1), EVERY)
    return jax.shard_map(
        on_device,
        mesh=split_mesh,
        in_specs=(
            P(EVERY, None, None, None),
            P(EVERY, None),
            P(EVERY, None),
            P(),
        ),
        out_specs=P(EVERY, None),
        check_vma=False,
    )
```

time: 152 us -> 151 us (level)
  the two profiles are of different devices: /device:TPU:24 before, /device:TPU:16 now
where the time goes in v6:
time: 151 us; the launch traced here: 150 us
  starting transfers between devices  57.9 us (38%)
  blocking collectives  54.9 us (36%)
  Pallas kernels  18.2 us (12%)
  waiting for transfers between devices  13.7 us (9%)
  other arithmetic  4.97 us (3%)
    ppermute x8, starting transfers between devices, along_ring(): return lax.ppermute(block, ('core', 'grp'), pairs)  34.2 us
    all_to_all x1, blocking collectives, on_device(): part = lax.all_to_all(part, 'x', 0, 0, tiled=True).sum(axis=0)  31.4 us
    all_to_all x1, blocking collectives, on_device(): return lax.all_to_all(part, 'z', 0, 0, tiled=True).sum(axis=0)  23.5 us
    ppermute x8, waiting for transfers between devices, along_ring(): return lax.ppermute(block, ('core', 'grp'), pairs)  13.7 us
    all_to_all x1, starting transfers between devices, on_device(): got = lax.all_to_all(sent, CHIPS, 0, 0, tiled=True)  13.2 us
    ppermute x5, starting transfers between devices, swap_core(): return lax.ppermute(block, 'core', [(0, 1), (1, 0)])  10.5 us
    pallas_call x2, Pallas kernels, product(): pl.pallas_call(lambda *refs: product_kernel(pieces, start, bool(extra), *...  10 us
    pallas_call x1, Pallas kernels, pack(): pl.pallas_call(pack_kernel, out_shape=jax.ShapeDtypeStruct((chips, HEAD +...  4.17 us
  transfers between devices with their start and end apart: 14, of which 4 were waited for; matrix products, arithmetic and copies ran while one was open for 3% of the time, Pallas kernels for 7%

profile of v6, /device:TPU:16, one launch (start us, length us, event | category | flops | bytes accessed | tf_op | source)
XLA Modules:
  0.0 150.1 jit_solution(6693530503713116825)
XLA Ops:
  0.0 4.2 %pack.1 = f32[32,136,128]{2,1,0:T(8,128)} custom-call(s32[128]{0:T(128)} %bitcast.7, s32[512]{0:T(512)} %place_ref.1, f32[128,16,128]{2,1,0:T(8,128)} %bitcast.6), custom_call_target="tpu_custom_call" | custom-call | bytes 8388608 | tf_op jit(solution)/shard_map/pack/pallas_call | solution.py:64
  4.2 13.2 %all-to-all-start = ((f32[32,136,128]{2,1,0:T(8,128)}), f32[32,136,128]{2,1,0:T(8,128)S(1)}, u32[]{:S(2)}, u32[]{:S(2)}) async-start(f32[32,136,128]{2,1,0:T(8,128)} %pack.1), calls=%async_computation | async-start | bytes 4456448 | tf_op jit(solution)/shard_map/all_to_all | solution.py:222
  17.3 3.5 %collective-permute-start.1 = (f32[128,1024]{1,0:T(8,128)}, f32[128,1024]{1,0:T(8,128)S(1)}, u32[]{:S(2)}, u32[]{:S(2)}) collective-permute-start(f32[128,1024]{1,0:T(8,128)} %refs_1_.1), channel_id=1, source_target_pairs={{0,1},{1,2},{2,3},{3,4},{4,5},{5,6},{6,7},{7,0},{8,15},{9,8},{10,9... | collective-permute-start | bytes 1572872 | tf_op jit(solution)/shard_map/ppermute | solution.py:181
  20.8 1.9 %collective-permute-start.2 = (f32[128,1024]{1,0:T(8,128)}, f32[128,1024]{1,0:T(8,128)S(1)}, u32[]{:S(2)}, u32[]{:S(2)}) collective-permute-start(f32[128,1024]{1,0:T(8,128)} %refs_1_.1), channel_id=1, source_target_pairs={{8,1},{9,2},{10,3},{11,4},{12,5},{13,6},{14,7},{15,0},{0,15},{1,8}... | collective-permute-start | bytes 1572872 | tf_op jit(solution)/shard_map/ppermute | solution.py:181
  22.8 8.5 %collective-permute-done.1.refs_3_ = f32[128,1024]{1,0:T(8,128)S(1)} collective-permute-done((f32[128,1024]{1,0:T(8,128)}, f32[128,1024]{1,0:T(8,128)S(1)}, u32[]{:S(2)}, u32[]{:S(2)}) %collective-permute-start.1) | collective-permute-done | bytes 524320 | tf_op jit(solution)/shard_map/ppermute | solution.py:181
  31.3 4.8 %collective-permute-start.4 = (f32[128,1024]{1,0:T(8,128)S(1)}, f32[128,1024]{1,0:T(8,128)S(1)}, u32[]{:S(2)}, u32[]{:S(2)}) collective-permute-start(f32[128,1024]{1,0:T(8,128)S(1)} %collective-permute-done.1.refs_3_), channel_id=1, source_target_pairs={{0,1},{1,2},{2,3},{3,4},{4,5},{5,6},{6,7},{7,0},{8,15},{9,8},{10,9... | collective-permute-start | bytes 1572872 | tf_op jit(solution)/shard_map/ppermute | solution.py:181
  36.1 5.5 %collective-permute-start.5 = (f32[128,1024]{1,0:T(8,128)S(1)}, f32[128,1024]{1,0:T(8,128)S(1)}, u32[]{:S(2)}, u32[]{:S(2)}) collective-permute-start(f32[128,1024]{1,0:T(8,128)S(1)} %collective-permute-done.2.refs_4_), channel_id=1, source_target_pairs={{0,1},{1,2},{2,3},{3,4},{4,5},{5,6},{6,7},{7,0},{8,15},{9,8},{10,9... | collective-permute-start | bytes 1572872 | tf_op jit(solution)/shard_map/ppermute | solution.py:181
  41.6 1.2 collective-permute-done.4.refs_6_
  42.7 5.5 %collective-permute-start.7 = (f32[128,1024]{1,0:T(8,128)S(1)}, f32[128,1024]{1,0:T(8,128)S(1)}, u32[]{:S(2)}, u32[]{:S(2)}) collective-permute-start(f32[128,1024]{1,0:T(8,128)S(1)} %collective-permute-done.4.refs_6_), channel_id=1, source_target_pairs={{0,1},{1,2},{2,3},{3,4},{4,5},{5,6},{6,7},{7,0},{8,15},{9,8},{10,9... | collective-permute-start | bytes 1572872 | tf_op jit(solution)/shard_map/ppermute | solution.py:181
  48.4 5.5 %collective-permute-start.8 = (f32[128,1024]{1,0:T(8,128)S(1)}, f32[128,1024]{1,0:T(8,128)S(1)}, u32[]{:S(2)}, u32[]{:S(2)}) collective-permute-start(f32[128,1024]{1,0:T(8,128)S(1)} %collective-permute-done.5.refs_7_), channel_id=1, source_target_pairs={{0,1},{1,2},{2,3},{3,4},{4,5},{5,6},{6,7},{7,0},{8,15},{9,8},{10,9... | collective-permute-start | bytes 1572872 | tf_op jit(solution)/shard_map/ppermute | solution.py:181
  54.9 1.9 %collective-permute-start.3 = (f32[256,1024]{1,0:T(8,128)}, f32[256,1024]{1,0:T(8,128)}, u32[]{:S(2)}, u32[]{:S(2)}) collective-permute-start(f32[256,1024]{1,0:T(8,128)} %pad_maximum_fusion), channel_id=1, source_target_pairs={{0,8},{8,0},{1,9},{9,1},{2,10},{10,2},{3,11},{11,3},{4,12},{12,4},... | collective-permute-start | bytes 3145736 | tf_op jit(solution)/shard_map/ppermute | solution.py:173
  56.8 1.1 pad_maximum_fusion.1
  58.0 2.4 %collective-permute-start.6 = (f32[256,1024]{1,0:T(8,128)}, f32[256,1024]{1,0:T(8,128)}, u32[]{:S(2)}, u32[]{:S(2)}) collective-permute-start(f32[256,1024]{1,0:T(8,128)} %pad_maximum_fusion.1), channel_id=1, source_target_pairs={{0,8},{8,0},{1,9},{9,1},{2,10},{10,2},{3,11},{11,3},{4,12},{12,4},... | collective-permute-start | bytes 3145736 | tf_op jit(solution)/shard_map/ppermute | solution.py:173
  60.4 5.6 %collective-permute-start.10 = (f32[64,1024]{1,0:T(8,128)S(1)}, f32[64,1024]{1,0:T(8,128)S(1)}, u32[]{:S(2)}, u32[]{:S(2)}) collective-permute-start(f32[64,1024]{1,0:T(8,128)S(1)} %slice.8), channel_id=1, source_target_pairs={{0,1},{1,2},{2,3},{3,4},{4,5},{5,6},{6,7},{7,0},{8,15},{9,8},{10,9... | collective-permute-start | bytes 786440 | tf_op jit(solution)/shard_map/ppermute | solution.py:181
  67.1 1.9 %collective-permute-start.9 = (f32[256,1024]{1,0:T(8,128)}, f32[256,1024]{1,0:T(8,128)}, u32[]{:S(2)}, u32[]{:S(2)}) collective-permute-start(f32[256,1024]{1,0:T(8,128)} %pad_maximum_fusion.2), channel_id=1, source_target_pairs={{0,8},{8,0},{1,9},{9,1},{2,10},{10,2},{3,11},{11,3},{4,12},{12,4},... | collective-permute-start | bytes 3145736 | tf_op jit(solution)/shard_map/ppermute | solution.py:173
  69.0 1.9 %collective-permute-start.11 = (f32[64,1024]{1,0:T(8,128)S(1)}, f32[64,1024]{1,0:T(8,128)S(1)}, u32[]{:S(2)}, u32[]{:S(2)}) collective-permute-start(f32[64,1024]{1,0:T(8,128)S(1)} %slice.9), channel_id=1, source_target_pairs={{0,1},{1,2},{2,3},{3,4},{4,5},{5,6},{6,7},{7,0},{8,15},{9,8},{10,9... | collective-permute-start | bytes 786440 | tf_op jit(solution)/shard_map/ppermute | solution.py:181
  71.0 2.4 %collective-permute-start = (f32[128,1024]{1,0:T(8,128)}, f32[128,1024]{1,0:T(8,128)}, u32[]{:S(2)}, u32[]{:S(2)}) collective-permute-start(f32[128,1024]{1,0:T(8,128)} %refs_1_.1), channel_id=1, source_target_pairs={{0,8},{8,0},{1,9},{9,1},{2,10},{10,2},{3,11},{11,3},{4,12},{12,4},... | collective-permute-start | bytes 1572872 | tf_op jit(solution)/shard_map/ppermute | solution.py:173
  73.4 3.9 %collective-permute-done.11.refs_7_ = f32[64,1024]{1,0:T(8,128)S(1)} collective-permute-done((f32[64,1024]{1,0:T(8,128)S(1)}, f32[64,1024]{1,0:T(8,128)S(1)}, u32[]{:S(2)}, u32[]{:S(2)}) %collective-permute-start.11) | collective-permute-done | bytes 262176 | tf_op jit(solution)/shard_map/ppermute | solution.py:181
  78.2 1.9 %collective-permute-start.12 = (f32[128,1024]{1,0:T(8,128)}, f32[128,1024]{1,0:T(8,128)}, u32[]{:S(2)}, u32[]{:S(2)}) collective-permute-start(f32[128,1024]{1,0:T(8,128)} %pad_maximum_fusion.3), channel_id=1, source_target_pairs={{0,8},{8,0},{1,9},{9,1},{2,10},{10,2},{3,11},{11,3},{4,12},{12,4},... | collective-permute-start | bytes 1572872 | tf_op jit(solution)/shard_map/ppermute | solution.py:173
  80.2 4.0 %spread.1.refs_0_ = bf16[1024,2176]{1,0:T(8,128)(2,1)S(1)} custom-call(f32[32,136,128]{2,1,0:T(8,128)S(1)} %all-to-all-done.got_ref), custom_call_target="tpu_custom_call" | custom-call | bytes 8388608 | tf_op jit(solution)/shard_map/spread/pallas_call | solution.py:109
  84.3 6.1 %product.2.refs_1_ = f32[512,1024]{1,0:T(8,128)S(1)} custom-call(bf16[1024,2176]{1,0:T(8,128)(2,1)S(1)} %spread.1.refs_0_, f32[128,1024]{1,0:T(8,128)} %refs_1_.1, f32[128,1024]{1,0:T(8,128)} %collective-permute-done.refs_2_, f32[128,1024]{1,0:T(8,128)S(1)} %copy-done.3, f32[128,1024]{1,0:T(8,128)S(1)} %copy-done.5, ...), custom_call_target="tpu_custom_call" | custom-call | flops 4026531840 | bytes 4194304 | tf_op jit(solution)/shard_map/product/pallas_call | solution.py:155
  90.4 4.0 %product.3 = f32[512,1024]{1,0:T(8,128)S(1)} custom-call(bf16[1024,2176]{1,0:T(8,128)(2,1)S(1)} %spread.1.refs_0_, f32[512,1024]{1,0:T(8,128)S(1)} %product.2.refs_1_, f32[128,1024]{1,0:T(8,128)S(1)} %collective-permute-done.7.refs_2_, f32[128,1024]{1,0:T(8,128)S(1)} %collective-permute-done.8.refs_3_, f32[256,1024]{1,0:T(8,128)} %collective-permute-done.9.refs_4_, ...), custom_call_target="tpu_custom_call" | custom-call | flops 2415919104 | bytes 4194304 | tf_op jit(solution)/shard_map/product/pallas_call | solution.py:155
  94.3 31.4 %all_to_all.15 = f32[4,128,1024]{2,1,0:T(8,128)S(1)} all-to-all(f32[4,128,1024]{2,1,0:T(8,128)S(1)} %bitcast.4), channel_id=1, replica_groups=mesh['x'=4,'z'=8,'core'=2,'grp'=8] {'x'}, dimensions={0} | all-to-all | bytes 4194304 | tf_op jit(solution)/shard_map/all_to_all | solution.py:232
  125.9 23.5 %all_to_all.16 = f32[8,16,1024]{2,1,0:T(8,128)S(1)} all-to-all(f32[8,16,1024]{2,1,0:T(8,128)S(1)} %bitcast.5), channel_id=1, replica_groups=mesh['x'=4,'z'=8,'core'=2,'grp'=8] {'z'}, dimensions={0} | all-to-all | bytes 1048576 | tf_op jit(solution)/shard_map/all_to_all | solution.py:234
  (38 shorter events, 4.1 us)
Async XLA Ops:
  4.2 76.0 %all-to-all-start = ((f32[32,136,128]{2,1,0:T(8,128)}), f32[32,136,128]{2,1,0:T(8,128)S(1)}, u32[]{:S(2)}, u32[]{:S(2)}) async-start(f32[32,136,128]{2,1,0:T(8,128)} %pack.1), calls=%async_computation | async-start | bytes 4456448 | tf_op jit(solution)/shard_map/all_to_all | solution.py:222
  17.3 13.9 %collective-permute-start.1 = (f32[128,1024]{1,0:T(8,128)}, f32[128,1024]{1,0:T(8,128)S(1)}, u32[]{:S(2)}, u32[]{:S(2)}) collective-permute-start(f32[128,1024]{1,0:T(8,128)} %refs_1_.1), channel_id=1, source_target_pairs={{0,1},{1,2},{2,3},{3,4},{4,5},{5,6},{6,7},{7,0},{8,15},{9,8},{10,9... | collective-permute-start | bytes 1572872 | tf_op jit(solution)/shard_map/ppermute | solution.py:181
  20.8 15.2 %collective-permute-start.2 = (f32[128,1024]{1,0:T(8,128)}, f32[128,1024]{1,0:T(8,128)S(1)}, u32[]{:S(2)}, u32[]{:S(2)}) collective-permute-start(f32[128,1024]{1,0:T(8,128)} %refs_1_.1), channel_id=1, source_target_pairs={{8,1},{9,2},{10,3},{11,4},{12,5},{13,6},{14,7},{15,0},{0,15},{1,8}... | collective-permute-start | bytes 1572872 | tf_op jit(solution)/shard_map/ppermute | solution.py:181
  31.3 29.1 %copy-start.2 = (f32[128,1024]{1,0:T(8,128)}, f32[128,1024]{1,0:T(8,128)S(1)}, u32[]{:S(2)}) copy-start(f32[128,1024]{1,0:T(8,128)S(1)} %collective-permute-done.1.refs_3_) | copy-start | bytes 1572868
  31.3 11.5 %collective-permute-start.4 = (f32[128,1024]{1,0:T(8,128)S(1)}, f32[128,1024]{1,0:T(8,128)S(1)}, u32[]{:S(2)}, u32[]{:S(2)}) collective-permute-start(f32[128,1024]{1,0:T(8,128)S(1)} %collective-permute-done.1.refs_3_), channel_id=1, source_target_pairs={{0,1},{1,2},{2,3},{3,4},{4,5},{5,6},{6,7},{7,0},{8,15},{9,8},{10,9... | collective-permute-start | bytes 1572872 | tf_op jit(solution)/shard_map/ppermute | solution.py:181
  36.1 24.3 %copy-start.4 = (f32[128,1024]{1,0:T(8,128)}, f32[128,1024]{1,0:T(8,128)S(1)}, u32[]{:S(2)}) copy-start(f32[128,1024]{1,0:T(8,128)S(1)} %collective-permute-done.2.refs_4_) | copy-start | bytes 1572868
  36.1 12.3 %collective-permute-start.5 = (f32[128,1024]{1,0:T(8,128)S(1)}, f32[128,1024]{1,0:T(8,128)S(1)}, u32[]{:S(2)}, u32[]{:S(2)}) collective-permute-start(f32[128,1024]{1,0:T(8,128)S(1)} %collective-permute-done.2.refs_4_), channel_id=1, source_target_pairs={{0,1},{1,2},{2,3},{3,4},{4,5},{5,6},{6,7},{7,0},{8,15},{9,8},{10,9... | collective-permute-start | bytes 1572872 | tf_op jit(solution)/shard_map/ppermute | solution.py:181
  42.7 17.7 %copy-start.6 = (f32[128,1024]{1,0:T(8,128)}, f32[128,1024]{1,0:T(8,128)S(1)}, u32[]{:S(2)}) copy-start(f32[128,1024]{1,0:T(8,128)S(1)} %collective-permute-done.4.refs_6_) | copy-start | bytes 1572868
  42.7 17.6 %collective-permute-start.7 = (f32[128,1024]{1,0:T(8,128)S(1)}, f32[128,1024]{1,0:T(8,128)S(1)}, u32[]{:S(2)}, u32[]{:S(2)}) collective-permute-start(f32[128,1024]{1,0:T(8,128)S(1)} %collective-permute-done.4.refs_6_), channel_id=1, source_target_pairs={{0,1},{1,2},{2,3},{3,4},{4,5},{5,6},{6,7},{7,0},{8,15},{9,8},{10,9... | collective-permute-start | bytes 1572872 | tf_op jit(solution)/shard_map/ppermute | solution.py:181
  48.3 12.1 %copy-start.8 = (f32[128,1024]{1,0:T(8,128)}, f32[128,1024]{1,0:T(8,128)S(1)}, u32[]{:S(2)}) copy-start(f32[128,1024]{1,0:T(8,128)S(1)} %collective-permute-done.5.refs_7_) | copy-start | bytes 1572868
  48.4 17.7 %collective-permute-start.8 = (f32[128,1024]{1,0:T(8,128)S(1)}, f32[128,1024]{1,0:T(8,128)S(1)}, u32[]{:S(2)}, u32[]{:S(2)}) collective-permute-start(f32[128,1024]{1,0:T(8,128)S(1)} %collective-permute-done.5.refs_7_), channel_id=1, source_target_pairs={{0,1},{1,2},{2,3},{3,4},{4,5},{5,6},{6,7},{7,0},{8,15},{9,8},{10,9... | collective-permute-start | bytes 1572872 | tf_op jit(solution)/shard_map/ppermute | solution.py:181
  54.9 29.3 %collective-permute-start.3 = (f32[256,1024]{1,0:T(8,128)}, f32[256,1024]{1,0:T(8,128)}, u32[]{:S(2)}, u32[]{:S(2)}) collective-permute-start(f32[256,1024]{1,0:T(8,128)} %pad_maximum_fusion), channel_id=1, source_target_pairs={{0,8},{8,0},{1,9},{9,1},{2,10},{10,2},{3,11},{11,3},{4,12},{12,4},... | collective-permute-start | bytes 3145736 | tf_op jit(solution)/shard_map/ppermute | solution.py:173
  58.0 26.2 %collective-permute-start.6 = (f32[256,1024]{1,0:T(8,128)}, f32[256,1024]{1,0:T(8,128)}, u32[]{:S(2)}, u32[]{:S(2)}) collective-permute-start(f32[256,1024]{1,0:T(8,128)} %pad_maximum_fusion.1), channel_id=1, source_target_pairs={{0,8},{8,0},{1,9},{9,1},{2,10},{10,2},{3,11},{11,3},{4,12},{12,4},... | collective-permute-start | bytes 3145736 | tf_op jit(solution)/shard_map/ppermute | solution.py:173
  60.4 10.5 %collective-permute-start.10 = (f32[64,1024]{1,0:T(8,128)S(1)}, f32[64,1024]{1,0:T(8,128)S(1)}, u32[]{:S(2)}, u32[]{:S(2)}) collective-permute-start(f32[64,1024]{1,0:T(8,128)S(1)} %slice.8), channel_id=1, source_target_pairs={{0,1},{1,2},{2,3},{3,4},{4,5},{5,6},{6,7},{7,0},{8,15},{9,8},{10,9... | collective-permute-start | bytes 786440 | tf_op jit(solution)/shard_map/ppermute | solution.py:181
  67.1 23.3 %collective-permute-start.9 = (f32[256,1024]{1,0:T(8,128)}, f32[256,1024]{1,0:T(8,128)}, u32[]{:S(2)}, u32[]{:S(2)}) collective-permute-start(f32[256,1024]{1,0:T(8,128)} %pad_maximum_fusion.2), channel_id=1, source_target_pairs={{0,8},{8,0},{1,9},{9,1},{2,10},{10,2},{3,11},{11,3},{4,12},{12,4},... | collective-permute-start | bytes 3145736 | tf_op jit(solution)/shard_map/ppermute | solution.py:173
  69.0 8.3 %collective-permute-start.11 = (f32[64,1024]{1,0:T(8,128)S(1)}, f32[64,1024]{1,0:T(8,128)S(1)}, u32[]{:S(2)}, u32[]{:S(2)}) collective-permute-start(f32[64,1024]{1,0:T(8,128)S(1)} %slice.9), channel_id=1, source_target_pairs={{0,1},{1,2},{2,3},{3,4},{4,5},{5,6},{6,7},{7,0},{8,15},{9,8},{10,9... | collective-permute-start | bytes 786440 | tf_op jit(solution)/shard_map/ppermute | solution.py:181
  71.0 13.2 %collective-permute-start = (f32[128,1024]{1,0:T(8,128)}, f32[128,1024]{1,0:T(8,128)}, u32[]{:S(2)}, u32[]{:S(2)}) collective-permute-start(f32[128,1024]{1,0:T(8,128)} %refs_1_.1), channel_id=1, source_target_pairs={{0,8},{8,0},{1,9},{9,1},{2,10},{10,2},{3,11},{11,3},{4,12},{12,4},... | collective-permute-start | bytes 1572872 | tf_op jit(solution)/shard_map/ppermute | solution.py:173
  77.3 0.9 copy-start
  78.2 12.1 %collective-permute-start.12 = (f32[128,1024]{1,0:T(8,128)}, f32[128,1024]{1,0:T(8,128)}, u32[]{:S(2)}, u32[]{:S(2)}) collective-permute-start(f32[128,1024]{1,0:T(8,128)} %pad_maximum_fusion.3), channel_id=1, source_target_pairs={{0,8},{8,0},{1,9},{9,1},{2,10},{10,2},{3,11},{11,3},{4,12},{12,4},... | collective-permute-start | bytes 1572872 | tf_op jit(solution)/shard_map/ppermute | solution.py:173
  80.1 4.1 %copy-start.3 = (f32[128,1024]{1,0:T(8,128)S(1)}, f32[128,1024]{1,0:T(8,128)}, u32[]{:S(2)}) copy-start(f32[128,1024]{1,0:T(8,128)} %copy-done.2) | copy-start | bytes 1572868
  80.1 4.1 %copy-start.5 = (f32[128,1024]{1,0:T(8,128)S(1)}, f32[128,1024]{1,0:T(8,128)}, u32[]{:S(2)}) copy-start(f32[128,1024]{1,0:T(8,128)} %copy-done.4) | copy-start | bytes 1572868
  80.2 4.1 %copy-start.7 = (f32[128,1024]{1,0:T(8,128)S(1)}, f32[128,1024]{1,0:T(8,128)}, u32[]{:S(2)}) copy-start(f32[128,1024]{1,0:T(8,128)} %copy-done.6) | copy-start | bytes 1572868
  80.2 4.1 %copy-start.9 = (f32[128,1024]{1,0:T(8,128)S(1)}, f32[128,1024]{1,0:T(8,128)}, u32[]{:S(2)}) copy-start(f32[128,1024]{1,0:T(8,128)} %copy-done.8) | copy-start | bytes 1572868
  84.2 6.2 %copy-start.1 = (f32[64,1024]{1,0:T(8,128)S(1)}, f32[64,1024]{1,0:T(8,128)}, u32[]{:S(2)}) copy-start(f32[64,1024]{1,0:T(8,128)} %copy-done) | copy-start | bytes 786436

commit v7 on v6

--- a/solution.py
+++ b/solution.py
@@ -11,7 +11,7 @@
 EVERY = ("x", "z", "core", "grp")
 LANES = 128
 HEAD = 8
-EARLY = 10
+EARLY = 12
 VMEM_LIMIT = 20 << 20
 VMEM = pl.BlockSpec(memory_space=pltpu.VMEM)
 SMEM = pl.BlockSpec(memory_space=pltpu.SMEM)
@@ -181,35 +181,33 @@
     return lax.ppermute(block, ("core", "grp"), pairs)
 
 
-def gather_panel(block):
+def gather_panel(block, after):
     n = lax.axis_size("grp")
     size = block.shape[0]
-    blocks, pieces = [], []
-
-    def place(block, start=0, length=None):
-        for known, other in enumerate(blocks):
-            if other is block:
-                break
-        else:
-            known = len(blocks)
-            blocks.append(block)
-        pieces.append((known, start, length or block.shape[0]))
-
-    place(block)
-    place(swap_core(block))
-    for step in range(n // 2 - 1):
-        own = along_ring(own if step else block)
-        mate = along_ring(mate) if step else along_ring(block, cross=True)
-        place(own)
-        place(mate)
-        place(swap_core(jnp.concatenate([own, mate], axis=0)))
     half = size // 2
-    top, bottom = along_ring(own[:half]), along_ring(mate[half:])
-    swapped = swap_core(jnp.concatenate([top, bottom], axis=0))
-    place(top)
-    place(swapped, half, half)
-    place(swapped, 0, half)
-    place(bottom)
+    own, mate = along_ring(block), along_ring(block, cross=True)
+    swapped = swap_core(block)
+    blocks = [block, swapped]
+    for step in range(1, n // 2):
+        blocks += [own, mate]
+        held, _ = lax.optimization_barrier((mate, swapped))
+        if step < n // 2 - 1:
+            swapped = swap_core(jnp.concatenate([own, mate], axis=0))
+            blocks.append(swapped)
+            own, mate = along_ring(own), along_ring(held)
+    top, bottom = along_ring(own[:half]), along_ring(held[half:])
+    held, _ = lax.optimization_barrier((top, after))
+    blocks.append(swap_core(jnp.concatenate([own, mate, held, bottom], axis=0)))
+    pieces = [(i, 0, b.shape[0]) for i, b in enumerate(blocks[:-1])]
+    last = len(blocks) - 1
+    blocks += [top, bottom]
+    pieces += [
+        (last, 0, 2 * size),
+        (last + 1, 0, half),
+        (last, 2 * size + half, half),
+        (last, 2 * size, half),
+        (last + 2, 0, half),
+    ]
     return blocks, pieces
 
 
@@ -220,8 +218,8 @@
     cols = integrals.shape[1]
     sent = pack(occupancy[0], tile_place, amplitudes[0], chips, per_chip)
     got = lax.all_to_all(sent, CHIPS, 0, 0, tiled=True)
-    blocks, pieces = gather_panel(integrals)
     left = spread(got, rows, per_chip * width)
+    blocks, pieces = gather_panel(integrals, left)
     early, depth = 0, 0
     while depth < EARLY * width:
         depth += pieces[early][2]

time: 151 us -> 152 us (level)
  the two profiles are of different devices: /device:TPU:16 before, /device:TPU:2 now
where the time goes in v7:
time: 152 us
  blocking collectives  53.8 us (35%)
  starting transfers between devices  43.7 us (29%)
  waiting for transfers between devices  29.9 us (20%)
  Pallas kernels  16.1 us (11%)
  local copies, waits for them, and re-layouts  4.22 us (3%)
  other arithmetic  3.72 us (2%)
    all_to_all x1, blocking collectives, on_device(): part = lax.all_to_all(part, 'x', 0, 0, tiled=True).sum(axis=0)  30.2 us
    ppermute x8, waiting for transfers between devices, along_ring(): return lax.ppermute(block, ('core', 'grp'), pairs)  29.9 us
    all_to_all x1, blocking collectives, on_device(): return lax.all_to_all(part, 'z', 0, 0, tiled=True).sum(axis=0)  23.5 us
    ppermute x8, starting transfers between devices, along_ring(): return lax.ppermute(block, ('core', 'grp'), pairs)  18.9 us
    all_to_all x1, starting transfers between devices, on_device(): got = lax.all_to_all(sent, CHIPS, 0, 0, tiled=True)  13.6 us
    ppermute x4, starting transfers between devices, swap_core(): return lax.ppermute(block, 'core', [(0, 1), (1, 0)])  11.2 us
    pallas_call x2, Pallas kernels, product(): pl.pallas_call(lambda *refs: product_kernel(pieces, start, bool(extra), *...  7.92 us
    pallas_call x1, Pallas kernels, pack(): pl.pallas_call(pack_kernel, out_shape=jax.ShapeDtypeStruct((chips, HEAD +...  4.2 us
  transfers between devices with their start and end apart: 13, of which 5 were waited for; matrix products, arithmetic and copies ran while one was open for 1% of the time, Pallas kernels for 6%

profile of v7, /device:TPU:2, one launch (start us, length us, event | category | flops | bytes accessed | tf_op | source)
XLA Modules:
  0.0 151.7 jit_solution(9351278347824100760)
XLA Ops:
  0.0 4.2 %pack.1 = f32[32,136,128]{2,1,0:T(8,128)} custom-call(s32[128]{0:T(128)} %bitcast.7, s32[512]{0:T(512)} %place_ref.1, f32[128,16,128]{2,1,0:T(8,128)} %bitcast.6), custom_call_target="tpu_custom_call" | custom-call | bytes 8388608 | tf_op jit(solution)/shard_map/pack/pallas_call | solution.py:64
  4.2 13.6 %all-to-all-start = ((f32[32,136,128]{2,1,0:T(8,128)}), f32[32,136,128]{2,1,0:T(8,128)S(1)}, u32[]{:S(2)}, u32[]{:S(2)}) async-start(f32[32,136,128]{2,1,0:T(8,128)} %pack.1), calls=%async_computation | async-start | bytes 4456448 | tf_op jit(solution)/shard_map/all_to_all | solution.py:220
  17.8 1.9 %collective-permute-start = (f32[128,1024]{1,0:T(8,128)S(1)}, f32[128,1024]{1,0:T(8,128)S(1)}, u32[]{:S(2)}, u32[]{:S(2)}) collective-permute-start(f32[128,1024]{1,0:T(8,128)S(1)} %copy-done.12), channel_id=1, source_target_pairs={{0,8},{8,0},{1,9},{9,1},{2,10},{10,2},{3,11},{11,3},{4,12},{12,4},... | collective-permute-start | bytes 1572872 | tf_op jit(solution)/shard_map/ppermute | solution.py:173
  19.7 5.5 %collective-permute-start.2 = (f32[128,1024]{1,0:T(8,128)S(1)}, f32[128,1024]{1,0:T(8,128)S(1)}, u32[]{:S(2)}, u32[]{:S(2)}) collective-permute-start(f32[128,1024]{1,0:T(8,128)S(1)} %copy-done.12), channel_id=1, source_target_pairs={{8,1},{9,2},{10,3},{11,4},{12,5},{13,6},{14,7},{15,0},{0,15},{1,8}... | collective-permute-start | bytes 1572872 | tf_op jit(solution)/shard_map/ppermute | solution.py:181
  25.2 1.9 %collective-permute-start.1 = (f32[128,1024]{1,0:T(8,128)S(1)}, f32[128,1024]{1,0:T(8,128)S(1)}, u32[]{:S(2)}, u32[]{:S(2)}) collective-permute-start(f32[128,1024]{1,0:T(8,128)S(1)} %copy-done.12), channel_id=1, source_target_pairs={{0,1},{1,2},{2,3},{3,4},{4,5},{5,6},{6,7},{7,0},{8,15},{9,8},{10,9... | collective-permute-start | bytes 1572872 | tf_op jit(solution)/shard_map/ppermute | solution.py:181
  28.0 8.1 %collective-permute-done.2.refs_4_ = f32[128,1024]{1,0:T(8,128)S(1)} collective-permute-done((f32[128,1024]{1,0:T(8,128)S(1)}, f32[128,1024]{1,0:T(8,128)S(1)}, u32[]{:S(2)}, u32[]{:S(2)}) %collective-permute-start.2) | collective-permute-done | bytes 524320 | tf_op jit(solution)/shard_map/ppermute | solution.py:181
  36.1 1.9 %collective-permute-start.5 = (f32[128,1024]{1,0:T(8,128)S(1)}, f32[128,1024]{1,0:T(8,128)S(1)}, u32[]{:S(2)}, u32[]{:S(2)}) collective-permute-start(f32[128,1024]{1,0:T(8,128)S(1)} %collective-permute-done.2.refs_4_), channel_id=1, source_target_pairs={{0,1},{1,2},{2,3},{3,4},{4,5},{5,6},{6,7},{7,0},{8,15},{9,8},{10,9... | collective-permute-start | bytes 1572872 | tf_op jit(solution)/shard_map/ppermute | solution.py:181
  38.1 1.9 %collective-permute-start.4 = (f32[128,1024]{1,0:T(8,128)S(1)}, f32[128,1024]{1,0:T(8,128)S(1)}, u32[]{:S(2)}, u32[]{:S(2)}) collective-permute-start(f32[128,1024]{1,0:T(8,128)S(1)} %collective-permute-done.1.refs_3_), channel_id=1, source_target_pairs={{0,1},{1,2},{2,3},{3,4},{4,5},{5,6},{6,7},{7,0},{8,15},{9,8},{10,9... | collective-permute-start | bytes 1572872 | tf_op jit(solution)/shard_map/ppermute | solution.py:181
  40.1 5.4 %collective-permute-start.3 = (f32[256,1024]{1,0:T(8,128)S(1)}, f32[256,1024]{1,0:T(8,128)S(1)}, u32[]{:S(2)}, u32[]{:S(2)}) collective-permute-start(f32[256,1024]{1,0:T(8,128)S(1)} %pad_maximum_fusion.1), channel_id=1, source_target_pairs={{0,8},{8,0},{1,9},{9,1},{2,10},{10,2},{3,11},{11,3},{4,12},{12,4},... | collective-permute-start | bytes 3145736 | tf_op jit(solution)/shard_map/ppermute | solution.py:173
  45.5 8.5 %collective-permute-done.4.refs_6_ = f32[128,1024]{1,0:T(8,128)S(1)} collective-permute-done((f32[128,1024]{1,0:T(8,128)S(1)}, f32[128,1024]{1,0:T(8,128)S(1)}, u32[]{:S(2)}, u32[]{:S(2)}) %collective-permute-start.4) | collective-permute-done | bytes 524320 | tf_op jit(solution)/shard_map/ppermute | solution.py:181
  54.2 1.9 %collective-permute-start.6 = (f32[256,1024]{1,0:T(8,128)S(1)}, f32[256,1024]{1,0:T(8,128)S(1)}, u32[]{:S(2)}, u32[]{:S(2)}) collective-permute-start(f32[256,1024]{1,0:T(8,128)S(1)} %pad_maximum_fusion.2), channel_id=1, source_target_pairs={{0,8},{8,0},{1,9},{9,1},{2,10},{10,2},{3,11},{11,3},{4,12},{12,4},... | collective-permute-start | bytes 3145736 | tf_op jit(solution)/shard_map/ppermute | solution.py:173
  56.1 1.9 %collective-permute-start.7 = (f32[128,1024]{1,0:T(8,128)S(1)}, f32[128,1024]{1,0:T(8,128)S(1)}, u32[]{:S(2)}, u32[]{:S(2)}) collective-permute-start(f32[128,1024]{1,0:T(8,128)S(1)} %collective-permute-done.4.refs_6_), channel_id=1, source_target_pairs={{0,1},{1,2},{2,3},{3,4},{4,5},{5,6},{6,7},{7,0},{8,15},{9,8},{10,9... | collective-permute-start | bytes 1572872 | tf_op jit(solution)/shard_map/ppermute | solution.py:181
  59.0 1.9 %collective-permute-start.8 = (f32[128,1024]{1,0:T(8,128)S(1)}, f32[128,1024]{1,0:T(8,128)S(1)}, u32[]{:S(2)}, u32[]{:S(2)}) collective-permute-start(f32[128,1024]{1,0:T(8,128)S(1)} %collective-permute-done.5.refs_7_), channel_id=1, source_target_pairs={{0,1},{1,2},{2,3},{3,4},{4,5},{5,6},{6,7},{7,0},{8,15},{9,8},{10,9... | collective-permute-start | bytes 1572872 | tf_op jit(solution)/shard_map/ppermute | solution.py:181
  60.9 7.4 %collective-permute-done.7.refs_9_ = f32[128,1024]{1,0:T(8,128)S(1)} collective-permute-done((f32[128,1024]{1,0:T(8,128)S(1)}, f32[128,1024]{1,0:T(8,128)S(1)}, u32[]{:S(2)}, u32[]{:S(2)}) %collective-permute-start.7) | collective-permute-done | bytes 524320 | tf_op jit(solution)/shard_map/ppermute | solution.py:181
  69.1 1.9 %collective-permute-start.9 = (f32[64,1024]{1,0:T(8,128)}, f32[64,1024]{1,0:T(8,128)S(1)}, u32[]{:S(2)}, u32[]{:S(2)}) collective-permute-start(f32[64,1024]{1,0:T(8,128)} %slice.8), channel_id=1, source_target_pairs={{0,1},{1,2},{2,3},{3,4},{4,5},{5,6},{6,7},{7,0},{8,15},{9,8},{10,9... | collective-permute-start | bytes 786440 | tf_op jit(solution)/shard_map/ppermute | solution.py:181
  72.0 2.0 %collective-permute-done.8.refs_10_ = f32[128,1024]{1,0:T(8,128)S(1)} collective-permute-done((f32[128,1024]{1,0:T(8,128)S(1)}, f32[128,1024]{1,0:T(8,128)S(1)}, u32[]{:S(2)}, u32[]{:S(2)}) %collective-permute-start.8) | collective-permute-done | bytes 524320 | tf_op jit(solution)/shard_map/ppermute | solution.py:181
  74.7 1.9 %collective-permute-start.10 = (f32[64,1024]{1,0:T(8,128)}, f32[64,1024]{1,0:T(8,128)}, u32[]{:S(2)}, u32[]{:S(2)}) collective-permute-start(f32[64,1024]{1,0:T(8,128)} %slice.7), channel_id=1, source_target_pairs={{0,1},{1,2},{2,3},{3,4},{4,5},{5,6},{6,7},{7,0},{8,15},{9,8},{10,9... | collective-permute-start | bytes 786440 | tf_op jit(solution)/shard_map/ppermute | solution.py:181
  76.7 4.0 %spread.1.refs_0_ = bf16[1024,2176]{1,0:T(8,128)(2,1)S(1)} custom-call(f32[32,136,128]{2,1,0:T(8,128)S(1)} %all-to-all-done.got_ref), custom_call_target="tpu_custom_call" | custom-call | bytes 8388608 | tf_op jit(solution)/shard_map/spread/pallas_call | solution.py:109
  80.7 3.8 %collective-permute-done.10.refs_4_ = f32[64,1024]{1,0:T(8,128)} collective-permute-done((f32[64,1024]{1,0:T(8,128)}, f32[64,1024]{1,0:T(8,128)}, u32[]{:S(2)}, u32[]{:S(2)}) %collective-permute-start.10) | collective-permute-done | bytes 262176 | tf_op jit(solution)/shard_map/ppermute | solution.py:181
  85.6 1.9 %collective-permute-start.11 = (f32[384,1024]{1,0:T(8,128)S(1)}, f32[384,1024]{1,0:T(8,128)S(1)}, u32[]{:S(2)}, u32[]{:S(2)}) collective-permute-start(f32[384,1024]{1,0:T(8,128)S(1)} %pad_maximum_fusion), channel_id=1, source_target_pairs={{0,8},{8,0},{1,9},{9,1},{2,10},{10,2},{3,11},{11,3},{4,12},{12,4},... | collective-permute-start | bytes 4718600 | tf_op jit(solution)/shard_map/ppermute | solution.py:173
  87.6 5.2 %product.2.refs_1_ = f32[512,1024]{1,0:T(8,128)S(1)} custom-call(bf16[1024,2176]{1,0:T(8,128)(2,1)S(1)} %spread.1.refs_0_, f32[128,1024]{1,0:T(8,128)S(1)} %copy-done.13, f32[128,1024]{1,0:T(8,128)S(1)} %copy-done.15, f32[128,1024]{1,0:T(8,128)S(1)} %copy-done.3, f32[128,1024]{1,0:T(8,128)S(1)} %copy-done.1, f32[256,1024]{1,0:T(8,128)S(1)} %copy-done.9, ...), custom_call_target="tpu_custom_call" | custom-call | flops 4831838208 | bytes 4194304 | tf_op jit(solution)/shard_map/product/pallas_call | solution.py:155
  92.7 2.8 %product.3 = f32[512,1024]{1,0:T(8,128)S(1)} custom-call(bf16[1024,2176]{1,0:T(8,128)(2,1)S(1)} %spread.1.refs_0_, f32[512,1024]{1,0:T(8,128)S(1)} %product.2.refs_1_, f32[384,1024]{1,0:T(8,128)S(1)} %collective-permute-done.11.refs_2_, f32[64,1024]{1,0:T(8,128)S(1)} %collective-permute-done.9.refs_3_, f32[64,1024]{1,0:T(8,128)} %collective-permute-done.10.refs_4_), custom_call_target="tpu_custom_call" | custom-call | flops 1610612736 | bytes 4194304 | tf_op jit(solution)/shard_map/product/pallas_call | solution.py:155
  95.5 30.2 %all_to_all.15 = f32[4,128,1024]{2,1,0:T(8,128)} all-to-all(f32[4,128,1024]{2,1,0:T(8,128)S(1)} %bitcast.4), channel_id=1, replica_groups=mesh['x'=4,'z'=8,'core'=2,'grp'=8] {'x'}, dimensions={0} | all-to-all | bytes 4194304 | tf_op jit(solution)/shard_map/all_to_all | solution.py:230
  127.5 23.5 %all_to_all.16 = f32[8,16,1024]{2,1,0:T(8,128)S(1)} all-to-all(f32[8,16,1024]{2,1,0:T(8,128)S(1)} %bitcast.5), channel_id=1, replica_groups=mesh['x'=4,'z'=8,'core'=2,'grp'=8] {'z'}, dimensions={0} | all-to-all | bytes 1048576 | tf_op jit(solution)/shard_map/all_to_all | solution.py:232
  (47 shorter events, 8.0 us)
Async XLA Ops:
  4.2 13.6 %copy-start.12 = (f32[128,1024]{1,0:T(8,128)S(1)}, f32[128,1024]{1,0:T(8,128)}, u32[]{:S(2)}) copy-start(f32[128,1024]{1,0:T(8,128)} %refs_1_.1) | copy-start | bytes 1572868
  4.2 72.4 %all-to-all-start = ((f32[32,136,128]{2,1,0:T(8,128)}), f32[32,136,128]{2,1,0:T(8,128)S(1)}, u32[]{:S(2)}, u32[]{:S(2)}) async-start(f32[32,136,128]{2,1,0:T(8,128)} %pack.1), calls=%async_computation | async-start | bytes 4456448 | tf_op jit(solution)/shard_map/all_to_all | solution.py:220
  17.8 9.3 %collective-permute-start = (f32[128,1024]{1,0:T(8,128)S(1)}, f32[128,1024]{1,0:T(8,128)S(1)}, u32[]{:S(2)}, u32[]{:S(2)}) collective-permute-start(f32[128,1024]{1,0:T(8,128)S(1)} %copy-done.12), channel_id=1, source_target_pairs={{0,8},{8,0},{1,9},{9,1},{2,10},{10,2},{3,11},{11,3},{4,12},{12,4},... | collective-permute-start | bytes 1572872 | tf_op jit(solution)/shard_map/ppermute | solution.py:173
  19.7 16.4 %collective-permute-start.2 = (f32[128,1024]{1,0:T(8,128)S(1)}, f32[128,1024]{1,0:T(8,128)S(1)}, u32[]{:S(2)}, u32[]{:S(2)}) collective-permute-start(f32[128,1024]{1,0:T(8,128)S(1)} %copy-done.12), channel_id=1, source_target_pairs={{8,1},{9,2},{10,3},{11,4},{12,5},{13,6},{14,7},{15,0},{0,15},{1,8}... | collective-permute-start | bytes 1572872 | tf_op jit(solution)/shard_map/ppermute | solution.py:181
  25.2 12.8 %collective-permute-start.1 = (f32[128,1024]{1,0:T(8,128)S(1)}, f32[128,1024]{1,0:T(8,128)S(1)}, u32[]{:S(2)}, u32[]{:S(2)}) collective-permute-start(f32[128,1024]{1,0:T(8,128)S(1)} %copy-done.12), channel_id=1, source_target_pairs={{0,1},{1,2},{2,3},{3,4},{4,5},{5,6},{6,7},{7,0},{8,15},{9,8},{10,9... | collective-permute-start | bytes 1572872 | tf_op jit(solution)/shard_map/ppermute | solution.py:181
  36.1 18.0 %copy-start = (f32[128,1024]{1,0:T(8,128)}, f32[128,1024]{1,0:T(8,128)S(1)}, u32[]{:S(2)}) copy-start(f32[128,1024]{1,0:T(8,128)S(1)} %collective-permute-done.2.refs_4_) | copy-start | bytes 1572868
  36.1 17.9 %collective-permute-start.5 = (f32[128,1024]{1,0:T(8,128)S(1)}, f32[128,1024]{1,0:T(8,128)S(1)}, u32[]{:S(2)}, u32[]{:S(2)}) collective-permute-start(f32[128,1024]{1,0:T(8,128)S(1)} %collective-permute-done.2.refs_4_), channel_id=1, source_target_pairs={{0,1},{1,2},{2,3},{3,4},{4,5},{5,6},{6,7},{7,0},{8,15},{9,8},{10,9... | collective-permute-start | bytes 1572872 | tf_op jit(solution)/shard_map/ppermute | solution.py:181
  38.1 16.1 %copy-start.2 = (f32[128,1024]{1,0:T(8,128)}, f32[128,1024]{1,0:T(8,128)S(1)}, u32[]{:S(2)}) copy-start(f32[128,1024]{1,0:T(8,128)S(1)} %collective-permute-done.1.refs_3_) | copy-start | bytes 1572868
  38.1 16.0 %collective-permute-start.4 = (f32[128,1024]{1,0:T(8,128)S(1)}, f32[128,1024]{1,0:T(8,128)S(1)}, u32[]{:S(2)}, u32[]{:S(2)}) collective-permute-start(f32[128,1024]{1,0:T(8,128)S(1)} %collective-permute-done.1.refs_3_), channel_id=1, source_target_pairs={{0,1},{1,2},{2,3},{3,4},{4,5},{5,6},{6,7},{7,0},{8,15},{9,8},{10,9... | collective-permute-start | bytes 1572872 | tf_op jit(solution)/shard_map/ppermute | solution.py:181
  40.1 17.9 %collective-permute-start.3 = (f32[256,1024]{1,0:T(8,128)S(1)}, f32[256,1024]{1,0:T(8,128)S(1)}, u32[]{:S(2)}, u32[]{:S(2)}) collective-permute-start(f32[256,1024]{1,0:T(8,128)S(1)} %pad_maximum_fusion.1), channel_id=1, source_target_pairs={{0,8},{8,0},{1,9},{9,1},{2,10},{10,2},{3,11},{11,3},{4,12},{12,4},... | collective-permute-start | bytes 3145736 | tf_op jit(solution)/shard_map/ppermute | solution.py:173
  54.0 20.7 %copy-start.6 = (f32[128,1024]{1,0:T(8,128)}, f32[128,1024]{1,0:T(8,128)S(1)}, u32[]{:S(2)}) copy-start(f32[128,1024]{1,0:T(8,128)S(1)} %collective-permute-done.4.refs_6_) | copy-start | bytes 1572868
  54.0 20.7 %copy-start.4 = (f32[128,1024]{1,0:T(8,128)}, f32[128,1024]{1,0:T(8,128)S(1)}, u32[]{:S(2)}) copy-start(f32[128,1024]{1,0:T(8,128)S(1)} %collective-permute-done.5.refs_7_) | copy-start | bytes 1572868
  54.2 16.8 %collective-permute-start.6 = (f32[256,1024]{1,0:T(8,128)S(1)}, f32[256,1024]{1,0:T(8,128)S(1)}, u32[]{:S(2)}, u32[]{:S(2)}) collective-permute-start(f32[256,1024]{1,0:T(8,128)S(1)} %pad_maximum_fusion.2), channel_id=1, source_target_pairs={{0,8},{8,0},{1,9},{9,1},{2,10},{10,2},{3,11},{11,3},{4,12},{12,4},... | collective-permute-start | bytes 3145736 | tf_op jit(solution)/shard_map/ppermute | solution.py:173
  56.1 12.3 %collective-permute-start.7 = (f32[128,1024]{1,0:T(8,128)S(1)}, f32[128,1024]{1,0:T(8,128)S(1)}, u32[]{:S(2)}, u32[]{:S(2)}) collective-permute-start(f32[128,1024]{1,0:T(8,128)S(1)} %collective-permute-done.4.refs_6_), channel_id=1, source_target_pairs={{0,1},{1,2},{2,3},{3,4},{4,5},{5,6},{6,7},{7,0},{8,15},{9,8},{10,9... | collective-permute-start | bytes 1572872 | tf_op jit(solution)/shard_map/ppermute | solution.py:181
  59.0 15.0 %collective-permute-start.8 = (f32[128,1024]{1,0:T(8,128)S(1)}, f32[128,1024]{1,0:T(8,128)S(1)}, u32[]{:S(2)}, u32[]{:S(2)}) collective-permute-start(f32[128,1024]{1,0:T(8,128)S(1)} %collective-permute-done.5.refs_7_), channel_id=1, source_target_pairs={{0,1},{1,2},{2,3},{3,4},{4,5},{5,6},{6,7},{7,0},{8,15},{9,8},{10,9... | collective-permute-start | bytes 1572872 | tf_op jit(solution)/shard_map/ppermute | solution.py:181
  69.1 11.7 %collective-permute-start.9 = (f32[64,1024]{1,0:T(8,128)}, f32[64,1024]{1,0:T(8,128)S(1)}, u32[]{:S(2)}, u32[]{:S(2)}) collective-permute-start(f32[64,1024]{1,0:T(8,128)} %slice.8), channel_id=1, source_target_pairs={{0,1},{1,2},{2,3},{3,4},{4,5},{5,6},{6,7},{7,0},{8,15},{9,8},{10,9... | collective-permute-start | bytes 786440 | tf_op jit(solution)/shard_map/ppermute | solution.py:181
  74.7 9.8 %collective-permute-start.10 = (f32[64,1024]{1,0:T(8,128)}, f32[64,1024]{1,0:T(8,128)}, u32[]{:S(2)}, u32[]{:S(2)}) collective-permute-start(f32[64,1024]{1,0:T(8,128)} %slice.7), channel_id=1, source_target_pairs={{0,1},{1,2},{2,3},{3,4},{4,5},{5,6},{6,7},{7,0},{8,15},{9,8},{10,9... | collective-permute-start | bytes 786440 | tf_op jit(solution)/shard_map/ppermute | solution.py:181
  76.6 10.8 %copy-start.11 = (f32[256,1024]{1,0:T(8,128)S(1)}, f32[256,1024]{1,0:T(8,128)}, u32[]{:S(2)}) copy-start(f32[256,1024]{1,0:T(8,128)} %copy-done.10) | copy-start | bytes 3145732
  76.7 10.8 %copy-start.13 = (f32[128,1024]{1,0:T(8,128)S(1)}, f32[128,1024]{1,0:T(8,128)}, u32[]{:S(2)}) copy-start(f32[128,1024]{1,0:T(8,128)} %refs_1_.1) | copy-start | bytes 1572868
  76.7 10.8 %copy-start.15 = (f32[128,1024]{1,0:T(8,128)S(1)}, f32[128,1024]{1,0:T(8,128)}, u32[]{:S(2)}) copy-start(f32[128,1024]{1,0:T(8,128)} %copy-done.14) | copy-start | bytes 1572868
  80.7 6.8 %copy-start.1 = (f32[128,1024]{1,0:T(8,128)S(1)}, f32[128,1024]{1,0:T(8,128)}, u32[]{:S(2)}) copy-start(f32[128,1024]{1,0:T(8,128)} %copy-done) | copy-start | bytes 1572868
  80.7 6.8 %copy-start.3 = (f32[128,1024]{1,0:T(8,128)S(1)}, f32[128,1024]{1,0:T(8,128)}, u32[]{:S(2)}) copy-start(f32[128,1024]{1,0:T(8,128)} %copy-done.2) | copy-start | bytes 1572868
  80.7 6.8 %copy-start.5 = (f32[128,1024]{1,0:T(8,128)S(1)}, f32[128,1024]{1,0:T(8,128)}, u32[]{:S(2)}) copy-start(f32[128,1024]{1,0:T(8,128)} %copy-done.4) | copy-start | bytes 1572868
  85.6 7.2 %collective-permute-start.11 = (f32[384,1024]{1,0:T(8,128)S(1)}, f32[384,1024]{1,0:T(8,128)S(1)}, u32[]{:S(2)}, u32[]{:S(2)}) collective-permute-start(f32[384,1024]{1,0:T(8,128)S(1)} %pad_maximum_fusion), channel_id=1, source_target_pairs={{0,8},{8,0},{1,9},{9,1},{2,10},{10,2},{3,11},{11,3},{4,12},{12,4},... | collective-permute-start | bytes 4718600 | tf_op jit(solution)/shard_map/ppermute | solution.py:173
  (5 other events, 16.4 us)

commit v8 on v7

--- a/solution.py
+++ b/solution.py
@@ -181,34 +181,20 @@
     return lax.ppermute(block, ("core", "grp"), pairs)
 
 
-def gather_panel(block, after):
+def gather_panel(block, partner, own):
     n = lax.axis_size("grp")
     size = block.shape[0]
-    half = size // 2
-    own, mate = along_ring(block), along_ring(block, cross=True)
-    swapped = swap_core(block)
-    blocks = [block, swapped]
-    for step in range(1, n // 2):
+    mate = along_ring(block, cross=True)
+    blocks = [block, partner, own, mate]
+    for _ in range(n // 2 - 2):
+        blocks.append(swap_core(jnp.concatenate([own, mate], axis=0)))
+        own, mate = along_ring(own), along_ring(mate)
         blocks += [own, mate]
-        held, _ = lax.optimization_barrier((mate, swapped))
-        if step < n // 2 - 1:
-            swapped = swap_core(jnp.concatenate([own, mate], axis=0))
-            blocks.append(swapped)
-            own, mate = along_ring(own), along_ring(held)
-    top, bottom = along_ring(own[:half]), along_ring(held[half:])
-    held, _ = lax.optimization_barrier((top, after))
-    blocks.append(swap_core(jnp.concatenate([own, mate, held, bottom], axis=0)))
-    pieces = [(i, 0, b.shape[0]) for i, b in enumerate(blocks[:-1])]
-    last = len(blocks) - 1
-    blocks += [top, bottom]
-    pieces += [
-        (last, 0, 2 * size),
-        (last + 1, 0, half),
-        (last, 2 * size + half, half),
-        (last, 2 * size, half),
-        (last + 2, 0, half),
-    ]
-    return blocks, pieces
+    far = along_ring(own)
+    pieces = [(i, 0, each.shape[0]) for i, each in enumerate(blocks)]
+    last = len(blocks)
+    blocks += [swap_core(jnp.concatenate([own, mate, far], axis=0)), far]
+    return blocks, pieces + [(last, 0, 2 * size), (last + 1, 0, size), (last, 2 * size, size)]
 
 
 def on_device(amplitudes, integrals, occupancy, tile_place):
@@ -217,9 +203,12 @@
     rows, width = amplitudes.shape[2:]
     cols = integrals.shape[1]
     sent = pack(occupancy[0], tile_place, amplitudes[0], chips, per_chip)
+    sent, first, partner = lax.optimization_barrier(
+        (sent, along_ring(integrals), swap_core(integrals))
+    )
     got = lax.all_to_all(sent, CHIPS, 0, 0, tiled=True)
+    blocks, pieces = gather_panel(integrals, partner, first)
     left = spread(got, rows, per_chip * width)
-    blocks, pieces = gather_panel(integrals, left)
     early, depth = 0, 0
     while depth < EARLY * width:
         depth += pieces[early][2]

time: 152 us -> 147 us (0.967)
  the two profiles are of different devices: /device:TPU:2 before, /device:TPU:32 now
where the time goes in v8:
time: 147 us; the launch traced here: 146 us
  blocking collectives  53.6 us (36%)
  starting transfers between devices  35.4 us (24%)
  waiting for transfers between devices  34.1 us (23%)
  Pallas kernels  17.9 us (12%)
  other arithmetic  4.37 us (3%)
    ppermute x7, waiting for transfers between devices, along_ring(): return lax.ppermute(block, ('core', 'grp'), pairs)  34.1 us
    all_to_all x1, blocking collectives, on_device(): part = lax.all_to_all(part, 'x', 0, 0, tiled=True).sum(axis=0)  30.9 us
    all_to_all x1, blocking collectives, on_device(): return lax.all_to_all(part, 'z', 0, 0, tiled=True).sum(axis=0)  22.7 us
    ppermute x7, starting transfers between devices, along_ring(): return lax.ppermute(block, ('core', 'grp'), pairs)  14.1 us
    all_to_all x1, starting transfers between devices, on_device(): got = lax.all_to_all(sent, CHIPS, 0, 0, tiled=True)  13.2 us
    pallas_call x2, Pallas kernels, product(): pl.pallas_call(lambda *refs: product_kernel(pieces, start, bool(extra), *...  9.75 us
    ppermute x4, starting transfers between devices, swap_core(): return lax.ppermute(block, 'core', [(0, 1), (1, 0)])  8.14 us
    pallas_call x1, Pallas kernels, pack(): pl.pallas_call(pack_kernel, out_shape=jax.ShapeDtypeStruct((chips, HEAD +...  4.18 us
  transfers between devices with their start and end apart: 12, of which 7 were waited for; matrix products, arithmetic and copies ran while one was open for 2% of the time, Pallas kernels for 10%

profile of v8, /device:TPU:32, one launch (start us, length us, event | category | flops | bytes accessed | tf_op | source)
XLA Modules:
  0.0 146.5 jit_solution(5499061523964120755)
XLA Ops:
  0.0 2.6 %collective-permute-start = (f32[128,1024]{1,0:T(8,128)}, f32[128,1024]{1,0:T(8,128)S(1)}, u32[]{:S(2)}, u32[]{:S(2)}) collective-permute-start(f32[128,1024]{1,0:T(8,128)} %refs_1_.1), channel_id=1, source_target_pairs={{0,1},{1,2},{2,3},{3,4},{4,5},{5,6},{6,7},{7,0},{8,15},{9,8},{10,9... | collective-permute-start | bytes 1572872 | tf_op jit(solution)/shard_map/ppermute | solution.py:181
  2.6 1.9 %collective-permute-start.1 = (f32[128,1024]{1,0:T(8,128)}, f32[128,1024]{1,0:T(8,128)S(1)}, u32[]{:S(2)}, u32[]{:S(2)}) collective-permute-start(f32[128,1024]{1,0:T(8,128)} %refs_1_.1), channel_id=1, source_target_pairs={{0,8},{8,0},{1,9},{9,1},{2,10},{10,2},{3,11},{11,3},{4,12},{12,4},... | collective-permute-start | bytes 1572872 | tf_op jit(solution)/shard_map/ppermute | solution.py:173
  4.5 4.2 %pack.1 = f32[32,136,128]{2,1,0:T(8,128)} custom-call(s32[128]{0:T(128)} %bitcast.7, s32[512]{0:T(512)} %place_ref.1, f32[128,16,128]{2,1,0:T(8,128)} %bitcast.6), custom_call_target="tpu_custom_call" | custom-call | bytes 8388608 | tf_op jit(solution)/shard_map/pack/pallas_call | solution.py:64
  8.7 3.8 %collective-permute-done.refs_3_ = f32[128,1024]{1,0:T(8,128)S(1)} collective-permute-done((f32[128,1024]{1,0:T(8,128)}, f32[128,1024]{1,0:T(8,128)S(1)}, u32[]{:S(2)}, u32[]{:S(2)}) %collective-permute-start) | collective-permute-done | bytes 524320 | tf_op jit(solution)/shard_map/ppermute | solution.py:181
  13.3 13.2 %all-to-all-start = ((f32[32,136,128]{2,1,0:T(8,128)}), f32[32,136,128]{2,1,0:T(8,128)S(1)}, u32[]{:S(2)}, u32[]{:S(2)}) async-start(f32[32,136,128]{2,1,0:T(8,128)} %pack.1), calls=%async_computation | async-start | bytes 4456448 | tf_op jit(solution)/shard_map/all_to_all | solution.py:209
  26.5 1.9 %collective-permute-start.2 = (f32[128,1024]{1,0:T(8,128)S(1)}, f32[128,1024]{1,0:T(8,128)S(1)}, u32[]{:S(2)}, u32[]{:S(2)}) collective-permute-start(f32[128,1024]{1,0:T(8,128)S(1)} %copy-done.10), channel_id=1, source_target_pairs={{8,1},{9,2},{10,3},{11,4},{12,5},{13,6},{14,7},{15,0},{0,15},{1,8}... | collective-permute-start | bytes 1572872 | tf_op jit(solution)/shard_map/ppermute | solution.py:181
  28.4 1.9 %collective-permute-start.4 = (f32[128,1024]{1,0:T(8,128)S(1)}, f32[128,1024]{1,0:T(8,128)S(1)}, u32[]{:S(2)}, u32[]{:S(2)}) collective-permute-start(f32[128,1024]{1,0:T(8,128)S(1)} %collective-permute-done.refs_3_), channel_id=1, source_target_pairs={{0,1},{1,2},{2,3},{3,4},{4,5},{5,6},{6,7},{7,0},{8,15},{9,8},{10,9... | collective-permute-start | bytes 1572872 | tf_op jit(solution)/shard_map/ppermute | solution.py:181
  30.3 10.9 %collective-permute-done.2.refs_4_ = f32[128,1024]{1,0:T(8,128)S(1)} collective-permute-done((f32[128,1024]{1,0:T(8,128)S(1)}, f32[128,1024]{1,0:T(8,128)S(1)}, u32[]{:S(2)}, u32[]{:S(2)}) %collective-permute-start.2) | collective-permute-done | bytes 524320 | tf_op jit(solution)/shard_map/ppermute | solution.py:181
  41.2 1.9 %collective-permute-start.5 = (f32[128,1024]{1,0:T(8,128)S(1)}, f32[128,1024]{1,0:T(8,128)S(1)}, u32[]{:S(2)}, u32[]{:S(2)}) collective-permute-start(f32[128,1024]{1,0:T(8,128)S(1)} %collective-permute-done.2.refs_4_), channel_id=1, source_target_pairs={{0,1},{1,2},{2,3},{3,4},{4,5},{5,6},{6,7},{7,0},{8,15},{9,8},{10,9... | collective-permute-start | bytes 1572872 | tf_op jit(solution)/shard_map/ppermute | solution.py:181
  43.8 1.9 %collective-permute-start.7 = (f32[128,1024]{1,0:T(8,128)S(1)}, f32[128,1024]{1,0:T(8,128)S(1)}, u32[]{:S(2)}, u32[]{:S(2)}) collective-permute-start(f32[128,1024]{1,0:T(8,128)S(1)} %collective-permute-done.4.refs_6_), channel_id=1, source_target_pairs={{0,1},{1,2},{2,3},{3,4},{4,5},{5,6},{6,7},{7,0},{8,15},{9,8},{10,9... | collective-permute-start | bytes 1572872 | tf_op jit(solution)/shard_map/ppermute | solution.py:181
  45.7 7.8 %collective-permute-done.5.refs_7_ = f32[128,1024]{1,0:T(8,128)S(1)} collective-permute-done((f32[128,1024]{1,0:T(8,128)S(1)}, f32[128,1024]{1,0:T(8,128)S(1)}, u32[]{:S(2)}, u32[]{:S(2)}) %collective-permute-start.5) | collective-permute-done | bytes 524320 | tf_op jit(solution)/shard_map/ppermute | solution.py:181
  53.5 1.9 %collective-permute-start.8 = (f32[128,1024]{1,0:T(8,128)S(1)}, f32[128,1024]{1,0:T(8,128)S(1)}, u32[]{:S(2)}, u32[]{:S(2)}) collective-permute-start(f32[128,1024]{1,0:T(8,128)S(1)} %collective-permute-done.5.refs_7_), channel_id=1, source_target_pairs={{0,1},{1,2},{2,3},{3,4},{4,5},{5,6},{6,7},{7,0},{8,15},{9,8},{10,9... | collective-permute-start | bytes 1572872 | tf_op jit(solution)/shard_map/ppermute | solution.py:181
  55.4 3.7 %collective-permute-done.7.refs_9_ = f32[128,1024]{1,0:T(8,128)S(1)} collective-permute-done((f32[128,1024]{1,0:T(8,128)S(1)}, f32[128,1024]{1,0:T(8,128)S(1)}, u32[]{:S(2)}, u32[]{:S(2)}) %collective-permute-start.7) | collective-permute-done | bytes 524320 | tf_op jit(solution)/shard_map/ppermute | solution.py:181
  59.1 1.9 %collective-permute-start.9 = (f32[128,1024]{1,0:T(8,128)S(1)}, f32[128,1024]{1,0:T(8,128)S(1)}, u32[]{:S(2)}, u32[]{:S(2)}) collective-permute-start(f32[128,1024]{1,0:T(8,128)S(1)} %collective-permute-done.7.refs_9_), channel_id=1, source_target_pairs={{0,1},{1,2},{2,3},{3,4},{4,5},{5,6},{6,7},{7,0},{8,15},{9,8},{10,9... | collective-permute-start | bytes 1572872 | tf_op jit(solution)/shard_map/ppermute | solution.py:181
  62.2 1.9 %collective-permute-start.3 = (f32[256,1024]{1,0:T(8,128)}, f32[256,1024]{1,0:T(8,128)}, u32[]{:S(2)}, u32[]{:S(2)}) collective-permute-start(f32[256,1024]{1,0:T(8,128)} %pad_maximum_fusion.1), channel_id=1, source_target_pairs={{0,8},{8,0},{1,9},{9,1},{2,10},{10,2},{3,11},{11,3},{4,12},{12,4},... | collective-permute-start | bytes 3145736 | tf_op jit(solution)/shard_map/ppermute | solution.py:173
  64.1 1.6 %collective-permute-done.8.refs_10_ = f32[128,1024]{1,0:T(8,128)S(1)} collective-permute-done((f32[128,1024]{1,0:T(8,128)S(1)}, f32[128,1024]{1,0:T(8,128)S(1)}, u32[]{:S(2)}, u32[]{:S(2)}) %collective-permute-start.8) | collective-permute-done | bytes 524320 | tf_op jit(solution)/shard_map/ppermute | solution.py:181
  65.8 5.6 %collective-permute-done.9.refs_3_ = f32[128,1024]{1,0:T(8,128)S(1)} collective-permute-done((f32[128,1024]{1,0:T(8,128)S(1)}, f32[128,1024]{1,0:T(8,128)S(1)}, u32[]{:S(2)}, u32[]{:S(2)}) %collective-permute-start.9) | collective-permute-done | bytes 524320 | tf_op jit(solution)/shard_map/ppermute | solution.py:181
  72.6 1.9 %collective-permute-start.10 = (f32[384,1024]{1,0:T(8,128)}, f32[384,1024]{1,0:T(8,128)}, u32[]{:S(2)}, u32[]{:S(2)}) collective-permute-start(f32[384,1024]{1,0:T(8,128)} %pad_maximum_fusion), channel_id=1, source_target_pairs={{0,8},{8,0},{1,9},{9,1},{2,10},{10,2},{3,11},{11,3},{4,12},{12,4},... | collective-permute-start | bytes 4718600 | tf_op jit(solution)/shard_map/ppermute | solution.py:173
  75.7 2.4 %collective-permute-start.6 = (f32[256,1024]{1,0:T(8,128)}, f32[256,1024]{1,0:T(8,128)}, u32[]{:S(2)}, u32[]{:S(2)}) collective-permute-start(f32[256,1024]{1,0:T(8,128)} %pad_maximum_fusion.2), channel_id=1, source_target_pairs={{0,8},{8,0},{1,9},{9,1},{2,10},{10,2},{3,11},{11,3},{4,12},{12,4},... | collective-permute-start | bytes 3145736 | tf_op jit(solution)/shard_map/ppermute | solution.py:173
  78.2 4.0 %spread.1.refs_0_ = bf16[1024,2176]{1,0:T(8,128)(2,1)S(1)} custom-call(f32[32,136,128]{2,1,0:T(8,128)S(1)} %all-to-all-done.got_ref), custom_call_target="tpu_custom_call" | custom-call | bytes 8388608 | tf_op jit(solution)/shard_map/spread/pallas_call | solution.py:109
  82.3 6.6 %product.2.refs_1_ = f32[512,1024]{1,0:T(8,128)S(1)} custom-call(bf16[1024,2176]{1,0:T(8,128)(2,1)S(1)} %spread.1.refs_0_, f32[128,1024]{1,0:T(8,128)S(1)} %copy-done.11, f32[128,1024]{1,0:T(8,128)S(1)} %copy-done.13, f32[128,1024]{1,0:T(8,128)S(1)} %collective-permute-done.refs_3_, f32[128,1024]{1,0:T(8,128)S(1)} %copy-done.1, ...), custom_call_target="tpu_custom_call" | custom-call | flops 4831838208 | bytes 4194304 | tf_op jit(solution)/shard_map/product/pallas_call | solution.py:155
  88.8 3.2 %product.3 = f32[512,1024]{1,0:T(8,128)S(1)} custom-call(bf16[1024,2176]{1,0:T(8,128)(2,1)S(1)} %spread.1.refs_0_, f32[512,1024]{1,0:T(8,128)S(1)} %product.2.refs_1_, f32[384,1024]{1,0:T(8,128)} %collective-permute-done.10.refs_2_, f32[128,1024]{1,0:T(8,128)S(1)} %collective-permute-done.9.refs_3_), custom_call_target="tpu_custom_call" | custom-call | flops 1610612736 | bytes 4194304 | tf_op jit(solution)/shard_map/product/pallas_call | solution.py:155
  92.0 30.9 %all_to_all.15 = f32[4,128,1024]{2,1,0:T(8,128)S(1)} all-to-all(f32[4,128,1024]{2,1,0:T(8,128)S(1)} %bitcast.4), channel_id=1, replica_groups=mesh['x'=4,'z'=8,'core'=2,'grp'=8] {'x'}, dimensions={0} | all-to-all | bytes 4194304 | tf_op jit(solution)/shard_map/all_to_all | solution.py:219
  123.1 22.7 %all_to_all.16 = f32[8,16,1024]{2,1,0:T(8,128)S(1)} all-to-all(f32[8,16,1024]{2,1,0:T(8,128)S(1)} %bitcast.5), channel_id=1, replica_groups=mesh['x'=4,'z'=8,'core'=2,'grp'=8] {'z'}, dimensions={0} | all-to-all | bytes 1048576 | tf_op jit(solution)/shard_map/all_to_all | solution.py:221
  (39 shorter events, 5.9 us)
Async XLA Ops:
  0.0 12.5 %collective-permute-start = (f32[128,1024]{1,0:T(8,128)}, f32[128,1024]{1,0:T(8,128)S(1)}, u32[]{:S(2)}, u32[]{:S(2)}) collective-permute-start(f32[128,1024]{1,0:T(8,128)} %refs_1_.1), channel_id=1, source_target_pairs={{0,1},{1,2},{2,3},{3,4},{4,5},{5,6},{6,7},{7,0},{8,15},{9,8},{10,9... | collective-permute-start | bytes 1572872 | tf_op jit(solution)/shard_map/ppermute | solution.py:181
  2.6 9.9 %collective-permute-start.1 = (f32[128,1024]{1,0:T(8,128)}, f32[128,1024]{1,0:T(8,128)S(1)}, u32[]{:S(2)}, u32[]{:S(2)}) collective-permute-start(f32[128,1024]{1,0:T(8,128)} %refs_1_.1), channel_id=1, source_target_pairs={{0,8},{8,0},{1,9},{9,1},{2,10},{10,2},{3,11},{11,3},{4,12},{12,4},... | collective-permute-start | bytes 1572872 | tf_op jit(solution)/shard_map/ppermute | solution.py:173
  8.7 17.8 %copy-start.10 = (f32[128,1024]{1,0:T(8,128)S(1)}, f32[128,1024]{1,0:T(8,128)}, u32[]{:S(2)}) copy-start(f32[128,1024]{1,0:T(8,128)} %refs_1_.1) | copy-start | bytes 1572868
  13.3 64.8 %all-to-all-start = ((f32[32,136,128]{2,1,0:T(8,128)}), f32[32,136,128]{2,1,0:T(8,128)S(1)}, u32[]{:S(2)}, u32[]{:S(2)}) async-start(f32[32,136,128]{2,1,0:T(8,128)} %pack.1), calls=%async_computation | async-start | bytes 4456448 | tf_op jit(solution)/shard_map/all_to_all | solution.py:209
  26.5 14.8 %collective-permute-start.2 = (f32[128,1024]{1,0:T(8,128)S(1)}, f32[128,1024]{1,0:T(8,128)S(1)}, u32[]{:S(2)}, u32[]{:S(2)}) collective-permute-start(f32[128,1024]{1,0:T(8,128)S(1)} %copy-done.10), channel_id=1, source_target_pairs={{8,1},{9,2},{10,3},{11,4},{12,5},{13,6},{14,7},{15,0},{0,15},{1,8}... | collective-permute-start | bytes 1572872 | tf_op jit(solution)/shard_map/ppermute | solution.py:181
  28.4 15.4 %collective-permute-start.4 = (f32[128,1024]{1,0:T(8,128)S(1)}, f32[128,1024]{1,0:T(8,128)S(1)}, u32[]{:S(2)}, u32[]{:S(2)}) collective-permute-start(f32[128,1024]{1,0:T(8,128)S(1)} %collective-permute-done.refs_3_), channel_id=1, source_target_pairs={{0,1},{1,2},{2,3},{3,4},{4,5},{5,6},{6,7},{7,0},{8,15},{9,8},{10,9... | collective-permute-start | bytes 1572872 | tf_op jit(solution)/shard_map/ppermute | solution.py:181
  41.2 22.9 %copy-start = (f32[128,1024]{1,0:T(8,128)}, f32[128,1024]{1,0:T(8,128)S(1)}, u32[]{:S(2)}) copy-start(f32[128,1024]{1,0:T(8,128)S(1)} %collective-permute-done.2.refs_4_) | copy-start | bytes 1572868
  41.2 12.3 %collective-permute-start.5 = (f32[128,1024]{1,0:T(8,128)S(1)}, f32[128,1024]{1,0:T(8,128)S(1)}, u32[]{:S(2)}, u32[]{:S(2)}) collective-permute-start(f32[128,1024]{1,0:T(8,128)S(1)} %collective-permute-done.2.refs_4_), channel_id=1, source_target_pairs={{0,1},{1,2},{2,3},{3,4},{4,5},{5,6},{6,7},{7,0},{8,15},{9,8},{10,9... | collective-permute-start | bytes 1572872 | tf_op jit(solution)/shard_map/ppermute | solution.py:181
  43.8 30.8 %copy-start.2 = (f32[128,1024]{1,0:T(8,128)}, f32[128,1024]{1,0:T(8,128)S(1)}, u32[]{:S(2)}) copy-start(f32[128,1024]{1,0:T(8,128)S(1)} %collective-permute-done.4.refs_6_) | copy-start | bytes 1572868
  43.8 15.3 %collective-permute-start.7 = (f32[128,1024]{1,0:T(8,128)S(1)}, f32[128,1024]{1,0:T(8,128)S(1)}, u32[]{:S(2)}, u32[]{:S(2)}) collective-permute-start(f32[128,1024]{1,0:T(8,128)S(1)} %collective-permute-done.4.refs_6_), channel_id=1, source_target_pairs={{0,1},{1,2},{2,3},{3,4},{4,5},{5,6},{6,7},{7,0},{8,15},{9,8},{10,9... | collective-permute-start | bytes 1572872 | tf_op jit(solution)/shard_map/ppermute | solution.py:181
  53.5 21.1 %copy-start.4 = (f32[128,1024]{1,0:T(8,128)}, f32[128,1024]{1,0:T(8,128)S(1)}, u32[]{:S(2)}) copy-start(f32[128,1024]{1,0:T(8,128)S(1)} %collective-permute-done.5.refs_7_) | copy-start | bytes 1572868
  53.5 12.3 %collective-permute-start.8 = (f32[128,1024]{1,0:T(8,128)S(1)}, f32[128,1024]{1,0:T(8,128)S(1)}, u32[]{:S(2)}, u32[]{:S(2)}) collective-permute-start(f32[128,1024]{1,0:T(8,128)S(1)} %collective-permute-done.5.refs_7_), channel_id=1, source_target_pairs={{0,1},{1,2},{2,3},{3,4},{4,5},{5,6},{6,7},{7,0},{8,15},{9,8},{10,9... | collective-permute-start | bytes 1572872 | tf_op jit(solution)/shard_map/ppermute | solution.py:181
  59.1 13.5 %copy-start.6 = (f32[128,1024]{1,0:T(8,128)}, f32[128,1024]{1,0:T(8,128)S(1)}, u32[]{:S(2)}) copy-start(f32[128,1024]{1,0:T(8,128)S(1)} %collective-permute-done.7.refs_9_) | copy-start | bytes 1572868
  59.1 12.3 %collective-permute-start.9 = (f32[128,1024]{1,0:T(8,128)S(1)}, f32[128,1024]{1,0:T(8,128)S(1)}, u32[]{:S(2)}, u32[]{:S(2)}) collective-permute-start(f32[128,1024]{1,0:T(8,128)S(1)} %collective-permute-done.7.refs_9_), channel_id=1, source_target_pairs={{0,1},{1,2},{2,3},{3,4},{4,5},{5,6},{6,7},{7,0},{8,15},{9,8},{10,9... | collective-permute-start | bytes 1572872 | tf_op jit(solution)/shard_map/ppermute | solution.py:181
  62.2 20.0 %collective-permute-start.3 = (f32[256,1024]{1,0:T(8,128)}, f32[256,1024]{1,0:T(8,128)}, u32[]{:S(2)}, u32[]{:S(2)}) collective-permute-start(f32[256,1024]{1,0:T(8,128)} %pad_maximum_fusion.1), channel_id=1, source_target_pairs={{0,8},{8,0},{1,9},{9,1},{2,10},{10,2},{3,11},{11,3},{4,12},{12,4},... | collective-permute-start | bytes 3145736 | tf_op jit(solution)/shard_map/ppermute | solution.py:173
  65.8 6.9 %copy-start.8 = (f32[128,1024]{1,0:T(8,128)}, f32[128,1024]{1,0:T(8,128)S(1)}, u32[]{:S(2)}) copy-start(f32[128,1024]{1,0:T(8,128)S(1)} %collective-permute-done.8.refs_10_) | copy-start | bytes 1572868
  72.6 16.2 %collective-permute-start.10 = (f32[384,1024]{1,0:T(8,128)}, f32[384,1024]{1,0:T(8,128)}, u32[]{:S(2)}, u32[]{:S(2)}) collective-permute-start(f32[384,1024]{1,0:T(8,128)} %pad_maximum_fusion), channel_id=1, source_target_pairs={{0,8},{8,0},{1,9},{9,1},{2,10},{10,2},{3,11},{11,3},{4,12},{12,4},... | collective-permute-start | bytes 4718600 | tf_op jit(solution)/shard_map/ppermute | solution.py:173
  75.7 6.5 %collective-permute-start.6 = (f32[256,1024]{1,0:T(8,128)}, f32[256,1024]{1,0:T(8,128)}, u32[]{:S(2)}, u32[]{:S(2)}) collective-permute-start(f32[256,1024]{1,0:T(8,128)} %pad_maximum_fusion.2), channel_id=1, source_target_pairs={{0,8},{8,0},{1,9},{9,1},{2,10},{10,2},{3,11},{11,3},{4,12},{12,4},... | collective-permute-start | bytes 3145736 | tf_op jit(solution)/shard_map/ppermute | solution.py:173
  78.1 4.1 %copy-start.1 = (f32[128,1024]{1,0:T(8,128)S(1)}, f32[128,1024]{1,0:T(8,128)}, u32[]{:S(2)}) copy-start(f32[128,1024]{1,0:T(8,128)} %copy-done) | copy-start | bytes 1572868
  78.1 4.1 %copy-start.3 = (f32[128,1024]{1,0:T(8,128)S(1)}, f32[128,1024]{1,0:T(8,128)}, u32[]{:S(2)}) copy-start(f32[128,1024]{1,0:T(8,128)} %copy-done.2) | copy-start | bytes 1572868
  78.1 4.1 %copy-start.5 = (f32[128,1024]{1,0:T(8,128)S(1)}, f32[128,1024]{1,0:T(8,128)}, u32[]{:S(2)}) copy-start(f32[128,1024]{1,0:T(8,128)} %copy-done.4) | copy-start | bytes 1572868
  78.1 4.1 %copy-start.7 = (f32[128,1024]{1,0:T(8,128)S(1)}, f32[128,1024]{1,0:T(8,128)}, u32[]{:S(2)}) copy-start(f32[128,1024]{1,0:T(8,128)} %copy-done.6) | copy-start | bytes 1572868
  78.2 4.1 %copy-start.9 = (f32[128,1024]{1,0:T(8,128)S(1)}, f32[128,1024]{1,0:T(8,128)}, u32[]{:S(2)}) copy-start(f32[128,1024]{1,0:T(8,128)} %copy-done.8) | copy-start | bytes 1572868
  78.2 4.1 %copy-start.11 = (f32[128,1024]{1,0:T(8,128)S(1)}, f32[128,1024]{1,0:T(8,128)}, u32[]{:S(2)}) copy-start(f32[128,1024]{1,0:T(8,128)} %refs_1_.1) | copy-start | bytes 1572868
  (2 other events, 4.9 us)

commit v9 on v8

--- a/solution.py
+++ b/solution.py
@@ -11,8 +11,7 @@
 EVERY = ("x", "z", "core", "grp")
 LANES = 128
 HEAD = 8
-EARLY = 12
-VMEM_LIMIT = 20 << 20
+PRODUCT_LIMIT = 30 << 20
 VMEM = pl.BlockSpec(memory_space=pltpu.VMEM)
 SMEM = pl.BlockSpec(memory_space=pltpu.SMEM)
 ANY = pl.BlockSpec(memory_space=pl.ANY)
@@ -77,12 +76,21 @@
     return high, (value - high.astype(jnp.float32)).astype(jnp.bfloat16)
 
 
-def spread_kernel(got_ref, left_ref, head, sem):
+def row_of(ahead, low, height):
+    spot = (1 - low) if ahead % 2 else 2 + low
+    return (((ahead + 3) % 4 // 2) * 4 + spot) * height
+
+
+def spread_kernel(got_ref, left_ref, head, start, sem):
     chips = got_ref.shape[0]
-    height = left_ref.shape[0] // 2
-    rows = height // chips
+    height = left_ref.shape[0] // (2 * NX)
+    rows = height // NZ
     copy = pltpu.make_async_copy(got_ref.at[:, pl.ds(0, HEAD), :], head, sem)
     copy.start()
+    here = lax.axis_index("x")
+    for ahead in range(NX):
+        for low in range(2):
+            start[low, (here + ahead) % NX] = row_of(ahead, low, height)
 
     def clear(i, carry):
         at = pl.ds(pl.multiple_of(i * 32, 32), 32)
@@ -93,12 +101,14 @@
     copy.wait()
 
     def step(n, carry):
-        row = pl.multiple_of(n * rows, rows)
+        row = (n % NZ) * rows
+        high_row = pl.multiple_of(start[0, n // NZ] + row, rows)
+        low_row = pl.multiple_of(start[1, n // NZ] + row, rows)
         for s in range(NC * CAP):
             col = pl.multiple_of(head[n, 0, s].astype(jnp.int32) * LANES, LANES)
             high, low = split(got_ref[n, HEAD + s * rows : HEAD + (s + 1) * rows, :])
-            left_ref[pl.ds(row, rows), pl.ds(col, LANES)] = high
-            left_ref[pl.ds(height + row, rows), pl.ds(col, LANES)] = low
+            left_ref[pl.ds(high_row, rows), pl.ds(col, LANES)] = high
+            left_ref[pl.ds(low_row, rows), pl.ds(col, LANES)] = low
         return carry
 
     lax.fori_loop(0, chips, step, 0, unroll=2)
@@ -113,60 +123,62 @@
         out_specs=VMEM,
         scratch_shapes=[
             pltpu.SMEM((chips, HEAD, LANES), jnp.float32),
+            pltpu.SMEM((2, NX), jnp.int32),
             pltpu.SemaphoreType.DMA,
         ],
         cost_estimate=pl.CostEstimate(flops=0, bytes_accessed=8 << 20, transcendentals=0),
-        compiler_params=pltpu.CompilerParams(vmem_limit_bytes=VMEM_LIMIT),
+        compiler_params=pltpu.CompilerParams(vmem_limit_bytes=20 << 20),
         name="spread",
     )(got)
 
 
-def product_kernel(pieces, start, has_total, *refs):
+def product_kernel(pair, pieces, *refs):
     left_ref, refs = refs[0], refs[1:]
-    if has_total:
-        total_ref, refs = refs[0], refs[1:]
-    panel, (out_ref, v_high, v_low) = refs[:-3], refs[-3:]
-    height = out_ref.shape[0]
+    if pieces:
+        panel, (first_ref, second_ref, v_high, v_low) = refs[:-4], refs[-4:]
+        at = 0
+        for block, start, size in pieces:
+            for i in range(0, size, 64):
+                value = panel[block][start + i : start + i + 64, :]
+                v_high[at : at + 64, :], v_low[at : at + 64, :] = split(value)
+                at += 64
+    else:
+        v_high, v_low, first_ref, second_ref = refs
+    height = first_ref.shape[0]
     depth = v_high.shape[0]
-    at = 0
-    for block, first, size in pieces:
-        for i in range(0, size, 64):
-            value = panel[block][first + i : first + i + 64, :]
-            v_high[at : at + 64, :], v_low[at : at + 64, :] = split(value)
-            at += 64
+    base = pair * 4 * height
     dot = lambda a, b: jnp.dot(a, b, preferred_element_type=jnp.float32)
     wide = 256
-    for i in range(0, out_ref.shape[1], wide):
+    for i in range(0, first_ref.shape[1], wide):
         cols = pl.ds(i, wide)
-        both = dot(left_ref[:, start : start + depth], v_high[:, cols])
-        part = both[height:] + dot(left_ref[:height, start : start + depth], v_low[:, cols])
-        part = both[:height] + part
-        out_ref[:, cols] = part + total_ref[:, cols] if has_total else part
-
-
-def product(left, start, blocks, pieces, total=None):
-    height = left.shape[0] // 2
-    depth = sum(size for _, _, size in pieces)
+        four = dot(left_ref[base : base + 4 * height, :depth], v_high[:, cols])
+        two = dot(left_ref[base + height : base + 3 * height, :depth], v_low[:, cols])
+        first_ref[:, cols] = four[height : 2 * height] + (four[:height] + two[:height])
+        second_ref[:, cols] = four[2 * height : 3 * height] + (four[3 * height :] + two[height:])
+
+
+def product(left, pair, blocks, pieces=()):
+    height = left.shape[0] // (2 * NX)
     cols = blocks[0].shape[1]
-    used = sorted({piece[0] for piece in pieces})
-    pieces = [(used.index(block), first, size) for block, first, size in pieces]
-    extra = [] if total is None else [total]
-    operands = [left] + extra + [blocks[i] for i in used]
+    depth = left.shape[1] - LANES
+    part = jax.ShapeDtypeStruct((height, cols), jnp.float32)
+    half = jax.ShapeDtypeStruct((depth, cols), jnp.bfloat16)
+    outs = (part, part, half, half) if pieces else (part, part)
     return pl.pallas_call(
-        lambda *refs: product_kernel(pieces, start, bool(extra), *refs),
-        out_shape=jax.ShapeDtypeStruct((height, cols), jnp.float32),
-        in_specs=[VMEM] * len(operands),
-        out_specs=VMEM,
-        scratch_shapes=[
-            pltpu.VMEM((depth, cols), jnp.bfloat16),
-            pltpu.VMEM((depth, cols), jnp.bfloat16),
-        ],
+        lambda *refs: product_kernel(pair, pieces, *refs),
+        out_shape=outs,
+        in_specs=[VMEM] * (1 + len(blocks)),
+        out_specs=(VMEM,) * len(outs),
         cost_estimate=pl.CostEstimate(
-            flops=6 * height * depth * cols, bytes_accessed=4 << 20, transcendentals=0
+            flops=12 * height * depth * cols, bytes_accessed=4 << 20, transcendentals=0
         ),
-        compiler_params=pltpu.CompilerParams(vmem_limit_bytes=VMEM_LIMIT),
+        compiler_params=pltpu.CompilerParams(vmem_limit_bytes=PRODUCT_LIMIT),
         name="product",
-    )(*operands)
+    )(left, *blocks)
+
+
+def shift_x(step):
+    return [(i, (i + step) % NX) for i in range(NX)]
 
 
 def swap_core(block):
@@ -209,14 +221,13 @@
     got = lax.all_to_all(sent, CHIPS, 0, 0, tiled=True)
     blocks, pieces = gather_panel(integrals, partner, first)
     left = spread(got, rows, per_chip * width)
-    early, depth = 0, 0
-    while depth < EARLY * width:
-        depth += pieces[early][2]
-        early += 1
-    part = product(left, 0, blocks, pieces[:early])
-    part = product(left, depth, blocks, pieces[early:], part)
-    part = part.reshape(NX, NZ * rows, cols)
-    part = lax.all_to_all(part, "x", 0, 0, tiled=True).sum(axis=0)
+    near, far, high, low = product(left, 0, blocks, pieces)
+    far = lax.ppermute(far, "x", shift_x(2))
+    near = lax.ppermute(near, "x", shift_x(1))
+    back, part = product(left, 1, [high, low])
+    far, near, part = lax.optimization_barrier((far, near, part))
+    back = lax.ppermute(back, "x", shift_x(-1))
+    part = part + near + far + back
     part = part.reshape(NZ, rows, cols)
     return lax.all_to_all(part, "z", 0, 0, tiled=True).sum(axis=0)
 

time: 147 us -> 148 us (level)
  blocking collectives: 53.6 us -> 24.1 us
  waiting for transfers between devices: 34.1 us -> 53.2 us
  starting transfers between devices: 35.4 us -> 47.6 us
    all_to_all x1 -> x0, blocking collectives: 30.9 us -> none  [on_device(): part = lax.all_to_all(part, 'x', 0, 0, tiled=True).sum(axis=0)]
    ppermute x0 -> x3, waiting for transfers between devices: none -> 13.6 us  [the longest x1 10.9 us: on_device(): near = lax.ppermute(near, 'x', shift_x(1))]
    ppermute x0 -> x3, starting transfers between devices: none -> 12.3 us  [the longest x1 5.21 us: on_device(): far = lax.ppermute(far, 'x', shift_x(2))]
    ppermute x7, waiting for transfers between devices: 34.1 us -> 39.5 us  [along_ring(): return lax.ppermute(block, ('core', 'grp'), pairs)]
  transfers between devices with their start and end apart: 12 -> 15, of which waited for: 7 -> 10; matrix products, arithmetic and copies ran while one was open for 2% -> 2% of each run, Pallas kernels for 10% -> 8%
where the time goes in v9:
time: 148 us; the launch traced here: 147 us
  waiting for transfers between devices  53.2 us (36%)
  starting transfers between devices  47.6 us (32%)
  blocking collectives  24.1 us (16%)
  Pallas kernels  17.4 us (12%)
  other arithmetic  4.4 us (3%)
    ppermute x7, waiting for transfers between devices, along_ring(): return lax.ppermute(block, ('core', 'grp'), pairs)  39.5 us
    all_to_all x1, blocking collectives, on_device(): return lax.all_to_all(part, 'z', 0, 0, tiled=True).sum(axis=0)  24.1 us
    ppermute x7, starting transfers between devices, along_ring(): return lax.ppermute(block, ('core', 'grp'), pairs)  14.1 us
    all_to_all x1, starting transfers between devices, on_device(): got = lax.all_to_all(sent, CHIPS, 0, 0, tiled=True)  13.2 us
    ppermute x1, waiting for transfers between devices, on_device(): near = lax.ppermute(near, 'x', shift_x(1))  10.9 us
    pallas_call x2, Pallas kernels, product(): pl.pallas_call(lambda *refs: product_kernel(pair, pieces, *refs), out_sha...  8.91 us
    ppermute x4, starting transfers between devices, swap_core(): return lax.ppermute(block, 'core', [(0, 1), (1, 0)])  8.13 us
    ppermute x1, starting transfers between devices, on_device(): far = lax.ppermute(far, 'x', shift_x(2))  5.21 us
  transfers between devices with their start and end apart: 15, of which 10 were waited for; matrix products, arithmetic and copies ran while one was open for 2% of the time, Pallas kernels for 8%

profile of v9, /device:TPU:32, one launch (start us, length us, event | category | flops | bytes accessed | tf_op | source)
XLA Modules:
  0.0 147.0 jit_solution(17392127168999885581)
XLA Ops:
  0.0 1.9 %collective-permute-start.1 = (f32[128,1024]{1,0:T(8,128)}, f32[128,1024]{1,0:T(8,128)S(1)}, u32[]{:S(2)}, u32[]{:S(2)}) collective-permute-start(f32[128,1024]{1,0:T(8,128)} %refs_1_.1), channel_id=1, source_target_pairs={{0,8},{8,0},{1,9},{9,1},{2,10},{10,2},{3,11},{11,3},{4,12},{12,4},... | collective-permute-start | bytes 1572872 | tf_op jit(solution)/shard_map/ppermute | solution.py:185
  1.9 2.6 %collective-permute-start = (f32[128,1024]{1,0:T(8,128)}, f32[128,1024]{1,0:T(8,128)S(1)}, u32[]{:S(2)}, u32[]{:S(2)}) collective-permute-start(f32[128,1024]{1,0:T(8,128)} %refs_1_.1), channel_id=1, source_target_pairs={{0,1},{1,2},{2,3},{3,4},{4,5},{5,6},{6,7},{7,0},{8,15},{9,8},{10,9... | collective-permute-start | bytes 1572872 | tf_op jit(solution)/shard_map/ppermute | solution.py:193
  4.5 4.2 %pack.1 = f32[32,136,128]{2,1,0:T(8,128)} custom-call(s32[128]{0:T(128)} %bitcast.5, s32[512]{0:T(512)} %place_ref.1, f32[128,16,128]{2,1,0:T(8,128)} %bitcast.4), custom_call_target="tpu_custom_call" | custom-call | bytes 8388608 | tf_op jit(solution)/shard_map/pack/pallas_call | solution.py:63
  8.7 5.7 %collective-permute-done.refs_3_ = f32[128,1024]{1,0:T(8,128)S(1)} collective-permute-done((f32[128,1024]{1,0:T(8,128)}, f32[128,1024]{1,0:T(8,128)S(1)}, u32[]{:S(2)}, u32[]{:S(2)}) %collective-permute-start) | collective-permute-done | bytes 524320 | tf_op jit(solution)/shard_map/ppermute | solution.py:193
  14.4 13.2 %all-to-all-start = ((f32[32,136,128]{2,1,0:T(8,128)}), f32[32,136,128]{2,1,0:T(8,128)S(1)}, u32[]{:S(2)}, u32[]{:S(2)}) async-start(f32[32,136,128]{2,1,0:T(8,128)} %pack.1), calls=%async_computation | async-start | bytes 4456448 | tf_op jit(solution)/shard_map/all_to_all | solution.py:221
  27.6 1.9 %collective-permute-start.2 = (f32[128,1024]{1,0:T(8,128)}, f32[128,1024]{1,0:T(8,128)S(1)}, u32[]{:S(2)}, u32[]{:S(2)}) collective-permute-start(f32[128,1024]{1,0:T(8,128)} %refs_1_.1), channel_id=1, source_target_pairs={{8,1},{9,2},{10,3},{11,4},{12,5},{13,6},{14,7},{15,0},{0,15},{1,8}... | collective-permute-start | bytes 1572872 | tf_op jit(solution)/shard_map/ppermute | solution.py:193
  29.5 1.9 %collective-permute-start.4 = (f32[128,1024]{1,0:T(8,128)S(1)}, f32[128,1024]{1,0:T(8,128)S(1)}, u32[]{:S(2)}, u32[]{:S(2)}) collective-permute-start(f32[128,1024]{1,0:T(8,128)S(1)} %collective-permute-done.refs_3_), channel_id=1, source_target_pairs={{0,1},{1,2},{2,3},{3,4},{4,5},{5,6},{6,7},{7,0},{8,15},{9,8},{10,9... | collective-permute-start | bytes 1572872 | tf_op jit(solution)/shard_map/ppermute | solution.py:193
  31.5 11.3 %collective-permute-done.2.refs_4_ = f32[128,1024]{1,0:T(8,128)S(1)} collective-permute-done((f32[128,1024]{1,0:T(8,128)}, f32[128,1024]{1,0:T(8,128)S(1)}, u32[]{:S(2)}, u32[]{:S(2)}) %collective-permute-start.2) | collective-permute-done | bytes 524320 | tf_op jit(solution)/shard_map/ppermute | solution.py:193
  47.1 8.0 %collective-permute-done.5.refs_7_ = f32[128,1024]{1,0:T(8,128)S(1)} collective-permute-done((f32[128,1024]{1,0:T(8,128)S(1)}, f32[128,1024]{1,0:T(8,128)S(1)}, u32[]{:S(2)}, u32[]{:S(2)}) %collective-permute-start.5) | collective-permute-done | bytes 524320 | tf_op jit(solution)/shard_map/ppermute | solution.py:193
  57.0 3.7 %collective-permute-done.7.refs_9_ = f32[128,1024]{1,0:T(8,128)S(1)} collective-permute-done((f32[128,1024]{1,0:T(8,128)S(1)}, f32[128,1024]{1,0:T(8,128)S(1)}, u32[]{:S(2)}, u32[]{:S(2)}) %collective-permute-start.7) | collective-permute-done | bytes 524320 | tf_op jit(solution)/shard_map/ppermute | solution.py:193
  62.6 4.7 %collective-permute-done.8.refs_10_ = f32[128,1024]{1,0:T(8,128)S(1)} collective-permute-done((f32[128,1024]{1,0:T(8,128)S(1)}, f32[128,1024]{1,0:T(8,128)S(1)}, u32[]{:S(2)}, u32[]{:S(2)}) %collective-permute-start.8) | collective-permute-done | bytes 524320 | tf_op jit(solution)/shard_map/ppermute | solution.py:193
  67.3 5.6 %collective-permute-done.9.refs_12_ = f32[128,1024]{1,0:T(8,128)S(1)} collective-permute-done((f32[128,1024]{1,0:T(8,128)S(1)}, f32[128,1024]{1,0:T(8,128)S(1)}, u32[]{:S(2)}, u32[]{:S(2)}) %collective-permute-start.9) | collective-permute-done | bytes 524320 | tf_op jit(solution)/shard_map/ppermute | solution.py:193
  74.3 1.9 %collective-permute-start.10 = (f32[384,1024]{1,0:T(8,128)}, f32[384,1024]{1,0:T(8,128)}, u32[]{:S(2)}, u32[]{:S(2)}) collective-permute-start(f32[384,1024]{1,0:T(8,128)} %pad_maximum_fusion), channel_id=1, source_target_pairs={{0,8},{8,0},{1,9},{9,1},{2,10},{10,2},{3,11},{11,3},{4,12},{12,4},... | collective-permute-start | bytes 4718600 | tf_op jit(solution)/shard_map/ppermute | solution.py:185
  77.4 2.4 %collective-permute-start.3 = (f32[256,1024]{1,0:T(8,128)}, f32[256,1024]{1,0:T(8,128)}, u32[]{:S(2)}, u32[]{:S(2)}) collective-permute-start(f32[256,1024]{1,0:T(8,128)} %pad_maximum_fusion.1), channel_id=1, source_target_pairs={{0,8},{8,0},{1,9},{9,1},{2,10},{10,2},{3,11},{11,3},{4,12},{12,4},... | collective-permute-start | bytes 3145736 | tf_op jit(solution)/shard_map/ppermute | solution.py:185
  80.9 1.9 %collective-permute-start.6 = (f32[256,1024]{1,0:T(8,128)}, f32[256,1024]{1,0:T(8,128)}, u32[]{:S(2)}, u32[]{:S(2)}) collective-permute-start(f32[256,1024]{1,0:T(8,128)} %pad_maximum_fusion.2), channel_id=1, source_target_pairs={{0,8},{8,0},{1,9},{9,1},{2,10},{10,2},{3,11},{11,3},{4,12},{12,4},... | collective-permute-start | bytes 3145736 | tf_op jit(solution)/shard_map/ppermute | solution.py:185
  82.9 4.3 %spread.1.refs_0_ = bf16[1024,2176]{1,0:T(8,128)(2,1)S(1)} custom-call(f32[32,136,128]{2,1,0:T(8,128)S(1)} %all-to-all-done.got_ref), custom_call_target="tpu_custom_call" | custom-call | bytes 8388608 | tf_op jit(solution)/shard_map/spread/pallas_call | solution.py:119
  87.3 5.5 %product.2 = (f32[128,1024]{1,0:T(8,128)S(1)}, f32[128,1024]{1,0:T(8,128)S(1)}, bf16[2048,1024]{1,0:T(8,128)(2,1)S(1)}, bf16[2048,1024]{1,0:T(8,128)(2,1)S(1)}) custom-call(bf16[1024,2176]{1,0:T(8,128)(2,1)S(1)} %spread.1.refs_0_, f32[128,1024]{1,0:T(8,128)S(1)} %copy-done.10, f32[128,1024]{1,0:T(8,128)S(1)} %copy-done.12, ...), custom_call_target="tpu_custom_call" | custom-call | flops 3221225472 | bytes 4194304 | tf_op jit(solution)/shard_map/product/pallas_call | solution.py:167
  92.8 5.2 %collective-permute-start.11 = (f32[128,1024]{1,0:T(8,128)S(1)}, f32[128,1024]{1,0:T(8,128)S(1)}, u32[]{:S(2)}, u32[]{:S(2)}) collective-permute-start(f32[128,1024]{1,0:T(8,128)S(1)} %get-tuple-element.20), channel_id=1, source_target_pairs={{0,256},{128,384},{256,0},{384,128},{1,257},{129,385},{257,1},{385... | collective-permute-start | bytes 1572872 | tf_op jit(solution)/shard_map/ppermute | solution.py:225
  98.0 2.5 %collective-permute-start.12 = (f32[128,1024]{1,0:T(8,128)S(1)}, f32[128,1024]{1,0:T(8,128)S(1)}, u32[]{:S(2)}, u32[]{:S(2)}) collective-permute-start(f32[128,1024]{1,0:T(8,128)S(1)} %get-tuple-element.21), channel_id=1, source_target_pairs={{0,128},{128,256},{256,384},{384,0},{1,129},{129,257},{257,385},{3... | collective-permute-start | bytes 1572872 | tf_op jit(solution)/shard_map/ppermute | solution.py:226
  100.5 3.4 %product.3 = (f32[128,1024]{1,0:T(8,128)S(1)}, f32[128,1024]{1,0:T(8,128)S(1)}) custom-call(bf16[1024,2176]{1,0:T(8,128)(2,1)S(1)} %spread.1.refs_0_, bf16[2048,1024]{1,0:T(8,128)(2,1)S(1)} %get-tuple-element.22.refs_1_, bf16[2048,1024]{1,0:T(8,128)(2,1)S(1)} %get-tuple-element.23.refs_2_), custom_call_target="tpu_custom_call" | custom-call | flops 3221225472 | bytes 4194304 | tf_op jit(solution)/shard_map/product/pallas_call | solution.py:167
  103.9 4.5 %collective-permute-start.13 = (f32[128,1024]{1,0:T(8,128)S(1)}, f32[128,1024]{1,0:T(8,128)S(1)}, u32[]{:S(2)}, u32[]{:S(2)}) collective-permute-start(f32[128,1024]{1,0:T(8,128)S(1)} %get-tuple-element.28), channel_id=1, source_target_pairs={{0,384},{128,0},{256,128},{384,256},{1,385},{129,1},{257,129},{385... | collective-permute-start | bytes 1572872 | tf_op jit(solution)/shard_map/ppermute | solution.py:229
  108.5 2.5 %collective-permute-done.11 = f32[128,1024]{1,0:T(8,128)S(1)} collective-permute-done((f32[128,1024]{1,0:T(8,128)S(1)}, f32[128,1024]{1,0:T(8,128)S(1)}, u32[]{:S(2)}, u32[]{:S(2)}) %collective-permute-start.11) | collective-permute-done | bytes 524320 | tf_op jit(solution)/shard_map/ppermute | solution.py:225
  111.0 10.9 %collective-permute-done.12 = f32[128,1024]{1,0:T(8,128)S(1)} collective-permute-done((f32[128,1024]{1,0:T(8,128)S(1)}, f32[128,1024]{1,0:T(8,128)S(1)}, u32[]{:S(2)}, u32[]{:S(2)}) %collective-permute-start.12) | collective-permute-done | bytes 524320 | tf_op jit(solution)/shard_map/ppermute | solution.py:226
  122.3 24.1 %all_to_all.10 = f32[8,16,1024]{2,1,0:T(8,128)S(1)} all-to-all(f32[8,16,1024]{2,1,0:T(8,128)S(1)} %bitcast.3), channel_id=1, replica_groups=mesh['x'=4,'z'=8,'core'=2,'grp'=8] {'z'}, dimensions={0} | all-to-all | bytes 1048576 | tf_op jit(solution)/shard_map/all_to_all | solution.py:232
  (42 shorter events, 12.9 us)
Async XLA Ops:
  0.0 8.7 %collective-permute-start.1 = (f32[128,1024]{1,0:T(8,128)}, f32[128,1024]{1,0:T(8,128)S(1)}, u32[]{:S(2)}, u32[]{:S(2)}) collective-permute-start(f32[128,1024]{1,0:T(8,128)} %refs_1_.1), channel_id=1, source_target_pairs={{0,8},{8,0},{1,9},{9,1},{2,10},{10,2},{3,11},{11,3},{4,12},{12,4},... | collective-permute-start | bytes 1572872 | tf_op jit(solution)/shard_map/ppermute | solution.py:185
  1.9 12.5 %collective-permute-start = (f32[128,1024]{1,0:T(8,128)}, f32[128,1024]{1,0:T(8,128)S(1)}, u32[]{:S(2)}, u32[]{:S(2)}) collective-permute-start(f32[128,1024]{1,0:T(8,128)} %refs_1_.1), channel_id=1, source_target_pairs={{0,1},{1,2},{2,3},{3,4},{4,5},{5,6},{6,7},{7,0},{8,15},{9,8},{10,9... | collective-permute-start | bytes 1572872 | tf_op jit(solution)/shard_map/ppermute | solution.py:193
  8.7 5.7 %copy-start.11 = (f32[128,1024]{1,0:T(8,128)}, f32[128,1024]{1,0:T(8,128)S(1)}, u32[]{:S(2)}) copy-start(f32[128,1024]{1,0:T(8,128)S(1)} %collective-permute-done.1.refs_2_) | copy-start | bytes 1572868
  14.4 68.4 %all-to-all-start = ((f32[32,136,128]{2,1,0:T(8,128)}), f32[32,136,128]{2,1,0:T(8,128)S(1)}, u32[]{:S(2)}, u32[]{:S(2)}) async-start(f32[32,136,128]{2,1,0:T(8,128)} %pack.1), calls=%async_computation | async-start | bytes 4456448 | tf_op jit(solution)/shard_map/all_to_all | solution.py:221
  27.6 15.2 %collective-permute-start.2 = (f32[128,1024]{1,0:T(8,128)}, f32[128,1024]{1,0:T(8,128)S(1)}, u32[]{:S(2)}, u32[]{:S(2)}) collective-permute-start(f32[128,1024]{1,0:T(8,128)} %refs_1_.1), channel_id=1, source_target_pairs={{8,1},{9,2},{10,3},{11,4},{12,5},{13,6},{14,7},{15,0},{0,15},{1,8}... | collective-permute-start | bytes 1572872 | tf_op jit(solution)/shard_map/ppermute | solution.py:193
  29.5 15.6 %collective-permute-start.4 = (f32[128,1024]{1,0:T(8,128)S(1)}, f32[128,1024]{1,0:T(8,128)S(1)}, u32[]{:S(2)}, u32[]{:S(2)}) collective-permute-start(f32[128,1024]{1,0:T(8,128)S(1)} %collective-permute-done.refs_3_), channel_id=1, source_target_pairs={{0,1},{1,2},{2,3},{3,4},{4,5},{5,6},{6,7},{7,0},{8,15},{9,8},{10,9... | collective-permute-start | bytes 1572872 | tf_op jit(solution)/shard_map/ppermute | solution.py:193
  42.8 12.3 %collective-permute-start.5 = (f32[128,1024]{1,0:T(8,128)S(1)}, f32[128,1024]{1,0:T(8,128)S(1)}, u32[]{:S(2)}, u32[]{:S(2)}) collective-permute-start(f32[128,1024]{1,0:T(8,128)S(1)} %collective-permute-done.2.refs_4_), channel_id=1, source_target_pairs={{0,1},{1,2},{2,3},{3,4},{4,5},{5,6},{6,7},{7,0},{8,15},{9,8},{10,9... | collective-permute-start | bytes 1572872 | tf_op jit(solution)/shard_map/ppermute | solution.py:193
  45.1 34.7 %copy-start = (f32[128,1024]{1,0:T(8,128)}, f32[128,1024]{1,0:T(8,128)S(1)}, u32[]{:S(2)}) copy-start(f32[128,1024]{1,0:T(8,128)S(1)} %collective-permute-done.4.refs_6_) | copy-start | bytes 1572868
  45.1 15.5 %collective-permute-start.7 = (f32[128,1024]{1,0:T(8,128)S(1)}, f32[128,1024]{1,0:T(8,128)S(1)}, u32[]{:S(2)}, u32[]{:S(2)}) collective-permute-start(f32[128,1024]{1,0:T(8,128)S(1)} %collective-permute-done.4.refs_6_), channel_id=1, source_target_pairs={{0,1},{1,2},{2,3},{3,4},{4,5},{5,6},{6,7},{7,0},{8,15},{9,8},{10,9... | collective-permute-start | bytes 1572872 | tf_op jit(solution)/shard_map/ppermute | solution.py:193
  55.1 24.8 %copy-start.2 = (f32[128,1024]{1,0:T(8,128)}, f32[128,1024]{1,0:T(8,128)S(1)}, u32[]{:S(2)}) copy-start(f32[128,1024]{1,0:T(8,128)S(1)} %collective-permute-done.5.refs_7_) | copy-start | bytes 1572868
  55.1 12.3 %collective-permute-start.8 = (f32[128,1024]{1,0:T(8,128)S(1)}, f32[128,1024]{1,0:T(8,128)S(1)}, u32[]{:S(2)}, u32[]{:S(2)}) collective-permute-start(f32[128,1024]{1,0:T(8,128)S(1)} %collective-permute-done.5.refs_7_), channel_id=1, source_target_pairs={{0,1},{1,2},{2,3},{3,4},{4,5},{5,6},{6,7},{7,0},{8,15},{9,8},{10,9... | collective-permute-start | bytes 1572872 | tf_op jit(solution)/shard_map/ppermute | solution.py:193
  60.7 13.6 %copy-start.4 = (f32[128,1024]{1,0:T(8,128)}, f32[128,1024]{1,0:T(8,128)S(1)}, u32[]{:S(2)}) copy-start(f32[128,1024]{1,0:T(8,128)S(1)} %collective-permute-done.7.refs_9_) | copy-start | bytes 1572868
  60.7 12.3 %collective-permute-start.9 = (f32[128,1024]{1,0:T(8,128)S(1)}, f32[128,1024]{1,0:T(8,128)S(1)}, u32[]{:S(2)}, u32[]{:S(2)}) collective-permute-start(f32[128,1024]{1,0:T(8,128)S(1)} %collective-permute-done.7.refs_9_), channel_id=1, source_target_pairs={{0,1},{1,2},{2,3},{3,4},{4,5},{5,6},{6,7},{7,0},{8,15},{9,8},{10,9... | collective-permute-start | bytes 1572872 | tf_op jit(solution)/shard_map/ppermute | solution.py:193
  67.3 7.0 %copy-start.6 = (f32[128,1024]{1,0:T(8,128)}, f32[128,1024]{1,0:T(8,128)S(1)}, u32[]{:S(2)}) copy-start(f32[128,1024]{1,0:T(8,128)S(1)} %collective-permute-done.8.refs_10_) | copy-start | bytes 1572868
  74.3 12.9 %collective-permute-start.10 = (f32[384,1024]{1,0:T(8,128)}, f32[384,1024]{1,0:T(8,128)}, u32[]{:S(2)}, u32[]{:S(2)}) collective-permute-start(f32[384,1024]{1,0:T(8,128)} %pad_maximum_fusion), channel_id=1, source_target_pairs={{0,8},{8,0},{1,9},{9,1},{2,10},{10,2},{3,11},{11,3},{4,12},{12,4},... | collective-permute-start | bytes 4718600 | tf_op jit(solution)/shard_map/ppermute | solution.py:185
  77.4 9.8 %collective-permute-start.3 = (f32[256,1024]{1,0:T(8,128)}, f32[256,1024]{1,0:T(8,128)}, u32[]{:S(2)}, u32[]{:S(2)}) collective-permute-start(f32[256,1024]{1,0:T(8,128)} %pad_maximum_fusion.1), channel_id=1, source_target_pairs={{0,8},{8,0},{1,9},{9,1},{2,10},{10,2},{3,11},{11,3},{4,12},{12,4},... | collective-permute-start | bytes 3145736 | tf_op jit(solution)/shard_map/ppermute | solution.py:185
  80.9 6.3 %collective-permute-start.6 = (f32[256,1024]{1,0:T(8,128)}, f32[256,1024]{1,0:T(8,128)}, u32[]{:S(2)}, u32[]{:S(2)}) collective-permute-start(f32[256,1024]{1,0:T(8,128)} %pad_maximum_fusion.2), channel_id=1, source_target_pairs={{0,8},{8,0},{1,9},{9,1},{2,10},{10,2},{3,11},{11,3},{4,12},{12,4},... | collective-permute-start | bytes 3145736 | tf_op jit(solution)/shard_map/ppermute | solution.py:185
  82.8 4.4 %copy-start.1 = (f32[128,1024]{1,0:T(8,128)S(1)}, f32[128,1024]{1,0:T(8,128)}, u32[]{:S(2)}) copy-start(f32[128,1024]{1,0:T(8,128)} %copy-done) | copy-start | bytes 1572868
  82.8 4.4 %copy-start.3 = (f32[128,1024]{1,0:T(8,128)S(1)}, f32[128,1024]{1,0:T(8,128)}, u32[]{:S(2)}) copy-start(f32[128,1024]{1,0:T(8,128)} %copy-done.2) | copy-start | bytes 1572868
  82.9 4.4 %copy-start.5 = (f32[128,1024]{1,0:T(8,128)S(1)}, f32[128,1024]{1,0:T(8,128)}, u32[]{:S(2)}) copy-start(f32[128,1024]{1,0:T(8,128)} %copy-done.4) | copy-start | bytes 1572868
  82.9 4.4 %copy-start.7 = (f32[128,1024]{1,0:T(8,128)S(1)}, f32[128,1024]{1,0:T(8,128)}, u32[]{:S(2)}) copy-start(f32[128,1024]{1,0:T(8,128)} %copy-done.6) | copy-start | bytes 1572868
  92.8 18.2 %collective-permute-start.11 = (f32[128,1024]{1,0:T(8,128)S(1)}, f32[128,1024]{1,0:T(8,128)S(1)}, u32[]{:S(2)}, u32[]{:S(2)}) collective-permute-start(f32[128,1024]{1,0:T(8,128)S(1)} %get-tuple-element.20), channel_id=1, source_target_pairs={{0,256},{128,384},{256,0},{384,128},{1,257},{129,385},{257,1},{385... | collective-permute-start | bytes 1572872 | tf_op jit(solution)/shard_map/ppermute | solution.py:225
  98.0 23.8 %collective-permute-start.12 = (f32[128,1024]{1,0:T(8,128)S(1)}, f32[128,1024]{1,0:T(8,128)S(1)}, u32[]{:S(2)}, u32[]{:S(2)}) collective-permute-start(f32[128,1024]{1,0:T(8,128)S(1)} %get-tuple-element.21), channel_id=1, source_target_pairs={{0,128},{128,256},{256,384},{384,0},{1,129},{129,257},{257,385},{3... | collective-permute-start | bytes 1572872 | tf_op jit(solution)/shard_map/ppermute | solution.py:226
  103.9 18.2 %collective-permute-start.13 = (f32[128,1024]{1,0:T(8,128)S(1)}, f32[128,1024]{1,0:T(8,128)S(1)}, u32[]{:S(2)}, u32[]{:S(2)}) collective-permute-start(f32[128,1024]{1,0:T(8,128)S(1)} %get-tuple-element.28), channel_id=1, source_target_pairs={{0,384},{128,0},{256,128},{384,256},{1,385},{129,1},{257,129},{385... | collective-permute-start | bytes 1572872 | tf_op jit(solution)/shard_map/ppermute | solution.py:229
  (4 other events, 14.5 us)

commit v10 on v9

--- a/solution.py
+++ b/solution.py
@@ -198,14 +198,16 @@
     size = block.shape[0]
     mate = along_ring(block, cross=True)
     blocks = [block, partner, own, mate]
+    swaps = []
     for _ in range(n // 2 - 2):
-        blocks.append(swap_core(jnp.concatenate([own, mate], axis=0)))
+        swaps.append(swap_core(jnp.concatenate([own, mate], axis=0)))
         own, mate = along_ring(own), along_ring(mate)
-        blocks += [own, mate]
+        blocks += [swaps[-1], own, mate]
     far = along_ring(own)
+    held, *_ = lax.optimization_barrier((mate, swaps[0]))
     pieces = [(i, 0, each.shape[0]) for i, each in enumerate(blocks)]
     last = len(blocks)
-    blocks += [swap_core(jnp.concatenate([own, mate, far], axis=0)), far]
+    blocks += [swap_core(jnp.concatenate([own, held, far], axis=0)), far]
     return blocks, pieces + [(last, 0, 2 * size), (last + 1, 0, size), (last, 2 * size, size)]
 
 

time: 148 us -> 144 us (0.973)
  the two profiles are of different devices: /device:TPU:32 before, /device:TPU:2 now
where the time goes in v10:
time: 144 us
  starting transfers between devices  51.5 us (36%)
  waiting for transfers between devices  46.2 us (32%)
  blocking collectives  24.1 us (17%)
  Pallas kernels  17.1 us (12%)
  other arithmetic  3.36 us (2%)
    ppermute x7, waiting for transfers between devices, along_ring(): return lax.ppermute(block, ('core', 'grp'), pairs)  30.9 us
    all_to_all x1, blocking collectives, on_device(): return lax.all_to_all(part, 'z', 0, 0, tiled=True).sum(axis=0)  24.1 us
    ppermute x7, starting transfers between devices, along_ring(): return lax.ppermute(block, ('core', 'grp'), pairs)  16.6 us
    all_to_all x1, starting transfers between devices, on_device(): got = lax.all_to_all(sent, CHIPS, 0, 0, tiled=True)  13.5 us
    ppermute x4, starting transfers between devices, swap_core(): return lax.ppermute(block, 'core', [(0, 1), (1, 0)])  11.5 us
    ppermute x1, waiting for transfers between devices, on_device(): near = lax.ppermute(near, 'x', shift_x(1))  10.3 us
    pallas_call x2, Pallas kernels, product(): pl.pallas_call(lambda *refs: product_kernel(pair, pieces, *refs), out_sha...  8.6 us
    ppermute x1, waiting for transfers between devices, on_device(): far = lax.ppermute(far, 'x', shift_x(2))  4.94 us
  transfers between devices with their start and end apart: 15, of which 8 were waited for; matrix products, arithmetic and copies ran while one was open for 2% of the time, Pallas kernels for 8%

profile of v10, /device:TPU:2, one launch (start us, length us, event | category | flops | bytes accessed | tf_op | source)
XLA Modules:
  0.0 143.6 jit_solution(18228701433172922800)
XLA Ops:
  1.9 3.5 %collective-permute-start = (f32[128,1024]{1,0:T(8,128)}, f32[128,1024]{1,0:T(8,128)S(1)}, u32[]{:S(2)}, u32[]{:S(2)}) collective-permute-start(f32[128,1024]{1,0:T(8,128)} %refs_1_.1), channel_id=1, source_target_pairs={{0,1},{1,2},{2,3},{3,4},{4,5},{5,6},{6,7},{7,0},{8,15},{9,8},{10,9... | collective-permute-start | bytes 1572872 | tf_op jit(solution)/shard_map/ppermute | solution.py:193
  5.4 4.2 %pack.1 = f32[32,136,128]{2,1,0:T(8,128)} custom-call(s32[128]{0:T(128)} %bitcast.5, s32[512]{0:T(512)} %place_ref.1, f32[128,16,128]{2,1,0:T(8,128)} %bitcast.4), custom_call_target="tpu_custom_call" | custom-call | bytes 8388608 | tf_op jit(solution)/shard_map/pack/pallas_call | solution.py:63
  9.6 5.0 %collective-permute-done.refs_3_ = f32[128,1024]{1,0:T(8,128)S(1)} collective-permute-done((f32[128,1024]{1,0:T(8,128)}, f32[128,1024]{1,0:T(8,128)S(1)}, u32[]{:S(2)}, u32[]{:S(2)}) %collective-permute-start) | collective-permute-done | bytes 524320 | tf_op jit(solution)/shard_map/ppermute | solution.py:193
  14.7 13.5 %all-to-all-start = ((f32[32,136,128]{2,1,0:T(8,128)}), f32[32,136,128]{2,1,0:T(8,128)S(1)}, u32[]{:S(2)}, u32[]{:S(2)}) async-start(f32[32,136,128]{2,1,0:T(8,128)} %pack.1), calls=%async_computation | async-start | bytes 4456448 | tf_op jit(solution)/shard_map/all_to_all | solution.py:223
  28.1 3.5 %collective-permute-start.2 = (f32[128,1024]{1,0:T(8,128)}, f32[128,1024]{1,0:T(8,128)S(1)}, u32[]{:S(2)}, u32[]{:S(2)}) collective-permute-start(f32[128,1024]{1,0:T(8,128)} %refs_1_.1), channel_id=1, source_target_pairs={{8,1},{9,2},{10,3},{11,4},{12,5},{13,6},{14,7},{15,0},{0,15},{1,8}... | collective-permute-start | bytes 1572872 | tf_op jit(solution)/shard_map/ppermute | solution.py:193
  31.7 1.9 %collective-permute-start.4 = (f32[128,1024]{1,0:T(8,128)S(1)}, f32[128,1024]{1,0:T(8,128)S(1)}, u32[]{:S(2)}, u32[]{:S(2)}) collective-permute-start(f32[128,1024]{1,0:T(8,128)S(1)} %collective-permute-done.refs_3_), channel_id=1, source_target_pairs={{0,1},{1,2},{2,3},{3,4},{4,5},{5,6},{6,7},{7,0},{8,15},{9,8},{10,9... | collective-permute-start | bytes 1572872 | tf_op jit(solution)/shard_map/ppermute | solution.py:193
  33.6 8.1 %collective-permute-done.2.refs_4_ = f32[128,1024]{1,0:T(8,128)S(1)} collective-permute-done((f32[128,1024]{1,0:T(8,128)}, f32[128,1024]{1,0:T(8,128)S(1)}, u32[]{:S(2)}, u32[]{:S(2)}) %collective-permute-start.2) | collective-permute-done | bytes 524320 | tf_op jit(solution)/shard_map/ppermute | solution.py:193
  43.8 5.3 %collective-permute-start.3 = (f32[256,1024]{1,0:T(8,128)S(1)}, f32[256,1024]{1,0:T(8,128)S(1)}, u32[]{:S(2)}, u32[]{:S(2)}) collective-permute-start(f32[256,1024]{1,0:T(8,128)S(1)} %pad_maximum_fusion.1), channel_id=1, source_target_pairs={{0,8},{8,0},{1,9},{9,1},{2,10},{10,2},{3,11},{11,3},{4,12},{12,4},... | collective-permute-start | bytes 3145736 | tf_op jit(solution)/shard_map/ppermute | solution.py:185
  49.1 1.9 %collective-permute-start.7 = (f32[128,1024]{1,0:T(8,128)S(1)}, f32[128,1024]{1,0:T(8,128)S(1)}, u32[]{:S(2)}, u32[]{:S(2)}) collective-permute-start(f32[128,1024]{1,0:T(8,128)S(1)} %collective-permute-done.4.refs_6_), channel_id=1, source_target_pairs={{0,1},{1,2},{2,3},{3,4},{4,5},{5,6},{6,7},{7,0},{8,15},{9,8},{10,9... | collective-permute-start | bytes 1572872 | tf_op jit(solution)/shard_map/ppermute | solution.py:193
  51.0 3.0 %collective-permute-done.5.refs_7_ = f32[128,1024]{1,0:T(8,128)S(1)} collective-permute-done((f32[128,1024]{1,0:T(8,128)S(1)}, f32[128,1024]{1,0:T(8,128)S(1)}, u32[]{:S(2)}, u32[]{:S(2)}) %collective-permute-start.5) | collective-permute-done | bytes 524320 | tf_op jit(solution)/shard_map/ppermute | solution.py:193
  55.9 5.5 %collective-permute-done.7.refs_9_ = f32[128,1024]{1,0:T(8,128)S(1)} collective-permute-done((f32[128,1024]{1,0:T(8,128)S(1)}, f32[128,1024]{1,0:T(8,128)S(1)}, u32[]{:S(2)}, u32[]{:S(2)}) %collective-permute-start.7) | collective-permute-done | bytes 524320 | tf_op jit(solution)/shard_map/ppermute | solution.py:193
  63.3 3.7 %collective-permute-done.8.refs_10_ = f32[128,1024]{1,0:T(8,128)S(1)} collective-permute-done((f32[128,1024]{1,0:T(8,128)S(1)}, f32[128,1024]{1,0:T(8,128)S(1)}, u32[]{:S(2)}, u32[]{:S(2)}) %collective-permute-start.8) | collective-permute-done | bytes 524320 | tf_op jit(solution)/shard_map/ppermute | solution.py:193
  68.0 5.6 %collective-permute-done.9.refs_12_ = f32[128,1024]{1,0:T(8,128)S(1)} collective-permute-done((f32[128,1024]{1,0:T(8,128)S(1)}, f32[128,1024]{1,0:T(8,128)S(1)}, u32[]{:S(2)}, u32[]{:S(2)}) %collective-permute-start.9) | collective-permute-done | bytes 524320 | tf_op jit(solution)/shard_map/ppermute | solution.py:193
  75.0 1.9 %collective-permute-start.10 = (f32[384,1024]{1,0:T(8,128)}, f32[384,1024]{1,0:T(8,128)}, u32[]{:S(2)}, u32[]{:S(2)}) collective-permute-start(f32[384,1024]{1,0:T(8,128)} %pad_maximum_fusion), channel_id=1, source_target_pairs={{0,8},{8,0},{1,9},{9,1},{2,10},{10,2},{3,11},{11,3},{4,12},{12,4},... | collective-permute-start | bytes 4718600 | tf_op jit(solution)/shard_map/ppermute | solution.py:185
  78.1 2.4 %collective-permute-start.6 = (f32[256,1024]{1,0:T(8,128)}, f32[256,1024]{1,0:T(8,128)}, u32[]{:S(2)}, u32[]{:S(2)}) collective-permute-start(f32[256,1024]{1,0:T(8,128)} %pad_maximum_fusion.2), channel_id=1, source_target_pairs={{0,8},{8,0},{1,9},{9,1},{2,10},{10,2},{3,11},{11,3},{4,12},{12,4},... | collective-permute-start | bytes 3145736 | tf_op jit(solution)/shard_map/ppermute | solution.py:185
  80.6 4.3 %spread.1.refs_0_ = bf16[1024,2176]{1,0:T(8,128)(2,1)S(1)} custom-call(f32[32,136,128]{2,1,0:T(8,128)S(1)} %all-to-all-done.got_ref), custom_call_target="tpu_custom_call" | custom-call | bytes 8388608 | tf_op jit(solution)/shard_map/spread/pallas_call | solution.py:119
  85.0 5.2 %product.2 = (f32[128,1024]{1,0:T(8,128)S(1)}, f32[128,1024]{1,0:T(8,128)S(1)}, bf16[2048,1024]{1,0:T(8,128)(2,1)S(1)}, bf16[2048,1024]{1,0:T(8,128)(2,1)S(1)}) custom-call(bf16[1024,2176]{1,0:T(8,128)(2,1)S(1)} %spread.1.refs_0_, f32[128,1024]{1,0:T(8,128)S(1)} %copy-done.12, f32[128,1024]{1,0:T(8,128)S(1)} %copy-done.14, ...), custom_call_target="tpu_custom_call" | custom-call | flops 3221225472 | bytes 4194304 | tf_op jit(solution)/shard_map/product/pallas_call | solution.py:167
  90.2 4.0 %collective-permute-start.11 = (f32[128,1024]{1,0:T(8,128)S(1)}, f32[128,1024]{1,0:T(8,128)S(1)}, u32[]{:S(2)}, u32[]{:S(2)}) collective-permute-start(f32[128,1024]{1,0:T(8,128)S(1)} %get-tuple-element.22), channel_id=1, source_target_pairs={{0,256},{128,384},{256,0},{384,128},{1,257},{129,385},{257,1},{385... | collective-permute-start | bytes 1572872 | tf_op jit(solution)/shard_map/ppermute | solution.py:227
  94.2 2.1 %collective-permute-start.12 = (f32[128,1024]{1,0:T(8,128)S(1)}, f32[128,1024]{1,0:T(8,128)S(1)}, u32[]{:S(2)}, u32[]{:S(2)}) collective-permute-start(f32[128,1024]{1,0:T(8,128)S(1)} %get-tuple-element.23), channel_id=1, source_target_pairs={{0,128},{128,256},{256,384},{384,0},{1,129},{129,257},{257,385},{3... | collective-permute-start | bytes 1572872 | tf_op jit(solution)/shard_map/ppermute | solution.py:228
  96.3 3.4 %product.3 = (f32[128,1024]{1,0:T(8,128)S(1)}, f32[128,1024]{1,0:T(8,128)S(1)}) custom-call(bf16[1024,2176]{1,0:T(8,128)(2,1)S(1)} %spread.1.refs_0_, bf16[2048,1024]{1,0:T(8,128)(2,1)S(1)} %get-tuple-element.24.refs_1_, bf16[2048,1024]{1,0:T(8,128)(2,1)S(1)} %get-tuple-element.25.refs_2_), custom_call_target="tpu_custom_call" | custom-call | flops 3221225472 | bytes 4194304 | tf_op jit(solution)/shard_map/product/pallas_call | solution.py:167
  99.7 3.8 %collective-permute-start.13 = (f32[128,1024]{1,0:T(8,128)S(1)}, f32[128,1024]{1,0:T(8,128)S(1)}, u32[]{:S(2)}, u32[]{:S(2)}) collective-permute-start(f32[128,1024]{1,0:T(8,128)S(1)} %get-tuple-element.30), channel_id=1, source_target_pairs={{0,384},{128,0},{256,128},{384,256},{1,385},{129,1},{257,129},{385... | collective-permute-start | bytes 1572872 | tf_op jit(solution)/shard_map/ppermute | solution.py:231
  103.5 4.9 %collective-permute-done.11 = f32[128,1024]{1,0:T(8,128)S(1)} collective-permute-done((f32[128,1024]{1,0:T(8,128)S(1)}, f32[128,1024]{1,0:T(8,128)S(1)}, u32[]{:S(2)}, u32[]{:S(2)}) %collective-permute-start.11) | collective-permute-done | bytes 524320 | tf_op jit(solution)/shard_map/ppermute | solution.py:227
  108.4 10.3 %collective-permute-done.12 = f32[128,1024]{1,0:T(8,128)S(1)} collective-permute-done((f32[128,1024]{1,0:T(8,128)S(1)}, f32[128,1024]{1,0:T(8,128)S(1)}, u32[]{:S(2)}, u32[]{:S(2)}) %collective-permute-start.12) | collective-permute-done | bytes 524320 | tf_op jit(solution)/shard_map/ppermute | solution.py:228
  118.8 24.1 %all_to_all.10 = f32[8,16,1024]{2,1,0:T(8,128)S(1)} all-to-all(f32[8,16,1024]{2,1,0:T(8,128)S(1)} %bitcast.3), channel_id=1, replica_groups=mesh['x'=4,'z'=8,'core'=2,'grp'=8] {'z'}, dimensions={0} | all-to-all | bytes 1048576 | tf_op jit(solution)/shard_map/all_to_all | solution.py:234
  (46 shorter events, 12.1 us)
Async XLA Ops:
  0.0 9.6 %collective-permute-start.1 = (f32[128,1024]{1,0:T(8,128)}, f32[128,1024]{1,0:T(8,128)S(1)}, u32[]{:S(2)}, u32[]{:S(2)}) collective-permute-start(f32[128,1024]{1,0:T(8,128)} %refs_1_.1), channel_id=1, source_target_pairs={{0,8},{8,0},{1,9},{9,1},{2,10},{10,2},{3,11},{11,3},{4,12},{12,4},... | collective-permute-start | bytes 1572872 | tf_op jit(solution)/shard_map/ppermute | solution.py:185
  1.9 12.7 %collective-permute-start = (f32[128,1024]{1,0:T(8,128)}, f32[128,1024]{1,0:T(8,128)S(1)}, u32[]{:S(2)}, u32[]{:S(2)}) collective-permute-start(f32[128,1024]{1,0:T(8,128)} %refs_1_.1), channel_id=1, source_target_pairs={{0,1},{1,2},{2,3},{3,4},{4,5},{5,6},{6,7},{7,0},{8,15},{9,8},{10,9... | collective-permute-start | bytes 1572872 | tf_op jit(solution)/shard_map/ppermute | solution.py:193
  9.6 5.0 %copy-start.13 = (f32[128,1024]{1,0:T(8,128)}, f32[128,1024]{1,0:T(8,128)S(1)}, u32[]{:S(2)}) copy-start(f32[128,1024]{1,0:T(8,128)S(1)} %collective-permute-done.1.refs_2_) | copy-start | bytes 1572868
  14.7 65.8 %all-to-all-start = ((f32[32,136,128]{2,1,0:T(8,128)}), f32[32,136,128]{2,1,0:T(8,128)S(1)}, u32[]{:S(2)}, u32[]{:S(2)}) async-start(f32[32,136,128]{2,1,0:T(8,128)} %pack.1), calls=%async_computation | async-start | bytes 4456448 | tf_op jit(solution)/shard_map/all_to_all | solution.py:223
  28.1 13.6 %collective-permute-start.2 = (f32[128,1024]{1,0:T(8,128)}, f32[128,1024]{1,0:T(8,128)S(1)}, u32[]{:S(2)}, u32[]{:S(2)}) collective-permute-start(f32[128,1024]{1,0:T(8,128)} %refs_1_.1), channel_id=1, source_target_pairs={{8,1},{9,2},{10,3},{11,4},{12,5},{13,6},{14,7},{15,0},{0,15},{1,8}... | collective-permute-start | bytes 1572872 | tf_op jit(solution)/shard_map/ppermute | solution.py:193
  31.7 17.4 %collective-permute-start.4 = (f32[128,1024]{1,0:T(8,128)S(1)}, f32[128,1024]{1,0:T(8,128)S(1)}, u32[]{:S(2)}, u32[]{:S(2)}) collective-permute-start(f32[128,1024]{1,0:T(8,128)S(1)} %collective-permute-done.refs_3_), channel_id=1, source_target_pairs={{0,1},{1,2},{2,3},{3,4},{4,5},{5,6},{6,7},{7,0},{8,15},{9,8},{10,9... | collective-permute-start | bytes 1572872 | tf_op jit(solution)/shard_map/ppermute | solution.py:193
  41.7 12.3 %collective-permute-start.5 = (f32[128,1024]{1,0:T(8,128)S(1)}, f32[128,1024]{1,0:T(8,128)S(1)}, u32[]{:S(2)}, u32[]{:S(2)}) collective-permute-start(f32[128,1024]{1,0:T(8,128)S(1)} %collective-permute-done.2.refs_4_), channel_id=1, source_target_pairs={{0,1},{1,2},{2,3},{3,4},{4,5},{5,6},{6,7},{7,0},{8,15},{9,8},{10,9... | collective-permute-start | bytes 1572872 | tf_op jit(solution)/shard_map/ppermute | solution.py:193
  43.8 23.3 %collective-permute-start.3 = (f32[256,1024]{1,0:T(8,128)S(1)}, f32[256,1024]{1,0:T(8,128)S(1)}, u32[]{:S(2)}, u32[]{:S(2)}) collective-permute-start(f32[256,1024]{1,0:T(8,128)S(1)} %pad_maximum_fusion.1), channel_id=1, source_target_pairs={{0,8},{8,0},{1,9},{9,1},{2,10},{10,2},{3,11},{11,3},{4,12},{12,4},... | collective-permute-start | bytes 3145736 | tf_op jit(solution)/shard_map/ppermute | solution.py:185
  49.1 27.8 %copy-start = (f32[128,1024]{1,0:T(8,128)}, f32[128,1024]{1,0:T(8,128)S(1)}, u32[]{:S(2)}) copy-start(f32[128,1024]{1,0:T(8,128)S(1)} %collective-permute-done.4.refs_6_) | copy-start | bytes 1572868
  49.1 12.3 %collective-permute-start.7 = (f32[128,1024]{1,0:T(8,128)S(1)}, f32[128,1024]{1,0:T(8,128)S(1)}, u32[]{:S(2)}, u32[]{:S(2)}) collective-permute-start(f32[128,1024]{1,0:T(8,128)S(1)} %collective-permute-done.4.refs_6_), channel_id=1, source_target_pairs={{0,1},{1,2},{2,3},{3,4},{4,5},{5,6},{6,7},{7,0},{8,15},{9,8},{10,9... | collective-permute-start | bytes 1572872 | tf_op jit(solution)/shard_map/ppermute | solution.py:193
  54.0 22.9 %copy-start.2 = (f32[128,1024]{1,0:T(8,128)}, f32[128,1024]{1,0:T(8,128)S(1)}, u32[]{:S(2)}) copy-start(f32[128,1024]{1,0:T(8,128)S(1)} %collective-permute-done.5.refs_7_) | copy-start | bytes 1572868
  54.0 13.0 %collective-permute-start.8 = (f32[128,1024]{1,0:T(8,128)S(1)}, f32[128,1024]{1,0:T(8,128)S(1)}, u32[]{:S(2)}, u32[]{:S(2)}) collective-permute-start(f32[128,1024]{1,0:T(8,128)S(1)} %collective-permute-done.5.refs_7_), channel_id=1, source_target_pairs={{0,1},{1,2},{2,3},{3,4},{4,5},{5,6},{6,7},{7,0},{8,15},{9,8},{10,9... | collective-permute-start | bytes 1572872 | tf_op jit(solution)/shard_map/ppermute | solution.py:193
  61.4 13.6 %copy-start.4 = (f32[128,1024]{1,0:T(8,128)}, f32[128,1024]{1,0:T(8,128)S(1)}, u32[]{:S(2)}) copy-start(f32[128,1024]{1,0:T(8,128)S(1)} %collective-permute-done.7.refs_9_) | copy-start | bytes 1572868
  61.4 12.3 %collective-permute-start.9 = (f32[128,1024]{1,0:T(8,128)S(1)}, f32[128,1024]{1,0:T(8,128)S(1)}, u32[]{:S(2)}, u32[]{:S(2)}) collective-permute-start(f32[128,1024]{1,0:T(8,128)S(1)} %collective-permute-done.7.refs_9_), channel_id=1, source_target_pairs={{0,1},{1,2},{2,3},{3,4},{4,5},{5,6},{6,7},{7,0},{8,15},{9,8},{10,9... | collective-permute-start | bytes 1572872 | tf_op jit(solution)/shard_map/ppermute | solution.py:193
  67.0 8.0 %copy-start.6 = (f32[128,1024]{1,0:T(8,128)}, f32[128,1024]{1,0:T(8,128)S(1)}, u32[]{:S(2)}) copy-start(f32[128,1024]{1,0:T(8,128)S(1)} %collective-permute-done.8.refs_10_) | copy-start | bytes 1572868
  75.0 9.9 %collective-permute-start.10 = (f32[384,1024]{1,0:T(8,128)}, f32[384,1024]{1,0:T(8,128)}, u32[]{:S(2)}, u32[]{:S(2)}) collective-permute-start(f32[384,1024]{1,0:T(8,128)} %pad_maximum_fusion), channel_id=1, source_target_pairs={{0,8},{8,0},{1,9},{9,1},{2,10},{10,2},{3,11},{11,3},{4,12},{12,4},... | collective-permute-start | bytes 4718600 | tf_op jit(solution)/shard_map/ppermute | solution.py:185
  78.1 6.8 %collective-permute-start.6 = (f32[256,1024]{1,0:T(8,128)}, f32[256,1024]{1,0:T(8,128)}, u32[]{:S(2)}, u32[]{:S(2)}) collective-permute-start(f32[256,1024]{1,0:T(8,128)} %pad_maximum_fusion.2), channel_id=1, source_target_pairs={{0,8},{8,0},{1,9},{9,1},{2,10},{10,2},{3,11},{11,3},{4,12},{12,4},... | collective-permute-start | bytes 3145736 | tf_op jit(solution)/shard_map/ppermute | solution.py:185
  80.5 4.4 %copy-start.1 = (f32[128,1024]{1,0:T(8,128)S(1)}, f32[128,1024]{1,0:T(8,128)}, u32[]{:S(2)}) copy-start(f32[128,1024]{1,0:T(8,128)} %copy-done) | copy-start | bytes 1572868
  80.5 4.4 %copy-start.3 = (f32[128,1024]{1,0:T(8,128)S(1)}, f32[128,1024]{1,0:T(8,128)}, u32[]{:S(2)}) copy-start(f32[128,1024]{1,0:T(8,128)} %copy-done.2) | copy-start | bytes 1572868
  80.5 4.4 %copy-start.5 = (f32[128,1024]{1,0:T(8,128)S(1)}, f32[128,1024]{1,0:T(8,128)}, u32[]{:S(2)}) copy-start(f32[128,1024]{1,0:T(8,128)} %copy-done.4) | copy-start | bytes 1572868
  80.5 4.4 %copy-start.7 = (f32[128,1024]{1,0:T(8,128)S(1)}, f32[128,1024]{1,0:T(8,128)}, u32[]{:S(2)}) copy-start(f32[128,1024]{1,0:T(8,128)} %copy-done.6) | copy-start | bytes 1572868
  90.2 18.2 %collective-permute-start.11 = (f32[128,1024]{1,0:T(8,128)S(1)}, f32[128,1024]{1,0:T(8,128)S(1)}, u32[]{:S(2)}, u32[]{:S(2)}) collective-permute-start(f32[128,1024]{1,0:T(8,128)S(1)} %get-tuple-element.22), channel_id=1, source_target_pairs={{0,256},{128,384},{256,0},{384,128},{1,257},{129,385},{257,1},{385... | collective-permute-start | bytes 1572872 | tf_op jit(solution)/shard_map/ppermute | solution.py:227
  94.2 24.5 %collective-permute-start.12 = (f32[128,1024]{1,0:T(8,128)S(1)}, f32[128,1024]{1,0:T(8,128)S(1)}, u32[]{:S(2)}, u32[]{:S(2)}) collective-permute-start(f32[128,1024]{1,0:T(8,128)S(1)} %get-tuple-element.23), channel_id=1, source_target_pairs={{0,128},{128,256},{256,384},{384,0},{1,129},{129,257},{257,385},{3... | collective-permute-start | bytes 1572872 | tf_op jit(solution)/shard_map/ppermute | solution.py:228
  99.7 19.0 %collective-permute-start.13 = (f32[128,1024]{1,0:T(8,128)S(1)}, f32[128,1024]{1,0:T(8,128)S(1)}, u32[]{:S(2)}, u32[]{:S(2)}) collective-permute-start(f32[128,1024]{1,0:T(8,128)S(1)} %get-tuple-element.30), channel_id=1, source_target_pairs={{0,384},{128,0},{256,128},{384,256},{1,385},{129,1},{257,129},{385... | collective-permute-start | bytes 1572872 | tf_op jit(solution)/shard_map/ppermute | solution.py:231
  (6 other events, 19.9 us)

commit v11 on v10

--- a/solution.py
+++ b/solution.py
@@ -132,45 +132,46 @@
     )(got)
 
 
-def product_kernel(pair, pieces, *refs):
-    left_ref, refs = refs[0], refs[1:]
-    if pieces:
-        panel, (first_ref, second_ref, v_high, v_low) = refs[:-4], refs[-4:]
-        at = 0
-        for block, start, size in pieces:
-            for i in range(0, size, 64):
-                value = panel[block][start + i : start + i + 64, :]
-                v_high[at : at + 64, :], v_low[at : at + 64, :] = split(value)
-                at += 64
-    else:
-        v_high, v_low, first_ref, second_ref = refs
-    height = first_ref.shape[0]
+def product_kernel(first, pieces, *refs):
+    left_ref, panel = refs[0], refs[1 : -NX - 2]
+    out_refs, (v_high, v_low) = refs[-NX - 2 : -2], refs[-2:]
+    height, wide_cols = out_refs[0].shape
     depth = v_high.shape[0]
-    base = pair * 4 * height
+    at = 0
+    for block, start, size in pieces:
+        for i in range(0, size, 64):
+            value = panel[block][start + i : start + i + 64, first : first + wide_cols]
+            v_high[at : at + 64, :], v_low[at : at + 64, :] = split(value)
+            at += 64
     dot = lambda a, b: jnp.dot(a, b, preferred_element_type=jnp.float32)
     wide = 256
-    for i in range(0, first_ref.shape[1], wide):
+    for i in range(0, wide_cols, wide):
         cols = pl.ds(i, wide)
-        four = dot(left_ref[base : base + 4 * height, :depth], v_high[:, cols])
-        two = dot(left_ref[base + height : base + 3 * height, :depth], v_low[:, cols])
-        first_ref[:, cols] = four[height : 2 * height] + (four[:height] + two[:height])
-        second_ref[:, cols] = four[2 * height : 3 * height] + (four[3 * height :] + two[height:])
-
-
-def product(left, pair, blocks, pieces=()):
+        for pair in range(NX // 2):
+            base = pair * 4 * height
+            four = dot(left_ref[base : base + 4 * height, :depth], v_high[:, cols])
+            two = dot(left_ref[base + height : base + 3 * height, :depth], v_low[:, cols])
+            odd, even = 2 * pair + 1, (2 * pair + 2) % NX
+            out_refs[odd][:, cols] = four[height : 2 * height] + (four[:height] + two[:height])
+            out_refs[even][:, cols] = four[2 * height : 3 * height] + (
+                four[3 * height :] + two[height:]
+            )
+
+
+def product(left, first, cols, blocks, pieces):
     height = left.shape[0] // (2 * NX)
-    cols = blocks[0].shape[1]
     depth = left.shape[1] - LANES
-    part = jax.ShapeDtypeStruct((height, cols), jnp.float32)
-    half = jax.ShapeDtypeStruct((depth, cols), jnp.bfloat16)
-    outs = (part, part, half, half) if pieces else (part, part)
     return pl.pallas_call(
-        lambda *refs: product_kernel(pair, pieces, *refs),
-        out_shape=outs,
+        lambda *refs: product_kernel(first, pieces, *refs),
+        out_shape=(jax.ShapeDtypeStruct((height, cols), jnp.float32),) * NX,
         in_specs=[VMEM] * (1 + len(blocks)),
-        out_specs=(VMEM,) * len(outs),
+        out_specs=(VMEM,) * NX,
+        scratch_shapes=[
+            pltpu.VMEM((depth, cols), jnp.bfloat16),
+            pltpu.VMEM((depth, cols), jnp.bfloat16),
+        ],
         cost_estimate=pl.CostEstimate(
-            flops=12 * height * depth * cols, bytes_accessed=4 << 20, transcendentals=0
+            flops=6 * NX * height * depth * cols, bytes_accessed=4 << 20, transcendentals=0
         ),
         compiler_params=pltpu.CompilerParams(vmem_limit_bytes=PRODUCT_LIMIT),
         name="product",
@@ -205,9 +206,10 @@
         blocks += [swaps[-1], own, mate]
     far = along_ring(own)
     held, *_ = lax.optimization_barrier((mate, swaps[0]))
+    held_far, *_ = lax.optimization_barrier((far, swaps[1]))
     pieces = [(i, 0, each.shape[0]) for i, each in enumerate(blocks)]
     last = len(blocks)
-    blocks += [swap_core(jnp.concatenate([own, held, far], axis=0)), far]
+    blocks += [swap_core(jnp.concatenate([own, held, held_far], axis=0)), far]
     return blocks, pieces + [(last, 0, 2 * size), (last + 1, 0, size), (last, 2 * size, size)]
 
 
@@ -223,15 +225,20 @@
     got = lax.all_to_all(sent, CHIPS, 0, 0, tiled=True)
     blocks, pieces = gather_panel(integrals, partner, first)
     left = spread(got, rows, per_chip * width)
-    near, far, high, low = product(left, 0, blocks, pieces)
-    far = lax.ppermute(far, "x", shift_x(2))
-    near = lax.ppermute(near, "x", shift_x(1))
-    back, part = product(left, 1, [high, low])
-    far, near, part = lax.optimization_barrier((far, near, part))
-    back = lax.ppermute(back, "x", shift_x(-1))
-    part = part + near + far + back
-    part = part.reshape(NZ, rows, cols)
-    return lax.all_to_all(part, "z", 0, 0, tiled=True).sum(axis=0)
+    wide = cols // 2
+    send = lambda parts: [lax.ppermute(parts[i], "x", shift_x(i)) for i in (2, 1, 3)]
+    one = product(left, 0, wide, blocks, pieces)
+    got_one = send(one)
+    two = product(left, wide, wide, blocks, pieces)
+    got_one, held = lax.optimization_barrier((got_one, two[0]))
+    got_two = send(two)
+    over_z = lambda part: lax.all_to_all(
+        part.reshape(NZ, rows, wide), "z", 0, 0, tiled=True
+    )
+    left_half = over_z(one[0] + got_one[0] + got_one[1] + got_one[2])
+    got_two, left_half = lax.optimization_barrier((got_two, left_half))
+    right_half = over_z(held + got_two[0] + got_two[1] + got_two[2])
+    return jnp.concatenate([left_half.sum(axis=0), right_half.sum(axis=0)], axis=1)
 
 
 def solution(mesh):

time: 144 us -> 157 us (1.090)
  the two profiles are of different devices: /device:TPU:2 before, /device:TPU:36 now
where the time goes in v11:
time: 157 us; the launch traced here: 156 us
  starting transfers between devices  66.4 us (42%)
  waiting for transfers between devices  64.4 us (41%)
  Pallas kernels  18.1 us (12%)
  other arithmetic  3.73 us (2%)
  local copies, waits for them, and re-layouts  2.91 us (2%)
    ppermute x7, waiting for transfers between devices, along_ring(): return lax.ppermute(block, ('core', 'grp'), pairs)  40.2 us
    ppermute x6, starting transfers between devices, on_device(): lax.ppermute(parts[i], 'x', shift_x(i))  17.6 us
    ppermute x7, starting transfers between devices, along_ring(): return lax.ppermute(block, ('core', 'grp'), pairs)  14.1 us
    all_to_all x2, starting transfers between devices, on_device(): lax.all_to_all(part.reshape(NZ, rows, wide), 'z', 0, 0, tiled=True)  13.6 us
    all_to_all x1, starting transfers between devices, on_device(): got = lax.all_to_all(sent, CHIPS, 0, 0, tiled=True)  13.4 us
    ppermute x6, waiting for transfers between devices, on_device(): lax.ppermute(parts[i], 'x', shift_x(i))  12.2 us
    all_to_all x2, waiting for transfers between devices, on_device(): lax.all_to_all(part.reshape(NZ, rows, wide), 'z', 0, 0, tiled=True)  12 us
    pallas_call x2, Pallas kernels, product(): pl.pallas_call(lambda *refs: product_kernel(first, pieces, *refs), out_sh...  9.61 us
  transfers between devices with their start and end apart: 20, of which 10 were waited for; matrix products, arithmetic and copies ran while one was open for 1% of the time, Pallas kernels for 9%

profile of v11, /device:TPU:36, one launch (start us, length us, event | category | flops | bytes accessed | tf_op | source)
XLA Modules:
  0.0 156.0 jit_solution(17219735876595563020)
XLA Ops:
  0.0 2.6 %collective-permute-start = (f32[128,1024]{1,0:T(8,128)}, f32[128,1024]{1,0:T(8,128)S(1)}, u32[]{:S(2)}, u32[]{:S(2)}) collective-permute-start(f32[128,1024]{1,0:T(8,128)} %refs_1_.3), channel_id=1, source_target_pairs={{0,1},{1,2},{2,3},{3,4},{4,5},{5,6},{6,7},{7,0},{8,15},{9,8},{10,9... | collective-permute-start | bytes 1572872 | tf_op jit(solution)/shard_map/ppermute | solution.py:194
  4.5 4.2 %pack.1 = f32[32,136,128]{2,1,0:T(8,128)} custom-call(s32[128]{0:T(128)} %bitcast.5, s32[512]{0:T(512)} %place_ref.1, f32[128,16,128]{2,1,0:T(8,128)} %bitcast.4), custom_call_target="tpu_custom_call" | custom-call | bytes 8388608 | tf_op jit(solution)/shard_map/pack/pallas_call | solution.py:63
  8.7 3.8 %collective-permute-done.refs_3_ = f32[128,1024]{1,0:T(8,128)S(1)} collective-permute-done((f32[128,1024]{1,0:T(8,128)}, f32[128,1024]{1,0:T(8,128)S(1)}, u32[]{:S(2)}, u32[]{:S(2)}) %collective-permute-start) | collective-permute-done | bytes 524320 | tf_op jit(solution)/shard_map/ppermute | solution.py:194
  13.3 13.4 %all-to-all-start = ((f32[32,136,128]{2,1,0:T(8,128)}), f32[32,136,128]{2,1,0:T(8,128)S(1)}, u32[]{:S(2)}, u32[]{:S(2)}) async-start(f32[32,136,128]{2,1,0:T(8,128)} %pack.1), calls=%async_computation | async-start | bytes 4456448 | tf_op jit(solution)/shard_map/all_to_all | solution.py:225
  30.6 11.3 %collective-permute-done.2.refs_4_ = f32[128,1024]{1,0:T(8,128)S(1)} collective-permute-done((f32[128,1024]{1,0:T(8,128)}, f32[128,1024]{1,0:T(8,128)S(1)}, u32[]{:S(2)}, u32[]{:S(2)}) %collective-permute-start.2) | collective-permute-done | bytes 524320 | tf_op jit(solution)/shard_map/ppermute | solution.py:194
  45.9 8.3 %collective-permute-done.5.refs_7_ = f32[128,1024]{1,0:T(8,128)S(1)} collective-permute-done((f32[128,1024]{1,0:T(8,128)S(1)}, f32[128,1024]{1,0:T(8,128)S(1)}, u32[]{:S(2)}, u32[]{:S(2)}) %collective-permute-start.5) | collective-permute-done | bytes 524320 | tf_op jit(solution)/shard_map/ppermute | solution.py:194
  60.1 8.4 %collective-permute-done.7.refs_9_ = f32[128,1024]{1,0:T(8,128)S(1)} collective-permute-done((f32[128,1024]{1,0:T(8,128)S(1)}, f32[128,1024]{1,0:T(8,128)S(1)}, u32[]{:S(2)}, u32[]{:S(2)}) %collective-permute-start.7) | collective-permute-done | bytes 524320 | tf_op jit(solution)/shard_map/ppermute | solution.py:194
  71.5 2.7 %collective-permute-done.8.refs_10_ = f32[128,1024]{1,0:T(8,128)S(1)} collective-permute-done((f32[128,1024]{1,0:T(8,128)S(1)}, f32[128,1024]{1,0:T(8,128)S(1)}, u32[]{:S(2)}, u32[]{:S(2)}) %collective-permute-start.8) | collective-permute-done | bytes 524320 | tf_op jit(solution)/shard_map/ppermute | solution.py:194
  75.2 5.6 %collective-permute-done.9.refs_12_ = f32[128,1024]{1,0:T(8,128)S(1)} collective-permute-done((f32[128,1024]{1,0:T(8,128)S(1)}, f32[128,1024]{1,0:T(8,128)S(1)}, u32[]{:S(2)}, u32[]{:S(2)}) %collective-permute-start.9) | collective-permute-done | bytes 524320 | tf_op jit(solution)/shard_map/ppermute | solution.py:194
  84.2 4.3 %spread.1.refs_0_ = bf16[1024,2176]{1,0:T(8,128)(2,1)S(1)} custom-call(f32[32,136,128]{2,1,0:T(8,128)S(1)} %all-to-all-done.got_ref), custom_call_target="tpu_custom_call" | custom-call | bytes 8388608 | tf_op jit(solution)/shard_map/spread/pallas_call | solution.py:119
  88.6 4.8 %product.3 = (f32[128,512]{1,0:T(8,128)S(1)}, f32[128,512]{1,0:T(8,128)S(1)}, f32[128,512]{1,0:T(8,128)S(1)}, f32[128,512]{1,0:T(8,128)S(1)}) custom-call(bf16[1024,2176]{1,0:T(8,128)(2,1)S(1)} %spread.1.refs_0_, f32[128,1024]{1,0:T(8,128)S(1)} %copy-done.14, f32[128,1024]{1,0:T(8,128)S(1)} %copy-done.16, f32[128,1024]{1,0:T(8,128)S(1)} %collective-permute-done.refs_3_, ...), custom_call_target="tpu_custom_call" | custom-call | flops 3221225472 | bytes 4194304 | tf_op jit(solution)/shard_map/product/pallas_call | solution.py:164
  93.4 2.1 %collective-permute-start.14 = (f32[128,512]{1,0:T(8,128)S(1)}, f32[128,512]{1,0:T(8,128)S(1)}, u32[]{:S(2)}, u32[]{:S(2)}) collective-permute-start(f32[128,512]{1,0:T(8,128)S(1)} %get-tuple-element.35), channel_id=1, source_target_pairs={{0,256},{128,384},{256,0},{384,128},{1,257},{129,385},{257,1},{385... | collective-permute-start | bytes 786440 | tf_op jit(solution)/shard_map/ppermute | solution.py:229
  95.5 4.3 %collective-permute-start.15 = (f32[128,512]{1,0:T(8,128)S(1)}, f32[128,512]{1,0:T(8,128)S(1)}, u32[]{:S(2)}, u32[]{:S(2)}) collective-permute-start(f32[128,512]{1,0:T(8,128)S(1)} %get-tuple-element.36), channel_id=1, source_target_pairs={{0,128},{128,256},{256,384},{384,0},{1,129},{129,257},{257,385},{3... | collective-permute-start | bytes 786440 | tf_op jit(solution)/shard_map/ppermute | solution.py:229
  99.9 2.0 %collective-permute-start.16 = (f32[128,512]{1,0:T(8,128)S(1)}, f32[128,512]{1,0:T(8,128)S(1)}, u32[]{:S(2)}, u32[]{:S(2)}) collective-permute-start(f32[128,512]{1,0:T(8,128)S(1)} %get-tuple-element.37), channel_id=1, source_target_pairs={{0,384},{128,0},{256,128},{384,256},{1,385},{129,1},{257,129},{385... | collective-permute-start | bytes 786440 | tf_op jit(solution)/shard_map/ppermute | solution.py:229
  101.8 4.8 %product.2 = (f32[128,512]{1,0:T(8,128)S(1)}, f32[128,512]{1,0:T(8,128)S(1)}, f32[128,512]{1,0:T(8,128)S(1)}, f32[128,512]{1,0:T(8,128)S(1)}) custom-call(bf16[1024,2176]{1,0:T(8,128)(2,1)S(1)} %spread.1.refs_0_, f32[128,1024]{1,0:T(8,128)S(1)} %copy-done.14, f32[128,1024]{1,0:T(8,128)S(1)} %copy-done.16, f32[128,1024]{1,0:T(8,128)S(1)} %collective-permute-done.refs_3_, ...), custom_call_target="tpu_custom_call" | custom-call | flops 3221225472 | bytes 4194304 | tf_op jit(solution)/shard_map/product/pallas_call | solution.py:164
  106.6 4.5 %collective-permute-done.15 = f32[128,512]{1,0:T(8,128)S(1)} collective-permute-done((f32[128,512]{1,0:T(8,128)S(1)}, f32[128,512]{1,0:T(8,128)S(1)}, u32[]{:S(2)}, u32[]{:S(2)}) %collective-permute-start.15) | collective-permute-done | bytes 262176 | tf_op jit(solution)/shard_map/ppermute | solution.py:229
  111.9 6.7 %all-to-all-start.1 = ((f32[8,16,512]{2,1,0:T(8,128)}), f32[8,16,512]{2,1,0:T(8,128)S(1)}, u32[]{:S(2)}, u32[]{:S(2)}) async-start(f32[8,16,512]{2,1,0:T(8,128)} %bitcast.2), calls=%async_computation.1 | async-start | bytes 524288 | tf_op jit(solution)/shard_map/all_to_all | solution.py:235
  118.6 2.5 %collective-permute-start.11 = (f32[128,512]{1,0:T(8,128)S(1)}, f32[128,512]{1,0:T(8,128)S(1)}, u32[]{:S(2)}, u32[]{:S(2)}) collective-permute-start(f32[128,512]{1,0:T(8,128)S(1)} %get-tuple-element.31), channel_id=1, source_target_pairs={{0,256},{128,384},{256,0},{384,128},{1,257},{129,385},{257,1},{385... | collective-permute-start | bytes 786440 | tf_op jit(solution)/shard_map/ppermute | solution.py:229
  121.1 4.0 %collective-permute-start.12 = (f32[128,512]{1,0:T(8,128)S(1)}, f32[128,512]{1,0:T(8,128)S(1)}, u32[]{:S(2)}, u32[]{:S(2)}) collective-permute-start(f32[128,512]{1,0:T(8,128)S(1)} %get-tuple-element.32), channel_id=1, source_target_pairs={{0,128},{128,256},{256,384},{384,0},{1,129},{129,257},{257,385},{3... | collective-permute-start | bytes 786440 | tf_op jit(solution)/shard_map/ppermute | solution.py:229
  125.1 2.8 %collective-permute-start.13 = (f32[128,512]{1,0:T(8,128)S(1)}, f32[128,512]{1,0:T(8,128)S(1)}, u32[]{:S(2)}, u32[]{:S(2)}) collective-permute-start(f32[128,512]{1,0:T(8,128)S(1)} %get-tuple-element.33), channel_id=1, source_target_pairs={{0,384},{128,0},{256,128},{384,256},{1,385},{129,1},{257,129},{385... | collective-permute-start | bytes 786440 | tf_op jit(solution)/shard_map/ppermute | solution.py:229
  127.8 3.4 %collective-permute-done.11 = f32[128,512]{1,0:T(8,128)S(1)} collective-permute-done((f32[128,512]{1,0:T(8,128)S(1)}, f32[128,512]{1,0:T(8,128)S(1)}, u32[]{:S(2)}, u32[]{:S(2)}) %collective-permute-start.11) | collective-permute-done | bytes 262176 | tf_op jit(solution)/shard_map/ppermute | solution.py:229
  131.2 4.4 %collective-permute-done.12 = f32[128,512]{1,0:T(8,128)S(1)} collective-permute-done((f32[128,512]{1,0:T(8,128)S(1)}, f32[128,512]{1,0:T(8,128)S(1)}, u32[]{:S(2)}, u32[]{:S(2)}) %collective-permute-start.12) | collective-permute-done | bytes 262176 | tf_op jit(solution)/shard_map/ppermute | solution.py:229
  136.4 6.9 %all-to-all-start.2 = ((f32[8,16,512]{2,1,0:T(8,128)}), f32[8,16,512]{2,1,0:T(8,128)S(1)}, u32[]{:S(2)}, u32[]{:S(2)}) async-start(f32[8,16,512]{2,1,0:T(8,128)} %bitcast.3), calls=%async_computation.2 | async-start | bytes 524288 | tf_op jit(solution)/shard_map/all_to_all | solution.py:235
  143.3 12.0 %all-to-all-done.2 = f32[8,16,512]{2,1,0:T(8,128)S(1)} async-done(((f32[8,16,512]{2,1,0:T(8,128)}), f32[8,16,512]{2,1,0:T(8,128)S(1)}, u32[]{:S(2)}, u32[]{:S(2)}) %all-to-all-start.2) | async-done | bytes 262176 | tf_op jit(solution)/shard_map/all_to_all | solution.py:235
  (62 shorter events, 25.8 us)
Async XLA Ops:
  0.0 12.5 %collective-permute-start = (f32[128,1024]{1,0:T(8,128)}, f32[128,1024]{1,0:T(8,128)S(1)}, u32[]{:S(2)}, u32[]{:S(2)}) collective-permute-start(f32[128,1024]{1,0:T(8,128)} %refs_1_.3), channel_id=1, source_target_pairs={{0,1},{1,2},{2,3},{3,4},{4,5},{5,6},{6,7},{7,0},{8,15},{9,8},{10,9... | collective-permute-start | bytes 1572872 | tf_op jit(solution)/shard_map/ppermute | solution.py:194
  2.6 9.9 %collective-permute-start.1 = (f32[128,1024]{1,0:T(8,128)}, f32[128,1024]{1,0:T(8,128)S(1)}, u32[]{:S(2)}, u32[]{:S(2)}) collective-permute-start(f32[128,1024]{1,0:T(8,128)} %refs_1_.3), channel_id=1, source_target_pairs={{0,8},{8,0},{1,9},{9,1},{2,10},{10,2},{3,11},{11,3},{4,12},{12,4},... | collective-permute-start | bytes 1572872 | tf_op jit(solution)/shard_map/ppermute | solution.py:186
  13.3 70.8 %all-to-all-start = ((f32[32,136,128]{2,1,0:T(8,128)}), f32[32,136,128]{2,1,0:T(8,128)S(1)}, u32[]{:S(2)}, u32[]{:S(2)}) async-start(f32[32,136,128]{2,1,0:T(8,128)} %pack.1), calls=%async_computation | async-start | bytes 4456448 | tf_op jit(solution)/shard_map/all_to_all | solution.py:225
  26.8 15.2 %collective-permute-start.2 = (f32[128,1024]{1,0:T(8,128)}, f32[128,1024]{1,0:T(8,128)S(1)}, u32[]{:S(2)}, u32[]{:S(2)}) collective-permute-start(f32[128,1024]{1,0:T(8,128)} %refs_1_.3), channel_id=1, source_target_pairs={{8,1},{9,2},{10,3},{11,4},{12,5},{13,6},{14,7},{15,0},{0,15},{1,8}... | collective-permute-start | bytes 1572872 | tf_op jit(solution)/shard_map/ppermute | solution.py:194
  28.7 17.2 %collective-permute-start.4 = (f32[128,1024]{1,0:T(8,128)S(1)}, f32[128,1024]{1,0:T(8,128)S(1)}, u32[]{:S(2)}, u32[]{:S(2)}) collective-permute-start(f32[128,1024]{1,0:T(8,128)S(1)} %collective-permute-done.refs_3_), channel_id=1, source_target_pairs={{0,1},{1,2},{2,3},{3,4},{4,5},{5,6},{6,7},{7,0},{8,15},{9,8},{10,9... | collective-permute-start | bytes 1572872 | tf_op jit(solution)/shard_map/ppermute | solution.py:194
  42.0 12.3 %collective-permute-start.5 = (f32[128,1024]{1,0:T(8,128)S(1)}, f32[128,1024]{1,0:T(8,128)S(1)}, u32[]{:S(2)}, u32[]{:S(2)}) collective-permute-start(f32[128,1024]{1,0:T(8,128)S(1)} %collective-permute-done.2.refs_4_), channel_id=1, source_target_pairs={{0,1},{1,2},{2,3},{3,4},{4,5},{5,6},{6,7},{7,0},{8,15},{9,8},{10,9... | collective-permute-start | bytes 1572872 | tf_op jit(solution)/shard_map/ppermute | solution.py:194
  44.0 26.5 %collective-permute-start.3 = (f32[256,1024]{1,0:T(8,128)S(1)}, f32[256,1024]{1,0:T(8,128)S(1)}, u32[]{:S(2)}, u32[]{:S(2)}) collective-permute-start(f32[256,1024]{1,0:T(8,128)S(1)} %pad_maximum_fusion.1), channel_id=1, source_target_pairs={{0,8},{8,0},{1,9},{9,1},{2,10},{10,2},{3,11},{11,3},{4,12},{12,4},... | collective-permute-start | bytes 3145736 | tf_op jit(solution)/shard_map/ppermute | solution.py:186
  45.9 10.4 %copy-start = (f32[128,1024]{1,0:T(8,128)}, f32[128,1024]{1,0:T(8,128)S(1)}, u32[]{:S(2)}) copy-start(f32[128,1024]{1,0:T(8,128)S(1)} %collective-permute-done.4.refs_6_) | copy-start | bytes 1572868
  54.2 14.3 %copy-start.2 = (f32[128,1024]{1,0:T(8,128)}, f32[128,1024]{1,0:T(8,128)S(1)}, u32[]{:S(2)}) copy-start(f32[128,1024]{1,0:T(8,128)S(1)} %collective-permute-done.5.refs_7_) | copy-start | bytes 1572868
  54.4 19.8 %collective-permute-start.6 = (f32[256,1024]{1,0:T(8,128)S(1)}, f32[256,1024]{1,0:T(8,128)S(1)}, u32[]{:S(2)}, u32[]{:S(2)}) collective-permute-start(f32[256,1024]{1,0:T(8,128)S(1)} %pad_maximum_fusion.2), channel_id=1, source_target_pairs={{0,8},{8,0},{1,9},{9,1},{2,10},{10,2},{3,11},{11,3},{4,12},{12,4},... | collective-permute-start | bytes 3145736 | tf_op jit(solution)/shard_map/ppermute | solution.py:186
  56.3 12.3 %collective-permute-start.7 = (f32[128,1024]{1,0:T(8,128)S(1)}, f32[128,1024]{1,0:T(8,128)S(1)}, u32[]{:S(2)}, u32[]{:S(2)}) collective-permute-start(f32[128,1024]{1,0:T(8,128)S(1)} %collective-permute-done.4.refs_6_), channel_id=1, source_target_pairs={{0,1},{1,2},{2,3},{3,4},{4,5},{5,6},{6,7},{7,0},{8,15},{9,8},{10,9... | collective-permute-start | bytes 1572872 | tf_op jit(solution)/shard_map/ppermute | solution.py:194
  58.2 16.0 %collective-permute-start.8 = (f32[128,1024]{1,0:T(8,128)S(1)}, f32[128,1024]{1,0:T(8,128)S(1)}, u32[]{:S(2)}, u32[]{:S(2)}) collective-permute-start(f32[128,1024]{1,0:T(8,128)S(1)} %collective-permute-done.5.refs_7_), channel_id=1, source_target_pairs={{0,1},{1,2},{2,3},{3,4},{4,5},{5,6},{6,7},{7,0},{8,15},{9,8},{10,9... | collective-permute-start | bytes 1572872 | tf_op jit(solution)/shard_map/ppermute | solution.py:194
  68.6 13.6 %copy-start.4 = (f32[128,1024]{1,0:T(8,128)}, f32[128,1024]{1,0:T(8,128)S(1)}, u32[]{:S(2)}) copy-start(f32[128,1024]{1,0:T(8,128)S(1)} %collective-permute-done.7.refs_9_) | copy-start | bytes 1572868
  68.6 12.3 %collective-permute-start.9 = (f32[128,1024]{1,0:T(8,128)S(1)}, f32[128,1024]{1,0:T(8,128)S(1)}, u32[]{:S(2)}, u32[]{:S(2)}) collective-permute-start(f32[128,1024]{1,0:T(8,128)S(1)} %collective-permute-done.7.refs_9_), channel_id=1, source_target_pairs={{0,1},{1,2},{2,3},{3,4},{4,5},{5,6},{6,7},{7,0},{8,15},{9,8},{10,9... | collective-permute-start | bytes 1572872 | tf_op jit(solution)/shard_map/ppermute | solution.py:194
  74.2 8.0 %copy-start.6 = (f32[128,1024]{1,0:T(8,128)}, f32[128,1024]{1,0:T(8,128)S(1)}, u32[]{:S(2)}) copy-start(f32[128,1024]{1,0:T(8,128)S(1)} %collective-permute-done.8.refs_10_) | copy-start | bytes 1572868
  82.2 6.3 %collective-permute-start.10 = (f32[384,1024]{1,0:T(8,128)}, f32[384,1024]{1,0:T(8,128)}, u32[]{:S(2)}, u32[]{:S(2)}) collective-permute-start(f32[384,1024]{1,0:T(8,128)} %pad_maximum_fusion), channel_id=1, source_target_pairs={{0,8},{8,0},{1,9},{9,1},{2,10},{10,2},{3,11},{11,3},{4,12},{12,4},... | collective-permute-start | bytes 4718600 | tf_op jit(solution)/shard_map/ppermute | solution.py:186
  93.4 13.2 %collective-permute-start.14 = (f32[128,512]{1,0:T(8,128)S(1)}, f32[128,512]{1,0:T(8,128)S(1)}, u32[]{:S(2)}, u32[]{:S(2)}) collective-permute-start(f32[128,512]{1,0:T(8,128)S(1)} %get-tuple-element.35), channel_id=1, source_target_pairs={{0,256},{128,384},{256,0},{384,128},{1,257},{129,385},{257,1},{385... | collective-permute-start | bytes 786440 | tf_op jit(solution)/shard_map/ppermute | solution.py:229
  95.5 15.6 %collective-permute-start.15 = (f32[128,512]{1,0:T(8,128)S(1)}, f32[128,512]{1,0:T(8,128)S(1)}, u32[]{:S(2)}, u32[]{:S(2)}) collective-permute-start(f32[128,512]{1,0:T(8,128)S(1)} %get-tuple-element.36), channel_id=1, source_target_pairs={{0,128},{128,256},{256,384},{384,0},{1,129},{129,257},{257,385},{3... | collective-permute-start | bytes 786440 | tf_op jit(solution)/shard_map/ppermute | solution.py:229
  99.9 11.3 %collective-permute-start.16 = (f32[128,512]{1,0:T(8,128)S(1)}, f32[128,512]{1,0:T(8,128)S(1)}, u32[]{:S(2)}, u32[]{:S(2)}) collective-permute-start(f32[128,512]{1,0:T(8,128)S(1)} %get-tuple-element.37), channel_id=1, source_target_pairs={{0,384},{128,0},{256,128},{384,256},{1,385},{129,1},{257,129},{385... | collective-permute-start | bytes 786440 | tf_op jit(solution)/shard_map/ppermute | solution.py:229
  111.9 23.7 %all-to-all-start.1 = ((f32[8,16,512]{2,1,0:T(8,128)}), f32[8,16,512]{2,1,0:T(8,128)S(1)}, u32[]{:S(2)}, u32[]{:S(2)}) async-start(f32[8,16,512]{2,1,0:T(8,128)} %bitcast.2), calls=%async_computation.1 | async-start | bytes 524288 | tf_op jit(solution)/shard_map/all_to_all | solution.py:235
  118.6 12.6 %collective-permute-start.11 = (f32[128,512]{1,0:T(8,128)S(1)}, f32[128,512]{1,0:T(8,128)S(1)}, u32[]{:S(2)}, u32[]{:S(2)}) collective-permute-start(f32[128,512]{1,0:T(8,128)S(1)} %get-tuple-element.31), channel_id=1, source_target_pairs={{0,256},{128,384},{256,0},{384,128},{1,257},{129,385},{257,1},{385... | collective-permute-start | bytes 786440 | tf_op jit(solution)/shard_map/ppermute | solution.py:229
  121.1 14.5 %collective-permute-start.12 = (f32[128,512]{1,0:T(8,128)S(1)}, f32[128,512]{1,0:T(8,128)S(1)}, u32[]{:S(2)}, u32[]{:S(2)}) collective-permute-start(f32[128,512]{1,0:T(8,128)S(1)} %get-tuple-element.32), channel_id=1, source_target_pairs={{0,128},{128,256},{256,384},{384,0},{1,129},{129,257},{257,385},{3... | collective-permute-start | bytes 786440 | tf_op jit(solution)/shard_map/ppermute | solution.py:229
  125.1 10.5 %collective-permute-start.13 = (f32[128,512]{1,0:T(8,128)S(1)}, f32[128,512]{1,0:T(8,128)S(1)}, u32[]{:S(2)}, u32[]{:S(2)}) collective-permute-start(f32[128,512]{1,0:T(8,128)S(1)} %get-tuple-element.33), channel_id=1, source_target_pairs={{0,384},{128,0},{256,128},{384,256},{1,385},{129,1},{257,129},{385... | collective-permute-start | bytes 786440 | tf_op jit(solution)/shard_map/ppermute | solution.py:229
  136.4 19.0 %all-to-all-start.2 = ((f32[8,16,512]{2,1,0:T(8,128)}), f32[8,16,512]{2,1,0:T(8,128)S(1)}, u32[]{:S(2)}, u32[]{:S(2)}) async-start(f32[8,16,512]{2,1,0:T(8,128)} %bitcast.3), calls=%async_computation.2 | async-start | bytes 524288 | tf_op jit(solution)/shard_map/all_to_all | solution.py:235
  (13 other events, 43.6 us)

commit v12 on v9

--- a/solution.py
+++ b/solution.py
@@ -198,15 +198,24 @@
     size = block.shape[0]
     mate = along_ring(block, cross=True)
     blocks = [block, partner, own, mate]
+    pairs = [(own, mate)]
     for _ in range(n // 2 - 2):
-        blocks.append(swap_core(jnp.concatenate([own, mate], axis=0)))
         own, mate = along_ring(own), along_ring(mate)
-        blocks += [own, mate]
+        pairs.append((own, mate))
+    blocks = blocks[:2] + [each for pair in pairs for each in pair]
+    early = [each for pair in pairs[:-1] for each in pair]
+    swap = swap_core(jnp.concatenate(early, axis=0))
     far = along_ring(own)
-    pieces = [(i, 0, each.shape[0]) for i, each in enumerate(blocks)]
-    last = len(blocks)
-    blocks += [swap_core(jnp.concatenate([own, mate, far], axis=0)), far]
-    return blocks, pieces + [(last, 0, 2 * size), (last + 1, 0, size), (last, 2 * size, size)]
+    final = swap_core(jnp.concatenate([own, mate, far], axis=0))
+    pieces = [(0, 0, size), (1, 0, size)]
+    count = len(blocks)
+    for i in range(len(pairs)):
+        pieces += [(2 + 2 * i, 0, size), (3 + 2 * i, 0, size)]
+        if i < len(pairs) - 1:
+            pieces.append((count, 2 * i * size, 2 * size))
+    blocks += [swap, final, far]
+    pieces += [(count + 1, 0, 2 * size), (count + 2, 0, size), (count + 1, 2 * size, size)]
+    return blocks, pieces
 
 
 def on_device(amplitudes, integrals, occupancy, tile_place):

time: 148 us -> 142 us (0.959)
  the two profiles are of different devices: /device:TPU:32 before, /device:TPU:24 now
where the time goes in v12:
time: 142 us; the launch traced here: 141 us
  starting transfers between devices  61.2 us (43%)
  waiting for transfers between devices  32.5 us (23%)
  blocking collectives  23.9 us (17%)
  Pallas kernels  17.3 us (12%)
  other arithmetic  4.86 us (3%)
    ppermute x7, starting transfers between devices, along_ring(): return lax.ppermute(block, ('core', 'grp'), pairs)  32.5 us
    all_to_all x1, blocking collectives, on_device(): return lax.all_to_all(part, 'z', 0, 0, tiled=True).sum(axis=0)  23.9 us
    ppermute x7, waiting for transfers between devices, along_ring(): return lax.ppermute(block, ('core', 'grp'), pairs)  14.3 us
    all_to_all x1, starting transfers between devices, on_device(): got = lax.all_to_all(sent, CHIPS, 0, 0, tiled=True)  13.2 us
    pallas_call x2, Pallas kernels, product(): pl.pallas_call(lambda *refs: product_kernel(pair, pieces, *refs), out_sha...  8.9 us
    all_to_all x1, waiting for transfers between devices, on_device(): got = lax.all_to_all(sent, CHIPS, 0, 0, tiled=True)  7.13 us
    ppermute x1, waiting for transfers between devices, on_device(): near = lax.ppermute(near, 'x', shift_x(1))  5.98 us
    ppermute x3, starting transfers between devices, swap_core(): return lax.ppermute(block, 'core', [(0, 1), (1, 0)])  5.74 us
  transfers between devices with their start and end apart: 14, of which 7 were waited for; matrix products, arithmetic and copies ran while one was open for 3% of the time, Pallas kernels for 8%

profile of v12, /device:TPU:24, one launch (start us, length us, event | category | flops | bytes accessed | tf_op | source)
XLA Modules:
  0.0 140.9 jit_solution(7341427474238120391)
XLA Ops:
  1.9 4.7 %collective-permute-start = (f32[128,1024]{1,0:T(8,128)}, f32[128,1024]{1,0:T(8,128)S(1)}, u32[]{:S(2)}, u32[]{:S(2)}) collective-permute-start(f32[128,1024]{1,0:T(8,128)} %refs_1_.1), channel_id=1, source_target_pairs={{0,1},{1,2},{2,3},{3,4},{4,5},{5,6},{6,7},{7,0},{8,15},{9,8},{10,9... | collective-permute-start | bytes 1572872 | tf_op jit(solution)/shard_map/ppermute | solution.py:193
  6.6 4.2 %pack.1 = f32[32,136,128]{2,1,0:T(8,128)} custom-call(s32[128]{0:T(128)} %bitcast.5, s32[512]{0:T(512)} %place_ref.1, f32[128,16,128]{2,1,0:T(8,128)} %bitcast.4), custom_call_target="tpu_custom_call" | custom-call | bytes 8388608 | tf_op jit(solution)/shard_map/pack/pallas_call | solution.py:63
  11.6 2.0 %collective-permute-done.refs_3_ = f32[128,1024]{1,0:T(8,128)S(1)} collective-permute-done((f32[128,1024]{1,0:T(8,128)}, f32[128,1024]{1,0:T(8,128)S(1)}, u32[]{:S(2)}, u32[]{:S(2)}) %collective-permute-start) | collective-permute-done | bytes 524320 | tf_op jit(solution)/shard_map/ppermute | solution.py:193
  13.6 13.2 %all-to-all-start = ((f32[32,136,128]{2,1,0:T(8,128)}), f32[32,136,128]{2,1,0:T(8,128)S(1)}, u32[]{:S(2)}, u32[]{:S(2)}) async-start(f32[32,136,128]{2,1,0:T(8,128)} %pack.1), calls=%async_computation | async-start | bytes 4456448 | tf_op jit(solution)/shard_map/all_to_all | solution.py:230
  28.7 5.5 %collective-permute-start.3 = (f32[128,1024]{1,0:T(8,128)S(1)}, f32[128,1024]{1,0:T(8,128)S(1)}, u32[]{:S(2)}, u32[]{:S(2)}) collective-permute-start(f32[128,1024]{1,0:T(8,128)S(1)} %collective-permute-done.refs_3_), channel_id=1, source_target_pairs={{0,1},{1,2},{2,3},{3,4},{4,5},{5,6},{6,7},{7,0},{8,15},{9,8},{10,9... | collective-permute-start | bytes 1572872 | tf_op jit(solution)/shard_map/ppermute | solution.py:193
  34.2 6.1 %collective-permute-done.2.refs_4_ = f32[128,1024]{1,0:T(8,128)S(1)} collective-permute-done((f32[128,1024]{1,0:T(8,128)S(1)}, f32[128,1024]{1,0:T(8,128)S(1)}, u32[]{:S(2)}, u32[]{:S(2)}) %collective-permute-start.2) | collective-permute-done | bytes 524320 | tf_op jit(solution)/shard_map/ppermute | solution.py:193
  40.3 6.7 %collective-permute-start.4 = (f32[128,1024]{1,0:T(8,128)S(1)}, f32[128,1024]{1,0:T(8,128)S(1)}, u32[]{:S(2)}, u32[]{:S(2)}) collective-permute-start(f32[128,1024]{1,0:T(8,128)S(1)} %collective-permute-done.2.refs_4_), channel_id=1, source_target_pairs={{0,1},{1,2},{2,3},{3,4},{4,5},{5,6},{6,7},{7,0},{8,15},{9,8},{10,9... | collective-permute-start | bytes 1572872 | tf_op jit(solution)/shard_map/ppermute | solution.py:193
  47.1 2.6 %collective-permute-start.5 = (f32[128,1024]{1,0:T(8,128)S(1)}, f32[128,1024]{1,0:T(8,128)S(1)}, u32[]{:S(2)}, u32[]{:S(2)}) collective-permute-start(f32[128,1024]{1,0:T(8,128)S(1)} %collective-permute-done.3.refs_5_), channel_id=1, source_target_pairs={{0,1},{1,2},{2,3},{3,4},{4,5},{5,6},{6,7},{7,0},{8,15},{9,8},{10,9... | collective-permute-start | bytes 1572872 | tf_op jit(solution)/shard_map/ppermute | solution.py:193
  49.6 4.1 %collective-permute-done.4.refs_6_ = f32[128,1024]{1,0:T(8,128)S(1)} collective-permute-done((f32[128,1024]{1,0:T(8,128)S(1)}, f32[128,1024]{1,0:T(8,128)S(1)}, u32[]{:S(2)}, u32[]{:S(2)}) %collective-permute-start.4) | collective-permute-done | bytes 524320 | tf_op jit(solution)/shard_map/ppermute | solution.py:193
  53.7 5.6 %collective-permute-start.6 = (f32[128,1024]{1,0:T(8,128)S(1)}, f32[128,1024]{1,0:T(8,128)S(1)}, u32[]{:S(2)}, u32[]{:S(2)}) collective-permute-start(f32[128,1024]{1,0:T(8,128)S(1)} %collective-permute-done.4.refs_6_), channel_id=1, source_target_pairs={{0,1},{1,2},{2,3},{3,4},{4,5},{5,6},{6,7},{7,0},{8,15},{9,8},{10,9... | collective-permute-start | bytes 1572872 | tf_op jit(solution)/shard_map/ppermute | solution.py:193
  59.3 5.6 %collective-permute-start.8 = (f32[128,1024]{1,0:T(8,128)S(1)}, f32[128,1024]{1,0:T(8,128)S(1)}, u32[]{:S(2)}, u32[]{:S(2)}) collective-permute-start(f32[128,1024]{1,0:T(8,128)S(1)} %collective-permute-done.5.refs_7_), channel_id=1, source_target_pairs={{0,1},{1,2},{2,3},{3,4},{4,5},{5,6},{6,7},{7,0},{8,15},{9,8},{10,9... | collective-permute-start | bytes 1572872 | tf_op jit(solution)/shard_map/ppermute | solution.py:193
  64.9 2.7 %pad_maximum_fusion = f32[512,1024]{1,0:T(8,128)} fusion(f32[128,1024]{1,0:T(8,128)S(1)} %collective-permute-done.4.refs_6_, f32[128,1024]{1,0:T(8,128)S(1)} %collective-permute-done.3.refs_5_, f32[128,1024]{1,0:T(8,128)S(1)} %collective-permute-done.2.refs_4_, f32[128,1024]{1,0:T(8,128)} %copy-done.2), kind=kLoop, calls=%fused_computation | loop fusion | flops 1572864 | bytes 4194304 | tf_op jit(solution)/shard_map/concatenate | solution.py:207
  69.5 2.1 %collective-permute-done.8.refs_11_ = f32[128,1024]{1,0:T(8,128)S(1)} collective-permute-done((f32[128,1024]{1,0:T(8,128)S(1)}, f32[128,1024]{1,0:T(8,128)S(1)}, u32[]{:S(2)}, u32[]{:S(2)}) %collective-permute-start.8) | collective-permute-done | bytes 524320 | tf_op jit(solution)/shard_map/ppermute | solution.py:193
  73.0 1.9 %collective-permute-start.9 = (f32[384,1024]{1,0:T(8,128)}, f32[384,1024]{1,0:T(8,128)}, u32[]{:S(2)}, u32[]{:S(2)}) collective-permute-start(f32[384,1024]{1,0:T(8,128)} %pad_maximum_fusion.1), channel_id=1, source_target_pairs={{0,8},{8,0},{1,9},{9,1},{2,10},{10,2},{3,11},{11,3},{4,12},{12,4},... | collective-permute-start | bytes 4718600 | tf_op jit(solution)/shard_map/ppermute | solution.py:185
  74.9 7.1 %all-to-all-done.got_ref = f32[32,136,128]{2,1,0:T(8,128)S(1)} async-done(((f32[32,136,128]{2,1,0:T(8,128)}), f32[32,136,128]{2,1,0:T(8,128)S(1)}, u32[]{:S(2)}, u32[]{:S(2)}) %all-to-all-start) | async-done | bytes 2228256 | tf_op jit(solution)/shard_map/all_to_all | solution.py:230
  82.1 4.3 %spread.1.refs_0_ = bf16[1024,2176]{1,0:T(8,128)(2,1)S(1)} custom-call(f32[32,136,128]{2,1,0:T(8,128)S(1)} %all-to-all-done.got_ref), custom_call_target="tpu_custom_call" | custom-call | bytes 8388608 | tf_op jit(solution)/shard_map/spread/pallas_call | solution.py:119
  86.5 5.5 %product.2 = (f32[128,1024]{1,0:T(8,128)S(1)}, f32[128,1024]{1,0:T(8,128)S(1)}, bf16[2048,1024]{1,0:T(8,128)(2,1)S(1)}, bf16[2048,1024]{1,0:T(8,128)(2,1)S(1)}) custom-call(bf16[1024,2176]{1,0:T(8,128)(2,1)S(1)} %spread.1.refs_0_, f32[128,1024]{1,0:T(8,128)S(1)} %copy-done.11, f32[128,1024]{1,0:T(8,128)S(1)} %copy-done.13, f32[128,1024]{1,0:T(8,128)S(1)} %copy-done.3, ...), custom_call_target="tpu_custom_call" | custom-call | flops 3221225472 | bytes 4194304 | tf_op jit(solution)/shard_map/product/pallas_call | solution.py:167
  92.0 2.7 %collective-permute-start.10 = (f32[128,1024]{1,0:T(8,128)S(1)}, f32[128,1024]{1,0:T(8,128)S(1)}, u32[]{:S(2)}, u32[]{:S(2)}) collective-permute-start(f32[128,1024]{1,0:T(8,128)S(1)} %get-tuple-element.20), channel_id=1, source_target_pairs={{0,256},{128,384},{256,0},{384,128},{1,257},{129,385},{257,1},{385... | collective-permute-start | bytes 1572872 | tf_op jit(solution)/shard_map/ppermute | solution.py:234
  94.7 2.9 %collective-permute-start.11 = (f32[128,1024]{1,0:T(8,128)S(1)}, f32[128,1024]{1,0:T(8,128)S(1)}, u32[]{:S(2)}, u32[]{:S(2)}) collective-permute-start(f32[128,1024]{1,0:T(8,128)S(1)} %get-tuple-element.21), channel_id=1, source_target_pairs={{0,128},{128,256},{256,384},{384,0},{1,129},{129,257},{257,385},{3... | collective-permute-start | bytes 1572872 | tf_op jit(solution)/shard_map/ppermute | solution.py:235
  97.6 3.4 %product.3 = (f32[128,1024]{1,0:T(8,128)S(1)}, f32[128,1024]{1,0:T(8,128)S(1)}) custom-call(bf16[1024,2176]{1,0:T(8,128)(2,1)S(1)} %spread.1.refs_0_, bf16[2048,1024]{1,0:T(8,128)(2,1)S(1)} %get-tuple-element.22.refs_1_, bf16[2048,1024]{1,0:T(8,128)(2,1)S(1)} %get-tuple-element.23.refs_2_), custom_call_target="tpu_custom_call" | custom-call | flops 3221225472 | bytes 4194304 | tf_op jit(solution)/shard_map/product/pallas_call | solution.py:167
  101.0 4.2 %collective-permute-start.12 = (f32[128,1024]{1,0:T(8,128)S(1)}, f32[128,1024]{1,0:T(8,128)S(1)}, u32[]{:S(2)}, u32[]{:S(2)}) collective-permute-start(f32[128,1024]{1,0:T(8,128)S(1)} %get-tuple-element.28), channel_id=1, source_target_pairs={{0,384},{128,0},{256,128},{384,256},{1,385},{129,1},{257,129},{385... | collective-permute-start | bytes 1572872 | tf_op jit(solution)/shard_map/ppermute | solution.py:238
  105.2 5.1 %collective-permute-done.10 = f32[128,1024]{1,0:T(8,128)S(1)} collective-permute-done((f32[128,1024]{1,0:T(8,128)S(1)}, f32[128,1024]{1,0:T(8,128)S(1)}, u32[]{:S(2)}, u32[]{:S(2)}) %collective-permute-start.10) | collective-permute-done | bytes 524320 | tf_op jit(solution)/shard_map/ppermute | solution.py:234
  110.2 6.0 %collective-permute-done.11 = f32[128,1024]{1,0:T(8,128)S(1)} collective-permute-done((f32[128,1024]{1,0:T(8,128)S(1)}, f32[128,1024]{1,0:T(8,128)S(1)}, u32[]{:S(2)}, u32[]{:S(2)}) %collective-permute-start.11) | collective-permute-done | bytes 524320 | tf_op jit(solution)/shard_map/ppermute | solution.py:235
  116.4 23.9 %all_to_all.10 = f32[8,16,1024]{2,1,0:T(8,128)S(1)} all-to-all(f32[8,16,1024]{2,1,0:T(8,128)S(1)} %bitcast.3), channel_id=1, replica_groups=mesh['x'=4,'z'=8,'core'=2,'grp'=8] {'z'}, dimensions={0} | all-to-all | bytes 1048576 | tf_op jit(solution)/shard_map/all_to_all | solution.py:241
  (41 shorter events, 8.8 us)
Async XLA Ops:
  0.0 10.8 %collective-permute-start.1 = (f32[128,1024]{1,0:T(8,128)}, f32[128,1024]{1,0:T(8,128)S(1)}, u32[]{:S(2)}, u32[]{:S(2)}) collective-permute-start(f32[128,1024]{1,0:T(8,128)} %refs_1_.1), channel_id=1, source_target_pairs={{0,8},{8,0},{1,9},{9,1},{2,10},{10,2},{3,11},{11,3},{4,12},{12,4},... | collective-permute-start | bytes 1572872 | tf_op jit(solution)/shard_map/ppermute | solution.py:185
  1.9 11.7 %collective-permute-start = (f32[128,1024]{1,0:T(8,128)}, f32[128,1024]{1,0:T(8,128)S(1)}, u32[]{:S(2)}, u32[]{:S(2)}) collective-permute-start(f32[128,1024]{1,0:T(8,128)} %refs_1_.1), channel_id=1, source_target_pairs={{0,1},{1,2},{2,3},{3,4},{4,5},{5,6},{6,7},{7,0},{8,15},{9,8},{10,9... | collective-permute-start | bytes 1572872 | tf_op jit(solution)/shard_map/ppermute | solution.py:193
  10.8 16.0 %copy-start.10 = (f32[128,1024]{1,0:T(8,128)S(1)}, f32[128,1024]{1,0:T(8,128)}, u32[]{:S(2)}) copy-start(f32[128,1024]{1,0:T(8,128)} %refs_1_.1) | copy-start | bytes 1572868
  13.6 15.1 %copy-start.2 = (f32[128,1024]{1,0:T(8,128)}, f32[128,1024]{1,0:T(8,128)S(1)}, u32[]{:S(2)}) copy-start(f32[128,1024]{1,0:T(8,128)S(1)} %collective-permute-done.refs_3_) | copy-start | bytes 1572868
  13.6 68.4 %all-to-all-start = ((f32[32,136,128]{2,1,0:T(8,128)}), f32[32,136,128]{2,1,0:T(8,128)S(1)}, u32[]{:S(2)}, u32[]{:S(2)}) async-start(f32[32,136,128]{2,1,0:T(8,128)} %pack.1), calls=%async_computation | async-start | bytes 4456448 | tf_op jit(solution)/shard_map/all_to_all | solution.py:230
  26.8 13.5 %collective-permute-start.2 = (f32[128,1024]{1,0:T(8,128)S(1)}, f32[128,1024]{1,0:T(8,128)S(1)}, u32[]{:S(2)}, u32[]{:S(2)}) collective-permute-start(f32[128,1024]{1,0:T(8,128)S(1)} %copy-done.10), channel_id=1, source_target_pairs={{8,1},{9,2},{10,3},{11,4},{12,5},{13,6},{14,7},{15,0},{0,15},{1,8}... | collective-permute-start | bytes 1572872 | tf_op jit(solution)/shard_map/ppermute | solution.py:193
  28.7 18.3 %collective-permute-start.3 = (f32[128,1024]{1,0:T(8,128)S(1)}, f32[128,1024]{1,0:T(8,128)S(1)}, u32[]{:S(2)}, u32[]{:S(2)}) collective-permute-start(f32[128,1024]{1,0:T(8,128)S(1)} %collective-permute-done.refs_3_), channel_id=1, source_target_pairs={{0,1},{1,2},{2,3},{3,4},{4,5},{5,6},{6,7},{7,0},{8,15},{9,8},{10,9... | collective-permute-start | bytes 1572872 | tf_op jit(solution)/shard_map/ppermute | solution.py:193
  40.3 32.7 %copy-start.4 = (f32[128,1024]{1,0:T(8,128)}, f32[128,1024]{1,0:T(8,128)S(1)}, u32[]{:S(2)}) copy-start(f32[128,1024]{1,0:T(8,128)S(1)} %collective-permute-done.2.refs_4_) | copy-start | bytes 1572868
  40.3 13.4 %collective-permute-start.4 = (f32[128,1024]{1,0:T(8,128)S(1)}, f32[128,1024]{1,0:T(8,128)S(1)}, u32[]{:S(2)}, u32[]{:S(2)}) collective-permute-start(f32[128,1024]{1,0:T(8,128)S(1)} %collective-permute-done.2.refs_4_), channel_id=1, source_target_pairs={{0,1},{1,2},{2,3},{3,4},{4,5},{5,6},{6,7},{7,0},{8,15},{9,8},{10,9... | collective-permute-start | bytes 1572872 | tf_op jit(solution)/shard_map/ppermute | solution.py:193
  47.1 25.9 %copy-start.6 = (f32[128,1024]{1,0:T(8,128)}, f32[128,1024]{1,0:T(8,128)S(1)}, u32[]{:S(2)}) copy-start(f32[128,1024]{1,0:T(8,128)S(1)} %collective-permute-done.3.refs_5_) | copy-start | bytes 1572868
  47.1 12.3 %collective-permute-start.5 = (f32[128,1024]{1,0:T(8,128)S(1)}, f32[128,1024]{1,0:T(8,128)S(1)}, u32[]{:S(2)}, u32[]{:S(2)}) collective-permute-start(f32[128,1024]{1,0:T(8,128)S(1)} %collective-permute-done.3.refs_5_), channel_id=1, source_target_pairs={{0,1},{1,2},{2,3},{3,4},{4,5},{5,6},{6,7},{7,0},{8,15},{9,8},{10,9... | collective-permute-start | bytes 1572872 | tf_op jit(solution)/shard_map/ppermute | solution.py:193
  53.7 19.3 %copy-start.8 = (f32[128,1024]{1,0:T(8,128)}, f32[128,1024]{1,0:T(8,128)S(1)}, u32[]{:S(2)}) copy-start(f32[128,1024]{1,0:T(8,128)S(1)} %collective-permute-done.4.refs_6_) | copy-start | bytes 1572868
  53.7 15.8 %collective-permute-start.6 = (f32[128,1024]{1,0:T(8,128)S(1)}, f32[128,1024]{1,0:T(8,128)S(1)}, u32[]{:S(2)}, u32[]{:S(2)}) collective-permute-start(f32[128,1024]{1,0:T(8,128)S(1)} %collective-permute-done.4.refs_6_), channel_id=1, source_target_pairs={{0,1},{1,2},{2,3},{3,4},{4,5},{5,6},{6,7},{7,0},{8,15},{9,8},{10,9... | collective-permute-start | bytes 1572872 | tf_op jit(solution)/shard_map/ppermute | solution.py:193
  59.3 12.3 %collective-permute-start.8 = (f32[128,1024]{1,0:T(8,128)S(1)}, f32[128,1024]{1,0:T(8,128)S(1)}, u32[]{:S(2)}, u32[]{:S(2)}) collective-permute-start(f32[128,1024]{1,0:T(8,128)S(1)} %collective-permute-done.5.refs_7_), channel_id=1, source_target_pairs={{0,1},{1,2},{2,3},{3,4},{4,5},{5,6},{6,7},{7,0},{8,15},{9,8},{10,9... | collective-permute-start | bytes 1572872 | tf_op jit(solution)/shard_map/ppermute | solution.py:193
  67.6 18.8 %collective-permute-start.7 = (f32[512,1024]{1,0:T(8,128)}, f32[512,1024]{1,0:T(8,128)}, u32[]{:S(2)}, u32[]{:S(2)}) collective-permute-start(f32[512,1024]{1,0:T(8,128)} %pad_maximum_fusion), channel_id=1, source_target_pairs={{0,8},{8,0},{1,9},{9,1},{2,10},{10,2},{3,11},{11,3},{4,12},{12,4},... | collective-permute-start | bytes 6291464 | tf_op jit(solution)/shard_map/ppermute | solution.py:185
  73.0 13.4 %collective-permute-start.9 = (f32[384,1024]{1,0:T(8,128)}, f32[384,1024]{1,0:T(8,128)}, u32[]{:S(2)}, u32[]{:S(2)}) collective-permute-start(f32[384,1024]{1,0:T(8,128)} %pad_maximum_fusion.1), channel_id=1, source_target_pairs={{0,8},{8,0},{1,9},{9,1},{2,10},{10,2},{3,11},{11,3},{4,12},{12,4},... | collective-permute-start | bytes 4718600 | tf_op jit(solution)/shard_map/ppermute | solution.py:185
  82.1 4.4 %copy-start.5 = (f32[128,1024]{1,0:T(8,128)S(1)}, f32[128,1024]{1,0:T(8,128)}, u32[]{:S(2)}) copy-start(f32[128,1024]{1,0:T(8,128)} %copy-done.4) | copy-start | bytes 1572868
  82.1 4.4 %copy-start.7 = (f32[128,1024]{1,0:T(8,128)S(1)}, f32[128,1024]{1,0:T(8,128)}, u32[]{:S(2)}) copy-start(f32[128,1024]{1,0:T(8,128)} %copy-done.6) | copy-start | bytes 1572868
  82.1 4.4 %copy-start.9 = (f32[128,1024]{1,0:T(8,128)S(1)}, f32[128,1024]{1,0:T(8,128)}, u32[]{:S(2)}) copy-start(f32[128,1024]{1,0:T(8,128)} %copy-done.8) | copy-start | bytes 1572868
  82.1 4.4 %copy-start.11 = (f32[128,1024]{1,0:T(8,128)S(1)}, f32[128,1024]{1,0:T(8,128)}, u32[]{:S(2)}) copy-start(f32[128,1024]{1,0:T(8,128)} %refs_1_.1) | copy-start | bytes 1572868
  82.1 4.4 %copy-start.13 = (f32[128,1024]{1,0:T(8,128)S(1)}, f32[128,1024]{1,0:T(8,128)}, u32[]{:S(2)}) copy-start(f32[128,1024]{1,0:T(8,128)} %copy-done.12) | copy-start | bytes 1572868
  92.0 18.3 %collective-permute-start.10 = (f32[128,1024]{1,0:T(8,128)S(1)}, f32[128,1024]{1,0:T(8,128)S(1)}, u32[]{:S(2)}, u32[]{:S(2)}) collective-permute-start(f32[128,1024]{1,0:T(8,128)S(1)} %get-tuple-element.20), channel_id=1, source_target_pairs={{0,256},{128,384},{256,0},{384,128},{1,257},{129,385},{257,1},{385... | collective-permute-start | bytes 1572872 | tf_op jit(solution)/shard_map/ppermute | solution.py:234
  94.7 21.5 %collective-permute-start.11 = (f32[128,1024]{1,0:T(8,128)S(1)}, f32[128,1024]{1,0:T(8,128)S(1)}, u32[]{:S(2)}, u32[]{:S(2)}) collective-permute-start(f32[128,1024]{1,0:T(8,128)S(1)} %get-tuple-element.21), channel_id=1, source_target_pairs={{0,128},{128,256},{256,384},{384,0},{1,129},{129,257},{257,385},{3... | collective-permute-start | bytes 1572872 | tf_op jit(solution)/shard_map/ppermute | solution.py:235
  101.0 15.3 %collective-permute-start.12 = (f32[128,1024]{1,0:T(8,128)S(1)}, f32[128,1024]{1,0:T(8,128)S(1)}, u32[]{:S(2)}, u32[]{:S(2)}) collective-permute-start(f32[128,1024]{1,0:T(8,128)S(1)} %get-tuple-element.28), channel_id=1, source_target_pairs={{0,384},{128,0},{256,128},{384,256},{1,385},{129,1},{257,129},{385... | collective-permute-start | bytes 1572872 | tf_op jit(solution)/shard_map/ppermute | solution.py:238
  (4 other events, 10.8 us)

commit v13 on v12

--- a/solution.py
+++ b/solution.py
@@ -224,9 +224,7 @@
     rows, width = amplitudes.shape[2:]
     cols = integrals.shape[1]
     sent = pack(occupancy[0], tile_place, amplitudes[0], chips, per_chip)
-    sent, first, partner = lax.optimization_barrier(
-        (sent, along_ring(integrals), swap_core(integrals))
-    )
+    first, partner = along_ring(integrals), swap_core(integrals)
     got = lax.all_to_all(sent, CHIPS, 0, 0, tiled=True)
     blocks, pieces = gather_panel(integrals, partner, first)
     left = spread(got, rows, per_chip * width)

time: 142 us -> 141 us (level)
  the two profiles are of different devices: /device:TPU:24 before, /device:TPU:32 now
where the time goes in v13:
time: 141 us; the launch traced here: 140 us
  waiting for transfers between devices  48.4 us (34%)
  starting transfers between devices  45.7 us (32%)
  blocking collectives  24.1 us (17%)
  Pallas kernels  17.7 us (13%)
  other arithmetic  3.82 us (3%)
    ppermute x7, waiting for transfers between devices, along_ring(): return lax.ppermute(block, ('core', 'grp'), pairs)  35.2 us
    all_to_all x1, blocking collectives, on_device(): return lax.all_to_all(part, 'z', 0, 0, tiled=True).sum(axis=0)  24.1 us
    ppermute x7, starting transfers between devices, along_ring(): return lax.ppermute(block, ('core', 'grp'), pairs)  14.1 us
    all_to_all x1, starting transfers between devices, on_device(): got = lax.all_to_all(sent, CHIPS, 0, 0, tiled=True)  13.2 us
    ppermute x1, waiting for transfers between devices, on_device(): near = lax.ppermute(near, 'x', shift_x(1))  10.3 us
    pallas_call x2, Pallas kernels, product(): pl.pallas_call(lambda *refs: product_kernel(pair, pieces, *refs), out_sha...  9.23 us
    ppermute x3, starting transfers between devices, swap_core(): return lax.ppermute(block, 'core', [(0, 1), (1, 0)])  6.24 us
    ppermute x1, starting transfers between devices, on_device(): far = lax.ppermute(far, 'x', shift_x(2))  5.21 us
  transfers between devices with their start and end apart: 14, of which 10 were waited for; matrix products, arithmetic and copies ran while one was open for 2% of the time, Pallas kernels for 5%

profile of v13, /device:TPU:32, one launch (start us, length us, event | category | flops | bytes accessed | tf_op | source)
XLA Modules:
  0.0 140.0 jit_solution(2768373357697595485)
XLA Ops:
  0.0 4.2 %pack.1 = f32[32,136,128]{2,1,0:T(8,128)} custom-call(s32[128]{0:T(128)} %bitcast.5, s32[512]{0:T(512)} %place_ref.1, f32[128,16,128]{2,1,0:T(8,128)} %bitcast.4), custom_call_target="tpu_custom_call" | custom-call | bytes 8388608 | tf_op jit(solution)/shard_map/pack/pallas_call | solution.py:63
  4.2 13.2 %all-to-all-start = ((f32[32,136,128]{2,1,0:T(8,128)}), f32[32,136,128]{2,1,0:T(8,128)S(1)}, u32[]{:S(2)}, u32[]{:S(2)}) async-start(f32[32,136,128]{2,1,0:T(8,128)} %pack.1), calls=%async_computation | async-start | bytes 4456448 | tf_op jit(solution)/shard_map/all_to_all | solution.py:228
  17.4 2.6 %collective-permute-start.1 = (f32[128,1024]{1,0:T(8,128)}, f32[128,1024]{1,0:T(8,128)S(1)}, u32[]{:S(2)}, u32[]{:S(2)}) collective-permute-start(f32[128,1024]{1,0:T(8,128)} %refs_1_.1), channel_id=1, source_target_pairs={{0,1},{1,2},{2,3},{3,4},{4,5},{5,6},{6,7},{7,0},{8,15},{9,8},{10,9... | collective-permute-start | bytes 1572872 | tf_op jit(solution)/shard_map/ppermute | solution.py:193
  20.0 1.9 %collective-permute-start.2 = (f32[128,1024]{1,0:T(8,128)}, f32[128,1024]{1,0:T(8,128)S(1)}, u32[]{:S(2)}, u32[]{:S(2)}) collective-permute-start(f32[128,1024]{1,0:T(8,128)} %refs_1_.1), channel_id=1, source_target_pairs={{8,1},{9,2},{10,3},{11,4},{12,5},{13,6},{14,7},{15,0},{0,15},{1,8}... | collective-permute-start | bytes 1572872 | tf_op jit(solution)/shard_map/ppermute | solution.py:193
  21.9 11.5 %collective-permute-done.1.refs_3_ = f32[128,1024]{1,0:T(8,128)S(1)} collective-permute-done((f32[128,1024]{1,0:T(8,128)}, f32[128,1024]{1,0:T(8,128)S(1)}, u32[]{:S(2)}, u32[]{:S(2)}) %collective-permute-start.1) | collective-permute-done | bytes 524320 | tf_op jit(solution)/shard_map/ppermute | solution.py:193
  35.5 1.9 %collective-permute-start.4 = (f32[128,1024]{1,0:T(8,128)S(1)}, f32[128,1024]{1,0:T(8,128)S(1)}, u32[]{:S(2)}, u32[]{:S(2)}) collective-permute-start(f32[128,1024]{1,0:T(8,128)S(1)} %collective-permute-done.2.refs_4_), channel_id=1, source_target_pairs={{0,1},{1,2},{2,3},{3,4},{4,5},{5,6},{6,7},{7,0},{8,15},{9,8},{10,9... | collective-permute-start | bytes 1572872 | tf_op jit(solution)/shard_map/ppermute | solution.py:193
  37.4 8.3 %collective-permute-done.3.refs_5_ = f32[128,1024]{1,0:T(8,128)S(1)} collective-permute-done((f32[128,1024]{1,0:T(8,128)S(1)}, f32[128,1024]{1,0:T(8,128)S(1)}, u32[]{:S(2)}, u32[]{:S(2)}) %collective-permute-start.3) | collective-permute-done | bytes 524320 | tf_op jit(solution)/shard_map/ppermute | solution.py:193
  47.6 3.7 %collective-permute-done.4.refs_6_ = f32[128,1024]{1,0:T(8,128)S(1)} collective-permute-done((f32[128,1024]{1,0:T(8,128)S(1)}, f32[128,1024]{1,0:T(8,128)S(1)}, u32[]{:S(2)}, u32[]{:S(2)}) %collective-permute-start.4) | collective-permute-done | bytes 524320 | tf_op jit(solution)/shard_map/ppermute | solution.py:193
  51.3 1.9 %collective-permute-start.6 = (f32[128,1024]{1,0:T(8,128)S(1)}, f32[128,1024]{1,0:T(8,128)S(1)}, u32[]{:S(2)}, u32[]{:S(2)}) collective-permute-start(f32[128,1024]{1,0:T(8,128)S(1)} %collective-permute-done.4.refs_6_), channel_id=1, source_target_pairs={{0,1},{1,2},{2,3},{3,4},{4,5},{5,6},{6,7},{7,0},{8,15},{9,8},{10,9... | collective-permute-start | bytes 1572872 | tf_op jit(solution)/shard_map/ppermute | solution.py:193
  53.2 4.7 %collective-permute-done.5.refs_7_ = f32[128,1024]{1,0:T(8,128)S(1)} collective-permute-done((f32[128,1024]{1,0:T(8,128)S(1)}, f32[128,1024]{1,0:T(8,128)S(1)}, u32[]{:S(2)}, u32[]{:S(2)}) %collective-permute-start.5) | collective-permute-done | bytes 524320 | tf_op jit(solution)/shard_map/ppermute | solution.py:193
  58.0 1.9 %collective-permute-start.8 = (f32[128,1024]{1,0:T(8,128)S(1)}, f32[128,1024]{1,0:T(8,128)S(1)}, u32[]{:S(2)}, u32[]{:S(2)}) collective-permute-start(f32[128,1024]{1,0:T(8,128)S(1)} %collective-permute-done.5.refs_7_), channel_id=1, source_target_pairs={{0,1},{1,2},{2,3},{3,4},{4,5},{5,6},{6,7},{7,0},{8,15},{9,8},{10,9... | collective-permute-start | bytes 1572872 | tf_op jit(solution)/shard_map/ppermute | solution.py:193
  61.5 1.9 %collective-permute-start.7 = (f32[512,1024]{1,0:T(8,128)}, f32[512,1024]{1,0:T(8,128)}, u32[]{:S(2)}, u32[]{:S(2)}) collective-permute-start(f32[512,1024]{1,0:T(8,128)} %pad_maximum_fusion), channel_id=1, source_target_pairs={{0,8},{8,0},{1,9},{9,1},{2,10},{10,2},{3,11},{11,3},{4,12},{12,4},... | collective-permute-start | bytes 6291464 | tf_op jit(solution)/shard_map/ppermute | solution.py:185
  63.6 6.7 %collective-permute-done.8.refs_11_ = f32[128,1024]{1,0:T(8,128)S(1)} collective-permute-done((f32[128,1024]{1,0:T(8,128)S(1)}, f32[128,1024]{1,0:T(8,128)S(1)}, u32[]{:S(2)}, u32[]{:S(2)}) %collective-permute-start.8) | collective-permute-done | bytes 524320 | tf_op jit(solution)/shard_map/ppermute | solution.py:193
  71.6 1.9 %collective-permute-start.9 = (f32[384,1024]{1,0:T(8,128)}, f32[384,1024]{1,0:T(8,128)}, u32[]{:S(2)}, u32[]{:S(2)}) collective-permute-start(f32[384,1024]{1,0:T(8,128)} %pad_maximum_fusion.1), channel_id=1, source_target_pairs={{0,8},{8,0},{1,9},{9,1},{2,10},{10,2},{3,11},{11,3},{4,12},{12,4},... | collective-permute-start | bytes 4718600 | tf_op jit(solution)/shard_map/ppermute | solution.py:185
  73.6 2.4 %collective-permute-start = (f32[128,1024]{1,0:T(8,128)}, f32[128,1024]{1,0:T(8,128)}, u32[]{:S(2)}, u32[]{:S(2)}) collective-permute-start(f32[128,1024]{1,0:T(8,128)} %refs_1_.1), channel_id=1, source_target_pairs={{0,8},{8,0},{1,9},{9,1},{2,10},{10,2},{3,11},{11,3},{4,12},{12,4},... | collective-permute-start | bytes 1572872 | tf_op jit(solution)/shard_map/ppermute | solution.py:185
  76.1 4.3 %spread.1.refs_0_ = bf16[1024,2176]{1,0:T(8,128)(2,1)S(1)} custom-call(f32[32,136,128]{2,1,0:T(8,128)S(1)} %all-to-all-done.got_ref), custom_call_target="tpu_custom_call" | custom-call | bytes 8388608 | tf_op jit(solution)/shard_map/spread/pallas_call | solution.py:119
  80.4 5.8 %product.2 = (f32[128,1024]{1,0:T(8,128)S(1)}, f32[128,1024]{1,0:T(8,128)S(1)}, bf16[2048,1024]{1,0:T(8,128)(2,1)S(1)}, bf16[2048,1024]{1,0:T(8,128)(2,1)S(1)}) custom-call(bf16[1024,2176]{1,0:T(8,128)(2,1)S(1)} %spread.1.refs_0_, f32[128,1024]{1,0:T(8,128)} %refs_1_.1, f32[128,1024]{1,0:T(8,128)} %collective-permute-done.refs_2_, ...), custom_call_target="tpu_custom_call" | custom-call | flops 3221225472 | bytes 4194304 | tf_op jit(solution)/shard_map/product/pallas_call | solution.py:167
  86.2 5.2 %collective-permute-start.10 = (f32[128,1024]{1,0:T(8,128)S(1)}, f32[128,1024]{1,0:T(8,128)S(1)}, u32[]{:S(2)}, u32[]{:S(2)}) collective-permute-start(f32[128,1024]{1,0:T(8,128)S(1)} %get-tuple-element.14), channel_id=1, source_target_pairs={{0,256},{128,384},{256,0},{384,128},{1,257},{129,385},{257,1},{385... | collective-permute-start | bytes 1572872 | tf_op jit(solution)/shard_map/ppermute | solution.py:232
  91.5 2.5 %collective-permute-start.11 = (f32[128,1024]{1,0:T(8,128)S(1)}, f32[128,1024]{1,0:T(8,128)S(1)}, u32[]{:S(2)}, u32[]{:S(2)}) collective-permute-start(f32[128,1024]{1,0:T(8,128)S(1)} %get-tuple-element.15), channel_id=1, source_target_pairs={{0,128},{128,256},{256,384},{384,0},{1,129},{129,257},{257,385},{3... | collective-permute-start | bytes 1572872 | tf_op jit(solution)/shard_map/ppermute | solution.py:233
  94.0 3.4 %product.3 = (f32[128,1024]{1,0:T(8,128)S(1)}, f32[128,1024]{1,0:T(8,128)S(1)}) custom-call(bf16[1024,2176]{1,0:T(8,128)(2,1)S(1)} %spread.1.refs_0_, bf16[2048,1024]{1,0:T(8,128)(2,1)S(1)} %get-tuple-element.16.refs_1_, bf16[2048,1024]{1,0:T(8,128)(2,1)S(1)} %get-tuple-element.17.refs_2_), custom_call_target="tpu_custom_call" | custom-call | flops 3221225472 | bytes 4194304 | tf_op jit(solution)/shard_map/product/pallas_call | solution.py:167
  97.4 4.5 %collective-permute-start.12 = (f32[128,1024]{1,0:T(8,128)S(1)}, f32[128,1024]{1,0:T(8,128)S(1)}, u32[]{:S(2)}, u32[]{:S(2)}) collective-permute-start(f32[128,1024]{1,0:T(8,128)S(1)} %get-tuple-element.22), channel_id=1, source_target_pairs={{0,384},{128,0},{256,128},{384,256},{1,385},{129,1},{257,129},{385... | collective-permute-start | bytes 1572872 | tf_op jit(solution)/shard_map/ppermute | solution.py:236
  101.9 2.5 %collective-permute-done.10 = f32[128,1024]{1,0:T(8,128)S(1)} collective-permute-done((f32[128,1024]{1,0:T(8,128)S(1)}, f32[128,1024]{1,0:T(8,128)S(1)}, u32[]{:S(2)}, u32[]{:S(2)}) %collective-permute-start.10) | collective-permute-done | bytes 524320 | tf_op jit(solution)/shard_map/ppermute | solution.py:232
  104.5 10.3 %collective-permute-done.11 = f32[128,1024]{1,0:T(8,128)S(1)} collective-permute-done((f32[128,1024]{1,0:T(8,128)S(1)}, f32[128,1024]{1,0:T(8,128)S(1)}, u32[]{:S(2)}, u32[]{:S(2)}) %collective-permute-start.11) | collective-permute-done | bytes 524320 | tf_op jit(solution)/shard_map/ppermute | solution.py:233
  115.2 24.1 %all_to_all.10 = f32[8,16,1024]{2,1,0:T(8,128)S(1)} all-to-all(f32[8,16,1024]{2,1,0:T(8,128)S(1)} %bitcast.3), channel_id=1, replica_groups=mesh['x'=4,'z'=8,'core'=2,'grp'=8] {'z'}, dimensions={0} | all-to-all | bytes 1048576 | tf_op jit(solution)/shard_map/all_to_all | solution.py:239
  (33 shorter events, 8.3 us)
Async XLA Ops:
  4.2 71.8 %all-to-all-start = ((f32[32,136,128]{2,1,0:T(8,128)}), f32[32,136,128]{2,1,0:T(8,128)S(1)}, u32[]{:S(2)}, u32[]{:S(2)}) async-start(f32[32,136,128]{2,1,0:T(8,128)} %pack.1), calls=%async_computation | async-start | bytes 4456448 | tf_op jit(solution)/shard_map/all_to_all | solution.py:228
  17.4 16.0 %collective-permute-start.1 = (f32[128,1024]{1,0:T(8,128)}, f32[128,1024]{1,0:T(8,128)S(1)}, u32[]{:S(2)}, u32[]{:S(2)}) collective-permute-start(f32[128,1024]{1,0:T(8,128)} %refs_1_.1), channel_id=1, source_target_pairs={{0,1},{1,2},{2,3},{3,4},{4,5},{5,6},{6,7},{7,0},{8,15},{9,8},{10,9... | collective-permute-start | bytes 1572872 | tf_op jit(solution)/shard_map/ppermute | solution.py:193
  20.0 15.5 %collective-permute-start.2 = (f32[128,1024]{1,0:T(8,128)}, f32[128,1024]{1,0:T(8,128)S(1)}, u32[]{:S(2)}, u32[]{:S(2)}) collective-permute-start(f32[128,1024]{1,0:T(8,128)} %refs_1_.1), channel_id=1, source_target_pairs={{8,1},{9,2},{10,3},{11,4},{12,5},{13,6},{14,7},{15,0},{0,15},{1,8}... | collective-permute-start | bytes 1572872 | tf_op jit(solution)/shard_map/ppermute | solution.py:193
  33.4 38.2 %copy-start.2 = (f32[128,1024]{1,0:T(8,128)}, f32[128,1024]{1,0:T(8,128)S(1)}, u32[]{:S(2)}) copy-start(f32[128,1024]{1,0:T(8,128)S(1)} %collective-permute-done.1.refs_3_) | copy-start | bytes 1572868
  33.4 12.3 %collective-permute-start.3 = (f32[128,1024]{1,0:T(8,128)S(1)}, f32[128,1024]{1,0:T(8,128)S(1)}, u32[]{:S(2)}, u32[]{:S(2)}) collective-permute-start(f32[128,1024]{1,0:T(8,128)S(1)} %collective-permute-done.1.refs_3_), channel_id=1, source_target_pairs={{0,1},{1,2},{2,3},{3,4},{4,5},{5,6},{6,7},{7,0},{8,15},{9,8},{10,9... | collective-permute-start | bytes 1572872 | tf_op jit(solution)/shard_map/ppermute | solution.py:193
  35.5 36.1 %copy-start.4 = (f32[128,1024]{1,0:T(8,128)}, f32[128,1024]{1,0:T(8,128)S(1)}, u32[]{:S(2)}) copy-start(f32[128,1024]{1,0:T(8,128)S(1)} %collective-permute-done.2.refs_4_) | copy-start | bytes 1572868
  35.5 15.8 %collective-permute-start.4 = (f32[128,1024]{1,0:T(8,128)S(1)}, f32[128,1024]{1,0:T(8,128)S(1)}, u32[]{:S(2)}, u32[]{:S(2)}) collective-permute-start(f32[128,1024]{1,0:T(8,128)S(1)} %collective-permute-done.2.refs_4_), channel_id=1, source_target_pairs={{0,1},{1,2},{2,3},{3,4},{4,5},{5,6},{6,7},{7,0},{8,15},{9,8},{10,9... | collective-permute-start | bytes 1572872 | tf_op jit(solution)/shard_map/ppermute | solution.py:193
  45.7 26.0 %copy-start.6 = (f32[128,1024]{1,0:T(8,128)}, f32[128,1024]{1,0:T(8,128)S(1)}, u32[]{:S(2)}) copy-start(f32[128,1024]{1,0:T(8,128)S(1)} %collective-permute-done.3.refs_5_) | copy-start | bytes 1572868
  45.7 12.3 %collective-permute-start.5 = (f32[128,1024]{1,0:T(8,128)S(1)}, f32[128,1024]{1,0:T(8,128)S(1)}, u32[]{:S(2)}, u32[]{:S(2)}) collective-permute-start(f32[128,1024]{1,0:T(8,128)S(1)} %collective-permute-done.3.refs_5_), channel_id=1, source_target_pairs={{0,1},{1,2},{2,3},{3,4},{4,5},{5,6},{6,7},{7,0},{8,15},{9,8},{10,9... | collective-permute-start | bytes 1572872 | tf_op jit(solution)/shard_map/ppermute | solution.py:193
  51.3 20.3 %copy-start.8 = (f32[128,1024]{1,0:T(8,128)}, f32[128,1024]{1,0:T(8,128)S(1)}, u32[]{:S(2)}) copy-start(f32[128,1024]{1,0:T(8,128)S(1)} %collective-permute-done.4.refs_6_) | copy-start | bytes 1572868
  51.3 12.3 %collective-permute-start.6 = (f32[128,1024]{1,0:T(8,128)S(1)}, f32[128,1024]{1,0:T(8,128)S(1)}, u32[]{:S(2)}, u32[]{:S(2)}) collective-permute-start(f32[128,1024]{1,0:T(8,128)S(1)} %collective-permute-done.4.refs_6_), channel_id=1, source_target_pairs={{0,1},{1,2},{2,3},{3,4},{4,5},{5,6},{6,7},{7,0},{8,15},{9,8},{10,9... | collective-permute-start | bytes 1572872 | tf_op jit(solution)/shard_map/ppermute | solution.py:193
  58.0 12.3 %collective-permute-start.8 = (f32[128,1024]{1,0:T(8,128)S(1)}, f32[128,1024]{1,0:T(8,128)S(1)}, u32[]{:S(2)}, u32[]{:S(2)}) collective-permute-start(f32[128,1024]{1,0:T(8,128)S(1)} %collective-permute-done.5.refs_7_), channel_id=1, source_target_pairs={{0,1},{1,2},{2,3},{3,4},{4,5},{5,6},{6,7},{7,0},{8,15},{9,8},{10,9... | collective-permute-start | bytes 1572872 | tf_op jit(solution)/shard_map/ppermute | solution.py:193
  61.5 18.8 %collective-permute-start.7 = (f32[512,1024]{1,0:T(8,128)}, f32[512,1024]{1,0:T(8,128)}, u32[]{:S(2)}, u32[]{:S(2)}) collective-permute-start(f32[512,1024]{1,0:T(8,128)} %pad_maximum_fusion), channel_id=1, source_target_pairs={{0,8},{8,0},{1,9},{9,1},{2,10},{10,2},{3,11},{11,3},{4,12},{12,4},... | collective-permute-start | bytes 6291464 | tf_op jit(solution)/shard_map/ppermute | solution.py:185
  70.2 3.3 %copy-start = (f32[128,1024]{1,0:T(8,128)}, f32[128,1024]{1,0:T(8,128)S(1)}, u32[]{:S(2)}) copy-start(f32[128,1024]{1,0:T(8,128)S(1)} %collective-permute-done.8.refs_11_) | copy-start | bytes 1572868
  71.6 8.7 %collective-permute-start.9 = (f32[384,1024]{1,0:T(8,128)}, f32[384,1024]{1,0:T(8,128)}, u32[]{:S(2)}, u32[]{:S(2)}) collective-permute-start(f32[384,1024]{1,0:T(8,128)} %pad_maximum_fusion.1), channel_id=1, source_target_pairs={{0,8},{8,0},{1,9},{9,1},{2,10},{10,2},{3,11},{11,3},{4,12},{12,4},... | collective-permute-start | bytes 4718600 | tf_op jit(solution)/shard_map/ppermute | solution.py:185
  73.6 6.8 %collective-permute-start = (f32[128,1024]{1,0:T(8,128)}, f32[128,1024]{1,0:T(8,128)}, u32[]{:S(2)}, u32[]{:S(2)}) collective-permute-start(f32[128,1024]{1,0:T(8,128)} %refs_1_.1), channel_id=1, source_target_pairs={{0,8},{8,0},{1,9},{9,1},{2,10},{10,2},{3,11},{11,3},{4,12},{12,4},... | collective-permute-start | bytes 1572872 | tf_op jit(solution)/shard_map/ppermute | solution.py:185
  76.0 4.4 %copy-start.1 = (f32[128,1024]{1,0:T(8,128)S(1)}, f32[128,1024]{1,0:T(8,128)}, u32[]{:S(2)}) copy-start(f32[128,1024]{1,0:T(8,128)} %copy-done) | copy-start | bytes 1572868
  76.0 4.4 %copy-start.3 = (f32[128,1024]{1,0:T(8,128)S(1)}, f32[128,1024]{1,0:T(8,128)}, u32[]{:S(2)}) copy-start(f32[128,1024]{1,0:T(8,128)} %copy-done.2) | copy-start | bytes 1572868
  76.0 4.4 %copy-start.5 = (f32[128,1024]{1,0:T(8,128)S(1)}, f32[128,1024]{1,0:T(8,128)}, u32[]{:S(2)}) copy-start(f32[128,1024]{1,0:T(8,128)} %copy-done.4) | copy-start | bytes 1572868
  76.0 4.4 %copy-start.7 = (f32[128,1024]{1,0:T(8,128)S(1)}, f32[128,1024]{1,0:T(8,128)}, u32[]{:S(2)}) copy-start(f32[128,1024]{1,0:T(8,128)} %copy-done.6) | copy-start | bytes 1572868
  76.0 4.4 %copy-start.9 = (f32[128,1024]{1,0:T(8,128)S(1)}, f32[128,1024]{1,0:T(8,128)}, u32[]{:S(2)}) copy-start(f32[128,1024]{1,0:T(8,128)} %copy-done.8) | copy-start | bytes 1572868
  86.2 18.2 %collective-permute-start.10 = (f32[128,1024]{1,0:T(8,128)S(1)}, f32[128,1024]{1,0:T(8,128)S(1)}, u32[]{:S(2)}, u32[]{:S(2)}) collective-permute-start(f32[128,1024]{1,0:T(8,128)S(1)} %get-tuple-element.14), channel_id=1, source_target_pairs={{0,256},{128,384},{256,0},{384,128},{1,257},{129,385},{257,1},{385... | collective-permute-start | bytes 1572872 | tf_op jit(solution)/shard_map/ppermute | solution.py:232
  91.5 23.3 %collective-permute-start.11 = (f32[128,1024]{1,0:T(8,128)S(1)}, f32[128,1024]{1,0:T(8,128)S(1)}, u32[]{:S(2)}, u32[]{:S(2)}) collective-permute-start(f32[128,1024]{1,0:T(8,128)S(1)} %get-tuple-element.15), channel_id=1, source_target_pairs={{0,128},{128,256},{256,384},{384,0},{1,129},{129,257},{257,385},{3... | collective-permute-start | bytes 1572872 | tf_op jit(solution)/shard_map/ppermute | solution.py:233
  97.4 17.7 %collective-permute-start.12 = (f32[128,1024]{1,0:T(8,128)S(1)}, f32[128,1024]{1,0:T(8,128)S(1)}, u32[]{:S(2)}, u32[]{:S(2)}) collective-permute-start(f32[128,1024]{1,0:T(8,128)S(1)} %get-tuple-element.22), channel_id=1, source_target_pairs={{0,384},{128,0},{256,128},{384,256},{1,385},{129,1},{257,129},{385... | collective-permute-start | bytes 1572872 | tf_op jit(solution)/shard_map/ppermute | solution.py:236
